TPU v7x, 32 devices: a whole 2x2x4 slice. The times are simulated.
32 devices in a mesh: dp: 8 (over z, x), tensor: 4 (over y, core).
Axes of the slice: x: 2, y: 2, z: 4, core: 2. Of those that a mesh axis runs over, the one named last changes fastest.
Arguments:
- layer_input: bfloat16 [16, 512, 768], P('dp', 'tensor'), may hold values from -6 to 6
- doc_lengths: int32 [16, 8], P('dp'), may hold values from 1 to 256, 512 in all within a row
- norm1_gain: float32 [768], replicated, may hold values from 0.5 to 1.5
- alpha_raw: float32 [16, 768], replicated, may hold values from -4.5 to 0.5
- delta_raw: float32 [16, 768], replicated, may hold values from -4.5 to 0.5
- ema_beta: float32 [16, 768], replicated, may hold values from -5 to 5
- ema_eta: float32 [16, 768], replicated, may hold values from -1.5 to 1.5
- ema_omega: float32 [768], replicated, may hold values from -4 to 4
- w_z: bfloat16 [768, 128], replicated, may hold values from -0.21875 to 0.21875
- q_gain: float32 [128], replicated, may hold values from -3.2 to 3.2
- q_bias: float32 [128], replicated, may hold values from -4 to 4
- k_gain: float32 [128], replicated, may hold values from -3.2 to 3.2
- w_value: bfloat16 [768, 1536], P(None, 'tensor'), may hold values from -0.21875 to 0.21875
- w_reset: bfloat16 [768, 1536], P(None, 'tensor'), may hold values from -0.21875 to 0.21875
- w_update: bfloat16 [768, 768], replicated, may hold values from -0.21875 to 0.21875
- w_hidden: bfloat16 [768, 768], P('tensor'), may hold values from -0.21875 to 0.21875
- w_out: bfloat16 [1536, 768], P('tensor'), may hold values from -0.625 to 0.625
- norm2_gain: float32 [768], replicated, may hold values from 0.5 to 1.5
- w_ffn_in: bfloat16 [768, 1536], P(None, 'tensor'), may hold values from -0.21875 to 0.21875
- w_ffn_out: bfloat16 [1536, 768], P('tensor'), may hold values from -0.15625 to 0.15625
- cotangent: bfloat16 [16, 512, 768], P('dp', 'tensor'), may hold values from -6 to 6
Outputs:
- layer_output: bfloat16 [16, 512, 768], P('dp', 'tensor')
- input_grad: bfloat16 [16, 512, 768], P('dp', 'tensor')
- norm1_gain_grad: float32 [768], replicated
- alpha_raw_grad: float32 [16, 768], replicated
- delta_raw_grad: float32 [16, 768], replicated
- ema_beta_grad: float32 [16, 768], replicated
- ema_eta_grad: float32 [16, 768], replicated
- ema_omega_grad: float32 [768], replicated
- w_z_grad: float32 [768, 128], replicated
- q_gain_grad: float32 [128], replicated
- q_bias_grad: float32 [128], replicated
- k_gain_grad: float32 [128], replicated
- w_value_grad: float32 [768, 1536], P(None, 'tensor')
- w_reset_grad: float32 [768, 1536], P(None, 'tensor')
- w_update_grad: float32 [768, 768], replicated
- w_hidden_grad: float32 [768, 768], P('tensor')
- w_out_grad: float32 [1536, 768], P('tensor')
- norm2_gain_grad: float32 [768], replicated
- w_ffn_in_grad: float32 [768, 1536], P(None, 'tensor')
- w_ffn_out_grad: float32 [1536, 768], P('tensor')
Inputs may be any that keep to these rules, and one draw needn't show every extreme that they name: `doc_lengths`: the 8 lengths of each row sum to 512, and the longest of each row is 256.
All inputs are finite; a program needn't handle non-finite values.
Results may differ from a plain program's by a relative error of at most 0.017.
Values may be sent and summed in bfloat16 or wider, within the bound.
No kernel may reach another device: no remote copies, remote signals or barrier semaphores. Data moves between devices by JAX's collectives and lax.ppermute only.
A program may use at most 256 MiB of HBM per device.

v0:
```python
import functools

import jax
import jax.numpy as jnp
from jax import lax
from jax.experimental import pallas as pl
from jax.experimental.pallas import tpu as pltpu
from jax.sharding import PartitionSpec as P

STRETCH = 128
LANES = 128
CHUNKS = 8
F32 = jnp.float32
LOW = jnp.bfloat16


def silu(v):
    return v * jax.nn.sigmoid(v)


def silu_slope(v):
    s = jax.nn.sigmoid(v)
    return s * (1.0 + v * (1.0 - s))


def dot(a, b):
    return jnp.dot(a, b, preferred_element_type=F32)


def dot_rows(a, b):
    return lax.dot_general(a, b, (((0,), (0,)), ((), ())), preferred_element_type=F32)


def dot_cols(a, b):
    return lax.dot_general(a, b, (((1,), (1,)), ((), ())), preferred_element_type=F32)


def norm_parts(v):
    center = v - jnp.mean(v, -1, keepdims=True)
    scale = lax.rsqrt(jnp.mean(center * center, -1, keepdims=True) + 1e-05)
    return center * scale, scale


def norm_back(grad, hat, scale):
    return scale * (
        grad - jnp.mean(grad, -1, keepdims=True) - hat * jnp.mean(grad * hat, -1, keepdims=True)
    )


def call(kernel, outs, args, flops, scratch=(), smem=(), limit=48 << 20):
    specs = [
        pl.BlockSpec(memory_space=pltpu.SMEM if i in smem else pltpu.VMEM)
        for i in range(len(args))
    ]
    outs = [jax.ShapeDtypeStruct(s, d) for s, d in outs]
    size = sum(a.size * a.dtype.itemsize for a in args) + sum(
        o.size * o.dtype.itemsize for o in outs
    )
    return pl.pallas_call(
        kernel,
        out_shape=outs,
        in_specs=specs,
        out_specs=[pl.BlockSpec(memory_space=pltpu.VMEM) for _ in outs],
        scratch_shapes=list(scratch),
        compiler_params=pltpu.CompilerParams(vmem_limit_bytes=limit),
        cost_estimate=pl.CostEstimate(flops=int(flops), bytes_accessed=int(size), transcendentals=0),
    )(*args)


def bcast(ref, row, lanes):
    return jnp.broadcast_to(ref[pl.ds(row, 1), lanes], (CHUNKS, LANES))


def shifted(v, by, fill):
    place = lax.broadcasted_iota(jnp.int32, v.shape, 0)
    if by > 0:
        return jnp.where(place >= by, pltpu.roll(v, by, 0), fill)
    return jnp.where(place < CHUNKS + by, pltpu.roll(v, CHUNKS + by, 0), fill)


def power(v, n):
    out = None
    while n:
        if n & 1:
            out = v if out is None else out * v
        n >>= 1
        if n:
            v = v * v
    return out


def chunk_powers(base, order):
    place = lax.broadcasted_iota(jnp.int32, base.shape, 0)
    place = place if order > 0 else (CHUNKS - 1) - place
    out = jnp.where(place & 1 == 1, base, 1.0)
    base = base * base
    out = out * jnp.where(place & 2 == 2, base, 1.0)
    base = base * base
    return out * jnp.where(place & 4 == 4, base, 1.0)


def rate_tables(al_ref, de_ref, be_ref, dec_ref, drv_ref):
    alpha = jax.nn.sigmoid(al_ref[...])
    dec_ref[...] = 1.0 - alpha * jax.nn.sigmoid(de_ref[...])
    drv_ref[...] = alpha * be_ref[...]


def steps_of(ref, base, steps):
    return [ref[pl.ds(base + k, CHUNKS, stride=steps), :] for k in range(steps)]


def into_slabs(ref, v):
    tokens = v.shape[0]
    for j in range(v.shape[1] // LANES):
        ref[j * tokens : (j + 1) * tokens, :] = v[:, j * LANES : (j + 1) * LANES]


def from_slabs(v, tokens):
    return jnp.concatenate(
        [v[at : at + tokens] for at in range(0, v.shape[0], tokens)], 1
    )


def product(values):
    out = values[0]
    for v in values[1:]:
        out = out * v
    return out


def first_pass(rows, x_ref, g_ref, al_ref, de_ref, be_ref, keep_ref, normed_ref, low_ref, init_ref, last_ref, dec_ref, drv_ref):
    hat, _ = norm_parts(x_ref[...].astype(F32))
    normed = hat * g_ref[...]
    into_slabs(normed_ref, normed)
    low_ref[...] = normed.astype(LOW)
    rate_tables(al_ref, de_ref, be_ref, dec_ref, drv_ref)
    dims, width = al_ref.shape
    tokens = x_ref.shape[0]
    length = tokens // rows
    steps = length // CHUNKS

    def lane(j, carry):
        lanes = pl.ds(pl.multiple_of(j * LANES, LANES), LANES)
        for row in range(rows):
            token = steps_of(normed_ref, j * tokens + row * length, steps)
            kept = steps_of(keep_ref, row * length, steps)
            whole = product(kept)
            for n in range(dims):
                d, b = bcast(dec_ref, n, lanes), bcast(drv_ref, n, lanes)
                s = b * token[0]
                for k in range(1, steps):
                    s = (kept[k] * d) * s + b * token[k]
                a = power(d, steps) * whole
                for by in (1, 2, 4):
                    s = s + a * shifted(s, by, 0.0)
                    a = a * shifted(a, by, 1.0)
                init_ref[pl.ds((row * dims + n) * CHUNKS, CHUNKS), lanes] = shifted(s, 1, 0.0)
                last_ref[pl.ds(row * dims + n, 1), lanes] = s[CHUNKS - 1 :, :]
        return carry

    lax.fori_loop(0, width // LANES, lane, 0)


def second_pass(rows, normed_ref, init_ref, f1_ref, f2_ref, keep_ref, flag_ref, al_ref, de_ref, be_ref, eta_ref, om_ref, wz_ref, wu_ref, qg_ref, qb_ref, kg_ref, mask_ref, pre_ref, mixed_ref, zpre_ref, gate_ref, probs_ref, dec_ref, drv_ref):
    rate_tables(al_ref, de_ref, be_ref, dec_ref, drv_ref)
    dims, width = al_ref.shape
    tokens = keep_ref.shape[0]
    length = tokens // rows
    steps = length // CHUNKS

    def lane(j, carry):
        lanes = pl.ds(pl.multiple_of(j * LANES, LANES), LANES)
        omega = bcast(om_ref, 0, lanes)
        for row in range(rows):
            base = j * tokens + row * length
            token = steps_of(normed_ref, base, steps)
            kept = steps_of(keep_ref, row * length, steps)
            reach = shifted(product(kept), 1, 1.0)
            for by in (1, 2, 4):
                reach = reach * shifted(reach, by, 1.0)
            flag = bcast(flag_ref, row, pl.ds(0, LANES))
            total = [omega * t for t in token]
            for n in range(dims):
                d, b, e = bcast(dec_ref, n, lanes), bcast(drv_ref, n, lanes), bcast(eta_ref, n, lanes)
                chunk = power(d, steps)
                entering = bcast(f1_ref, row * dims + n, lanes) + (
                    power(chunk, CHUNKS) * flag
                ) * bcast(f2_ref, row * dims + n, lanes)
                s = (
                    init_ref[pl.ds((row * dims + n) * CHUNKS, CHUNKS), lanes]
                    + reach * chunk_powers(chunk, 1) * entering
                )
                for k in range(steps):
                    s = (kept[k] * d) * s + b * token[k]
                    total[k] = total[k] + e * s
            for k in range(steps):
                pre_ref[pl.ds(base + k, CHUNKS, stride=steps), :] = total[k]
        return carry

    lax.fori_loop(0, width // LANES, lane, 0)
    mixed_low = from_slabs(silu(pre_ref[...]).astype(LOW), tokens)
    mixed_ref[...] = mixed_low
    z_pre = dot(mixed_low, wz_ref[...])
    zpre_ref[...] = z_pre
    gate_ref[...] = jax.nn.sigmoid(dot(mixed_low, wu_ref[...]))
    z_low = silu(z_pre).astype(LOW).astype(F32)
    queries = (z_low * qg_ref[...] + qb_ref[...]).astype(LOW)
    keys = (z_low * kg_ref[...]).astype(LOW)
    for start in range(0, z_low.shape[0], STRETCH):
        block = slice(start, start + STRETCH)
        scores = dot_cols(queries[block], keys[block]) * z_low.shape[1] ** (-0.5)
        scores = jnp.where(mask_ref[block, :] > 0.5, scores, -1e30)
        shift = jnp.exp(scores - jnp.max(scores, -1, keepdims=True))
        probs_ref[block, :] = shift / jnp.sum(shift, -1, keepdims=True)


def value_part(normed_ref, mixed_ref, probs_ref, wa_ref, wb_ref, vpre_ref, rpre_ref, att_ref, united_ref):
    depth = normed_ref.shape[1]
    tokens = normed_ref.shape[0]
    for i, w_ref in enumerate((wa_ref, wb_ref)):
        value_pre = dot(normed_ref[...], w_ref[:depth, :])
        reset_pre = dot(mixed_ref[...], w_ref[depth:, :])
        vpre_ref[i] = value_pre
        rpre_ref[i] = reset_pre
        values = silu(value_pre).astype(LOW)
        for start in range(0, tokens, STRETCH):
            block = slice(start, start + STRETCH)
            att_ref[i, block, :] = dot(probs_ref[block, :].astype(LOW), values[block])
        united_ref[i] = (silu(reset_pre) * att_ref[i]).astype(LOW)


def blend_part(offs_ref, x_ref, mixed_ref, gate_ref, u0_ref, u1_ref, g0_ref, g1_ref, g2_ref, g3_ref, gain_ref, hpre_ref, blended_ref, second_ref, whid_ref):
    cols = whid_ref.shape[0] // 4
    packs = (g0_ref, g1_ref, g2_ref, g3_ref)
    for r, g_ref in enumerate(packs):
        whid_ref[pl.ds(pl.multiple_of(offs_ref[r], 64), cols), :] = g_ref[:cols, :]
    hidden_pre = dot(mixed_ref[...], whid_ref[...])
    for r, g_ref in enumerate(packs):
        united = (u0_ref, u1_ref)[r // 2][r % 2]
        hidden_pre = hidden_pre + dot(united, g_ref[cols:, :])
    hpre_ref[...] = hidden_pre
    x = x_ref[...].astype(F32)
    blended = x + gate_ref[...] * (silu(hidden_pre) - x)
    blended_ref[...] = blended
    hat, _ = norm_parts(blended)
    second_ref[...] = (hat * gain_ref[...]).astype(LOW)


def ffn_part(second_ref, cot_ref, ia_ref, ib_ref, oa_ref, ob_ref, out_ref, sg_ref, keep_ref, send_ref):
    second, cot = second_ref[...], cot_ref[...]
    depth, units = ia_ref.shape
    half = depth // 2
    for i, (in_ref, fo_ref, pack_ref) in enumerate(
        ((ia_ref, oa_ref, keep_ref), (ib_ref, ob_ref, send_ref))
    ):
        up_pre = dot(second, in_ref[...])
        activated = silu(up_pre).astype(LOW)
        up_grad = (dot_cols(cot, fo_ref[...]) * silu_slope(up_pre)).astype(LOW)
        out = dot(activated, fo_ref[...])
        back = dot_cols(up_grad, in_ref[...])
        out_ref[...] = out if i == 0 else out_ref[...] + out
        sg_ref[...] = back if i == 0 else sg_ref[...] + back
        kind = pack_ref.dtype
        pack_ref[:depth, :] = dot_rows(second, up_grad).astype(kind)
        for h in range(2):
            pack_ref[depth + h * units : depth + (h + 1) * units, :] = dot_rows(
                activated, cot[:, h * half : (h + 1) * half]
            ).astype(kind)


def blend_back(offs_ref, x_ref, cot_ref, blended_ref, s0_ref, s1_ref, o0_ref, o1_ref, hpre_ref, gate_ref, mixed_ref, gain_ref, wu_ref, whid_ref, y_ref, direct_ref, hidden_ref, mg_ref, gg_ref, keep_ref, send_ref, full_ref):
    blended = blended_ref[...]
    y_ref[...] = (blended + (o0_ref[...] + o1_ref[...])).astype(LOW)
    second_grad = s0_ref[...] + s1_ref[...]
    hat, scale = norm_parts(blended)
    gg_ref[...] = jnp.sum(second_grad * hat, 0, keepdims=True)
    grad = cot_ref[...].astype(F32) + norm_back(second_grad * gain_ref[...], hat, scale)
    gate, hidden_pre, x = gate_ref[...], hpre_ref[...], x_ref[...].astype(F32)
    direct_ref[...] = grad * (1.0 - gate)
    hidden_low = (grad * gate * silu_slope(hidden_pre)).astype(LOW)
    gate_low = (grad * (silu(hidden_pre) - x) * gate * (1.0 - gate)).astype(LOW)
    hidden_ref[...] = hidden_low
    mg_ref[...] = dot_cols(gate_low, wu_ref[...]) + dot_cols(hidden_low, whid_ref[...])
    width = x.shape[1]
    cols, half = width // 4, width // 2
    for i, low in enumerate((gate_low, hidden_low)):
        full_ref[...] = dot_rows(mixed_ref[...], low)
        for r in range(4):
            pack_ref = (keep_ref, send_ref)[r % 2]
            rows = pl.ds(pl.multiple_of(offs_ref[r], 64), cols)
            for h in range(2):
                at = (2 * i + h) * cols
                pack_ref[r // 2, at : at + cols, :] = full_ref[
                    rows, h * half : (h + 1) * half
                ].astype(pack_ref.dtype)


def value_back(hidden_ref, normed_ref, mixed_ref, probs_ref, vpre_ref, rpre_ref, att_ref, united_ref, ga_ref, gb_ref, wa_ref, wb_ref, ng_ref, mg_ref, pg_ref, keep_ref, send_ref):
    hidden, normed, mixed = hidden_ref[...], normed_ref[...], mixed_ref[...]
    tokens, depth = hidden.shape
    units = wa_ref.shape[1]
    cols = ga_ref.shape[0] - units
    half = depth // 2
    for i, (g_ref, w_ref, pack_ref) in enumerate(
        ((ga_ref, wa_ref, keep_ref), (gb_ref, wb_ref, send_ref))
    ):
        kind = pack_ref.dtype
        united_grad = dot_cols(hidden, g_ref[cols:, :])
        reset_pre, value_pre = rpre_ref[i], vpre_ref[i]
        reset_low = (united_grad * att_ref[i] * silu_slope(reset_pre)).astype(LOW)
        attended_low = (united_grad * silu(reset_pre)).astype(LOW)
        values = silu(value_pre).astype(LOW)
        parts = []
        for start in range(0, tokens, STRETCH):
            block = slice(start, start + STRETCH)
            parts.append(dot_rows(probs_ref[block, :].astype(LOW), attended_low[block]))
            back = dot_cols(attended_low[block], values[block])
            pg_ref[block, :] = back if i == 0 else pg_ref[block, :] + back
        value_low = (jnp.concatenate(parts, 0) * silu_slope(value_pre)).astype(LOW)
        into_normed = dot_cols(value_low, w_ref[:depth, :])
        into_mixed = dot_cols(reset_low, w_ref[depth:, :])
        ng_ref[...] = into_normed if i == 0 else ng_ref[...] + into_normed
        mg_ref[...] = into_mixed if i == 0 else mg_ref[...] + into_mixed
        pack_ref[:depth, :] = dot_rows(mixed, reset_low).astype(kind)
        for h in range(2):
            pack_ref[depth + h * units : depth + (h + 1) * units, :] = dot_rows(
                united_ref[i], hidden[:, h * half : (h + 1) * half]
            ).astype(kind)
        pack_ref[2 * depth :, :] = dot_rows(normed, value_low).astype(kind)


def third_pass(rows, zpre_ref, probs_ref, p0_ref, p1_ref, qg_ref, qb_ref, kg_ref, wz_ref, mixed_ref, m0_ref, m1_ref, m2_ref, pre_ref, keep_ref, al_ref, de_ref, pg_ref, dz_ref, small_ref, im_ref, iv_ref, lm_ref, lv_ref, qk_ref):
    z_pre = zpre_ref[...]
    z_low = silu(z_pre).astype(LOW).astype(F32)
    queries = (z_low * qg_ref[...] + qb_ref[...]).astype(LOW)
    keys = (z_low * kg_ref[...]).astype(LOW)
    for start in range(0, z_low.shape[0], STRETCH):
        block = slice(start, start + STRETCH)
        probs = probs_ref[block, :]
        grad = p0_ref[block, :] + p1_ref[block, :]
        grad = probs * (grad - jnp.sum(probs * grad, -1, keepdims=True)) * z_low.shape[1] ** (-0.5)
        high = grad.astype(LOW)
        rest = (grad - high.astype(F32)).astype(LOW)
        qk_ref[0, block, :] = dot(high, keys[block]) + dot(rest, keys[block])
        qk_ref[1, block, :] = dot_rows(high, queries[block]) + dot_rows(rest, queries[block])
    query_grad, key_grad = qk_ref[0], qk_ref[1]
    small_ref[...] = jnp.zeros_like(small_ref)
    small_ref[0:1, :] = jnp.sum(query_grad * z_low, 0, keepdims=True)
    small_ref[1:2, :] = jnp.sum(query_grad, 0, keepdims=True)
    small_ref[2:3, :] = jnp.sum(key_grad * z_low, 0, keepdims=True)
    z_grad = ((query_grad * qg_ref[...] + key_grad * kg_ref[...]) * silu_slope(z_pre)).astype(LOW)
    dz_ref[...] = dot_rows(mixed_ref[...], z_grad)
    mixed_grad = m0_ref[...] + m1_ref[...] + m2_ref[...] + dot_cols(z_grad, wz_ref[...])
    into_slabs(pg_ref, mixed_grad)
    pg_ref[...] = pg_ref[...] * silu_slope(pre_ref[...])
    dims, width = al_ref.shape
    tokens = z_pre.shape[0]
    length = tokens // rows
    steps = length // CHUNKS

    def lane(j, carry):
        lanes = pl.ds(pl.multiple_of(j * LANES, LANES), LANES)
        for row in range(rows):
            token = steps_of(pg_ref, j * tokens + row * length, steps)
            kept = steps_of(keep_ref, row * length, steps)
            whole = product(kept)
            for n in range(dims):
                alpha = jax.nn.sigmoid(bcast(al_ref, n, lanes))
                d = 1.0 - alpha * jax.nn.sigmoid(bcast(de_ref, n, lanes))
                mu = token[steps - 1]
                m = (kept[steps - 1] * d) * mu
                v = kept[steps - 1] * mu
                for k in range(steps - 2, -1, -1):
                    mu = token[k] + m
                    rate = kept[k] * d
                    m = rate * mu
                    v = kept[k] * mu + rate * v
                a = power(d, steps) * whole
                b = steps * power(d, steps - 1) * whole
                for by in (-1, -2, -4):
                    mp, vp = shifted(m, by, 0.0), shifted(v, by, 0.0)
                    ap, bp = shifted(a, by, 1.0), shifted(b, by, 0.0)
                    v = v + a * vp + b * mp
                    m = m + a * mp
                    b = a * bp + b * ap
                    a = a * ap
                at = pl.ds((row * dims + n) * CHUNKS, CHUNKS)
                im_ref[at, lanes] = shifted(m, -1, 0.0)
                iv_ref[at, lanes] = shifted(v, -1, 0.0)
                lm_ref[pl.ds(row * dims + n, 1), lanes] = m[0:1, :]
                lv_ref[pl.ds(row * dims + n, 1), lanes] = v[0:1, :]
        return carry

    lax.fori_loop(0, width // LANES, lane, 0)


def fourth_pass(rows, pg_ref, normed_ref, im_ref, iv_ref, near_ref, far_ref, keep_ref, flag_ref, al_ref, de_ref, be_ref, eta_ref, om_ref, n0_ref, n1_ref, x_ref, g_ref, direct_ref, gg_ref, qk_ref, xg_ref, sums_ref, dec_ref, drv_ref, ng_ref):
    rate_tables(al_ref, de_ref, be_ref, dec_ref, drv_ref)
    dims, width = al_ref.shape
    tokens = keep_ref.shape[0]
    length = tokens // rows
    steps = length // CHUNKS
    span = rows * dims
    sums_ref[...] = jnp.zeros_like(sums_ref)

    def lane(j, carry):
        lanes = pl.ds(pl.multiple_of(j * LANES, LANES), LANES)
        omega = bcast(om_ref, 0, lanes)
        for row in range(rows):
            base = j * tokens + row * length
            grad = steps_of(pg_ref, base, steps)
            token = steps_of(normed_ref, base, steps)
            kept = steps_of(keep_ref, row * length, steps)
            reach = shifted(product(kept), -1, 1.0)
            for by in (-1, -2, -4):
                reach = reach * shifted(reach, by, 1.0)
            place = lax.broadcasted_iota(jnp.int32, (CHUNKS, LANES), 0)
            later = (steps * (CHUNKS - 1 - place)).astype(F32)
            flag = bcast(flag_ref, row, pl.ds(0, LANES))
            total = [omega * t for t in grad]
            for n in range(dims):
                d, b, e = bcast(dec_ref, n, lanes), bcast(drv_ref, n, lanes), bcast(eta_ref, n, lanes)
                chunk = power(d, steps)
                inverse = 1.0 / d
                part = power(chunk, CHUNKS) * flag
                slope = (float(length) * part) * inverse
                at = row * dims + n
                m2 = bcast(far_ref, at, lanes)
                m_in = bcast(near_ref, at, lanes) + part * m2
                v_in = bcast(near_ref, span + at, lanes) + part * bcast(far_ref, span + at, lanes) + slope * m2
                through = reach * chunk_powers(chunk, -1)
                at = pl.ds(at * CHUNKS, CHUNKS)
                m = im_ref[at, lanes] + through * m_in
                v = iv_ref[at, lanes] + through * v_in + (later * through * inverse) * m_in
                coef = e * b
                sum_m = jnp.zeros((CHUNKS, LANES), F32)
                sum_v = jnp.zeros((CHUNKS, LANES), F32)
                for k in range(steps - 1, -1, -1):
                    mu = grad[k] + m
                    sum_m = sum_m + token[k] * mu
                    sum_v = sum_v + token[k] * v
                    total[k] = total[k] + coef * mu
                    rate = kept[k] * d
                    m = rate * mu
                    v = kept[k] * mu + rate * v
                sums_ref[pl.ds(n, 1), lanes] += jnp.sum(sum_m, 0, keepdims=True)
                sums_ref[pl.ds(dims + n, 1), lanes] += jnp.sum(sum_v, 0, keepdims=True)
            for k in range(steps):
                ng_ref[pl.ds(base + k, CHUNKS, stride=steps), :] = total[k]
        return carry

    lax.fori_loop(0, width // LANES, lane, 0)
    normed_grad = from_slabs(ng_ref[...], tokens) + n0_ref[...] + n1_ref[...]
    hat, scale = norm_parts(x_ref[...].astype(F32))
    at = 2 * dims
    for j in range(width // LANES):
        slab = slice(j * tokens, (j + 1) * tokens)
        sums_ref[at : at + 1, j * LANES : (j + 1) * LANES] = jnp.sum(
            pg_ref[slab, :] * normed_ref[slab, :], 0, keepdims=True
        )
    sums_ref[at + 1 : at + 2, :] = jnp.sum(normed_grad * hat, 0, keepdims=True)
    sums_ref[at + 2 : at + 3, :] = gg_ref[...]
    zd = qk_ref.shape[1]
    for i in range(3):
        sums_ref[at + 3 : at + 4, i * zd : (i + 1) * zd] = qk_ref[i : i + 1, :]
    xg_ref[...] = (direct_ref[...] + norm_back(normed_grad * g_ref[...], hat, scale)).astype(LOW)


def swap(x, axis, bit):
    size = lax.axis_size(axis)
    return lax.ppermute(x, axis, [(i, i ^ bit) for i in range(size)])


def shift(x, by):
    size = lax.axis_size("tensor")
    return lax.ppermute(
        x, "tensor", [(i, i + by) for i in range(size) if 0 <= i + by < size]
    )


def rounded(v):
    return lax.reduce_precision(v, 8, 7)


def sum_over_rows(s):
    size, index = lax.axis_size("dp"), lax.axis_index("dp")
    bits = size.bit_length() - 1
    halvings = min(2, bits - 1)
    for b in range(halvings):
        bit, half = (index >> b) & 1, s.shape[0] // 2
        away = lax.dynamic_slice_in_dim(s, (1 - bit) * half, half).astype(LOW)
        mine = lax.dynamic_slice_in_dim(s, bit * half, half)
        s = mine + swap(away, "dp", 1 << b).astype(F32)
    s = rounded(s)
    for b in range(halvings, bits):
        s = rounded(s + swap(s.astype(LOW), "dp", 1 << b).astype(F32))
    low = s.astype(LOW)
    for b in reversed(range(halvings)):
        bit = (index >> b) & 1
        got = swap(low, "dp", 1 << b)
        low = jnp.where(
            bit == 0, jnp.concatenate([low, got], 0), jnp.concatenate([got, low], 0)
        )
    return low


def reduced(keep0, send0, keep1, send1):
    got1 = swap(send1, "tensor", 1)
    across = (keep1 + got1.astype(F32)).astype(LOW)
    got0 = swap(send0, "tensor", 1)
    over = swap(across, "tensor", 2)
    return sum_over_rows(keep0 + got0.astype(F32) + over.astype(F32))


def side_by_side(pack):
    half = pack.shape[0] // 2
    return jnp.concatenate([pack[:half], pack[half:]], 1)


def butterfly(v, low):
    for axis in ("tensor", "dp"):
        size = lax.axis_size(axis)
        for b in range(size.bit_length() - 1):
            if low:
                v = rounded(v)
                v = v + swap(v.astype(LOW), axis, 1 << b).astype(F32)
            else:
                v = v + swap(v, axis, 1 << b)
    return v


def shards(
    layer_input,
    doc_lengths,
    norm1_gain,
    alpha_raw,
    delta_raw,
    ema_beta,
    ema_eta,
    ema_omega,
    w_z,
    q_gain,
    q_bias,
    k_gain,
    w_value,
    w_reset,
    w_update,
    w_hidden,
    w_out,
    norm2_gain,
    w_ffn_in,
    w_ffn_out,
    cotangent,
):
    member = lax.axis_index("tensor")
    rows, length, width = layer_input.shape
    tokens = rows * length
    dims = alpha_raw.shape[0]
    zd = w_z.shape[1]
    units = w_value.shape[1]
    cols = w_hidden.shape[0]
    x = layer_input.reshape(tokens, width)
    cot = cotangent.reshape(tokens, width)
    g1, g2, om = norm1_gain[None], norm2_gain[None], ema_omega[None]
    qg, qb, kg = q_gain[None], q_bias[None], k_gain[None]

    pack_a = jnp.concatenate([w_value, w_reset], 0)
    pack_g = jnp.concatenate([w_hidden, w_out], 0)
    shares = (pack_a, pack_g, w_ffn_in, w_ffn_out)
    over = [swap(w, "tensor", 2) for w in shares]
    beside = [swap(w, "tensor", 1) for w in shares]
    both = [swap(w, "tensor", 1) for w in over]
    wa, wg, wi, wo = (
        (own, b, o, d) for own, b, o, d in zip(shares, beside, over, both, strict=True)
    )

    docs = doc_lengths.shape[1]
    order = jnp.arange(docs)
    ends = jnp.sum(
        jnp.where(order[:, None] <= order[None, :], doc_lengths[:, :, None], 0), 1
    ).astype(jnp.int32)
    starts = ends - doc_lengths
    places = member * length + jnp.arange(length, dtype=jnp.int32)
    docid = jnp.sum((places[None, :, None] >= ends[:, None, :]).astype(jnp.int32), 2)
    keep = 1.0 - jnp.any(places[None, :, None] == starts[:, None, :], 2).astype(F32)
    keep = jnp.broadcast_to(keep.reshape(tokens, 1), (tokens, LANES))
    blocks = docid.reshape(tokens // STRETCH, STRETCH)
    spot = jnp.arange(STRETCH)
    mask = (spot[None, :] <= spot[:, None])[None] & (blocks[:, :, None] == blocks[:, None, :])
    mask = mask.astype(F32).reshape(tokens, STRETCH)

    def unbroken(part):
        low, high = part * length, (part + 1) * length
        inside = jnp.any((starts >= low) & (starts < high), 1)
        return jnp.broadcast_to(1.0 - inside.astype(F32)[:, None], (rows, LANES))

    offs = (member ^ jnp.arange(4, dtype=jnp.int32)) * cols

    vm = lambda shape: pltpu.VMEM(shape, F32)
    tab = (dims, width)
    wide = (tokens, width)
    mat = 2.0 * tokens * width
    ema = 8.0 * tokens * width * dims
    chunked = (rows * dims * CHUNKS, width)
    finals = (rows * dims, width)
    slabs = (tokens * width // LANES, LANES)

    normed, normed_low, init, last = call(
        functools.partial(first_pass, rows),
        [(slabs, F32), (wide, LOW), (chunked, F32), (finals, F32)],
        (x, g1, alpha_raw, delta_raw, ema_beta, keep),
        ema,
        [vm(tab), vm(tab)],
    )
    f1, f2 = shift(last, 1), shift(last, 2)
    pre, mixed_low, z_pre, gate, probs = call(
        functools.partial(second_pass, rows),
        [(slabs, F32), (wide, LOW), ((tokens, zd), F32), (wide, F32), ((tokens, STRETCH), F32)],
        (normed, init, f1, f2, keep, unbroken(member - 1), alpha_raw, delta_raw, ema_beta,
         ema_eta, om, w_z, w_update, qg, qb, kg, mask),
        ema + mat * width,
        [vm(tab), vm(tab)],
    )
    split = (2, tokens, units)
    kept_parts = []
    for p in range(2):
        kept_parts.append(
            call(
                value_part,
                [(split, F32), (split, F32), (split, F32), (split, LOW)],
                (normed_low, mixed_low, probs, wa[2 * p], wa[2 * p + 1]),
                4 * mat * units,
            )
        )
    hidden_pre, blended, second, whid = call(
        blend_part,
        [(wide, F32), (wide, F32), (wide, LOW), ((width, width), LOW)],
        (offs, x, mixed_low, gate, kept_parts[0][3], kept_parts[1][3], *wg, g2),
        mat * (width + 4 * units),
        smem=(0,),
    )
    ffn_rows = width + 2 * units
    ffn = [None, None]
    for p in (1, 0):
        ffn[p] = call(
            ffn_part,
            [(wide, F32), (wide, F32), ((ffn_rows, units), F32), ((ffn_rows, units), LOW)],
            (second, cot, wi[2 * p], wi[2 * p + 1], wo[2 * p], wo[2 * p + 1]),
            12 * mat * units,
        )
    ffn_sum = reduced(ffn[0][2], ffn[0][3], ffn[1][2], ffn[1][3])
    own = (2, 4 * cols, width // 2)
    output, direct, hidden_low, mixed0, gain2, keep_u, send_u = call(
        blend_back,
        [(wide, LOW), (wide, F32), (wide, LOW), (wide, F32), ((1, width), F32), (own, F32), (own, LOW)],
        (offs, x, cot, blended, ffn[0][1], ffn[1][1], ffn[0][0], ffn[1][0], hidden_pre, gate,
         mixed_low, g2, w_update, whid),
        4 * mat * width,
        [vm((width, width))],
        smem=(0,),
    )
    pair_sum = reduced(keep_u[0], send_u[0], keep_u[1], send_u[1])
    rest = [None, None]
    pack_rows = 2 * width + 2 * units
    for p in (1, 0):
        rest[p] = call(
            value_back,
            [(wide, F32), (wide, F32), ((tokens, STRETCH), F32), ((pack_rows, units), F32), ((pack_rows, units), LOW)],
            (hidden_low, normed_low, mixed_low, probs, *kept_parts[p], wg[2 * p], wg[2 * p + 1],
             wa[2 * p], wa[2 * p + 1]),
            14 * mat * units,
        )
    cut = width + 2 * units
    sums_c = reduced(*(rest[p][i][:cut] for p in range(2) for i in (3, 4)))
    sums_d = reduced(*(rest[p][i][cut:] for p in range(2) for i in (3, 4)))
    pre_grad, dz, small, im, iv, lm, lv = call(
        functools.partial(third_pass, rows),
        [(slabs, F32), ((width, zd), F32), ((8, zd), F32), (chunked, F32), (chunked, F32), (finals, F32), (finals, F32)],
        (z_pre, probs, rest[0][2], rest[1][2], qg, qb, kg, w_z, mixed_low, mixed0, rest[0][1],
         rest[1][1], pre, keep, alpha_raw, delta_raw),
        2 * ema,
        [vm((2, tokens, zd))],
    )
    dz_sum = butterfly(dz, True)
    back = jnp.concatenate([lm, lv], 0)
    near, far = shift(back, -1), shift(back, -2)
    input_grad, sums = call(
        functools.partial(fourth_pass, rows),
        [(wide, LOW), ((2 * dims + 8, width), F32)],
        (pre_grad, normed, im, iv, near, far, keep, unbroken(member + 1), alpha_raw, delta_raw,
         ema_beta, ema_eta, om, rest[0][0], rest[1][0], x, g1, direct, gain2, small),
        2 * ema,
        [vm(tab), vm(tab), vm(slabs)],
    )
    sums = butterfly(sums, False)

    alpha, sigma = jax.nn.sigmoid(alpha_raw), jax.nn.sigmoid(delta_raw)
    with_mu, with_nu = sums[:dims], sums[dims : 2 * dims]
    drive_grad = ema_eta * with_mu
    decay_grad = ema_eta * (alpha * ema_beta) * with_nu
    at = 2 * dims
    quarter = side_by_side(pair_sum[: 2 * cols])
    pair = jnp.stack([quarter, swap(quarter, "tensor", 2)])
    quarters = jnp.stack([pair, swap(pair, "tensor", 1)], 1).reshape(4, cols, width)
    update_grad = jnp.concatenate(
        [lax.dynamic_index_in_dim(quarters, g ^ member, 0, False) for g in range(4)], 0
    )
    return (
        output.reshape(layer_input.shape),
        input_grad.reshape(layer_input.shape),
        sums[at + 1],
        (ema_beta * drive_grad - sigma * decay_grad) * alpha * (1.0 - alpha),
        -alpha * decay_grad * sigma * (1.0 - sigma),
        alpha * drive_grad,
        (alpha * ema_beta) * with_mu,
        sums[at],
        dz_sum,
        sums[at + 3, :zd],
        sums[at + 3, zd : 2 * zd],
        sums[at + 3, 2 * zd : 3 * zd],
        sums_d.astype(F32),
        sums_c[:width].astype(F32),
        update_grad.astype(F32),
        side_by_side(pair_sum[2 * cols :]).astype(F32),
        side_by_side(sums_c[width:]).astype(F32),
        sums[at + 2],
        ffn_sum[:width].astype(F32),
        side_by_side(ffn_sum[width:]).astype(F32),
    )


def solution(mesh):
    whole, by_row = P(), P("dp", "tensor", None)
    by_col, by_unit = P(None, "tensor"), P("tensor", None)
    return jax.shard_map(
        shards,
        mesh=mesh,
        in_specs=(by_row, P("dp", None), *(whole,) * 10, by_col, by_col, whole, by_unit, by_unit, whole, by_col, by_unit, by_row),
        out_specs=(by_row, by_row, *(whole,) * 10, by_col, by_col, whole, by_unit, by_unit, whole, by_col, by_unit),
        check_vma=False,
    )
```

profile of v0, /device:TPU:0, one launch (start us, length us, event | category | flops | bytes accessed | tf_op | source)
XLA Modules:
  0.0 371.7 jit_solution(5000512720162421600)
XLA Ops:
  2.1 3.1 collective-permute-start.3
  5.5 2.0 collective-permute-start.10
  8.0 3.0 shard_map.356
  12.3 2.6 collective-permute-start.1
  14.9 48.2 %collective-permute-start.2 = (bf16[1536,384]{1,0:T(8,128)(2,1)S(1)}, bf16[1536,384]{1,0:T(8,128)(2,1)S(1)}, u32[]{:S(2)}, u32[]{:S(2)}) collective-permute-start(bf16[1536,384]{1,0:T(8,128)(2,1)S(1)} %constant_dynamic-update-slice_fusion.wa_ref), channel_id=1, source_target_pairs={{0,1},{1,0},{2,3},{3,2},{4,5},{5,4},{6,7},{7,6},{8,9},{9,8},{10,11... | collective-permute-start | bytes 3538952 | tf_op jit(solution)/shard_map/ppermute | solution.py:471
  63.1 2.1 collective-permute-done.1.f2_ref
  65.2 2.5 collective-permute-start.12
  68.0 13.9 %collective-permute-done.12.oa_ref = bf16[384,768]{1,0:T(8,128)(2,1)S(1)} collective-permute-done((bf16[384,768]{1,0:T(8,128)(2,1)}, bf16[384,768]{1,0:T(8,128)(2,1)S(1)}, u32[]{:S(2)}, u32[]{:S(2)}) %collective-permute-start.12) | collective-permute-done | bytes 589856 | tf_op jit(solution)/shard_map/ppermute | solution.py:471
  84.7 4.8 %shard_map.357 = (f32[1536,128]{1,0:T(8,128)S(1)}, bf16[256,768]{1,0:T(8,128)(2,1)S(1)}, f32[256,128]{1,0:T(8,128)S(1)}, f32[256,768]{1,0:T(8,128)S(1)}, f32[256,128]{1,0:T(8,128)S(1)}) custom-call(f32[1536,128]{1,0:T(8,128)S(1)} %get-tuple-element.75.normed_ref, f32[256,768]{1,0:T(8,128)S(1)} %get-tuple-element.76.init_ref, ...), custom_call_target="tpu_custom_call" | custom-call | flops 327155712 | bytes 5838336 | tf_op jit(solution)/shard_map/pallas_call | solution.py:59
  92.5 2.9 shard_map.359
  96.4 3.3 shard_map.360
  101.5 4.8 %shard_map.362 = (f32[256,768]{1,0:T(8,128)S(1)}, f32[256,768]{1,0:T(8,128)S(1)}, f32[1536,384]{1,0:T(8,128)}, bf16[1536,384]{1,0:T(8,128)(2,1)S(1)}) custom-call(bf16[256,768]{1,0:T(8,128)(2,1)S(1)} %get-tuple-element.85.second_ref, bf16[256,768]{1,0:T(8,128)(2,1)S(1)} %bitcast.55, bf16[768,384]{1,0:T(8,128)(2,1)} %collective-permute-done.10.ia_ref, ...), custom_call_target="tpu_custom_call" | custom-call | flops 1811939328 | bytes 8257536 | tf_op jit(solution)/shard_map/pallas_call | solution.py:59
  107.3 4.7 %shard_map.361 = (f32[256,768]{1,0:T(8,128)S(1)}, f32[256,768]{1,0:T(8,128)S(1)}, f32[1536,384]{1,0:T(8,128)}, bf16[1536,384]{1,0:T(8,128)(2,1)S(1)}) custom-call(bf16[256,768]{1,0:T(8,128)(2,1)S(1)} %get-tuple-element.85.second_ref, bf16[256,768]{1,0:T(8,128)(2,1)S(1)} %bitcast.56, bf16[768,384]{1,0:T(8,128)(2,1)} %ia_ref.1, ...), custom_call_target="tpu_custom_call" | custom-call | flops 1811939328 | bytes 8257536 | tf_op jit(solution)/shard_map/pallas_call | solution.py:59
  112.8 7.3 %shard_map.363 = (bf16[256,768]{1,0:T(8,128)(2,1)}, f32[256,768]{1,0:T(8,128)S(1)}, bf16[256,768]{1,0:T(8,128)(2,1)S(1)}, f32[256,768]{1,0:T(8,128)S(1)}, f32[1,...) custom-call(s32[4]{0:T(128)S(1)} %xor_multiply_fusion.offs_ref, ...), custom_call_target="tpu_custom_call" | custom-call | flops 1207959552 | bytes 14948368 | tf_op jit(solution)/shard_map/pallas_call | solution.py:59
  120.2 7.8 %shard_map.365 = (f32[256,768]{1,0:T(8,128)S(1)}, f32[256,768]{1,0:T(8,128)S(1)}, f32[256,128]{1,0:T(8,128)S(1)}, f32[2304,384]{1,0:T(8,128)}, bf16[2304,384]{1,0:T(8,128)(2,1)}) custom-call(bf16[256,768]{1,0:T(8,128)(2,1)S(1)} %get-tuple-element.94.hidden_ref, bf16[256,768]{1,0:T(8,128)(2,1)S(1)} %get-tuple-element.80.normed_ref, ...), custom_call_target="tpu_custom_call" | custom-call | flops 2113929216 | bytes 15204352 | tf_op jit(solution)/shard_map/pallas_call | solution.py:59
  128.0 7.6 %shard_map.364 = (f32[256,768]{1,0:T(8,128)S(1)}, f32[256,768]{1,0:T(8,128)S(1)}, f32[256,128]{1,0:T(8,128)S(1)}, f32[2304,384]{1,0:T(8,128)}, bf16[2304,384]{1,0:T(8,128)(2,1)}) custom-call(bf16[256,768]{1,0:T(8,128)(2,1)S(1)} %get-tuple-element.94.hidden_ref, bf16[256,768]{1,0:T(8,128)(2,1)S(1)} %get-tuple-element.80.normed_ref, ...), custom_call_target="tpu_custom_call" | custom-call | flops 2113929216 | bytes 15204352 | tf_op jit(solution)/shard_map/pallas_call | solution.py:59
  135.6 6.7 %shard_map.366 = (f32[1536,128]{1,0:T(8,128)S(1)}, f32[768,128]{1,0:T(8,128)S(1)}, f32[8,128]{1,0:T(8,128)S(1)}, f32[256,768]{1,0:T(8,128)S(1)}, f32[256,768]{1,...) custom-call(f32[256,128]{1,0:T(8,128)S(1)} %get-tuple-element.93.zpre_ref, ...), custom_call_target="tpu_custom_call" | custom-call | flops 50331648 | bytes 7443968 | tf_op jit(solution)/shard_map/pallas_call | solution.py:59
  147.1 6.8 %collective-permute-done.15.far_ref = f32[64,768]{1,0:T(8,128)S(1)} collective-permute-done((f32[64,768]{1,0:T(8,128)S(1)}, f32[64,768]{1,0:T(8,128)S(1)}, u32[]{:S(2)}, u32[]{:S(2)}) %collective-permute-start.15) | collective-permute-done | bytes 196640 | tf_op jit(solution)/shard_map/ppermute | solution.py:476
  153.9 9.7 %shard_map.367 = (bf16[256,768]{1,0:T(8,128)(2,1)}, f32[40,768]{1,0:T(8,128)S(1)}) custom-call(f32[1536,128]{1,0:T(8,128)S(1)} %get-tuple-element.107.pg_ref, f32[1536,128]{1,0:T(8,128)S(1)} %get-tuple-element.75.normed_ref, f32[256,768]{1,0:T(8,128)S(1)} %get-tuple-element.108.im_ref, f32[256,768]{1,0:T(8,128)S(1)} %get-tuple-element.109.iv_ref, ...), custom_call_target="tpu_custom_call" | custom-call | flops 50331648 | bytes 7149568 | tf_op jit(solution)/shard_map/pallas_call | solution.py:59
  169.7 4.9 %collective-permute-done.17 = f32[40,768]{1,0:T(8,128)} collective-permute-done((f32[40,768]{1,0:T(8,128)S(1)}, f32[40,768]{1,0:T(8,128)}, u32[]{:S(2)}, u32[]{:S(2)}) %collective-permute-start.17) | collective-permute-done | bytes 122912 | tf_op jit(solution)/shard_map/ppermute | solution.py:471
  177.2 4.2 %collective-permute-done.18 = f32[40,768]{1,0:T(8,128)S(1)} collective-permute-done((f32[40,768]{1,0:T(8,128)S(1)}, f32[40,768]{1,0:T(8,128)S(1)}, u32[]{:S(2)}, u32[]{:S(2)}) %collective-permute-start.18) | collective-permute-done | bytes 122912 | tf_op jit(solution)/shard_map/ppermute | solution.py:471
  184.3 4.5 %collective-permute-done.23 = bf16[768,128]{1,0:T(8,128)(2,1)S(1)} collective-permute-done((bf16[768,128]{1,0:T(8,128)(2,1)S(1)}, bf16[768,128]{1,0:T(8,128)(2,1)S(1)}, u32[]{:S(2)}, u32[]{:S(2)}) %collective-permute-start.23) | collective-permute-done | bytes 196640 | tf_op jit(solution)/shard_map/ppermute | solution.py:471
  191.2 3.6 collective-permute-done.19
  195.1 2.8 collective-permute-done.24
  197.9 2.6 collective-permute-start.20
  200.5 5.1 %collective-permute-done.20 = f32[40,768]{1,0:T(8,128)S(1)} collective-permute-done((f32[40,768]{1,0:T(8,128)S(1)}, f32[40,768]{1,0:T(8,128)S(1)}, u32[]{:S(2)}, u32[]{:S(2)}) %collective-permute-start.20) | collective-permute-done | bytes 122912 | tf_op jit(solution)/shard_map/ppermute | solution.py:471
  208.6 2.0 collective-permute-start.25
  212.7 11.5 %collective-permute-done.28 = bf16[768,384]{1,0:T(8,128)(2,1)S(1)} collective-permute-done((bf16[768,384]{1,0:T(8,128)(2,1)S(1)}, bf16[768,384]{1,0:T(8,128)(2,1)S(1)}, u32[]{:S(2)}, u32[]{:S(2)}) %collective-permute-start.28) | collective-permute-done | bytes 589856 | tf_op jit(solution)/shard_map/ppermute | solution.py:471
  225.9 5.5 %collective-permute-done.45 = bf16[384,384]{1,0:T(8,128)(2,1)S(1)} collective-permute-done((bf16[384,384]{1,0:T(8,128)(2,1)S(1)}, bf16[384,384]{1,0:T(8,128)(2,1)S(1)}, u32[]{:S(2)}, u32[]{:S(2)}) %collective-permute-start.45) | collective-permute-done | bytes 294944 | tf_op jit(solution)/shard_map/ppermute | solution.py:471
  233.0 5.1 %collective-permute-done.29 = bf16[384,384]{1,0:T(8,128)(2,1)S(1)} collective-permute-done((bf16[384,384]{1,0:T(8,128)(2,1)S(1)}, bf16[384,384]{1,0:T(8,128)(2,1)S(1)}, u32[]{:S(2)}, u32[]{:S(2)}) %collective-permute-start.29) | collective-permute-done | bytes 294944 | tf_op jit(solution)/shard_map/ppermute | solution.py:471
  239.4 5.5 %collective-permute-done.46 = bf16[192,384]{1,0:T(8,128)(2,1)S(1)} collective-permute-done((bf16[192,384]{1,0:T(8,128)(2,1)S(1)}, bf16[192,384]{1,0:T(8,128)(2,1)S(1)}, u32[]{:S(2)}, u32[]{:S(2)}) %collective-permute-start.46) | collective-permute-done | bytes 147488 | tf_op jit(solution)/shard_map/ppermute | solution.py:471
  245.2 6.1 %collective-permute-done.30 = bf16[192,384]{1,0:T(8,128)(2,1)S(1)} collective-permute-done((bf16[192,384]{1,0:T(8,128)(2,1)S(1)}, bf16[192,384]{1,0:T(8,128)(2,1)S(1)}, u32[]{:S(2)}, u32[]{:S(2)}) %collective-permute-start.30) | collective-permute-done | bytes 147488 | tf_op jit(solution)/shard_map/ppermute | solution.py:471
  253.1 8.1 %collective-permute-done.47 = bf16[192,384]{1,0:T(8,128)(2,1)S(1)} collective-permute-done((bf16[192,384]{1,0:T(8,128)(2,1)S(1)}, bf16[192,384]{1,0:T(8,128)(2,1)S(1)}, u32[]{:S(2)}, u32[]{:S(2)}) %collective-permute-start.47) | collective-permute-done | bytes 147488 | tf_op jit(solution)/shard_map/ppermute | solution.py:471
  261.3 7.2 %collective-permute-done.31 = bf16[192,384]{1,0:T(8,128)(2,1)S(1)} collective-permute-done((bf16[192,384]{1,0:T(8,128)(2,1)S(1)}, bf16[192,384]{1,0:T(8,128)(2,1)S(1)}, u32[]{:S(2)}, u32[]{:S(2)}) %collective-permute-start.31) | collective-permute-done | bytes 147488 | tf_op jit(solution)/shard_map/ppermute | solution.py:471
  268.8 1.9 collective-permute-start.32
  271.0 2.6 collective-permute-done.48
  277.6 5.7 %collective-permute-done.49 = bf16[384,384]{1,0:T(8,128)(2,1)S(1)} collective-permute-done((bf16[384,384]{1,0:T(8,128)(2,1)S(1)}, bf16[384,384]{1,0:T(8,128)(2,1)S(1)}, u32[]{:S(2)}, u32[]{:S(2)}) %collective-permute-start.49) | collective-permute-done | bytes 294944 | tf_op jit(solution)/shard_map/ppermute | solution.py:471
  286.1 16.1 %collective-permute-done.36 = bf16[1536,384]{1,0:T(8,128)(2,1)S(1)} collective-permute-done((bf16[1536,384]{1,0:T(8,128)(2,1)S(1)}, bf16[1536,384]{1,0:T(8,128)(2,1)S(1)}, u32[]{:S(2)}, u32[]{:S(2)}) %collective-permute-start.36) | collective-permute-done | bytes 1179680 | tf_op jit(solution)/shard_map/ppermute | solution.py:471
  304.7 2.5 collective-permute-start.50
  308.3 4.3 %collective-permute-done.56 = bf16[384,384]{1,0:T(8,128)(2,1)S(1)} collective-permute-done((bf16[384,384]{1,0:T(8,128)(2,1)S(1)}, bf16[384,384]{1,0:T(8,128)(2,1)S(1)}, u32[]{:S(2)}, u32[]{:S(2)}) %collective-permute-start.56) | collective-permute-done | bytes 294944 | tf_op jit(solution)/shard_map/ppermute | solution.py:471
  313.6 3.9 %collective-permute-done.37 = bf16[768,384]{1,0:T(8,128)(2,1)S(1)} collective-permute-done((bf16[768,384]{1,0:T(8,128)(2,1)S(1)}, bf16[768,384]{1,0:T(8,128)(2,1)S(1)}, u32[]{:S(2)}, u32[]{:S(2)}) %collective-permute-start.37) | collective-permute-done | bytes 589856 | tf_op jit(solution)/shard_map/ppermute | solution.py:471
  318.2 9.1 %collective-permute-done.57 = bf16[384,384]{1,0:T(8,128)(2,1)S(1)} collective-permute-done((bf16[384,384]{1,0:T(8,128)(2,1)S(1)}, bf16[384,384]{1,0:T(8,128)(2,1)S(1)}, u32[]{:S(2)}, u32[]{:S(2)}) %collective-permute-start.57) | collective-permute-done | bytes 294944 | tf_op jit(solution)/shard_map/ppermute | solution.py:471
  327.5 5.5 %collective-permute-done.38 = bf16[384,384]{1,0:T(8,128)(2,1)S(1)} collective-permute-done((bf16[384,384]{1,0:T(8,128)(2,1)S(1)}, bf16[384,384]{1,0:T(8,128)(2,1)S(1)}, u32[]{:S(2)}, u32[]{:S(2)}) %collective-permute-start.38) | collective-permute-done | bytes 294944 | tf_op jit(solution)/shard_map/ppermute | solution.py:471
  334.2 6.6 %collective-permute-done.58 = bf16[384,384]{1,0:T(8,128)(2,1)S(1)} collective-permute-done((bf16[384,384]{1,0:T(8,128)(2,1)S(1)}, bf16[384,384]{1,0:T(8,128)(2,1)S(1)}, u32[]{:S(2)}, u32[]{:S(2)}) %collective-permute-start.58) | collective-permute-done | bytes 294944 | tf_op jit(solution)/shard_map/ppermute | solution.py:471
  341.3 5.5 %collective-permute-done.39 = bf16[384,384]{1,0:T(8,128)(2,1)S(1)} collective-permute-done((bf16[384,384]{1,0:T(8,128)(2,1)S(1)}, bf16[384,384]{1,0:T(8,128)(2,1)S(1)}, u32[]{:S(2)}, u32[]{:S(2)}) %collective-permute-start.39) | collective-permute-done | bytes 294944 | tf_op jit(solution)/shard_map/ppermute | solution.py:471
  348.7 5.0 %collective-permute-done.40 = bf16[384,384]{1,0:T(8,128)(2,1)S(1)} collective-permute-done((bf16[384,384]{1,0:T(8,128)(2,1)S(1)}, bf16[384,384]{1,0:T(8,128)(2,1)S(1)}, u32[]{:S(2)}, u32[]{:S(2)}) %collective-permute-start.40) | collective-permute-done | bytes 294944 | tf_op jit(solution)/shard_map/ppermute | solution.py:471
  354.0 2.6 collective-permute-start.41
  358.1 9.6 %collective-permute-done.41 = bf16[768,384]{1,0:T(8,128)(2,1)S(1)} collective-permute-done((bf16[768,384]{1,0:T(8,128)(2,1)S(1)}, bf16[768,384]{1,0:T(8,128)(2,1)S(1)}, u32[]{:S(2)}, u32[]{:S(2)}) %collective-permute-start.41) | collective-permute-done | bytes 589856 | tf_op jit(solution)/shard_map/ppermute | solution.py:471
  (287 shorter events, 66.4 us)
Async XLA Ops:
  2.1 61.0 %collective-permute-start.3 = (bf16[1536,384]{1,0:T(8,128)(2,1)S(1)}, bf16[1536,384]{1,0:T(8,128)(2,1)}, u32[]{:S(2)}, u32[]{:S(2)}) collective-permute-start(bf16[1536,384]{1,0:T(8,128)(2,1)S(1)} %constant_dynamic-update-slice_fusion.wa_ref), channel_id=1, source_target_pairs={{0,2},{1,3},{2,0},{3,1},{4,6},{5,7},{6,4},{7,5},{8,10},{9,11},{10,... | collective-permute-start | bytes 3538952 | tf_op jit(solution)/shard_map/ppermute | solution.py:471
  5.4 62.3 %collective-permute-start.6 = (bf16[576,768]{1,0:T(8,128)(2,1)S(1)}, bf16[576,768]{1,0:T(8,128)(2,1)}, u32[]{:S(2)}, u32[]{:S(2)}) collective-permute-start(bf16[576,768]{1,0:T(8,128)(2,1)S(1)} %constant_dynamic-update-slice_fusion.2.g0_ref.ga_ref), channel_id=1, source_target_pairs={{0,2},{1,3},{2,0},{3,1},{4,6},{5,7},{6,4},{7,5},{8,10},{9,11},{10,... | collective-permute-start | bytes 2654216 | tf_op jit(solution)/shard_map/ppermute | solution.py:471
  5.5 59.8 %collective-permute-start.10 = (bf16[768,384]{1,0:T(8,128)(2,1)}, bf16[768,384]{1,0:T(8,128)(2,1)}, u32[]{:S(2)}, u32[]{:S(2)}) collective-permute-start(bf16[768,384]{1,0:T(8,128)(2,1)} %ia_ref.1), channel_id=1, source_target_pairs={{0,2},{1,3},{2,0},{3,1},{4,6},{5,7},{6,4},{7,5},{8,10},{9,11},{10,... | collective-permute-start | bytes 1769480 | tf_op jit(solution)/shard_map/ppermute | solution.py:471
  12.3 52.9 %collective-permute-start.1 = (f32[32,768]{1,0:T(8,128)S(1)}, f32[32,768]{1,0:T(8,128)S(1)}, u32[]{:S(2)}, u32[]{:S(2)}) collective-permute-start(f32[32,768]{1,0:T(8,128)S(1)} %get-tuple-element.77), channel_id=1, source_target_pairs={{0,2},{1,3},{4,6},{5,7},{8,10},{9,11},{12,14},{13,15},{16,18},{17,... | collective-permute-start | bytes 294920 | tf_op jit(solution)/shard_map/ppermute | solution.py:476
  14.9 67.7 %collective-permute-start.2 = (bf16[1536,384]{1,0:T(8,128)(2,1)S(1)}, bf16[1536,384]{1,0:T(8,128)(2,1)S(1)}, u32[]{:S(2)}, u32[]{:S(2)}) collective-permute-start(bf16[1536,384]{1,0:T(8,128)(2,1)S(1)} %constant_dynamic-update-slice_fusion.wa_ref), channel_id=1, source_target_pairs={{0,1},{1,0},{2,3},{3,2},{4,5},{5,4},{6,7},{7,6},{8,9},{9,8},{10,11... | collective-permute-start | bytes 3538952 | tf_op jit(solution)/shard_map/ppermute | solution.py:471
  63.1 19.6 %collective-permute-start.4 = (bf16[1536,384]{1,0:T(8,128)(2,1)}, bf16[1536,384]{1,0:T(8,128)(2,1)S(1)}, u32[]{:S(2)}, u32[]{:S(2)}) collective-permute-start(bf16[1536,384]{1,0:T(8,128)(2,1)} %collective-permute-done.3.wa_ref), channel_id=1, source_target_pairs={{0,1},{1,0},{2,3},{3,2},{4,5},{5,4},{6,7},{7,6},{8,9},{9,8},{10,11... | collective-permute-start | bytes 3538952 | tf_op jit(solution)/shard_map/ppermute | solution.py:471
  65.2 16.7 %collective-permute-start.5 = (bf16[576,768]{1,0:T(8,128)(2,1)S(1)}, bf16[576,768]{1,0:T(8,128)(2,1)S(1)}, u32[]{:S(2)}, u32[]{:S(2)}) collective-permute-start(bf16[576,768]{1,0:T(8,128)(2,1)S(1)} %constant_dynamic-update-slice_fusion.2.g0_ref.ga_ref), channel_id=1, source_target_pairs={{0,1},{1,0},{2,3},{3,2},{4,5},{5,4},{6,7},{7,6},{8,9},{9,8},{10,11... | collective-permute-start | bytes 2654216 | tf_op jit(solution)/shard_map/ppermute | solution.py:471
  65.2 16.7 %collective-permute-start.12 = (bf16[384,768]{1,0:T(8,128)(2,1)}, bf16[384,768]{1,0:T(8,128)(2,1)S(1)}, u32[]{:S(2)}, u32[]{:S(2)}) collective-permute-start(bf16[384,768]{1,0:T(8,128)(2,1)} %oa_ref.1), channel_id=1, source_target_pairs={{0,2},{1,3},{2,0},{3,1},{4,6},{5,7},{6,4},{7,5},{8,10},{9,11},{10,... | collective-permute-start | bytes 1769480 | tf_op jit(solution)/shard_map/ppermute | solution.py:471
  67.7 28.6 %collective-permute-start.7 = (bf16[576,768]{1,0:T(8,128)(2,1)}, bf16[576,768]{1,0:T(8,128)(2,1)}, u32[]{:S(2)}, u32[]{:S(2)}) collective-permute-start(bf16[576,768]{1,0:T(8,128)(2,1)} %collective-permute-done.6.g2_ref.ga_ref), channel_id=1, source_target_pairs={{0,1},{1,0},{2,3},{3,2},{4,5},{5,4},{6,7},{7,6},{8,9},{9,8},{10,11... | collective-permute-start | bytes 2654216 | tf_op jit(solution)/shard_map/ppermute | solution.py:471
  81.9 19.6 %collective-permute-start.11 = (bf16[768,384]{1,0:T(8,128)(2,1)}, bf16[768,384]{1,0:T(8,128)(2,1)S(1)}, u32[]{:S(2)}, u32[]{:S(2)}) collective-permute-start(bf16[768,384]{1,0:T(8,128)(2,1)} %collective-permute-done.10.ia_ref), channel_id=1, source_target_pairs={{0,1},{1,0},{2,3},{3,2},{4,5},{5,4},{6,7},{7,6},{8,9},{9,8},{10,11... | collective-permute-start | bytes 1769480 | tf_op jit(solution)/shard_map/ppermute | solution.py:471
  81.9 19.6 %collective-permute-start.13 = (bf16[384,768]{1,0:T(8,128)(2,1)S(1)}, bf16[384,768]{1,0:T(8,128)(2,1)S(1)}, u32[]{:S(2)}, u32[]{:S(2)}) collective-permute-start(bf16[384,768]{1,0:T(8,128)(2,1)S(1)} %collective-permute-done.12.oa_ref), channel_id=1, source_target_pairs={{0,1},{1,0},{2,3},{3,2},{4,5},{5,4},{6,7},{7,6},{8,9},{9,8},{10,11... | collective-permute-start | bytes 1769480 | tf_op jit(solution)/shard_map/ppermute | solution.py:471
  82.6 24.6 %collective-permute-start.8 = (bf16[768,384]{1,0:T(8,128)(2,1)}, bf16[768,384]{1,0:T(8,128)(2,1)}, u32[]{:S(2)}, u32[]{:S(2)}) collective-permute-start(bf16[768,384]{1,0:T(8,128)(2,1)} %ia_ref.1), channel_id=1, source_target_pairs={{0,1},{1,0},{2,3},{3,2},{4,5},{5,4},{6,7},{7,6},{8,9},{9,8},{10,11... | collective-permute-start | bytes 1769480 | tf_op jit(solution)/shard_map/ppermute | solution.py:471
  82.7 24.5 %collective-permute-start.9 = (bf16[384,768]{1,0:T(8,128)(2,1)}, bf16[384,768]{1,0:T(8,128)(2,1)}, u32[]{:S(2)}, u32[]{:S(2)}) collective-permute-start(bf16[384,768]{1,0:T(8,128)(2,1)} %oa_ref.1), channel_id=1, source_target_pairs={{0,1},{1,0},{2,3},{3,2},{4,5},{5,4},{6,7},{7,6},{8,9},{9,8},{10,11... | collective-permute-start | bytes 1769480 | tf_op jit(solution)/shard_map/ppermute | solution.py:471
  143.6 10.3 %collective-permute-start.15 = (f32[64,768]{1,0:T(8,128)S(1)}, f32[64,768]{1,0:T(8,128)S(1)}, u32[]{:S(2)}, u32[]{:S(2)}) collective-permute-start(f32[64,768]{1,0:T(8,128)S(1)} %constant_dynamic-update-slice_fusion.4), channel_id=1, source_target_pairs={{2,0},{3,1},{6,4},{7,5},{10,8},{11,9},{14,12},{15,13},{18,16},{19,... | collective-permute-start | bytes 589832 | tf_op jit(solution)/shard_map/ppermute | solution.py:476
  144.9 18.7 %collective-permute-start.21 = (bf16[768,128]{1,0:T(8,128)(2,1)S(1)}, bf16[768,128]{1,0:T(8,128)(2,1)S(1)}, u32[]{:S(2)}, u32[]{:S(2)}) collective-permute-start(bf16[768,128]{1,0:T(8,128)(2,1)S(1)} %reduce-precision_convert_fusion.2), channel_id=1, source_target_pairs={{0,1},{1,0},{2,3},{3,2},{4,5},{5,4},{6,7},{7,6},{8,9},{9,8},{10,11... | collective-permute-start | bytes 589832 | tf_op jit(solution)/shard_map/ppermute | solution.py:471
  147.0 34.4 %collective-permute-start.43 = (bf16[768,384]{1,0:T(8,128)(2,1)}, bf16[768,384]{1,0:T(8,128)(2,1)}, u32[]{:S(2)}, u32[]{:S(2)}) collective-permute-start(bf16[768,384]{1,0:T(8,128)(2,1)} %get-tuple-element.147), channel_id=1, source_target_pairs={{0,1},{1,0},{2,3},{3,2},{4,5},{5,4},{6,7},{7,6},{8,9},{9,8},{10,11... | collective-permute-start | bytes 1769480 | tf_op jit(solution)/shard_map/ppermute | solution.py:471
  164.4 11.2 %collective-permute-start.22 = (bf16[768,128]{1,0:T(8,128)(2,1)}, bf16[768,128]{1,0:T(8,128)(2,1)S(1)}, u32[]{:S(2)}, u32[]{:S(2)}) collective-permute-start(bf16[768,128]{1,0:T(8,128)(2,1)} %fusion.11), channel_id=1, source_target_pairs={{0,2},{1,3},{2,0},{3,1},{4,6},{5,7},{6,4},{7,5},{8,10},{9,11},{10,... | collective-permute-start | bytes 589832 | tf_op jit(solution)/shard_map/ppermute | solution.py:471
  165.0 9.6 %collective-permute-start.17 = (f32[40,768]{1,0:T(8,128)S(1)}, f32[40,768]{1,0:T(8,128)}, u32[]{:S(2)}, u32[]{:S(2)}) collective-permute-start(f32[40,768]{1,0:T(8,128)S(1)} %add.179), channel_id=1, source_target_pairs={{0,2},{1,3},{2,0},{3,1},{4,6},{5,7},{6,4},{7,5},{8,10},{9,11},{10,... | collective-permute-start | bytes 368648 | tf_op jit(solution)/shard_map/ppermute | solution.py:471
  169.2 39.3 %collective-permute-start.53 = (bf16[1536,384]{1,0:T(8,128)(2,1)S(1)}, bf16[1536,384]{1,0:T(8,128)(2,1)S(1)}, u32[]{:S(2)}, u32[]{:S(2)}) collective-permute-start(bf16[1536,384]{1,0:T(8,128)(2,1)S(1)} %copy-done.38), channel_id=1, source_target_pairs={{0,1},{1,0},{2,3},{3,2},{4,5},{5,4},{6,7},{7,6},{8,9},{9,8},{10,11... | collective-permute-start | bytes 3538952 | tf_op jit(solution)/shard_map/ppermute | solution.py:471
  169.6 115.4 %collective-permute-start.52 = (bf16[1536,384]{1,0:T(8,128)(2,1)S(1)}, bf16[1536,384]{1,0:T(8,128)(2,1)S(1)}, u32[]{:S(2)}, u32[]{:S(2)}) collective-permute-start(bf16[1536,384]{1,0:T(8,128)(2,1)S(1)} %copy-done.36), channel_id=1, source_target_pairs={{0,1},{1,0},{2,3},{3,2},{4,5},{5,4},{6,7},{7,6},{8,9},{9,8},{10,11... | collective-permute-start | bytes 3538952 | tf_op jit(solution)/shard_map/ppermute | solution.py:471
  174.6 15.9 %collective-permute-start.27 = (bf16[768,384]{1,0:T(8,128)(2,1)S(1)}, bf16[768,384]{1,0:T(8,128)(2,1)S(1)}, u32[]{:S(2)}, u32[]{:S(2)}) collective-permute-start(bf16[768,384]{1,0:T(8,128)(2,1)S(1)} %slice.112), channel_id=1, source_target_pairs={{0,1},{1,0},{2,3},{3,2},{4,5},{5,4},{6,7},{7,6},{8,9},{9,8},{10,11... | collective-permute-start | bytes 1769480 | tf_op jit(solution)/shard_map/ppermute | solution.py:471
  181.4 26.1 %collective-permute-start.42 = (bf16[768,384]{1,0:T(8,128)(2,1)S(1)}, bf16[768,384]{1,0:T(8,128)(2,1)S(1)}, u32[]{:S(2)}, u32[]{:S(2)}) collective-permute-start(bf16[768,384]{1,0:T(8,128)(2,1)S(1)} %get-tuple-element.146), channel_id=1, source_target_pairs={{0,1},{1,0},{2,3},{3,2},{4,5},{5,4},{6,7},{7,6},{8,9},{9,8},{10,11... | collective-permute-start | bytes 1769480 | tf_op jit(solution)/shard_map/ppermute | solution.py:471
  181.4 7.4 %collective-permute-start.23 = (bf16[768,128]{1,0:T(8,128)(2,1)S(1)}, bf16[768,128]{1,0:T(8,128)(2,1)S(1)}, u32[]{:S(2)}, u32[]{:S(2)}) collective-permute-start(bf16[768,128]{1,0:T(8,128)(2,1)S(1)} %fusion.5), channel_id=1, source_target_pairs={{0,4},{4,0},{8,12},{12,8},{16,20},{20,16},{24,28},{28,24},{1,5},{5... | collective-permute-start | bytes 589832 | tf_op jit(solution)/shard_map/ppermute | solution.py:471
  190.5 7.4 %collective-permute-start.24 = (bf16[768,128]{1,0:T(8,128)(2,1)S(1)}, bf16[768,128]{1,0:T(8,128)(2,1)S(1)}, u32[]{:S(2)}, u32[]{:S(2)}) collective-permute-start(bf16[768,128]{1,0:T(8,128)(2,1)S(1)} %get-tuple-element.135), channel_id=1, source_target_pairs={{0,8},{4,12},{8,0},{12,4},{16,24},{20,28},{24,16},{28,20},{1,9},{5... | collective-permute-start | bytes 589832 | tf_op jit(solution)/shard_map/ppermute | solution.py:471
  194.8 13.2 %collective-permute-start.44 = (bf16[768,384]{1,0:T(8,128)(2,1)S(1)}, bf16[768,384]{1,0:T(8,128)(2,1)S(1)}, u32[]{:S(2)}, u32[]{:S(2)}) collective-permute-start(bf16[768,384]{1,0:T(8,128)(2,1)S(1)} %fusion), channel_id=1, source_target_pairs={{0,2},{1,3},{2,0},{3,1},{4,6},{5,7},{6,4},{7,5},{8,10},{9,11},{10,... | collective-permute-start | bytes 1769480 | tf_op jit(solution)/shard_map/ppermute | solution.py:471
  197.9 7.8 %collective-permute-start.20 = (f32[40,768]{1,0:T(8,128)S(1)}, f32[40,768]{1,0:T(8,128)S(1)}, u32[]{:S(2)}, u32[]{:S(2)}) collective-permute-start(f32[40,768]{1,0:T(8,128)S(1)} %add.182), channel_id=1, source_target_pairs={{0,16},{4,20},{8,24},{12,28},{16,0},{20,4},{24,8},{28,12},{1,17},{... | collective-permute-start | bytes 368648 | tf_op jit(solution)/shard_map/ppermute | solution.py:471
  205.6 63.2 %collective-permute-start.35 = (bf16[1536,384]{1,0:T(8,128)(2,1)S(1)}, bf16[1536,384]{1,0:T(8,128)(2,1)S(1)}, u32[]{:S(2)}, u32[]{:S(2)}) collective-permute-start(bf16[1536,384]{1,0:T(8,128)(2,1)S(1)} %slice.116), channel_id=1, source_target_pairs={{0,1},{1,0},{2,3},{3,2},{4,5},{5,4},{6,7},{7,6},{8,9},{9,8},{10,11... | collective-permute-start | bytes 3538952 | tf_op jit(solution)/shard_map/ppermute | solution.py:471
  208.0 16.2 %collective-permute-start.28 = (bf16[768,384]{1,0:T(8,128)(2,1)S(1)}, bf16[768,384]{1,0:T(8,128)(2,1)S(1)}, u32[]{:S(2)}, u32[]{:S(2)}) collective-permute-start(bf16[768,384]{1,0:T(8,128)(2,1)S(1)} %add_convert_fusion.2), channel_id=1, source_target_pairs={{0,2},{1,3},{2,0},{3,1},{4,6},{5,7},{6,4},{7,5},{8,10},{9,11},{10,... | collective-permute-start | bytes 1769480 | tf_op jit(solution)/shard_map/ppermute | solution.py:471
  208.6 65.1 %collective-permute-start.25 = (bf16[768,128]{1,0:T(8,128)(2,1)S(1)}, bf16[768,128]{1,0:T(8,128)(2,1)S(1)}, u32[]{:S(2)}, u32[]{:S(2)}) collective-permute-start(bf16[768,128]{1,0:T(8,128)(2,1)S(1)} %fusion.6), channel_id=1, source_target_pairs={{0,16},{4,20},{8,24},{12,28},{16,0},{20,4},{24,8},{28,12},{1,17},{... | collective-permute-start | bytes 589832 | tf_op jit(solution)/shard_map/ppermute | solution.py:471
  210.9 74.1 %collective-permute-start.54 = (bf16[1536,384]{1,0:T(8,128)(2,1)S(1)}, bf16[1536,384]{1,0:T(8,128)(2,1)S(1)}, u32[]{:S(2)}, u32[]{:S(2)}) collective-permute-start(bf16[1536,384]{1,0:T(8,128)(2,1)S(1)} %add_convert_fusion), channel_id=1, source_target_pairs={{0,2},{1,3},{2,0},{3,1},{4,6},{5,7},{6,4},{7,5},{8,10},{9,11},{10,... | collective-permute-start | bytes 3538952 | tf_op jit(solution)/shard_map/ppermute | solution.py:471
  224.2 7.2 %collective-permute-start.45 = (bf16[384,384]{1,0:T(8,128)(2,1)S(1)}, bf16[384,384]{1,0:T(8,128)(2,1)S(1)}, u32[]{:S(2)}, u32[]{:S(2)}) collective-permute-start(bf16[384,384]{1,0:T(8,128)(2,1)S(1)} %dynamic-slice_convert_fusion.3), channel_id=1, source_target_pairs={{0,4},{4,0},{8,12},{12,8},{16,20},{20,16},{24,28},{28,24},{1,5},{5... | collective-permute-start | bytes 884744 | tf_op jit(solution)/shard_map/ppermute | solution.py:471
  251.4 9.8 %collective-permute-start.47 = (bf16[192,384]{1,0:T(8,128)(2,1)S(1)}, bf16[192,384]{1,0:T(8,128)(2,1)S(1)}, u32[]{:S(2)}, u32[]{:S(2)}) collective-permute-start(bf16[192,384]{1,0:T(8,128)(2,1)S(1)} %fusion.8), channel_id=1, source_target_pairs={{0,16},{4,20},{8,24},{12,28},{16,0},{20,4},{24,8},{28,12},{1,17},{... | collective-permute-start | bytes 442376 | tf_op jit(solution)/shard_map/ppermute | solution.py:471
  261.2 7.3 %collective-permute-start.31 = (bf16[192,384]{1,0:T(8,128)(2,1)S(1)}, bf16[192,384]{1,0:T(8,128)(2,1)S(1)}, u32[]{:S(2)}, u32[]{:S(2)}) collective-permute-start(bf16[192,384]{1,0:T(8,128)(2,1)S(1)} %fusion.7), channel_id=1, source_target_pairs={{0,16},{4,20},{8,24},{12,28},{16,0},{20,4},{24,8},{28,12},{1,17},{... | collective-permute-start | bytes 442376 | tf_op jit(solution)/shard_map/ppermute | solution.py:471
  273.6 12.5 %collective-permute-start.34 = (bf16[1536,384]{1,0:T(8,128)(2,1)S(1)}, bf16[1536,384]{1,0:T(8,128)(2,1)S(1)}, u32[]{:S(2)}, u32[]{:S(2)}) collective-permute-start(bf16[1536,384]{1,0:T(8,128)(2,1)S(1)} %slice.114), channel_id=1, source_target_pairs={{0,1},{1,0},{2,3},{3,2},{4,5},{5,4},{6,7},{7,6},{8,9},{9,8},{10,11... | collective-permute-start | bytes 3538952 | tf_op jit(solution)/shard_map/ppermute | solution.py:471
  273.7 28.4 %collective-permute-start.36 = (bf16[1536,384]{1,0:T(8,128)(2,1)S(1)}, bf16[1536,384]{1,0:T(8,128)(2,1)S(1)}, u32[]{:S(2)}, u32[]{:S(2)}) collective-permute-start(bf16[1536,384]{1,0:T(8,128)(2,1)S(1)} %add_convert_fusion.1), channel_id=1, source_target_pairs={{0,2},{1,3},{2,0},{3,1},{4,6},{5,7},{6,4},{7,5},{8,10},{9,11},{10,... | collective-permute-start | bytes 3538952 | tf_op jit(solution)/shard_map/ppermute | solution.py:471
  275.2 8.1 %collective-permute-start.49 = (bf16[384,384]{1,0:T(8,128)(2,1)S(1)}, bf16[384,384]{1,0:T(8,128)(2,1)S(1)}, u32[]{:S(2)}, u32[]{:S(2)}) collective-permute-start(bf16[384,384]{1,0:T(8,128)(2,1)S(1)} %maximum_select_fusion.7), channel_id=1, source_target_pairs={{0,4},{4,0},{8,12},{12,8},{16,20},{20,16},{24,28},{28,24},{1,5},{5... | collective-permute-start | bytes 884744 | tf_op jit(solution)/shard_map/ppermute | solution.py:471
  283.3 23.9 %collective-permute-start.33 = (bf16[384,384]{1,0:T(8,128)(2,1)S(1)}, bf16[384,384]{1,0:T(8,128)(2,1)S(1)}, u32[]{:S(2)}, u32[]{:S(2)}) collective-permute-start(bf16[384,384]{1,0:T(8,128)(2,1)S(1)} %maximum_select_fusion.6), channel_id=1, source_target_pairs={{0,4},{4,0},{8,12},{12,8},{16,20},{20,16},{24,28},{28,24},{1,5},{5... | collective-permute-start | bytes 884744 | tf_op jit(solution)/shard_map/ppermute | solution.py:471
  285.5 18.6 %collective-permute-start.55 = (bf16[768,384]{1,0:T(8,128)(2,1)S(1)}, bf16[768,384]{1,0:T(8,128)(2,1)S(1)}, u32[]{:S(2)}, u32[]{:S(2)}) collective-permute-start(bf16[768,384]{1,0:T(8,128)(2,1)S(1)} %dynamic-slice_convert_fusion), channel_id=1, source_target_pairs={{0,4},{4,0},{8,12},{12,8},{16,20},{20,16},{24,28},{28,24},{1,5},{5... | collective-permute-start | bytes 1769480 | tf_op jit(solution)/shard_map/ppermute | solution.py:471
  302.6 14.9 %collective-permute-start.37 = (bf16[768,384]{1,0:T(8,128)(2,1)S(1)}, bf16[768,384]{1,0:T(8,128)(2,1)S(1)}, u32[]{:S(2)}, u32[]{:S(2)}) collective-permute-start(bf16[768,384]{1,0:T(8,128)(2,1)S(1)} %dynamic-slice_convert_fusion.1), channel_id=1, source_target_pairs={{0,4},{4,0},{8,12},{12,8},{16,20},{20,16},{24,28},{28,24},{1,5},{5... | collective-permute-start | bytes 1769480 | tf_op jit(solution)/shard_map/ppermute | solution.py:471
  304.3 8.3 %collective-permute-start.56 = (bf16[384,384]{1,0:T(8,128)(2,1)S(1)}, bf16[384,384]{1,0:T(8,128)(2,1)S(1)}, u32[]{:S(2)}, u32[]{:S(2)}) collective-permute-start(bf16[384,384]{1,0:T(8,128)(2,1)S(1)} %dynamic-slice_convert_fusion.2), channel_id=1, source_target_pairs={{0,8},{4,12},{8,0},{12,4},{16,24},{20,28},{24,16},{28,20},{1,9},{5... | collective-permute-start | bytes 884744 | tf_op jit(solution)/shard_map/ppermute | solution.py:471
  304.7 13.3 %collective-permute-start.50 = (bf16[192,768]{1,0:T(8,128)(2,1)S(1)}, bf16[192,768]{1,0:T(8,128)(2,1)S(1)}, u32[]{:S(2)}, u32[]{:S(2)}) collective-permute-start(bf16[192,768]{1,0:T(8,128)(2,1)S(1)} %get-tuple-element.157), channel_id=1, source_target_pairs={{0,2},{1,3},{2,0},{3,1},{4,6},{5,7},{6,4},{7,5},{8,10},{9,11},{10,... | collective-permute-start | bytes 884744 | tf_op jit(solution)/shard_map/ppermute | solution.py:471
  312.7 14.6 %collective-permute-start.57 = (bf16[384,384]{1,0:T(8,128)(2,1)S(1)}, bf16[384,384]{1,0:T(8,128)(2,1)S(1)}, u32[]{:S(2)}, u32[]{:S(2)}) collective-permute-start(bf16[384,384]{1,0:T(8,128)(2,1)S(1)} %fusion.4), channel_id=1, source_target_pairs={{0,16},{4,20},{8,24},{12,28},{16,0},{20,4},{24,8},{28,12},{1,17},{... | collective-permute-start | bytes 884744 | tf_op jit(solution)/shard_map/ppermute | solution.py:471
  317.7 15.3 %collective-permute-start.38 = (bf16[384,384]{1,0:T(8,128)(2,1)S(1)}, bf16[384,384]{1,0:T(8,128)(2,1)S(1)}, u32[]{:S(2)}, u32[]{:S(2)}) collective-permute-start(bf16[384,384]{1,0:T(8,128)(2,1)S(1)} %dynamic-slice_convert_fusion.4), channel_id=1, source_target_pairs={{0,8},{4,12},{8,0},{12,4},{16,24},{20,28},{24,16},{28,20},{1,9},{5... | collective-permute-start | bytes 884744 | tf_op jit(solution)/shard_map/ppermute | solution.py:471
  318.1 15.9 %collective-permute-start.51 = (bf16[2,192,768]{2,1,0:T(8,128)(2,1)S(1)}, bf16[2,192,768]{2,1,0:T(8,128)(2,1)S(1)}, u32[]{:S(2)}, u32[]{:S(2)}) collective-permute-start(bf16[2,192,768]{2,1,0:T(8,128)(2,1)S(1)} %get-tuple-element.153), channel_id=1, source_target_pairs={{0,1},{1,0},{2,3},{3,2},{4,5},{5,4},{6,7},{7,6},{8,9},{9,8},{10,11... | collective-permute-start | bytes 1769480 | tf_op jit(solution)/shard_map/ppermute | solution.py:471
  327.4 13.3 %collective-permute-start.58 = (bf16[384,384]{1,0:T(8,128)(2,1)S(1)}, bf16[384,384]{1,0:T(8,128)(2,1)S(1)}, u32[]{:S(2)}, u32[]{:S(2)}) collective-permute-start(bf16[384,384]{1,0:T(8,128)(2,1)S(1)} %reduce-precision_convert_fusion), channel_id=1, source_target_pairs={{0,8},{4,12},{8,0},{12,4},{16,24},{20,28},{24,16},{28,20},{1,9},{5... | collective-permute-start | bytes 884744 | tf_op jit(solution)/shard_map/ppermute | solution.py:471
  333.0 13.8 %collective-permute-start.39 = (bf16[384,384]{1,0:T(8,128)(2,1)S(1)}, bf16[384,384]{1,0:T(8,128)(2,1)S(1)}, u32[]{:S(2)}, u32[]{:S(2)}) collective-permute-start(bf16[384,384]{1,0:T(8,128)(2,1)S(1)} %fusion.3), channel_id=1, source_target_pairs={{0,16},{4,20},{8,24},{12,28},{16,0},{20,4},{24,8},{28,12},{1,17},{... | collective-permute-start | bytes 884744 | tf_op jit(solution)/shard_map/ppermute | solution.py:471
  341.0 15.6 %collective-permute-start.59 = (bf16[768,384]{1,0:T(8,128)(2,1)S(1)}, bf16[768,384]{1,0:T(8,128)(2,1)S(1)}, u32[]{:S(2)}, u32[]{:S(2)}) collective-permute-start(bf16[768,384]{1,0:T(8,128)(2,1)S(1)} %maximum_select_fusion.5), channel_id=1, source_target_pairs={{0,4},{4,0},{8,12},{12,8},{16,20},{20,16},{24,28},{28,24},{1,5},{5... | collective-permute-start | bytes 1769480 | tf_op jit(solution)/shard_map/ppermute | solution.py:471
  354.0 13.8 %collective-permute-start.41 = (bf16[768,384]{1,0:T(8,128)(2,1)S(1)}, bf16[768,384]{1,0:T(8,128)(2,1)S(1)}, u32[]{:S(2)}, u32[]{:S(2)}) collective-permute-start(bf16[768,384]{1,0:T(8,128)(2,1)S(1)} %maximum_select_fusion.3), channel_id=1, source_target_pairs={{0,4},{4,0},{8,12},{12,8},{16,20},{20,16},{24,28},{28,24},{1,5},{5... | collective-permute-start | bytes 1769480 | tf_op jit(solution)/shard_map/ppermute | solution.py:471
  (67 other events, 1048.3 us)
where the time goes:
time: 376 us; the launch traced here: 372 us
  waiting for transfers between devices  173 us (46%)
  starting transfers between devices  100 us (27%)
  Pallas kernels  63.7 us (17%)
  other arithmetic  18 us (5%)
  local copies, waits for them, and re-layouts  15.4 us (4%)
    ppermute x56, waiting for transfers between devices, swap(): return lax.ppermute(x, axis, [(i, i ^ bit) for i in range(size)])  164 us
    ppermute x56, starting transfers between devices, swap(): return lax.ppermute(x, axis, [(i, i ^ bit) for i in range(size)])  93.6 us
    pallas_call x12, Pallas kernels, call(): pl.pallas_call(kernel, out_shape=outs, in_specs=specs, out_specs=[pl.Bloc...  63.7 us
    unnamed x113, local copies, waits for them, and re-layouts  11.8 us
    ppermute x4, waiting for transfers between devices, shift(): lax.ppermute(x, 'tensor', [(i, i + by) for i in range(size) if 0 <= i + b...  8.88 us
  transfers between devices with their start and end apart: 60, of which 29 were waited for; matrix products, arithmetic and copies ran while one was open for 5% of the time, Pallas kernels for 8%

commit v1 on v0

--- a/solution.py
+++ b/solution.py
@@ -12,6 +12,19 @@
 CHUNKS = 8
 F32 = jnp.float32
 LOW = jnp.bfloat16
+KINDS = {"F": "w", "P": "x", "R": "x", "O": "z", "N": "x"}
+ORDER = (
+    "+F0", "+F1", "Kbb", "-F0", "-F1", "+P0", "Kv1", "-P0", "+V1", "+F",
+    "+P", "Kv0", "-V1", "+V0", "Kt3", "-V0", "+dz", "+E", "-P", "+R",
+    "-dz", "+O", "-F", "+N", "-R", "+P", "-O", "+F", "-E", "Kt4",
+    "-P", "+R", "+sm", "-N", "+P", "-sm", "+N", "-F", "+F", "-P",
+    "+P", "-R", "+dz", "+R", "-F", "+sm", "-N", "+F", "-R", "+O",
+    "-P", "-dz", "+N", "+dz", "-sm", "+P", "-dz", "-O", "-N", "+R",
+    "+sm", "+dz", "-P", "+O", "-F", "+P", "-sm", "+N", "-O", "+sm",
+    "-dz", "+O", "-R", "+F", "-P", "+R", "-sm", "+dz", "-N", "+N",
+    "-F", "-R", "+R", "+F", "-O", "+O", "-N", "+N", "-dz", "-R",
+    "-O", "+sm", "+O", "-F", "-N", "-sm", "-O",
+)
 
 
 def silu(v):
@@ -214,12 +227,11 @@
         probs_ref[block, :] = shift / jnp.sum(shift, -1, keepdims=True)
 
 
-def value_part(normed_ref, mixed_ref, probs_ref, wa_ref, wb_ref, vpre_ref, rpre_ref, att_ref, united_ref):
-    depth = normed_ref.shape[1]
+def value_part(normed_ref, mixed_ref, probs_ref, va_ref, ra_ref, vb_ref, rb_ref, vpre_ref, rpre_ref, att_ref, united_ref):
     tokens = normed_ref.shape[0]
-    for i, w_ref in enumerate((wa_ref, wb_ref)):
-        value_pre = dot(normed_ref[...], w_ref[:depth, :])
-        reset_pre = dot(mixed_ref[...], w_ref[depth:, :])
+    for i, (v_ref, r_ref) in enumerate(((va_ref, ra_ref), (vb_ref, rb_ref))):
+        value_pre = dot(normed_ref[...], v_ref[...])
+        reset_pre = dot(mixed_ref[...], r_ref[...])
         vpre_ref[i] = value_pre
         rpre_ref[i] = reset_pre
         values = silu(value_pre).astype(LOW)
@@ -229,15 +241,14 @@
         united_ref[i] = (silu(reset_pre) * att_ref[i]).astype(LOW)
 
 
-def blend_part(offs_ref, x_ref, mixed_ref, gate_ref, u0_ref, u1_ref, g0_ref, g1_ref, g2_ref, g3_ref, gain_ref, hpre_ref, blended_ref, second_ref, whid_ref):
+def blend_part(offs_ref, x_ref, mixed_ref, gate_ref, u0_ref, u1_ref, ga_ref, gb_ref, gain_ref, hpre_ref, blended_ref, second_ref, whid_ref):
     cols = whid_ref.shape[0] // 4
-    packs = (g0_ref, g1_ref, g2_ref, g3_ref)
-    for r, g_ref in enumerate(packs):
-        whid_ref[pl.ds(pl.multiple_of(offs_ref[r], 64), cols), :] = g_ref[:cols, :]
+    for r in range(4):
+        whid_ref[pl.ds(pl.multiple_of(offs_ref[r], 64), cols), :] = (ga_ref, gb_ref)[r % 2][r // 2, :cols, :]
     hidden_pre = dot(mixed_ref[...], whid_ref[...])
-    for r, g_ref in enumerate(packs):
+    for r in range(4):
         united = (u0_ref, u1_ref)[r // 2][r % 2]
-        hidden_pre = hidden_pre + dot(united, g_ref[cols:, :])
+        hidden_pre = hidden_pre + dot(united, (ga_ref, gb_ref)[r % 2][r // 2, cols:, :])
     hpre_ref[...] = hidden_pre
     x = x_ref[...].astype(F32)
     blended = x + gate_ref[...] * (silu(hidden_pre) - x)
@@ -295,17 +306,17 @@
                 ].astype(pack_ref.dtype)
 
 
-def value_back(hidden_ref, normed_ref, mixed_ref, probs_ref, vpre_ref, rpre_ref, att_ref, united_ref, ga_ref, gb_ref, wa_ref, wb_ref, ng_ref, mg_ref, pg_ref, keep_ref, send_ref):
+def value_back(part, hidden_ref, normed_ref, mixed_ref, probs_ref, vpre_ref, rpre_ref, att_ref, united_ref, ga_ref, gb_ref, va_ref, ra_ref, vb_ref, rb_ref, ng_ref, mg_ref, pg_ref, keep_ref, send_ref):
     hidden, normed, mixed = hidden_ref[...], normed_ref[...], mixed_ref[...]
     tokens, depth = hidden.shape
-    units = wa_ref.shape[1]
-    cols = ga_ref.shape[0] - units
+    units = va_ref.shape[1]
+    cols = ga_ref.shape[1] - units
     half = depth // 2
-    for i, (g_ref, w_ref, pack_ref) in enumerate(
-        ((ga_ref, wa_ref, keep_ref), (gb_ref, wb_ref, send_ref))
+    for i, (g_ref, v_ref, r_ref, pack_ref) in enumerate(
+        ((ga_ref, va_ref, ra_ref, keep_ref), (gb_ref, vb_ref, rb_ref, send_ref))
     ):
         kind = pack_ref.dtype
-        united_grad = dot_cols(hidden, g_ref[cols:, :])
+        united_grad = dot_cols(hidden, g_ref[part, cols:, :])
         reset_pre, value_pre = rpre_ref[i], vpre_ref[i]
         reset_low = (united_grad * att_ref[i] * silu_slope(reset_pre)).astype(LOW)
         attended_low = (united_grad * silu(reset_pre)).astype(LOW)
@@ -317,8 +328,8 @@
             back = dot_cols(attended_low[block], values[block])
             pg_ref[block, :] = back if i == 0 else pg_ref[block, :] + back
         value_low = (jnp.concatenate(parts, 0) * silu_slope(value_pre)).astype(LOW)
-        into_normed = dot_cols(value_low, w_ref[:depth, :])
-        into_mixed = dot_cols(reset_low, w_ref[depth:, :])
+        into_normed = dot_cols(value_low, v_ref[...])
+        into_mixed = dot_cols(reset_low, r_ref[...])
         ng_ref[...] = into_normed if i == 0 else ng_ref[...] + into_normed
         mg_ref[...] = into_mixed if i == 0 else mg_ref[...] + into_mixed
         pack_ref[:depth, :] = dot_rows(mixed, reset_low).astype(kind)
@@ -478,55 +489,115 @@
     )
 
 
+def parity_of(bit):
+    return (lax.axis_index("dp") // bit) & 1
+
+
+def half_of(share, bit):
+    half = share.shape[0] // 2
+    return lax.dynamic_slice_in_dim(share, parity_of(bit) * half, half)
+
+
+def joined(mine, other, bit):
+    return jnp.where(
+        parity_of(bit) == 0,
+        jnp.concatenate([mine, other], 0),
+        jnp.concatenate([other, mine], 0),
+    )
+
+
+tied = lax.optimization_barrier
+
+
 def rounded(v):
     return lax.reduce_precision(v, 8, 7)
 
 
-def sum_over_rows(s):
-    size, index = lax.axis_size("dp"), lax.axis_index("dp")
-    bits = size.bit_length() - 1
-    halvings = min(2, bits - 1)
-    for b in range(halvings):
-        bit, half = (index >> b) & 1, s.shape[0] // 2
-        away = lax.dynamic_slice_in_dim(s, (1 - bit) * half, half).astype(LOW)
-        mine = lax.dynamic_slice_in_dim(s, bit * half, half)
-        s = mine + swap(away, "dp", 1 << b).astype(F32)
-    s = rounded(s)
-    for b in range(halvings, bits):
-        s = rounded(s + swap(s.astype(LOW), "dp", 1 << b).astype(F32))
-    low = s.astype(LOW)
-    for b in reversed(range(halvings)):
-        bit = (index >> b) & 1
-        got = swap(low, "dp", 1 << b)
-        low = jnp.where(
-            bit == 0, jnp.concatenate([low, got], 0), jnp.concatenate([got, low], 0)
-        )
+def halves(v, bit):
+    half, parity = v.shape[0] // 2, parity_of(bit)
+    return (
+        lax.dynamic_slice_in_dim(v, parity * half, half),
+        lax.dynamic_slice_in_dim(v, (1 - parity) * half, half).astype(LOW),
+    )
+
+
+def reduction(kind, near, far):
+    bits = [1 << b for b in range(lax.axis_size("dp").bit_length() - 1)]
+    lead = {"x": [1], "z": [2]}.get(kind, [])
+    spread = {"x": [2], "z": [1], "y": [1, 2], "w": [2, 1]}[kind]
+    near, far = near(), far()
+    for bit in lead:
+        near, away = halves(near, bit)
+        far, far_away = halves(far, bit)
+        got = yield "dp", bit, jnp.concatenate([away, far_away], 0)
+        got = got.astype(F32)
+        near, far = near + got[: near.shape[0]], far + got[near.shape[0] :]
+    got = yield "tensor", 2, far.astype(LOW)
+    total = near + got.astype(F32)
+    for bit in spread:
+        total, away = halves(total, bit)
+        got = yield "dp", bit, away
+        total = total + got.astype(F32)
+    for bit in bits[2:]:
+        total = rounded(total)
+        got = yield "dp", bit, total.astype(LOW)
+        total = total + got.astype(F32)
+    low = total.astype(LOW)
+    for bit in reversed(lead + spread):
+        got = yield "dp", bit, low
+        low = joined(low, got, bit)
     return low
 
 
-def reduced(keep0, send0, keep1, send1):
-    got1 = swap(send1, "tensor", 1)
-    across = (keep1 + got1.astype(F32)).astype(LOW)
-    got0 = swap(send0, "tensor", 1)
-    over = swap(across, "tensor", 2)
-    return sum_over_rows(keep0 + got0.astype(F32) + over.astype(F32))
+def one_swap(axis, bit, v):
+    got = yield axis, bit, v
+    return got
+
+
+def everywhere(v, kind):
+    for axis in ("tensor", "dp"):
+        for b in range(lax.axis_size(axis).bit_length() - 1):
+            v = lax.reduce_precision(v, 8, 7) if kind == LOW else v
+            got = yield axis, 1 << b, v.astype(kind)
+            v = v + got.astype(F32)
+    return v
+
+
+class Pump:
+    def __init__(self, token):
+        self.token = token
+        self.flows, self.ready, self.flying, self.done = {}, {}, {}, {}
+
+    def gate(self, v):
+        v, self.token = tied((v, self.token))
+        return v
+
+    def add(self, name, flow):
+        self.flows[name] = flow
+        self.ready[name] = next(flow)
+
+    def issue(self, name):
+        axis, bit, v = self.ready.pop(name)
+        self.flying[name] = swap(self.gate(v), axis, bit)
+
+    def finish(self, name):
+        got = self.gate(self.flying.pop(name))
+        try:
+            self.ready[name] = self.flows[name].send(got)
+        except StopIteration as end:
+            self.done[name] = end.value
+
+    def drain(self):
+        while self.ready or self.flying:
+            for name in list(self.ready):
+                self.issue(name)
+            for name in list(self.flying):
+                self.finish(name)
 
 
 def side_by_side(pack):
     half = pack.shape[0] // 2
     return jnp.concatenate([pack[:half], pack[half:]], 1)
-
-
-def butterfly(v, low):
-    for axis in ("tensor", "dp"):
-        size = lax.axis_size(axis)
-        for b in range(size.bit_length() - 1):
-            if low:
-                v = rounded(v)
-                v = v + swap(v.astype(LOW), axis, 1 << b).astype(F32)
-            else:
-                v = v + swap(v, axis, 1 << b)
-    return v
 
 
 def shards(
@@ -564,16 +635,6 @@
     g1, g2, om = norm1_gain[None], norm2_gain[None], ema_omega[None]
     qg, qb, kg = q_gain[None], q_bias[None], k_gain[None]
 
-    pack_a = jnp.concatenate([w_value, w_reset], 0)
-    pack_g = jnp.concatenate([w_hidden, w_out], 0)
-    shares = (pack_a, pack_g, w_ffn_in, w_ffn_out)
-    over = [swap(w, "tensor", 2) for w in shares]
-    beside = [swap(w, "tensor", 1) for w in shares]
-    both = [swap(w, "tensor", 1) for w in over]
-    wa, wg, wi, wo = (
-        (own, b, o, d) for own, b, o, d in zip(shares, beside, over, both, strict=True)
-    )
-
     docs = doc_lengths.shape[1]
     order = jnp.arange(docs)
     ends = jnp.sum(
@@ -605,6 +666,17 @@
     finals = (rows * dims, width)
     slabs = (tokens * width // LANES, LANES)
 
+    w_join = jnp.concatenate([w_hidden, w_out], 0)
+    shares = (w_value, w_reset, w_join, w_ffn_in, w_ffn_out)
+    bits = (1, 1, 2, 1, 1)
+    pump = Pump(offs)
+    beside = [swap(w_value, "tensor", 1), swap(w_reset, "tensor", 1)]
+    half_v, half_r, half_g, half_i, half_o = (
+        half_of(w, bit) for w, bit in zip(shares, bits, strict=True)
+    )
+
+    over_v = swap(half_v, "tensor", 2)
+
     normed, normed_low, init, last = call(
         functools.partial(first_pass, rows),
         [(slabs, F32), (wide, LOW), (chunked, F32), (finals, F32)],
@@ -613,6 +685,10 @@
         [vm(tab), vm(tab)],
     )
     f1, f2 = shift(last, 1), shift(last, 2)
+    f1, f2 = pump.gate(f1), pump.gate(f2)
+    beside = [pump.gate(w) for w in beside]
+    over_r = swap(pump.gate(half_r), "tensor", 2)
+    beside += [swap(pump.gate(w), "tensor", 1) for w in (w_ffn_in, w_ffn_out)]
     pre, mixed_low, z_pre, gate, probs = call(
         functools.partial(second_pass, rows),
         [(slabs, F32), (wide, LOW), ((tokens, zd), F32), (wide, F32), ((tokens, STRETCH), F32)],
@@ -622,77 +698,176 @@
         [vm(tab), vm(tab)],
     )
     split = (2, tokens, units)
-    kept_parts = []
-    for p in range(2):
-        kept_parts.append(
-            call(
-                value_part,
-                [(split, F32), (split, F32), (split, F32), (split, LOW)],
-                (normed_low, mixed_low, probs, wa[2 * p], wa[2 * p + 1]),
-                4 * mat * units,
-            )
+    mixed_low = pump.gate(mixed_low)
+    over_v = pump.gate(over_v)
+    other_v = swap(over_v, "dp", 1)
+    over_g = swap(pump.gate(half_g), "tensor", 2)
+    beside = [pump.gate(w) for w in beside]
+    mixed_low = pump.gate(mixed_low)
+
+    def values(weights):
+        return call(
+            value_part,
+            [(split, F32), (split, F32), (split, F32), (split, LOW)],
+            (normed_low, mixed_low, probs, *weights),
+            4 * mat * units,
         )
+
+    own_part = values((w_value, w_reset, beside[0], beside[1]))
+    united0 = pump.gate(own_part[3])
+    over_r = pump.gate(over_r)
+    other_r = swap(over_r, "dp", 1)
+    over_i = swap(pump.gate(half_i), "tensor", 2)
+    other_v = pump.gate(other_v)
+    full_v = pump.gate(joined(over_v, other_v, 1))
+    both_v = swap(full_v, "tensor", 1)
+    over_g = pump.gate(over_g)
+    other_g = swap(over_g, "dp", 2)
+    over_o = swap(pump.gate(half_o), "tensor", 2)
+    other_r = pump.gate(other_r)
+    full_r = pump.gate(joined(over_r, other_r, 1))
+    both_r = swap(full_r, "tensor", 1)
+    both_v, both_r = pump.gate(both_v), pump.gate(both_r)
+    over_i = pump.gate(over_i)
+    full_v = pump.gate(full_v)
+    far_part = values((full_v, full_r, both_v, both_r))
+    united1 = pump.gate(far_part[3])
+    other_i = swap(over_i, "dp", 1)
+    over_o = pump.gate(over_o)
+    other_o = swap(over_o, "dp", 1)
+    other_g = pump.gate(other_g)
+    near_g = pump.gate(jnp.stack([w_join, joined(over_g, other_g, 2)]))
+    beside_g = swap(near_g, "tensor", 1)
+    other_i = pump.gate(other_i)
+    full_i = pump.gate(joined(over_i, other_i, 1))
+    both_i = swap(full_i, "tensor", 1)
+    beside_g = pump.gate(beside_g)
+    wg = (near_g, beside_g)
+    wv, wr = (w_value, beside[0], full_v, both_v), (w_reset, beside[1], full_r, both_r)
+    kept_parts = ((*own_part[:3], united0), (*far_part[:3], united1))
     hidden_pre, blended, second, whid = call(
         blend_part,
         [(wide, F32), (wide, F32), (wide, LOW), ((width, width), LOW)],
-        (offs, x, mixed_low, gate, kept_parts[0][3], kept_parts[1][3], *wg, g2),
+        (offs, x, mixed_low, gate, united0, united1, *wg, g2),
         mat * (width + 4 * units),
         smem=(0,),
     )
+    second = pump.gate(second)
     ffn_rows = width + 2 * units
-    ffn = [None, None]
-    for p in (1, 0):
-        ffn[p] = call(
+
+    def ffn_of(weights):
+        return call(
             ffn_part,
             [(wide, F32), (wide, F32), ((ffn_rows, units), F32), ((ffn_rows, units), LOW)],
-            (second, cot, wi[2 * p], wi[2 * p + 1], wo[2 * p], wo[2 * p + 1]),
+            (second, cot, *weights),
             12 * mat * units,
         )
-    ffn_sum = reduced(ffn[0][2], ffn[0][3], ffn[1][2], ffn[1][3])
+
+    ffn0 = ffn_of((w_ffn_in, beside[2], w_ffn_out, beside[3]))
+    back0 = pump.gate(ffn0[1])
+    other_o = pump.gate(other_o)
+    full_o = pump.gate(joined(over_o, other_o, 1))
+    both_o = swap(full_o, "tensor", 1)
+    both_i, both_o = pump.gate(both_i), pump.gate(both_o)
+    ffn1 = ffn_of((full_i, both_i, full_o, both_o))
+    pump.add("F0", one_swap("tensor", 1, ffn0[3]))
+    pump.add("F1", one_swap("tensor", 1, ffn1[3]))
     own = (2, 4 * cols, width // 2)
-    output, direct, hidden_low, mixed0, gain2, keep_u, send_u = call(
-        blend_back,
-        [(wide, LOW), (wide, F32), (wide, LOW), (wide, F32), ((1, width), F32), (own, F32), (own, LOW)],
-        (offs, x, cot, blended, ffn[0][1], ffn[1][1], ffn[0][0], ffn[1][0], hidden_pre, gate,
-         mixed_low, g2, w_update, whid),
-        4 * mat * width,
-        [vm((width, width))],
-        smem=(0,),
-    )
-    pair_sum = reduced(keep_u[0], send_u[0], keep_u[1], send_u[1])
-    rest = [None, None]
     pack_rows = 2 * width + 2 * units
-    for p in (1, 0):
-        rest[p] = call(
-            value_back,
+    held = {}
+
+    def run_blend():
+        held["bb"] = call(
+            blend_back,
+            [(wide, LOW), (wide, F32), (wide, LOW), (wide, F32), ((1, width), F32), (own, F32), (own, LOW)],
+            (offs, x, cot, pump.gate(blended), ffn1[1], back0, ffn0[0], ffn1[0], hidden_pre, gate,
+             mixed_low, g2, w_update, whid),
+            4 * mat * width,
+            [vm((width, width))],
+            smem=(0,),
+        )
+        held["hidden"] = pump.gate(held["bb"][2])
+        pump.add("P0", one_swap("tensor", 1, held["bb"][6]))
+
+    def run_values(p):
+        held[p] = [*call(
+            functools.partial(value_back, p),
             [(wide, F32), (wide, F32), ((tokens, STRETCH), F32), ((pack_rows, units), F32), ((pack_rows, units), LOW)],
-            (hidden_low, normed_low, mixed_low, probs, *kept_parts[p], wg[2 * p], wg[2 * p + 1],
-             wa[2 * p], wa[2 * p + 1]),
+            (pump.gate(held["hidden"]), normed_low, mixed_low, probs, *kept_parts[p], *wg,
+             wv[2 * p], wr[2 * p], wv[2 * p + 1], wr[2 * p + 1]),
             14 * mat * units,
+        )]
+        pump.token, held[p][2] = tied((pump.token, held[p][2]))
+        pump.add(f"V{p}", one_swap("tensor", 1, held[p][4]))
+
+    def run_third():
+        held["t3"] = call(
+            functools.partial(third_pass, rows),
+            [(slabs, F32), ((width, zd), F32), ((8, zd), F32), (chunked, F32), (chunked, F32), (finals, F32), (finals, F32)],
+            (pump.gate(z_pre), probs, held[0][2], held[1][2], qg, qb, kg, w_z, mixed_low, held["bb"][3],
+             held[0][1], held[1][1], pre, keep, alpha_raw, delta_raw),
+            2 * ema,
+            [vm((2, tokens, zd))],
         )
-    cut = width + 2 * units
-    sums_c = reduced(*(rest[p][i][:cut] for p in range(2) for i in (3, 4)))
-    sums_d = reduced(*(rest[p][i][cut:] for p in range(2) for i in (3, 4)))
-    pre_grad, dz, small, im, iv, lm, lv = call(
-        functools.partial(third_pass, rows),
-        [(slabs, F32), ((width, zd), F32), ((8, zd), F32), (chunked, F32), (chunked, F32), (finals, F32), (finals, F32)],
-        (z_pre, probs, rest[0][2], rest[1][2], qg, qb, kg, w_z, mixed_low, mixed0, rest[0][1],
-         rest[1][1], pre, keep, alpha_raw, delta_raw),
-        2 * ema,
-        [vm((2, tokens, zd))],
-    )
-    dz_sum = butterfly(dz, True)
-    back = jnp.concatenate([lm, lv], 0)
-    near, far = shift(back, -1), shift(back, -2)
-    input_grad, sums = call(
-        functools.partial(fourth_pass, rows),
-        [(wide, LOW), ((2 * dims + 8, width), F32)],
-        (pre_grad, normed, im, iv, near, far, keep, unbroken(member + 1), alpha_raw, delta_raw,
-         ema_beta, ema_eta, om, rest[0][0], rest[1][0], x, g1, direct, gain2, small),
-        2 * ema,
-        [vm(tab), vm(tab), vm(slabs)],
-    )
-    sums = butterfly(sums, False)
+        pump.add("dz", everywhere(held["t3"][1], LOW))
+
+    def send_back():
+        back = pump.gate(jnp.concatenate([held["t3"][5], held["t3"][6]], 0))
+        held["back"] = shift(back, -1), shift(back, -2)
+
+    def take_back():
+        held["back"] = [pump.gate(v) for v in held["back"]]
+
+    def run_fourth():
+        t3 = held["t3"]
+        held["t4"] = call(
+            functools.partial(fourth_pass, rows),
+            [(wide, LOW), ((2 * dims + 8, width), F32)],
+            (t3[0], normed, t3[3], t3[4], *held["back"], keep, unbroken(member + 1), alpha_raw,
+             delta_raw, ema_beta, ema_eta, om, held[0][0], held[1][0], x, g1, held["bb"][1],
+             held["bb"][4], t3[2]),
+            2 * ema,
+            [vm(tab), vm(tab), vm(slabs)],
+        )
+        pump.add("sm", everywhere(pump.gate(held["t4"][1]), F32))
+
+    def pack(p, source, at, end):
+        kept = (ffn0, ffn1)[p][2] if source == "F" else held[p][3]
+        return kept[at:end] + pump.done[f"{source}{p}"][at:end].astype(F32)
+
+    def add_flow(name):
+        if name == "P":
+            kept, got = held["bb"][5], pump.done["P0"].astype(F32)
+            near, far = (lambda: kept[0] + got[0]), (lambda: kept[1] + got[1])
+        else:
+            source = "F" if name == "F" else "V"
+            at, end = {"F": (0, 2 * width), "R": (0, width), "O": (width, 2 * width), "N": (2 * width, 3 * width)}[name]
+            near, far = (lambda: pack(0, source, at, end)), (lambda: pack(1, source, at, end))
+        pump.add(name, reduction(KINDS[name], near, far))
+
+    kernels = {
+        "bb": run_blend,
+        "v1": lambda: run_values(1),
+        "v0": lambda: run_values(0),
+        "t3": run_third,
+        "t4": run_fourth,
+    }
+    for word in ORDER:
+        sign, name = word[0], word[1:]
+        if sign == "K":
+            kernels[name]()
+        elif name == "E":
+            (send_back if sign == "+" else take_back)()
+        elif sign == "+":
+            if name in KINDS and name not in pump.flows:
+                add_flow(name)
+            pump.issue(name)
+        else:
+            pump.finish(name)
+    pump.drain()
+    output, input_grad = held["bb"][0], held["t4"][0]
+    sums, dz_sum, pair_sum, ffn_sum = (pump.done[n] for n in ("sm", "dz", "P", "F"))
+    reset_sum, out_sum, value_sum = (pump.done[n] for n in "RON")
 
     alpha, sigma = jax.nn.sigmoid(alpha_raw), jax.nn.sigmoid(delta_raw)
     with_mu, with_nu = sums[:dims], sums[dims : 2 * dims]
@@ -718,11 +893,11 @@
         sums[at + 3, :zd],
         sums[at + 3, zd : 2 * zd],
         sums[at + 3, 2 * zd : 3 * zd],
-        sums_d.astype(F32),
-        sums_c[:width].astype(F32),
+        value_sum.astype(F32),
+        reset_sum.astype(F32),
         update_grad.astype(F32),
         side_by_side(pair_sum[2 * cols :]).astype(F32),
-        side_by_side(sums_c[width:]).astype(F32),
+        side_by_side(out_sum).astype(F32),
         sums[at + 2],
         ffn_sum[:width].astype(F32),
         side_by_side(ffn_sum[width:]).astype(F32),

time: 376 us -> 303 us (0.81)
  waiting for transfers between devices: 173 us -> 74.3 us
  local copies, waits for them, and re-layouts: 15.4 us -> 42.2 us
  starting transfers between devices: 100 us -> 81.8 us
  other arithmetic: 18 us -> 35.7 us
    ppermute x56 -> x66, waiting for transfers between devices: 164 us -> 74.3 us  [swap(): return lax.ppermute(x, axis, [(i, i ^ bit) for i in range(size)])]
    unnamed x113 -> x205, local copies, waits for them, and re-layouts: 11.8 us -> 32.9 us
    ppermute x56 -> x66, starting transfers between devices: 93.6 us -> 72.8 us  [swap(): return lax.ppermute(x, axis, [(i, i ^ bit) for i in range(size)])]
    ppermute x4, waiting for transfers between devices: 8.88 us -> 0.01 us  [shift(): lax.ppermute(x, 'tensor', [(i, i + by) for i in range(size) if 0 <= i + b...]
    select_n x7 -> x13, other arithmetic: 1.59 us -> 8.41 us  [joined(): jnp.where(parity_of(bit) == 0, jnp.concatenate([mine, other], 0), jnp.con...]
    add x14 -> x15, other arithmetic: 3.21 us -> 7.54 us  [the longest x2 3.71 us: pack(): return kept[at:end] + pump.done[f'{source}{p}'][at:end].astype(F32)]
    dynamic_slice x0 -> x5, local copies, waits for them, and re-layouts: none -> 4.26 us  [half_of(): return lax.dynamic_slice_in_dim(share, parity_of(bit) * half, half)]
    convert_element_type x20 -> x27, other arithmetic: 7.09 us -> 9.75 us  [the longest x4 3.55 us: reduction(): got = (yield ('tensor', 2, far.astype(LOW)))]
  transfers between devices with their start and end apart: 60 -> 70, of which waited for: 29 -> 21; matrix products, arithmetic and copies ran while one was open for 5% -> 13% of each run, Pallas kernels for 8% -> 20%
where the time goes in v1:
time: 303 us; the launch traced here: 299 us
  starting transfers between devices  81.8 us (27%)
  waiting for transfers between devices  74.3 us (25%)
  Pallas kernels  62.3 us (21%)
  local copies, waits for them, and re-layouts  42.2 us (14%)
  other arithmetic  35.7 us (12%)
    ppermute x66, waiting for transfers between devices, swap(): return lax.ppermute(x, axis, [(i, i ^ bit) for i in range(size)])  74.3 us
    ppermute x66, starting transfers between devices, swap(): return lax.ppermute(x, axis, [(i, i ^ bit) for i in range(size)])  72.8 us
    pallas_call x12, Pallas kernels, call(): pl.pallas_call(kernel, out_shape=outs, in_specs=specs, out_specs=[pl.Bloc...  62.3 us
    unnamed x205, local copies, waits for them, and re-layouts  32.9 us
    ppermute x4, starting transfers between devices, shift(): lax.ppermute(x, 'tensor', [(i, i + by) for i in range(size) if 0 <= i + b...  8.94 us
    select_n x13, other arithmetic, joined(): jnp.where(parity_of(bit) == 0, jnp.concatenate([mine, other], 0), jnp.con...  8.41 us
  transfers between devices with their start and end apart: 70, of which 21 were waited for; matrix products, arithmetic and copies ran while one was open for 13% of the time, Pallas kernels for 20%

profile of v1, /device:TPU:0, one launch (start us, length us, event | category | flops | bytes accessed | tf_op | source)
XLA Modules:
  0.0 298.9 jit_solution(8858420435105849859)
XLA Ops:
  7.1 3.0 %shard_map.356 = (f32[1536,128]{1,0:T(8,128)S(1)}, bf16[256,768]{1,0:T(8,128)(2,1)S(1)}, f32[256,768]{1,0:T(8,128)S(1)}, f32[32,768]{1,0:T(8,128)S(1)}) custom-call(bf16[256,768]{1,0:T(8,128)(2,1)S(1)} %bitcast.50, f32[1,768]{1,0:T(1,128)S(1)} %broadcast_in_dim.34.g_ref, f32[16,768]{1,0:T(8,128)S(1)} %copy-done.21, f32[16,768]{1,0:T(8,128)S(1)} %copy-done.24, ...), custom_call_target="tpu_custom_call" | custom-call | flops 25165824 | bytes 2739200 | tf_op jit(solution)/shard_map/pallas_call | solution.py:72
  11.8 4.9 %collective-permute-start.1 = (f32[32,768]{1,0:T(8,128)S(1)}, f32[32,768]{1,0:T(8,128)S(1)}, u32[]{:S(2)}, u32[]{:S(2)}) collective-permute-start(f32[32,768]{1,0:T(8,128)S(1)} %get-tuple-element.332), channel_id=1, source_target_pairs={{0,2},{1,3},{4,6},{5,7},{8,10},{9,11},{12,14},{13,15},{16,18},{17,... | collective-permute-start | bytes 294920 | tf_op jit(solution)/shard_map/ppermute | solution.py:487
  18.8 1.7 constant_dynamic-slice_fusion.2
  23.7 2.1 collective-permute-start.8
  27.8 4.4 %shard_map.357 = (f32[1536,128]{1,0:T(8,128)S(1)}, bf16[256,768]{1,0:T(8,128)(2,1)S(1)}, f32[256,128]{1,0:T(8,128)S(1)}, f32[256,768]{1,0:T(8,128)S(1)}, f32[256,128]{1,0:T(8,128)S(1)}) custom-call(f32[1536,128]{1,0:T(8,128)S(1)} %copy-done.12, f32[256,768]{1,0:T(8,128)S(1)} %copy-done.35, f32[32,768]{1,0:T(8,128)S(1)} %copy-done.68, ...), custom_call_target="tpu_custom_call" | custom-call | flops 327155712 | bytes 5838336 | tf_op jit(solution)/shard_map/pallas_call | solution.py:72
  37.0 2.2 shard_map.358
  42.5 1.7 constant_dynamic-slice_fusion
  45.9 4.7 %collective-permute-done.10 = bf16[384,384]{1,0:T(8,128)(2,1)} collective-permute-done((bf16[384,384]{1,0:T(8,128)(2,1)}, bf16[384,384]{1,0:T(8,128)(2,1)}, u32[]{:S(2)}, u32[]{:S(2)}) %collective-permute-start.10) | collective-permute-done | bytes 294944 | tf_op jit(solution)/shard_map/ppermute | solution.py:482
  53.9 1.7 collective-permute-start.9
  55.9 8.0 %collective-permute-done.9 = bf16[384,384]{1,0:T(8,128)(2,1)} collective-permute-done((bf16[384,384]{1,0:T(8,128)(2,1)S(1)}, bf16[384,384]{1,0:T(8,128)(2,1)}, u32[]{:S(2)}, u32[]{:S(2)}) %collective-permute-start.9) | collective-permute-done | bytes 294944 | tf_op jit(solution)/shard_map/ppermute | solution.py:482
  63.9 2.1 shard_map.359
  66.1 3.3 %collective-permute-done.15 = bf16[192,768]{1,0:T(8,128)(2,1)} collective-permute-done((bf16[192,768]{1,0:T(8,128)(2,1)}, bf16[192,768]{1,0:T(8,128)(2,1)}, u32[]{:S(2)}, u32[]{:S(2)}) %collective-permute-start.15) | collective-permute-done | bytes 294944 | tf_op jit(solution)/shard_map/ppermute | solution.py:482
  73.5 8.1 %collective-permute-done.17 = bf16[384,384]{1,0:T(8,128)(2,1)S(1)} collective-permute-done((bf16[384,384]{1,0:T(8,128)(2,1)}, bf16[384,384]{1,0:T(8,128)(2,1)S(1)}, u32[]{:S(2)}, u32[]{:S(2)}) %collective-permute-start.17) | collective-permute-done | bytes 294944 | tf_op jit(solution)/shard_map/ppermute | solution.py:482
  84.1 3.8 %shard_map.360 = (f32[256,768]{1,0:T(8,128)S(1)}, f32[256,768]{1,0:T(8,128)S(1)}, bf16[256,768]{1,0:T(8,128)(2,1)S(1)}, bf16[768,768]{1,0:T(8,128)(2,1)S(1)}) custom-call(s32[4]{0:T(128)S(1)} %xor_multiply_fusion.offs_ref, bf16[256,768]{1,0:T(8,128)(2,1)S(1)} %bitcast.51, bf16[256,768]{1,0:T(8,128)(2,1)S(1)} %get-tuple-element.355.mixed_ref, ...), custom_call_target="tpu_custom_call" | custom-call | flops 905969664 | bytes 9047056 | tf_op jit(solution)/shard_map/pallas_call | solution.py:72
  89.8 3.6 %shard_map.361 = (f32[256,768]{1,0:T(8,128)S(1)}, f32[256,768]{1,0:T(8,128)S(1)}, f32[1536,384]{1,0:T(8,128)}, bf16[1536,384]{1,0:T(8,128)(2,1)S(1)}) custom-call(bf16[256,768]{1,0:T(8,128)(2,1)S(1)} %get-tuple-element.407.second_ref, bf16[256,768]{1,0:T(8,128)(2,1)S(1)} %bitcast.54, bf16[768,384]{1,0:T(8,128)(2,1)S(1)} %copy-done.57, ...), custom_call_target="tpu_custom_call" | custom-call | flops 1811939328 | bytes 8257536 | tf_op jit(solution)/shard_map/pallas_call | solution.py:72
  98.1 3.6 %shard_map.362 = (f32[256,768]{1,0:T(8,128)S(1)}, f32[256,768]{1,0:T(8,128)S(1)}, f32[1536,384]{1,0:T(8,128)}, bf16[1536,384]{1,0:T(8,128)(2,1)S(1)}) custom-call(bf16[256,768]{1,0:T(8,128)(2,1)S(1)} %get-tuple-element.407.second_ref, bf16[256,768]{1,0:T(8,128)(2,1)S(1)} %bitcast.55, bf16[768,384]{1,0:T(8,128)(2,1)S(1)} %maximum_select_fusion.4.ia_ref, ...), custom_call_target="tpu_custom_call" | custom-call | flops 1811939328 | bytes 8257536 | tf_op jit(solution)/shard_map/pallas_call | solution.py:72
  102.8 7.1 %shard_map.363 = (bf16[256,768]{1,0:T(8,128)(2,1)}, f32[256,768]{1,0:T(8,128)S(1)}, bf16[256,768]{1,0:T(8,128)(2,1)S(1)}, f32[256,768]{1,0:T(8,128)S(1)}, f32[1,...) custom-call(s32[4]{0:T(128)S(1)} %xor_multiply_fusion.offs_ref, ...), custom_call_target="tpu_custom_call" | custom-call | flops 1207959552 | bytes 14948368 | tf_op jit(solution)/shard_map/pallas_call | solution.py:72
  111.2 8.0 %shard_map.364 = (f32[256,768]{1,0:T(8,128)S(1)}, f32[256,768]{1,0:T(8,128)S(1)}, f32[256,128]{1,0:T(8,128)S(1)}, f32[2304,384]{1,0:T(8,128)}, bf16[2304,384]{1,0:T(8,128)(2,1)}) custom-call(bf16[256,768]{1,0:T(8,128)(2,1)S(1)} %get-tuple-element.463.hidden_ref, bf16[256,768]{1,0:T(8,128)(2,1)S(1)} %get-tuple-element.357.normed_ref, ...), custom_call_target="tpu_custom_call" | custom-call | flops 2113929216 | bytes 16973824 | tf_op jit(solution)/shard_map/pallas_call | solution.py:72
  121.8 3.2 %add_convert_fusion = bf16[1536,384]{1,0:T(8,128)(2,1)} fusion(f32[1536,384]{1,0:T(8,128)} %get-tuple-element.456, bf16[1536,384]{1,0:T(8,128)(2,1)} %collective-permute-done.21), kind=kLoop, calls=%fused_computation.1 | loop fusion | flops 1769472 | bytes 4718592 | tf_op jit(solution)/shard_map/convert_element_type | solution.py:535
  130.0 8.1 %shard_map.365 = (f32[256,768]{1,0:T(8,128)S(1)}, f32[256,768]{1,0:T(8,128)S(1)}, f32[256,128]{1,0:T(8,128)S(1)}, f32[2304,384]{1,0:T(8,128)}, bf16[2304,384]{1,0:T(8,128)(2,1)}) custom-call(bf16[256,768]{1,0:T(8,128)(2,1)S(1)} %get-tuple-element.463.hidden_ref, bf16[256,768]{1,0:T(8,128)(2,1)S(1)} %get-tuple-element.357.normed_ref, ...), custom_call_target="tpu_custom_call" | custom-call | flops 2113929216 | bytes 16973824 | tf_op jit(solution)/shard_map/pallas_call | solution.py:72
  147.2 7.0 %shard_map.366 = (f32[1536,128]{1,0:T(8,128)S(1)}, f32[768,128]{1,0:T(8,128)S(1)}, f32[8,128]{1,0:T(8,128)S(1)}, f32[256,768]{1,0:T(8,128)S(1)}, f32[256,768]{1,...) custom-call(f32[256,128]{1,0:T(8,128)S(1)} %copy-done.60, f32[256,128]{1,0:T(8,128)S(1)} %copy-done.8, ...), custom_call_target="tpu_custom_call" | custom-call | flops 50331648 | bytes 7443968 | tf_op jit(solution)/shard_map/pallas_call | solution.py:72
  154.2 2.0 convert_add_fusion.2
  161.4 1.7 convert_add_fusion.3
  166.0 3.6 %collective-permute-done.27 = bf16[1536,384]{1,0:T(8,128)(2,1)} collective-permute-done((bf16[1536,384]{1,0:T(8,128)(2,1)}, bf16[1536,384]{1,0:T(8,128)(2,1)}, u32[]{:S(2)}, u32[]{:S(2)}) %collective-permute-start.27) | collective-permute-done | bytes 1179680 | tf_op jit(solution)/shard_map/ppermute | solution.py:482
  171.6 2.1 convert_add_fusion
  173.7 5.8 %collective-permute-done.31 = bf16[768,384]{1,0:T(8,128)(2,1)S(1)} collective-permute-done((bf16[768,384]{1,0:T(8,128)(2,1)S(1)}, bf16[768,384]{1,0:T(8,128)(2,1)S(1)}, u32[]{:S(2)}, u32[]{:S(2)}) %collective-permute-start.31) | collective-permute-done | bytes 589856 | tf_op jit(solution)/shard_map/ppermute | solution.py:482
  179.9 2.7 collective-permute-start.33
  184.2 9.4 %shard_map.367 = (bf16[256,768]{1,0:T(8,128)(2,1)}, f32[40,768]{1,0:T(8,128)S(1)}) custom-call(f32[1536,128]{1,0:T(8,128)S(1)} %get-tuple-element.481.pg_ref, f32[1536,128]{1,0:T(8,128)S(1)} %copy-done.13, f32[256,768]{1,0:T(8,128)S(1)} %get-tuple-element.482.im_ref, f32[256,768]{1,0:T(8,128)S(1)} %get-tuple-element.483.iv_ref, ...), custom_call_target="tpu_custom_call" | custom-call | flops 50331648 | bytes 7149568 | tf_op jit(solution)/shard_map/pallas_call | solution.py:72
  199.5 8.4 %collective-permute-done.36 = bf16[768,384]{1,0:T(8,128)(2,1)S(1)} collective-permute-done((bf16[768,384]{1,0:T(8,128)(2,1)}, bf16[768,384]{1,0:T(8,128)(2,1)S(1)}, u32[]{:S(2)}, u32[]{:S(2)}) %collective-permute-start.36) | collective-permute-done | bytes 589856 | tf_op jit(solution)/shard_map/ppermute | solution.py:482
  211.8 2.6 collective-permute-start.42
  216.3 2.2 collective-permute-start.40
  218.8 3.3 %collective-permute-start.50 = (bf16[384,384]{1,0:T(8,128)(2,1)S(1)}, bf16[384,384]{1,0:T(8,128)(2,1)S(1)}, u32[]{:S(2)}, u32[]{:S(2)}) collective-permute-start(bf16[384,384]{1,0:T(8,128)(2,1)S(1)} %fusion.10), channel_id=1, source_target_pairs={{0,16},{4,20},{8,24},{12,28},{16,0},{20,4},{24,8},{28,12},{1,17},{... | collective-permute-start | bytes 884744 | tf_op jit(solution)/shard_map/ppermute | solution.py:482
  222.4 4.1 %collective-permute-start.46 = (bf16[384,384]{1,0:T(8,128)(2,1)S(1)}, bf16[384,384]{1,0:T(8,128)(2,1)S(1)}, u32[]{:S(2)}, u32[]{:S(2)}) collective-permute-start(bf16[384,384]{1,0:T(8,128)(2,1)S(1)} %fusion.2), channel_id=1, source_target_pairs={{0,2},{1,3},{2,0},{3,1},{4,6},{5,7},{6,4},{7,5},{8,10},{9,11},{10,... | collective-permute-start | bytes 884744 | tf_op jit(solution)/shard_map/ppermute | solution.py:482
  226.5 2.9 collective-permute-start.45
  231.2 2.6 collective-permute-done.45
  233.8 1.8 collective-permute-done.49
  236.2 4.2 %collective-permute-start.58 = (bf16[192,384]{1,0:T(8,128)(2,1)S(1)}, bf16[192,384]{1,0:T(8,128)(2,1)S(1)}, u32[]{:S(2)}, u32[]{:S(2)}) collective-permute-start(bf16[192,384]{1,0:T(8,128)(2,1)S(1)} %fusion.17), channel_id=1, source_target_pairs={{0,16},{4,20},{8,24},{12,28},{16,0},{20,4},{24,8},{28,12},{1,17},{... | collective-permute-start | bytes 442376 | tf_op jit(solution)/shard_map/ppermute | solution.py:482
  240.6 2.1 collective-permute-start.51
  244.5 2.3 collective-permute-start.55
  246.9 5.0 %collective-permute-start.52 = (f32[40,768]{1,0:T(8,128)S(1)}, f32[40,768]{1,0:T(8,128)S(1)}, u32[]{:S(2)}, u32[]{:S(2)}) collective-permute-start(f32[40,768]{1,0:T(8,128)S(1)} %add.280), channel_id=1, source_target_pairs={{0,8},{4,12},{8,0},{12,4},{16,24},{20,28},{24,16},{28,20},{1,9},{5... | collective-permute-start | bytes 368648 | tf_op jit(solution)/shard_map/ppermute | solution.py:482
  252.5 3.6 %collective-permute-done.54 = bf16[768,128]{1,0:T(8,128)(2,1)S(1)} collective-permute-done((bf16[768,128]{1,0:T(8,128)(2,1)S(1)}, bf16[768,128]{1,0:T(8,128)(2,1)S(1)}, u32[]{:S(2)}, u32[]{:S(2)}) %collective-permute-start.54) | collective-permute-done | bytes 196640 | tf_op jit(solution)/shard_map/ppermute | solution.py:482
  258.2 6.2 %collective-permute-done.66 = bf16[192,384]{1,0:T(8,128)(2,1)S(1)} collective-permute-done((bf16[192,384]{1,0:T(8,128)(2,1)S(1)}, bf16[192,384]{1,0:T(8,128)(2,1)S(1)}, u32[]{:S(2)}, u32[]{:S(2)}) %collective-permute-start.66) | collective-permute-done | bytes 147488 | tf_op jit(solution)/shard_map/ppermute | solution.py:482
  264.4 3.0 collective-permute-start.56
  267.5 2.1 collective-permute-start.67
  270.0 2.1 collective-permute-start.60
  273.3 1.7 collective-permute-done.56
  279.2 2.1 collective-permute-start.68
  284.1 8.4 %collective-permute-done.68 = bf16[384,384]{1,0:T(8,128)(2,1)S(1)} collective-permute-done((bf16[384,384]{1,0:T(8,128)(2,1)S(1)}, bf16[384,384]{1,0:T(8,128)(2,1)S(1)}, u32[]{:S(2)}, u32[]{:S(2)}) %collective-permute-start.68) | collective-permute-done | bytes 294944 | tf_op jit(solution)/shard_map/ppermute | solution.py:482
  (423 shorter events, 106.0 us)
Async XLA Ops:
  11.8 10.2 %collective-permute-start.1 = (f32[32,768]{1,0:T(8,128)S(1)}, f32[32,768]{1,0:T(8,128)S(1)}, u32[]{:S(2)}, u32[]{:S(2)}) collective-permute-start(f32[32,768]{1,0:T(8,128)S(1)} %get-tuple-element.332), channel_id=1, source_target_pairs={{0,2},{1,3},{4,6},{5,7},{8,10},{9,11},{12,14},{13,15},{16,18},{17,... | collective-permute-start | bytes 294920 | tf_op jit(solution)/shard_map/ppermute | solution.py:487
  20.5 13.2 %collective-permute-start.6 = (bf16[384,384]{1,0:T(8,128)(2,1)}, bf16[384,384]{1,0:T(8,128)(2,1)}, u32[]{:S(2)}, u32[]{:S(2)}) collective-permute-start(bf16[384,384]{1,0:T(8,128)(2,1)} %constant_dynamic-slice_fusion.2), channel_id=1, source_target_pairs={{0,2},{1,3},{2,0},{3,1},{4,6},{5,7},{6,4},{7,5},{8,10},{9,11},{10,... | collective-permute-start | bytes 884744 | tf_op jit(solution)/shard_map/ppermute | solution.py:482
  22.1 14.0 %collective-permute-start.4 = (bf16[384,768]{1,0:T(8,128)(2,1)}, bf16[384,768]{1,0:T(8,128)(2,1)S(1)}, u32[]{:S(2)}, u32[]{:S(2)}) collective-permute-start(bf16[384,768]{1,0:T(8,128)(2,1)} %oa_ref.1), channel_id=1, source_target_pairs={{0,1},{1,0},{2,3},{3,2},{4,5},{5,4},{6,7},{7,6},{8,9},{9,8},{10,11... | collective-permute-start | bytes 1769480 | tf_op jit(solution)/shard_map/ppermute | solution.py:482
  22.2 13.1 %collective-permute-start.5 = (bf16[768,384]{1,0:T(8,128)(2,1)}, bf16[768,384]{1,0:T(8,128)(2,1)S(1)}, u32[]{:S(2)}, u32[]{:S(2)}) collective-permute-start(bf16[768,384]{1,0:T(8,128)(2,1)} %ia_ref.1), channel_id=1, source_target_pairs={{0,1},{1,0},{2,3},{3,2},{4,5},{5,4},{6,7},{7,6},{8,9},{9,8},{10,11... | collective-permute-start | bytes 1769480 | tf_op jit(solution)/shard_map/ppermute | solution.py:482
  23.7 18.2 %collective-permute-start.8 = (bf16[384,384]{1,0:T(8,128)(2,1)S(1)}, bf16[384,384]{1,0:T(8,128)(2,1)}, u32[]{:S(2)}, u32[]{:S(2)}) collective-permute-start(bf16[384,384]{1,0:T(8,128)(2,1)S(1)} %constant_dynamic-slice_fusion.4), channel_id=1, source_target_pairs={{0,2},{1,3},{2,0},{3,1},{4,6},{5,7},{6,4},{7,5},{8,10},{9,11},{10,... | collective-permute-start | bytes 884744 | tf_op jit(solution)/shard_map/ppermute | solution.py:482
  33.7 12.2 %collective-permute-start.11 = (bf16[288,768]{1,0:T(8,128)(2,1)}, bf16[288,768]{1,0:T(8,128)(2,1)}, u32[]{:S(2)}, u32[]{:S(2)}) collective-permute-start(bf16[288,768]{1,0:T(8,128)(2,1)} %constant_dynamic-slice_fusion.3), channel_id=1, source_target_pairs={{0,2},{1,3},{2,0},{3,1},{4,6},{5,7},{6,4},{7,5},{8,10},{9,11},{10,... | collective-permute-start | bytes 1327112 | tf_op jit(solution)/shard_map/ppermute | solution.py:482
  33.8 10.5 %collective-permute-start.7 = (bf16[384,384]{1,0:T(8,128)(2,1)}, bf16[384,384]{1,0:T(8,128)(2,1)}, u32[]{:S(2)}, u32[]{:S(2)}) collective-permute-start(bf16[384,384]{1,0:T(8,128)(2,1)} %collective-permute-done.6), channel_id=1, source_target_pairs={{0,4},{4,0},{8,12},{12,8},{16,20},{20,16},{24,28},{28,24},{1,5},{5... | collective-permute-start | bytes 884744 | tf_op jit(solution)/shard_map/ppermute | solution.py:482
  45.9 10.0 %collective-permute-start.13 = (bf16[768,384]{1,0:T(8,128)(2,1)S(1)}, bf16[768,384]{1,0:T(8,128)(2,1)S(1)}, u32[]{:S(2)}, u32[]{:S(2)}) collective-permute-start(bf16[768,384]{1,0:T(8,128)(2,1)S(1)} %maximum_select_fusion.2.va_ref), channel_id=1, source_target_pairs={{0,1},{1,0},{2,3},{3,2},{4,5},{5,4},{6,7},{7,6},{8,9},{9,8},{10,11... | collective-permute-start | bytes 1769480 | tf_op jit(solution)/shard_map/ppermute | solution.py:482
  52.2 17.1 %collective-permute-start.14 = (bf16[288,768]{1,0:T(8,128)(2,1)}, bf16[288,768]{1,0:T(8,128)(2,1)}, u32[]{:S(2)}, u32[]{:S(2)}) collective-permute-start(bf16[288,768]{1,0:T(8,128)(2,1)} %collective-permute-done.11), channel_id=1, source_target_pairs={{0,8},{4,12},{8,0},{12,4},{16,24},{20,28},{24,16},{28,20},{1,9},{5... | collective-permute-start | bytes 1327112 | tf_op jit(solution)/shard_map/ppermute | solution.py:482
  53.9 10.0 %collective-permute-start.9 = (bf16[384,384]{1,0:T(8,128)(2,1)S(1)}, bf16[384,384]{1,0:T(8,128)(2,1)}, u32[]{:S(2)}, u32[]{:S(2)}) collective-permute-start(bf16[384,384]{1,0:T(8,128)(2,1)S(1)} %constant_dynamic-slice_fusion.1), channel_id=1, source_target_pairs={{0,2},{1,3},{2,0},{3,1},{4,6},{5,7},{6,4},{7,5},{8,10},{9,11},{10,... | collective-permute-start | bytes 884744 | tf_op jit(solution)/shard_map/ppermute | solution.py:482
  55.5 13.8 %collective-permute-start.15 = (bf16[192,768]{1,0:T(8,128)(2,1)}, bf16[192,768]{1,0:T(8,128)(2,1)}, u32[]{:S(2)}, u32[]{:S(2)}) collective-permute-start(bf16[192,768]{1,0:T(8,128)(2,1)} %constant_dynamic-slice_fusion), channel_id=1, source_target_pairs={{0,2},{1,3},{2,0},{3,1},{4,6},{5,7},{6,4},{7,5},{8,10},{9,11},{10,... | collective-permute-start | bytes 884744 | tf_op jit(solution)/shard_map/ppermute | solution.py:482
  71.3 11.5 %collective-permute-start.16 = (bf16[2,576,768]{2,1,0:T(8,128)(2,1)S(1)}, bf16[2,576,768]{2,1,0:T(8,128)(2,1)S(1)}, u32[]{:S(2)}, u32[]{:S(2)}) collective-permute-start(bf16[2,576,768]{2,1,0:T(8,128)(2,1)S(1)} %pad_maximum_fusion.ga_ref), channel_id=1, source_target_pairs={{0,1},{1,0},{2,3},{3,2},{4,5},{5,4},{6,7},{7,6},{8,9},{9,8},{10,11... | collective-permute-start | bytes 5308424 | tf_op jit(solution)/shard_map/ppermute | solution.py:482
  71.4 10.2 %collective-permute-start.17 = (bf16[384,384]{1,0:T(8,128)(2,1)}, bf16[384,384]{1,0:T(8,128)(2,1)S(1)}, u32[]{:S(2)}, u32[]{:S(2)}) collective-permute-start(bf16[384,384]{1,0:T(8,128)(2,1)} %collective-permute-done.9), channel_id=1, source_target_pairs={{0,4},{4,0},{8,12},{12,8},{16,20},{20,16},{24,28},{28,24},{1,5},{5... | collective-permute-start | bytes 884744 | tf_op jit(solution)/shard_map/ppermute | solution.py:482
  72.0 22.4 %collective-permute-start.19 = (bf16[192,768]{1,0:T(8,128)(2,1)}, bf16[192,768]{1,0:T(8,128)(2,1)S(1)}, u32[]{:S(2)}, u32[]{:S(2)}) collective-permute-start(bf16[192,768]{1,0:T(8,128)(2,1)} %collective-permute-done.15), channel_id=1, source_target_pairs={{0,4},{4,0},{8,12},{12,8},{16,20},{20,16},{24,28},{28,24},{1,5},{5... | collective-permute-start | bytes 884744 | tf_op jit(solution)/shard_map/ppermute | solution.py:482
  82.8 13.4 %collective-permute-start.18 = (bf16[768,384]{1,0:T(8,128)(2,1)S(1)}, bf16[768,384]{1,0:T(8,128)(2,1)S(1)}, u32[]{:S(2)}, u32[]{:S(2)}) collective-permute-start(bf16[768,384]{1,0:T(8,128)(2,1)S(1)} %maximum_select_fusion.4.ia_ref), channel_id=1, source_target_pairs={{0,1},{1,0},{2,3},{3,2},{4,5},{5,4},{6,7},{7,6},{8,9},{9,8},{10,11... | collective-permute-start | bytes 1769480 | tf_op jit(solution)/shard_map/ppermute | solution.py:482
  97.8 13.0 %collective-permute-start.22 = (bf16[1536,384]{1,0:T(8,128)(2,1)S(1)}, bf16[1536,384]{1,0:T(8,128)(2,1)}, u32[]{:S(2)}, u32[]{:S(2)}) collective-permute-start(bf16[1536,384]{1,0:T(8,128)(2,1)S(1)} %get-tuple-element.442), channel_id=1, source_target_pairs={{0,1},{1,0},{2,3},{3,2},{4,5},{5,4},{6,7},{7,6},{8,9},{9,8},{10,11... | collective-permute-start | bytes 3538952 | tf_op jit(solution)/shard_map/ppermute | solution.py:482
  110.8 10.8 %collective-permute-start.23 = (bf16[2,768,384]{2,1,0:T(8,128)(2,1)}, bf16[2,768,384]{2,1,0:T(8,128)(2,1)}, u32[]{:S(2)}, u32[]{:S(2)}) collective-permute-start(bf16[2,768,384]{2,1,0:T(8,128)(2,1)} %get-tuple-element.446), channel_id=1, source_target_pairs={{0,1},{1,0},{2,3},{3,2},{4,5},{5,4},{6,7},{7,6},{8,9},{9,8},{10,11... | collective-permute-start | bytes 3538952 | tf_op jit(solution)/shard_map/ppermute | solution.py:482
  121.6 18.0 %collective-permute-start.24 = (bf16[2304,384]{1,0:T(8,128)(2,1)}, bf16[2304,384]{1,0:T(8,128)(2,1)}, u32[]{:S(2)}, u32[]{:S(2)}) collective-permute-start(bf16[2304,384]{1,0:T(8,128)(2,1)} %get-tuple-element.468), channel_id=1, source_target_pairs={{0,1},{1,0},{2,3},{3,2},{4,5},{5,4},{6,7},{7,6},{8,9},{9,8},{10,11... | collective-permute-start | bytes 5308424 | tf_op jit(solution)/shard_map/ppermute | solution.py:482
  139.6 18.0 %collective-permute-start.25 = (bf16[2304,384]{1,0:T(8,128)(2,1)}, bf16[2304,384]{1,0:T(8,128)(2,1)}, u32[]{:S(2)}, u32[]{:S(2)}) collective-permute-start(bf16[2304,384]{1,0:T(8,128)(2,1)} %get-tuple-element.487), channel_id=1, source_target_pairs={{0,1},{1,0},{2,3},{3,2},{4,5},{5,4},{6,7},{7,6},{8,9},{9,8},{10,11... | collective-permute-start | bytes 5308424 | tf_op jit(solution)/shard_map/ppermute | solution.py:482
  139.9 20.3 %collective-permute-start.29 = (bf16[768,384]{1,0:T(8,128)(2,1)}, bf16[768,384]{1,0:T(8,128)(2,1)S(1)}, u32[]{:S(2)}, u32[]{:S(2)}) collective-permute-start(bf16[768,384]{1,0:T(8,128)(2,1)} %pad_maximum_fusion.2), channel_id=1, source_target_pairs={{0,4},{4,0},{8,12},{12,8},{16,20},{20,16},{24,28},{28,24},{1,5},{5... | collective-permute-start | bytes 1769480 | tf_op jit(solution)/shard_map/ppermute | solution.py:482
  140.5 29.2 %collective-permute-start.27 = (bf16[1536,384]{1,0:T(8,128)(2,1)}, bf16[1536,384]{1,0:T(8,128)(2,1)}, u32[]{:S(2)}, u32[]{:S(2)}) collective-permute-start(bf16[1536,384]{1,0:T(8,128)(2,1)} %add_convert_fusion), channel_id=1, source_target_pairs={{0,2},{1,3},{2,0},{3,1},{4,6},{5,7},{6,4},{7,5},{8,10},{9,11},{10,... | collective-permute-start | bytes 3538952 | tf_op jit(solution)/shard_map/ppermute | solution.py:482
  157.6 26.5 %collective-permute-start.32 = (f32[64,768]{1,0:T(8,128)S(1)}, f32[64,768]{1,0:T(8,128)S(1)}, u32[]{:S(2)}, u32[]{:S(2)}) collective-permute-start(f32[64,768]{1,0:T(8,128)S(1)} %pad_maximum_fusion.8), channel_id=1, source_target_pairs={{2,0},{3,1},{6,4},{7,5},{10,8},{11,9},{14,12},{15,13},{18,16},{19,... | collective-permute-start | bytes 589832 | tf_op jit(solution)/shard_map/ppermute | solution.py:487
  158.9 25.2 %collective-permute-start.26 = (f32[64,768]{1,0:T(8,128)S(1)}, f32[64,768]{1,0:T(8,128)S(1)}, u32[]{:S(2)}, u32[]{:S(2)}) collective-permute-start(f32[64,768]{1,0:T(8,128)S(1)} %pad_maximum_fusion.8), channel_id=1, source_target_pairs={{1,0},{2,1},{3,2},{5,4},{6,5},{7,6},{9,8},{10,9},{11,10},{13,12},{... | collective-permute-start | bytes 589832 | tf_op jit(solution)/shard_map/ppermute | solution.py:487
  163.3 16.3 %collective-permute-start.31 = (bf16[768,384]{1,0:T(8,128)(2,1)S(1)}, bf16[768,384]{1,0:T(8,128)(2,1)S(1)}, u32[]{:S(2)}, u32[]{:S(2)}) collective-permute-start(bf16[768,384]{1,0:T(8,128)(2,1)S(1)} %pad_maximum_fusion.4), channel_id=1, source_target_pairs={{0,4},{4,0},{8,12},{12,8},{16,20},{20,16},{24,28},{28,24},{1,5},{5... | collective-permute-start | bytes 1769480 | tf_op jit(solution)/shard_map/ppermute | solution.py:482
  169.6 25.3 %collective-permute-start.35 = (bf16[768,384]{1,0:T(8,128)(2,1)}, bf16[768,384]{1,0:T(8,128)(2,1)S(1)}, u32[]{:S(2)}, u32[]{:S(2)}) collective-permute-start(bf16[768,384]{1,0:T(8,128)(2,1)} %pad_maximum_fusion.5), channel_id=1, source_target_pairs={{0,4},{4,0},{8,12},{12,8},{16,20},{20,16},{24,28},{28,24},{1,5},{5... | collective-permute-start | bytes 1769480 | tf_op jit(solution)/shard_map/ppermute | solution.py:482
  171.1 13.0 %collective-permute-start.30 = (bf16[768,384]{1,0:T(8,128)(2,1)S(1)}, bf16[768,384]{1,0:T(8,128)(2,1)S(1)}, u32[]{:S(2)}, u32[]{:S(2)}) collective-permute-start(bf16[768,384]{1,0:T(8,128)(2,1)S(1)} %pad_maximum_fusion.3), channel_id=1, source_target_pairs={{0,8},{4,12},{8,0},{12,4},{16,24},{20,28},{24,16},{28,20},{1,9},{5... | collective-permute-start | bytes 1769480 | tf_op jit(solution)/shard_map/ppermute | solution.py:482
  179.9 15.0 %collective-permute-start.33 = (bf16[384,384]{1,0:T(8,128)(2,1)S(1)}, bf16[384,384]{1,0:T(8,128)(2,1)S(1)}, u32[]{:S(2)}, u32[]{:S(2)}) collective-permute-start(bf16[384,384]{1,0:T(8,128)(2,1)S(1)} %get-tuple-element.529), channel_id=1, source_target_pairs={{0,2},{1,3},{2,0},{3,1},{4,6},{5,7},{6,4},{7,5},{8,10},{9,11},{10,... | collective-permute-start | bytes 884744 | tf_op jit(solution)/shard_map/ppermute | solution.py:482
  193.6 14.3 %collective-permute-start.36 = (bf16[768,384]{1,0:T(8,128)(2,1)}, bf16[768,384]{1,0:T(8,128)(2,1)S(1)}, u32[]{:S(2)}, u32[]{:S(2)}) collective-permute-start(bf16[768,384]{1,0:T(8,128)(2,1)} %dynamic-slice_convert_fusion), channel_id=1, source_target_pairs={{0,8},{4,12},{8,0},{12,4},{16,24},{20,28},{24,16},{28,20},{1,9},{5... | collective-permute-start | bytes 1769480 | tf_op jit(solution)/shard_map/ppermute | solution.py:482
  196.3 13.2 %collective-permute-start.39 = (bf16[192,384]{1,0:T(8,128)(2,1)S(1)}, bf16[192,384]{1,0:T(8,128)(2,1)S(1)}, u32[]{:S(2)}, u32[]{:S(2)}) collective-permute-start(bf16[192,384]{1,0:T(8,128)(2,1)S(1)} %dynamic-slice_convert_fusion.13), channel_id=1, source_target_pairs={{0,8},{4,12},{8,0},{12,4},{16,24},{20,28},{24,16},{28,20},{1,9},{5... | collective-permute-start | bytes 442376 | tf_op jit(solution)/shard_map/ppermute | solution.py:482
  197.2 12.4 %collective-permute-start.38 = (bf16[384,384]{1,0:T(8,128)(2,1)S(1)}, bf16[384,384]{1,0:T(8,128)(2,1)S(1)}, u32[]{:S(2)}, u32[]{:S(2)}) collective-permute-start(bf16[384,384]{1,0:T(8,128)(2,1)S(1)} %get-tuple-element.547), channel_id=1, source_target_pairs={{0,2},{1,3},{2,0},{3,1},{4,6},{5,7},{6,4},{7,5},{8,10},{9,11},{10,... | collective-permute-start | bytes 884744 | tf_op jit(solution)/shard_map/ppermute | solution.py:482
  199.0 19.5 %collective-permute-start.44 = (bf16[384,384]{1,0:T(8,128)(2,1)S(1)}, bf16[384,384]{1,0:T(8,128)(2,1)S(1)}, u32[]{:S(2)}, u32[]{:S(2)}) collective-permute-start(bf16[384,384]{1,0:T(8,128)(2,1)S(1)} %fusion.4), channel_id=1, source_target_pairs={{0,2},{1,3},{2,0},{3,1},{4,6},{5,7},{6,4},{7,5},{8,10},{9,11},{10,... | collective-permute-start | bytes 884744 | tf_op jit(solution)/shard_map/ppermute | solution.py:482
  211.8 10.4 %collective-permute-start.42 = (bf16[192,384]{1,0:T(8,128)(2,1)S(1)}, bf16[192,384]{1,0:T(8,128)(2,1)S(1)}, u32[]{:S(2)}, u32[]{:S(2)}) collective-permute-start(bf16[192,384]{1,0:T(8,128)(2,1)S(1)} %fusion.15), channel_id=1, source_target_pairs={{0,16},{4,20},{8,24},{12,28},{16,0},{20,4},{24,8},{28,12},{1,17},{... | collective-permute-start | bytes 442376 | tf_op jit(solution)/shard_map/ppermute | solution.py:482
  216.3 13.0 %collective-permute-start.40 = (f32[40,768]{1,0:T(8,128)S(1)}, f32[40,768]{1,0:T(8,128)S(1)}, u32[]{:S(2)}, u32[]{:S(2)}) collective-permute-start(f32[40,768]{1,0:T(8,128)S(1)} %add.258), channel_id=1, source_target_pairs={{0,2},{1,3},{2,0},{3,1},{4,6},{5,7},{6,4},{7,5},{8,10},{9,11},{10,... | collective-permute-start | bytes 368648 | tf_op jit(solution)/shard_map/ppermute | solution.py:482
  218.8 17.3 %collective-permute-start.50 = (bf16[384,384]{1,0:T(8,128)(2,1)S(1)}, bf16[384,384]{1,0:T(8,128)(2,1)S(1)}, u32[]{:S(2)}, u32[]{:S(2)}) collective-permute-start(bf16[384,384]{1,0:T(8,128)(2,1)S(1)} %fusion.10), channel_id=1, source_target_pairs={{0,16},{4,20},{8,24},{12,28},{16,0},{20,4},{24,8},{28,12},{1,17},{... | collective-permute-start | bytes 884744 | tf_op jit(solution)/shard_map/ppermute | solution.py:482
  242.7 13.4 %collective-permute-start.54 = (bf16[768,128]{1,0:T(8,128)(2,1)S(1)}, bf16[768,128]{1,0:T(8,128)(2,1)S(1)}, u32[]{:S(2)}, u32[]{:S(2)}) collective-permute-start(bf16[768,128]{1,0:T(8,128)(2,1)S(1)} %get-tuple-element.610), channel_id=1, source_target_pairs={{0,8},{4,12},{8,0},{12,4},{16,24},{20,28},{24,16},{28,20},{1,9},{5... | collective-permute-start | bytes 589832 | tf_op jit(solution)/shard_map/ppermute | solution.py:482
  244.0 25.7 %collective-permute-start.62 = (bf16[384,384]{1,0:T(8,128)(2,1)S(1)}, bf16[384,384]{1,0:T(8,128)(2,1)S(1)}, u32[]{:S(2)}, u32[]{:S(2)}) collective-permute-start(bf16[384,384]{1,0:T(8,128)(2,1)S(1)} %add_convert_fusion.1), channel_id=1, source_target_pairs={{0,4},{4,0},{8,12},{12,8},{16,20},{20,16},{24,28},{28,24},{1,5},{5... | collective-permute-start | bytes 884744 | tf_op jit(solution)/shard_map/ppermute | solution.py:482
  244.5 25.5 %collective-permute-start.55 = (bf16[384,384]{1,0:T(8,128)(2,1)S(1)}, bf16[384,384]{1,0:T(8,128)(2,1)S(1)}, u32[]{:S(2)}, u32[]{:S(2)}) collective-permute-start(bf16[384,384]{1,0:T(8,128)(2,1)S(1)} %maximum_select_fusion.11), channel_id=1, source_target_pairs={{0,4},{4,0},{8,12},{12,8},{16,20},{20,16},{24,28},{28,24},{1,5},{5... | collective-permute-start | bytes 884744 | tf_op jit(solution)/shard_map/ppermute | solution.py:482
  246.9 10.6 %collective-permute-start.52 = (f32[40,768]{1,0:T(8,128)S(1)}, f32[40,768]{1,0:T(8,128)S(1)}, u32[]{:S(2)}, u32[]{:S(2)}) collective-permute-start(f32[40,768]{1,0:T(8,128)S(1)} %add.280), channel_id=1, source_target_pairs={{0,8},{4,12},{8,0},{12,4},{16,24},{20,28},{24,16},{28,20},{1,9},{5... | collective-permute-start | bytes 368648 | tf_op jit(solution)/shard_map/ppermute | solution.py:482
  252.0 12.4 %collective-permute-start.59 = (bf16[192,384]{1,0:T(8,128)(2,1)S(1)}, bf16[192,384]{1,0:T(8,128)(2,1)S(1)}, u32[]{:S(2)}, u32[]{:S(2)}) collective-permute-start(bf16[192,384]{1,0:T(8,128)(2,1)S(1)} %add_convert_fusion.3), channel_id=1, source_target_pairs={{0,8},{4,12},{8,0},{12,4},{16,24},{20,28},{24,16},{28,20},{1,9},{5... | collective-permute-start | bytes 442376 | tf_op jit(solution)/shard_map/ppermute | solution.py:482
  257.5 10.0 %collective-permute-start.61 = (bf16[192,384]{1,0:T(8,128)(2,1)S(1)}, bf16[192,384]{1,0:T(8,128)(2,1)S(1)}, u32[]{:S(2)}, u32[]{:S(2)}) collective-permute-start(bf16[192,384]{1,0:T(8,128)(2,1)S(1)} %add_convert_fusion.4), channel_id=1, source_target_pairs={{0,8},{4,12},{8,0},{12,4},{16,24},{20,28},{24,16},{28,20},{1,9},{5... | collective-permute-start | bytes 442376 | tf_op jit(solution)/shard_map/ppermute | solution.py:482
  264.3 14.0 %collective-permute-start.57 = (bf16[768,128]{1,0:T(8,128)(2,1)S(1)}, bf16[768,128]{1,0:T(8,128)(2,1)S(1)}, u32[]{:S(2)}, u32[]{:S(2)}) collective-permute-start(bf16[768,128]{1,0:T(8,128)(2,1)S(1)} %fusion.14), channel_id=1, source_target_pairs={{0,16},{4,20},{8,24},{12,28},{16,0},{20,4},{24,8},{28,12},{1,17},{... | collective-permute-start | bytes 589832 | tf_op jit(solution)/shard_map/ppermute | solution.py:482
  264.4 10.5 %collective-permute-start.56 = (f32[40,768]{1,0:T(8,128)S(1)}, f32[40,768]{1,0:T(8,128)S(1)}, u32[]{:S(2)}, u32[]{:S(2)}) collective-permute-start(f32[40,768]{1,0:T(8,128)S(1)} %add.285), channel_id=1, source_target_pairs={{0,16},{4,20},{8,24},{12,28},{16,0},{20,4},{24,8},{28,12},{1,17},{... | collective-permute-start | bytes 368648 | tf_op jit(solution)/shard_map/ppermute | solution.py:482
  267.5 11.6 %collective-permute-start.67 = (bf16[192,384]{1,0:T(8,128)(2,1)S(1)}, bf16[192,384]{1,0:T(8,128)(2,1)S(1)}, u32[]{:S(2)}, u32[]{:S(2)}) collective-permute-start(bf16[192,384]{1,0:T(8,128)(2,1)S(1)} %add_convert_fusion.2), channel_id=1, source_target_pairs={{0,4},{4,0},{8,12},{12,8},{16,20},{20,16},{24,28},{28,24},{1,5},{5... | collective-permute-start | bytes 442376 | tf_op jit(solution)/shard_map/ppermute | solution.py:482
  269.7 12.1 %collective-permute-start.63 = (bf16[384,384]{1,0:T(8,128)(2,1)S(1)}, bf16[384,384]{1,0:T(8,128)(2,1)S(1)}, u32[]{:S(2)}, u32[]{:S(2)}) collective-permute-start(bf16[384,384]{1,0:T(8,128)(2,1)S(1)} %maximum_select_fusion.13), channel_id=1, source_target_pairs={{0,4},{4,0},{8,12},{12,8},{16,20},{20,16},{24,28},{28,24},{1,5},{5... | collective-permute-start | bytes 884744 | tf_op jit(solution)/shard_map/ppermute | solution.py:482
  270.0 11.8 %collective-permute-start.60 = (bf16[384,384]{1,0:T(8,128)(2,1)S(1)}, bf16[384,384]{1,0:T(8,128)(2,1)S(1)}, u32[]{:S(2)}, u32[]{:S(2)}) collective-permute-start(bf16[384,384]{1,0:T(8,128)(2,1)S(1)} %maximum_select_fusion.12), channel_id=1, source_target_pairs={{0,4},{4,0},{8,12},{12,8},{16,20},{20,16},{24,28},{28,24},{1,5},{5... | collective-permute-start | bytes 884744 | tf_op jit(solution)/shard_map/ppermute | solution.py:482
  278.3 15.6 %collective-permute-start.69 = (bf16[768,384]{1,0:T(8,128)(2,1)S(1)}, bf16[768,384]{1,0:T(8,128)(2,1)S(1)}, u32[]{:S(2)}, u32[]{:S(2)}) collective-permute-start(bf16[768,384]{1,0:T(8,128)(2,1)S(1)} %maximum_select_fusion.10), channel_id=1, source_target_pairs={{0,8},{4,12},{8,0},{12,4},{16,24},{20,28},{24,16},{28,20},{1,9},{5... | collective-permute-start | bytes 1769480 | tf_op jit(solution)/shard_map/ppermute | solution.py:482
  279.2 13.4 %collective-permute-start.68 = (bf16[384,384]{1,0:T(8,128)(2,1)S(1)}, bf16[384,384]{1,0:T(8,128)(2,1)S(1)}, u32[]{:S(2)}, u32[]{:S(2)}) collective-permute-start(bf16[384,384]{1,0:T(8,128)(2,1)S(1)} %maximum_select_fusion.14), channel_id=1, source_target_pairs={{0,8},{4,12},{8,0},{12,4},{16,24},{20,28},{24,16},{28,20},{1,9},{5... | collective-permute-start | bytes 884744 | tf_op jit(solution)/shard_map/ppermute | solution.py:482
  281.8 14.9 %collective-permute-start.65 = (bf16[2,192,768]{2,1,0:T(8,128)(2,1)S(1)}, bf16[2,192,768]{2,1,0:T(8,128)(2,1)S(1)}, u32[]{:S(2)}, u32[]{:S(2)}) collective-permute-start(bf16[2,192,768]{2,1,0:T(8,128)(2,1)S(1)} %get-tuple-element.669), channel_id=1, source_target_pairs={{0,1},{1,0},{2,3},{3,2},{4,5},{5,4},{6,7},{7,6},{8,9},{9,8},{10,11... | collective-permute-start | bytes 1769480 | tf_op jit(solution)/shard_map/ppermute | solution.py:482
  (124 other events, 650.8 us)

commit v2 on v1

--- a/solution.py
+++ b/solution.py
@@ -60,7 +60,7 @@
     )
 
 
-def call(kernel, outs, args, flops, scratch=(), smem=(), limit=48 << 20):
+def call(kernel, outs, args, flops, scratch=(), smem=(), limit=12 << 20):
     specs = [
         pl.BlockSpec(memory_space=pltpu.SMEM if i in smem else pltpu.VMEM)
         for i in range(len(args))
@@ -489,20 +489,18 @@
     )
 
 
-def parity_of(bit):
-    return (lax.axis_index("dp") // bit) & 1
-
-
-def half_of(share, bit):
-    half = share.shape[0] // 2
-    return lax.dynamic_slice_in_dim(share, parity_of(bit) * half, half)
-
-
-def joined(mine, other, bit):
-    return jnp.where(
-        parity_of(bit) == 0,
-        jnp.concatenate([mine, other], 0),
-        jnp.concatenate([other, mine], 0),
+def pick(first, pair):
+    return jnp.where(first, *pair)
+
+
+def split_rows(v):
+    half = v.shape[0] // 2
+    return v[:half], v[half:]
+
+
+def joined(mine, other, first):
+    return pick(
+        first, (jnp.concatenate([mine, other], 0), jnp.concatenate([other, mine], 0))
     )
 
 
@@ -513,29 +511,26 @@
     return lax.reduce_precision(v, 8, 7)
 
 
-def halves(v, bit):
-    half, parity = v.shape[0] // 2, parity_of(bit)
-    return (
-        lax.dynamic_slice_in_dim(v, parity * half, half),
-        lax.dynamic_slice_in_dim(v, (1 - parity) * half, half).astype(LOW),
-    )
-
-
-def reduction(kind, near, far):
+def halves(v, first):
+    low, high = split_rows(v)
+    return pick(first, (low, high)), pick(first, (high, low)).astype(LOW)
+
+
+def reduction(kind, near, far, firsts):
     bits = [1 << b for b in range(lax.axis_size("dp").bit_length() - 1)]
     lead = {"x": [1], "z": [2]}.get(kind, [])
     spread = {"x": [2], "z": [1], "y": [1, 2], "w": [2, 1]}[kind]
     near, far = near(), far()
     for bit in lead:
-        near, away = halves(near, bit)
-        far, far_away = halves(far, bit)
+        near, away = halves(near, firsts[bit])
+        far, far_away = halves(far, firsts[bit])
         got = yield "dp", bit, jnp.concatenate([away, far_away], 0)
         got = got.astype(F32)
         near, far = near + got[: near.shape[0]], far + got[near.shape[0] :]
     got = yield "tensor", 2, far.astype(LOW)
     total = near + got.astype(F32)
     for bit in spread:
-        total, away = halves(total, bit)
+        total, away = halves(total, firsts[bit])
         got = yield "dp", bit, away
         total = total + got.astype(F32)
     for bit in bits[2:]:
@@ -545,7 +540,7 @@
     low = total.astype(LOW)
     for bit in reversed(lead + spread):
         got = yield "dp", bit, low
-        low = joined(low, got, bit)
+        low = joined(low, got, firsts[bit])
     return low
 
 
@@ -624,6 +619,20 @@
     cotangent,
 ):
     member = lax.axis_index("tensor")
+    place = lax.axis_index("dp")
+    layer_input, begin, offs, *firsts = tied(
+        (
+            layer_input,
+            member * layer_input.shape[1],
+            (member ^ jnp.arange(4, dtype=jnp.int32)) * w_hidden.shape[0],
+            (place & 1) == 0,
+            (place & 2) == 0,
+            (member & 1) == 0,
+            (member & 2) == 0,
+        )
+    )
+    first_core, first_chip = firsts[2:]
+    firsts = dict(zip((1, 2), firsts[:2], strict=True))
     rows, length, width = layer_input.shape
     tokens = rows * length
     dims = alpha_raw.shape[0]
@@ -641,7 +650,8 @@
         jnp.where(order[:, None] <= order[None, :], doc_lengths[:, :, None], 0), 1
     ).astype(jnp.int32)
     starts = ends - doc_lengths
-    places = member * length + jnp.arange(length, dtype=jnp.int32)
+    starts, ends = starts - begin, ends - begin
+    places = jnp.arange(length, dtype=jnp.int32)
     docid = jnp.sum((places[None, :, None] >= ends[:, None, :]).astype(jnp.int32), 2)
     keep = 1.0 - jnp.any(places[None, :, None] == starts[:, None, :], 2).astype(F32)
     keep = jnp.broadcast_to(keep.reshape(tokens, 1), (tokens, LANES))
@@ -654,8 +664,6 @@
         low, high = part * length, (part + 1) * length
         inside = jnp.any((starts >= low) & (starts < high), 1)
         return jnp.broadcast_to(1.0 - inside.astype(F32)[:, None], (rows, LANES))
-
-    offs = (member ^ jnp.arange(4, dtype=jnp.int32)) * cols
 
     vm = lambda shape: pltpu.VMEM(shape, F32)
     tab = (dims, width)
@@ -672,7 +680,7 @@
     pump = Pump(offs)
     beside = [swap(w_value, "tensor", 1), swap(w_reset, "tensor", 1)]
     half_v, half_r, half_g, half_i, half_o = (
-        half_of(w, bit) for w, bit in zip(shares, bits, strict=True)
+        pick(firsts[bit], split_rows(w)) for w, bit in zip(shares, bits, strict=True)
     )
 
     over_v = swap(half_v, "tensor", 2)
@@ -692,7 +700,7 @@
     pre, mixed_low, z_pre, gate, probs = call(
         functools.partial(second_pass, rows),
         [(slabs, F32), (wide, LOW), ((tokens, zd), F32), (wide, F32), ((tokens, STRETCH), F32)],
-        (normed, init, f1, f2, keep, unbroken(member - 1), alpha_raw, delta_raw, ema_beta,
+        (normed, init, f1, f2, keep, unbroken(-1), alpha_raw, delta_raw, ema_beta,
          ema_eta, om, w_z, w_update, qg, qb, kg, mask),
         ema + mat * width,
         [vm(tab), vm(tab)],
@@ -719,13 +727,13 @@
     other_r = swap(over_r, "dp", 1)
     over_i = swap(pump.gate(half_i), "tensor", 2)
     other_v = pump.gate(other_v)
-    full_v = pump.gate(joined(over_v, other_v, 1))
+    full_v = pump.gate(joined(over_v, other_v, firsts[1]))
     both_v = swap(full_v, "tensor", 1)
     over_g = pump.gate(over_g)
     other_g = swap(over_g, "dp", 2)
     over_o = swap(pump.gate(half_o), "tensor", 2)
     other_r = pump.gate(other_r)
-    full_r = pump.gate(joined(over_r, other_r, 1))
+    full_r = pump.gate(joined(over_r, other_r, firsts[1]))
     both_r = swap(full_r, "tensor", 1)
     both_v, both_r = pump.gate(both_v), pump.gate(both_r)
     over_i = pump.gate(over_i)
@@ -736,10 +744,10 @@
     over_o = pump.gate(over_o)
     other_o = swap(over_o, "dp", 1)
     other_g = pump.gate(other_g)
-    near_g = pump.gate(jnp.stack([w_join, joined(over_g, other_g, 2)]))
+    near_g = pump.gate(jnp.stack([w_join, joined(over_g, other_g, firsts[2])]))
     beside_g = swap(near_g, "tensor", 1)
     other_i = pump.gate(other_i)
-    full_i = pump.gate(joined(over_i, other_i, 1))
+    full_i = pump.gate(joined(over_i, other_i, firsts[1]))
     both_i = swap(full_i, "tensor", 1)
     beside_g = pump.gate(beside_g)
     wg = (near_g, beside_g)
@@ -766,7 +774,7 @@
     ffn0 = ffn_of((w_ffn_in, beside[2], w_ffn_out, beside[3]))
     back0 = pump.gate(ffn0[1])
     other_o = pump.gate(other_o)
-    full_o = pump.gate(joined(over_o, other_o, 1))
+    full_o = pump.gate(joined(over_o, other_o, firsts[1]))
     both_o = swap(full_o, "tensor", 1)
     both_i, both_o = pump.gate(both_i), pump.gate(both_o)
     ffn1 = ffn_of((full_i, both_i, full_o, both_o))
@@ -823,7 +831,7 @@
         held["t4"] = call(
             functools.partial(fourth_pass, rows),
             [(wide, LOW), ((2 * dims + 8, width), F32)],
-            (t3[0], normed, t3[3], t3[4], *held["back"], keep, unbroken(member + 1), alpha_raw,
+            (t3[0], normed, t3[3], t3[4], *held["back"], keep, unbroken(1), alpha_raw,
              delta_raw, ema_beta, ema_eta, om, held[0][0], held[1][0], x, g1, held["bb"][1],
              held["bb"][4], t3[2]),
             2 * ema,
@@ -843,7 +851,7 @@
             source = "F" if name == "F" else "V"
             at, end = {"F": (0, 2 * width), "R": (0, width), "O": (width, 2 * width), "N": (2 * width, 3 * width)}[name]
             near, far = (lambda: pack(0, source, at, end)), (lambda: pack(1, source, at, end))
-        pump.add(name, reduction(KINDS[name], near, far))
+        pump.add(name, reduction(KINDS[name], near, far, firsts))
 
     kernels = {
         "bb": run_blend,
@@ -875,11 +883,8 @@
     decay_grad = ema_eta * (alpha * ema_beta) * with_nu
     at = 2 * dims
     quarter = side_by_side(pair_sum[: 2 * cols])
-    pair = jnp.stack([quarter, swap(quarter, "tensor", 2)])
-    quarters = jnp.stack([pair, swap(pair, "tensor", 1)], 1).reshape(4, cols, width)
-    update_grad = jnp.concatenate(
-        [lax.dynamic_index_in_dim(quarters, g ^ member, 0, False) for g in range(4)], 0
-    )
+    update_grad = joined(quarter, swap(quarter, "tensor", 1), first_core)
+    update_grad = joined(update_grad, swap(update_grad, "tensor", 2), first_chip)
     return (
         output.reshape(layer_input.shape),
         input_grad.reshape(layer_input.shape),

time: 303 us -> 263 us (0.87)
  waiting for transfers between devices: 74.3 us -> 122 us
  local copies, waits for them, and re-layouts: 42.2 us -> 5.82 us
  Pallas kernels: 62.3 us -> 41.1 us
  other arithmetic: 35.7 us -> 21.1 us
  starting transfers between devices: 81.8 us -> 68.2 us
    ppermute x66, waiting for transfers between devices: 74.3 us -> 122 us  [swap(): return lax.ppermute(x, axis, [(i, i ^ bit) for i in range(size)])]
    unnamed x205 -> x47, local copies, waits for them, and re-layouts: 32.9 us -> 3.52 us
    pallas_call x12, Pallas kernels: 62.3 us -> 41.1 us  [call(): pl.pallas_call(kernel, out_shape=outs, in_specs=specs, out_specs=[pl.Bloc...]
    ppermute x66, starting transfers between devices: 72.8 us -> 58.9 us  [swap(): return lax.ppermute(x, axis, [(i, i ^ bit) for i in range(size)])]
    select_n x13 -> x19, other arithmetic: 8.41 us -> 3.92 us  [pick(): return jnp.where(first, *pair)]
    dynamic_slice x5 -> x0, local copies, waits for them, and re-layouts: 4.26 us -> none  [half_of(): return lax.dynamic_slice_in_dim(share, parity_of(bit) * half, half)]
  transfers between devices with their start and end apart: 70 -> 70, of which waited for: 21 -> 27; matrix products, arithmetic and copies ran while one was open for 13% -> 7% of each run, Pallas kernels for 20% -> 15%
where the time goes in v2:
time: 263 us; the launch traced here: 260 us
  waiting for transfers between devices  122 us (46%)
  starting transfers between devices  68.2 us (26%)
  Pallas kernels  41.1 us (16%)
  other arithmetic  21.1 us (8%)
  local copies, waits for them, and re-layouts  5.82 us (2%)
    ppermute x66, waiting for transfers between devices, swap(): return lax.ppermute(x, axis, [(i, i ^ bit) for i in range(size)])  122 us
    ppermute x66, starting transfers between devices, swap(): return lax.ppermute(x, axis, [(i, i ^ bit) for i in range(size)])  58.9 us
    pallas_call x12, Pallas kernels, call(): pl.pallas_call(kernel, out_shape=outs, in_specs=specs, out_specs=[pl.Bloc...  41.1 us
    ppermute x4, starting transfers between devices, shift(): lax.ppermute(x, 'tensor', [(i, i + by) for i in range(size) if 0 <= i + b...  9.21 us
  transfers between devices with their start and end apart: 70, of which 27 were waited for; matrix products, arithmetic and copies ran while one was open for 7% of the time, Pallas kernels for 15%

profile of v2, /device:TPU:0, one launch (start us, length us, event | category | flops | bytes accessed | tf_op | source)
XLA Modules:
  0.0 259.9 jit_solution(17192542838631958667)
XLA Ops:
  6.6 3.0 %shard_map.356 = (f32[1536,128]{1,0:T(8,128)S(1)}, bf16[256,768]{1,0:T(8,128)(2,1)S(1)}, f32[256,768]{1,0:T(8,128)S(1)}, f32[32,768]{1,0:T(8,128)S(1)}) custom-call(bf16[256,768]{1,0:T(8,128)(2,1)S(1)} %bitcast.35, f32[1,768]{1,0:T(1,128)S(1)} %broadcast_in_dim.34.g_ref, f32[16,768]{1,0:T(8,128)S(1)} %copy-done.5, f32[16,768]{1,0:T(8,128)S(1)} %copy-done.7, ...), custom_call_target="tpu_custom_call" | custom-call | flops 25165824 | bytes 2739200 | tf_op jit(solution)/shard_map/pallas_call | solution.py:72
  9.6 4.9 %collective-permute-start.1 = (f32[32,768]{1,0:T(8,128)S(1)}, f32[32,768]{1,0:T(8,128)S(1)}, u32[]{:S(2)}, u32[]{:S(2)}) collective-permute-start(f32[32,768]{1,0:T(8,128)S(1)} %get-tuple-element.342), channel_id=1, source_target_pairs={{0,2},{1,3},{4,6},{5,7},{8,10},{9,11},{12,14},{13,15},{16,18},{17,... | collective-permute-start | bytes 294920 | tf_op jit(solution)/shard_map/ppermute | solution.py:487
  20.3 4.4 %shard_map.357 = (f32[1536,128]{1,0:T(8,128)S(1)}, bf16[256,768]{1,0:T(8,128)(2,1)S(1)}, f32[256,128]{1,0:T(8,128)S(1)}, f32[256,768]{1,0:T(8,128)S(1)}, f32[256,128]{1,0:T(8,128)S(1)}) custom-call(f32[1536,128]{1,0:T(8,128)S(1)} %get-tuple-element.340.normed_ref, f32[256,768]{1,0:T(8,128)S(1)} %get-tuple-element.341.init_ref, ...), custom_call_target="tpu_custom_call" | custom-call | flops 327155712 | bytes 5838336 | tf_op jit(solution)/shard_map/pallas_call | solution.py:72
  24.7 1.9 collective-permute-start.8
  26.9 1.6 collective-permute-start.7
  29.6 5.1 %collective-permute-done.8 = bf16[384,384]{1,0:T(8,128)(2,1)S(1)} collective-permute-done((bf16[384,384]{1,0:T(8,128)(2,1)S(1)}, bf16[384,384]{1,0:T(8,128)(2,1)S(1)}, u32[]{:S(2)}, u32[]{:S(2)}) %collective-permute-start.8) | collective-permute-done | bytes 294944 | tf_op jit(solution)/shard_map/ppermute | solution.py:482
  36.4 7.1 %collective-permute-done.11 = bf16[288,768]{1,0:T(8,128)(2,1)S(1)} collective-permute-done((bf16[288,768]{1,0:T(8,128)(2,1)S(1)}, bf16[288,768]{1,0:T(8,128)(2,1)S(1)}, u32[]{:S(2)}, u32[]{:S(2)}) %collective-permute-start.11) | collective-permute-done | bytes 442400 | tf_op jit(solution)/shard_map/ppermute | solution.py:482
  44.4 1.6 collective-permute-start.14
  45.9 1.7 collective-permute-start.9
  48.0 7.8 %collective-permute-done.9 = bf16[384,384]{1,0:T(8,128)(2,1)S(1)} collective-permute-done((bf16[384,384]{1,0:T(8,128)(2,1)S(1)}, bf16[384,384]{1,0:T(8,128)(2,1)S(1)}, u32[]{:S(2)}, u32[]{:S(2)}) %collective-permute-start.9) | collective-permute-done | bytes 294944 | tf_op jit(solution)/shard_map/ppermute | solution.py:482
  56.9 4.1 %collective-permute-done.15 = bf16[192,768]{1,0:T(8,128)(2,1)S(1)} collective-permute-done((bf16[192,768]{1,0:T(8,128)(2,1)S(1)}, bf16[192,768]{1,0:T(8,128)(2,1)S(1)}, u32[]{:S(2)}, u32[]{:S(2)}) %collective-permute-start.15) | collective-permute-done | bytes 294944 | tf_op jit(solution)/shard_map/ppermute | solution.py:482
  61.6 1.6 collective-permute-start.17
  63.7 7.8 %collective-permute-done.17 = bf16[384,384]{1,0:T(8,128)(2,1)S(1)} collective-permute-done((bf16[384,384]{1,0:T(8,128)(2,1)S(1)}, bf16[384,384]{1,0:T(8,128)(2,1)S(1)}, u32[]{:S(2)}, u32[]{:S(2)}) %collective-permute-start.17) | collective-permute-done | bytes 294944 | tf_op jit(solution)/shard_map/ppermute | solution.py:482
  71.9 2.1 shard_map.360
  74.0 2.6 %shard_map.361 = (f32[256,768]{1,0:T(8,128)S(1)}, f32[256,768]{1,0:T(8,128)S(1)}, f32[1536,384]{1,0:T(8,128)S(1)}, bf16[1536,384]{1,0:T(8,128)(2,1)S(1)}) custom-call(bf16[256,768]{1,0:T(8,128)(2,1)S(1)} %get-tuple-element.419.second_ref, bf16[256,768]{1,0:T(8,128)(2,1)S(1)} %bitcast.39, bf16[768,384]{1,0:T(8,128)(2,1)S(1)} %copy-done.12, ...), custom_call_target="tpu_custom_call" | custom-call | flops 1811939328 | bytes 8257536 | tf_op jit(solution)/shard_map/pallas_call | solution.py:72
  77.6 2.0 collective-permute-done.20.ob_ref
  79.7 2.6 %shard_map.362 = (f32[256,768]{1,0:T(8,128)S(1)}, f32[256,768]{1,0:T(8,128)S(1)}, f32[1536,384]{1,0:T(8,128)S(1)}, bf16[1536,384]{1,0:T(8,128)(2,1)S(1)}) custom-call(bf16[256,768]{1,0:T(8,128)(2,1)S(1)} %get-tuple-element.419.second_ref, bf16[256,768]{1,0:T(8,128)(2,1)S(1)} %bitcast.40, bf16[768,384]{1,0:T(8,128)(2,1)S(1)} %maximum_select_fusion.5.ia_ref, ...), custom_call_target="tpu_custom_call" | custom-call | flops 1811939328 | bytes 8257536 | tf_op jit(solution)/shard_map/pallas_call | solution.py:72
  82.8 4.0 %shard_map.363 = (bf16[256,768]{1,0:T(8,128)(2,1)}, f32[256,768]{1,0:T(8,128)S(1)}, bf16[256,768]{1,0:T(8,128)(2,1)S(1)}, f32[256,768]{1,0:T(8,128)S(1)}, f32[1,...) custom-call(s32[4]{0:T(128)S(1)} %xor_multiply_fusion.offs_ref, ...), custom_call_target="tpu_custom_call" | custom-call | flops 1207959552 | bytes 14948368 | tf_op jit(solution)/shard_map/pallas_call | solution.py:72
  87.0 3.3 %shard_map.364 = (f32[256,768]{1,0:T(8,128)S(1)}, f32[256,768]{1,0:T(8,128)S(1)}, f32[256,128]{1,0:T(8,128)S(1)}, f32[2304,384]{1,0:T(8,128)S(1)}, bf16[2304,384]{1,0:T(8,128)(2,1)S(1)}) custom-call(bf16[256,768]{1,0:T(8,128)(2,1)S(1)} %get-tuple-element.475.hidden_ref, bf16[256,768]{1,0:T(8,128)(2,1)S(1)} %get-tuple-element.369.normed_ref, ...), custom_call_target="tpu_custom_call" | custom-call | flops 2113929216 | bytes 16973824 | tf_op jit(solution)/shard_map/pallas_call | solution.py:72
  91.6 3.3 %shard_map.365 = (f32[256,768]{1,0:T(8,128)S(1)}, f32[256,768]{1,0:T(8,128)S(1)}, f32[256,128]{1,0:T(8,128)S(1)}, f32[2304,384]{1,0:T(8,128)S(1)}, bf16[2304,384]{1,0:T(8,128)(2,1)S(1)}) custom-call(bf16[256,768]{1,0:T(8,128)(2,1)S(1)} %get-tuple-element.475.hidden_ref, bf16[256,768]{1,0:T(8,128)(2,1)S(1)} %get-tuple-element.369.normed_ref, ...), custom_call_target="tpu_custom_call" | custom-call | flops 2113929216 | bytes 16973824 | tf_op jit(solution)/shard_map/pallas_call | solution.py:72
  96.7 1.7 collective-permute-start.27
  98.3 5.2 %shard_map.366 = (f32[1536,128]{1,0:T(8,128)S(1)}, f32[768,128]{1,0:T(8,128)S(1)}, f32[8,128]{1,0:T(8,128)S(1)}, f32[256,768]{1,0:T(8,128)S(1)}, f32[256,768]{1,...) custom-call(f32[256,128]{1,0:T(8,128)S(1)} %get-tuple-element.486.zpre_ref, ...), custom_call_target="tpu_custom_call" | custom-call | flops 50331648 | bytes 7443968 | tf_op jit(solution)/shard_map/pallas_call | solution.py:72
  107.1 3.7 %collective-permute-done.29 = bf16[768,384]{1,0:T(8,128)(2,1)S(1)} collective-permute-done((bf16[768,384]{1,0:T(8,128)(2,1)S(1)}, bf16[768,384]{1,0:T(8,128)(2,1)S(1)}, u32[]{:S(2)}, u32[]{:S(2)}) %collective-permute-start.29) | collective-permute-done | bytes 589856 | tf_op jit(solution)/shard_map/ppermute | solution.py:482
  113.4 12.2 %collective-permute-done.27 = bf16[1536,384]{1,0:T(8,128)(2,1)S(1)} collective-permute-done((bf16[1536,384]{1,0:T(8,128)(2,1)S(1)}, bf16[1536,384]{1,0:T(8,128)(2,1)S(1)}, u32[]{:S(2)}, u32[]{:S(2)}) %collective-permute-start.27) | collective-permute-done | bytes 1179680 | tf_op jit(solution)/shard_map/ppermute | solution.py:482
  127.1 1.7 collective-permute-start.33
  129.1 10.0 %collective-permute-done.30 = bf16[768,384]{1,0:T(8,128)(2,1)S(1)} collective-permute-done((bf16[768,384]{1,0:T(8,128)(2,1)S(1)}, bf16[768,384]{1,0:T(8,128)(2,1)S(1)}, u32[]{:S(2)}, u32[]{:S(2)}) %collective-permute-start.30) | collective-permute-done | bytes 589856 | tf_op jit(solution)/shard_map/ppermute | solution.py:482
  139.2 8.2 %shard_map.367 = (bf16[256,768]{1,0:T(8,128)(2,1)}, f32[40,768]{1,0:T(8,128)S(1)}) custom-call(f32[1536,128]{1,0:T(8,128)S(1)} %get-tuple-element.493.pg_ref, f32[1536,128]{1,0:T(8,128)S(1)} %get-tuple-element.340.normed_ref, f32[256,768]{1,0:T(8,128)S(1)} %get-tuple-element.494.im_ref, f32[256,768]{1,0:T(8,128)S(1)} %get-tuple-element.495.iv_ref, ...), custom_call_target="tpu_custom_call" | custom-call | flops 50331648 | bytes 7149568 | tf_op jit(solution)/shard_map/pallas_call | solution.py:72
  148.2 1.6 collective-permute-start.39
  149.8 1.7 collective-permute-start.38
  152.1 9.6 %collective-permute-done.36 = bf16[768,384]{1,0:T(8,128)(2,1)S(1)} collective-permute-done((bf16[768,384]{1,0:T(8,128)(2,1)S(1)}, bf16[768,384]{1,0:T(8,128)(2,1)S(1)}, u32[]{:S(2)}, u32[]{:S(2)}) %collective-permute-start.36) | collective-permute-done | bytes 589856 | tf_op jit(solution)/shard_map/ppermute | solution.py:482
  163.3 4.2 %collective-permute-start.42 = (bf16[192,384]{1,0:T(8,128)(2,1)S(1)}, bf16[192,384]{1,0:T(8,128)(2,1)S(1)}, u32[]{:S(2)}, u32[]{:S(2)}) collective-permute-start(bf16[192,384]{1,0:T(8,128)(2,1)S(1)} %fusion.20), channel_id=1, source_target_pairs={{0,16},{4,20},{8,24},{12,28},{16,0},{20,4},{24,8},{28,12},{1,17},{... | collective-permute-start | bytes 442376 | tf_op jit(solution)/shard_map/ppermute | solution.py:482
  167.6 1.9 collective-permute-start.41
  170.4 7.1 %collective-permute-done.37 = bf16[384,384]{1,0:T(8,128)(2,1)S(1)} collective-permute-done((bf16[384,384]{1,0:T(8,128)(2,1)S(1)}, bf16[384,384]{1,0:T(8,128)(2,1)S(1)}, u32[]{:S(2)}, u32[]{:S(2)}) %collective-permute-start.37) | collective-permute-done | bytes 294944 | tf_op jit(solution)/shard_map/ppermute | solution.py:482
  178.0 2.1 collective-permute-start.46
  186.9 2.7 %collective-permute-done.49 = bf16[192,384]{1,0:T(8,128)(2,1)S(1)} collective-permute-done((bf16[192,384]{1,0:T(8,128)(2,1)S(1)}, bf16[192,384]{1,0:T(8,128)(2,1)S(1)}, u32[]{:S(2)}, u32[]{:S(2)}) %collective-permute-start.49) | collective-permute-done | bytes 147488 | tf_op jit(solution)/shard_map/ppermute | solution.py:482
  189.7 2.5 collective-permute-start.48
  192.3 4.9 %collective-permute-start.58 = (bf16[192,384]{1,0:T(8,128)(2,1)S(1)}, bf16[192,384]{1,0:T(8,128)(2,1)S(1)}, u32[]{:S(2)}, u32[]{:S(2)}) collective-permute-start(bf16[192,384]{1,0:T(8,128)(2,1)S(1)} %fusion.22), channel_id=1, source_target_pairs={{0,16},{4,20},{8,24},{12,28},{16,0},{20,4},{24,8},{28,12},{1,17},{... | collective-permute-start | bytes 442376 | tf_op jit(solution)/shard_map/ppermute | solution.py:482
  197.9 2.0 collective-permute-start.55
  200.7 5.7 %collective-permute-done.58 = bf16[192,384]{1,0:T(8,128)(2,1)S(1)} collective-permute-done((bf16[192,384]{1,0:T(8,128)(2,1)S(1)}, bf16[192,384]{1,0:T(8,128)(2,1)S(1)}, u32[]{:S(2)}, u32[]{:S(2)}) %collective-permute-start.58) | collective-permute-done | bytes 147488 | tf_op jit(solution)/shard_map/ppermute | solution.py:482
  206.5 1.9 collective-permute-done.53
  213.0 6.3 %collective-permute-done.66 = bf16[192,384]{1,0:T(8,128)(2,1)S(1)} collective-permute-done((bf16[192,384]{1,0:T(8,128)(2,1)S(1)}, bf16[192,384]{1,0:T(8,128)(2,1)S(1)}, u32[]{:S(2)}, u32[]{:S(2)}) %collective-permute-start.66) | collective-permute-done | bytes 147488 | tf_op jit(solution)/shard_map/ppermute | solution.py:482
  219.4 3.0 %collective-permute-start.56 = (f32[40,768]{1,0:T(8,128)S(1)}, f32[40,768]{1,0:T(8,128)S(1)}, u32[]{:S(2)}, u32[]{:S(2)}) collective-permute-start(f32[40,768]{1,0:T(8,128)S(1)} %add.178), channel_id=1, source_target_pairs={{0,16},{4,20},{8,24},{12,28},{16,0},{20,4},{24,8},{28,12},{1,17},{... | collective-permute-start | bytes 368648 | tf_op jit(solution)/shard_map/ppermute | solution.py:482
  222.5 2.0 collective-permute-start.67
  225.0 2.0 collective-permute-start.60
  228.1 1.7 collective-permute-done.56
  232.7 2.1 collective-permute-start.68
  237.3 16.5 %collective-permute-done.68 = bf16[384,384]{1,0:T(8,128)(2,1)S(1)} collective-permute-done((bf16[384,384]{1,0:T(8,128)(2,1)S(1)}, bf16[384,384]{1,0:T(8,128)(2,1)S(1)}, u32[]{:S(2)}, u32[]{:S(2)}) %collective-permute-start.68) | collective-permute-done | bytes 294944 | tf_op jit(solution)/shard_map/ppermute | solution.py:482
  257.8 1.6 fusion
  (262 shorter events, 59.4 us)
Async XLA Ops:
  9.6 8.6 %collective-permute-start.1 = (f32[32,768]{1,0:T(8,128)S(1)}, f32[32,768]{1,0:T(8,128)S(1)}, u32[]{:S(2)}, u32[]{:S(2)}) collective-permute-start(f32[32,768]{1,0:T(8,128)S(1)} %get-tuple-element.342), channel_id=1, source_target_pairs={{0,2},{1,3},{4,6},{5,7},{8,10},{9,11},{12,14},{13,15},{16,18},{17,... | collective-permute-start | bytes 294920 | tf_op jit(solution)/shard_map/ppermute | solution.py:487
  17.1 9.5 %collective-permute-start.6 = (bf16[384,384]{1,0:T(8,128)(2,1)S(1)}, bf16[384,384]{1,0:T(8,128)(2,1)S(1)}, u32[]{:S(2)}, u32[]{:S(2)}) collective-permute-start(bf16[384,384]{1,0:T(8,128)(2,1)S(1)} %slice_select_fusion.3), channel_id=1, source_target_pairs={{0,2},{1,3},{2,0},{3,1},{4,6},{5,7},{6,4},{7,5},{8,10},{9,11},{10,... | collective-permute-start | bytes 884744 | tf_op jit(solution)/shard_map/ppermute | solution.py:482
  19.4 9.1 %collective-permute-start.4 = (bf16[384,768]{1,0:T(8,128)(2,1)S(1)}, bf16[384,768]{1,0:T(8,128)(2,1)S(1)}, u32[]{:S(2)}, u32[]{:S(2)}) collective-permute-start(bf16[384,768]{1,0:T(8,128)(2,1)S(1)} %copy-done.13), channel_id=1, source_target_pairs={{0,1},{1,0},{2,3},{3,2},{4,5},{5,4},{6,7},{7,6},{8,9},{9,8},{10,11... | collective-permute-start | bytes 1769480 | tf_op jit(solution)/shard_map/ppermute | solution.py:482
  19.8 8.7 %collective-permute-start.5 = (bf16[768,384]{1,0:T(8,128)(2,1)S(1)}, bf16[768,384]{1,0:T(8,128)(2,1)S(1)}, u32[]{:S(2)}, u32[]{:S(2)}) collective-permute-start(bf16[768,384]{1,0:T(8,128)(2,1)S(1)} %copy-done.12), channel_id=1, source_target_pairs={{0,1},{1,0},{2,3},{3,2},{4,5},{5,4},{6,7},{7,6},{8,9},{9,8},{10,11... | collective-permute-start | bytes 1769480 | tf_op jit(solution)/shard_map/ppermute | solution.py:482
  24.7 9.9 %collective-permute-start.8 = (bf16[384,384]{1,0:T(8,128)(2,1)S(1)}, bf16[384,384]{1,0:T(8,128)(2,1)S(1)}, u32[]{:S(2)}, u32[]{:S(2)}) collective-permute-start(bf16[384,384]{1,0:T(8,128)(2,1)S(1)} %slice_select_fusion.4), channel_id=1, source_target_pairs={{0,2},{1,3},{2,0},{3,1},{4,6},{5,7},{6,4},{7,5},{8,10},{9,11},{10,... | collective-permute-start | bytes 884744 | tf_op jit(solution)/shard_map/ppermute | solution.py:482
  26.6 16.9 %collective-permute-start.11 = (bf16[288,768]{1,0:T(8,128)(2,1)S(1)}, bf16[288,768]{1,0:T(8,128)(2,1)S(1)}, u32[]{:S(2)}, u32[]{:S(2)}) collective-permute-start(bf16[288,768]{1,0:T(8,128)(2,1)S(1)} %slice_select_fusion), channel_id=1, source_target_pairs={{0,2},{1,3},{2,0},{3,1},{4,6},{5,7},{6,4},{7,5},{8,10},{9,11},{10,... | collective-permute-start | bytes 1327112 | tf_op jit(solution)/shard_map/ppermute | solution.py:482
  26.9 9.3 %collective-permute-start.7 = (bf16[384,384]{1,0:T(8,128)(2,1)S(1)}, bf16[384,384]{1,0:T(8,128)(2,1)S(1)}, u32[]{:S(2)}, u32[]{:S(2)}) collective-permute-start(bf16[384,384]{1,0:T(8,128)(2,1)S(1)} %collective-permute-done.6), channel_id=1, source_target_pairs={{0,4},{4,0},{8,12},{12,8},{16,20},{20,16},{24,28},{28,24},{1,5},{5... | collective-permute-start | bytes 884744 | tf_op jit(solution)/shard_map/ppermute | solution.py:482
  34.7 8.9 %collective-permute-start.10 = (bf16[384,384]{1,0:T(8,128)(2,1)S(1)}, bf16[384,384]{1,0:T(8,128)(2,1)S(1)}, u32[]{:S(2)}, u32[]{:S(2)}) collective-permute-start(bf16[384,384]{1,0:T(8,128)(2,1)S(1)} %collective-permute-done.8), channel_id=1, source_target_pairs={{0,4},{4,0},{8,12},{12,8},{16,20},{20,16},{24,28},{28,24},{1,5},{5... | collective-permute-start | bytes 884744 | tf_op jit(solution)/shard_map/ppermute | solution.py:482
  44.4 16.6 %collective-permute-start.14 = (bf16[288,768]{1,0:T(8,128)(2,1)S(1)}, bf16[288,768]{1,0:T(8,128)(2,1)S(1)}, u32[]{:S(2)}, u32[]{:S(2)}) collective-permute-start(bf16[288,768]{1,0:T(8,128)(2,1)S(1)} %collective-permute-done.11), channel_id=1, source_target_pairs={{0,8},{4,12},{8,0},{12,4},{16,24},{20,28},{24,16},{28,20},{1,9},{5... | collective-permute-start | bytes 1327112 | tf_op jit(solution)/shard_map/ppermute | solution.py:482
  45.9 9.9 %collective-permute-start.9 = (bf16[384,384]{1,0:T(8,128)(2,1)S(1)}, bf16[384,384]{1,0:T(8,128)(2,1)S(1)}, u32[]{:S(2)}, u32[]{:S(2)}) collective-permute-start(bf16[384,384]{1,0:T(8,128)(2,1)S(1)} %slice_select_fusion.2), channel_id=1, source_target_pairs={{0,2},{1,3},{2,0},{3,1},{4,6},{5,7},{6,4},{7,5},{8,10},{9,11},{10,... | collective-permute-start | bytes 884744 | tf_op jit(solution)/shard_map/ppermute | solution.py:482
  47.6 13.4 %collective-permute-start.15 = (bf16[192,768]{1,0:T(8,128)(2,1)S(1)}, bf16[192,768]{1,0:T(8,128)(2,1)S(1)}, u32[]{:S(2)}, u32[]{:S(2)}) collective-permute-start(bf16[192,768]{1,0:T(8,128)(2,1)S(1)} %slice_select_fusion.1), channel_id=1, source_target_pairs={{0,2},{1,3},{2,0},{3,1},{4,6},{5,7},{6,4},{7,5},{8,10},{9,11},{10,... | collective-permute-start | bytes 884744 | tf_op jit(solution)/shard_map/ppermute | solution.py:482
  61.5 10.3 %collective-permute-start.16 = (bf16[2,576,768]{2,1,0:T(8,128)(2,1)S(1)}, bf16[2,576,768]{2,1,0:T(8,128)(2,1)S(1)}, u32[]{:S(2)}, u32[]{:S(2)}) collective-permute-start(bf16[2,576,768]{2,1,0:T(8,128)(2,1)S(1)} %pad_maximum_fusion.ga_ref), channel_id=1, source_target_pairs={{0,1},{1,0},{2,3},{3,2},{4,5},{5,4},{6,7},{7,6},{8,9},{9,8},{10,11... | collective-permute-start | bytes 5308424 | tf_op jit(solution)/shard_map/ppermute | solution.py:482
  61.6 9.9 %collective-permute-start.17 = (bf16[384,384]{1,0:T(8,128)(2,1)S(1)}, bf16[384,384]{1,0:T(8,128)(2,1)S(1)}, u32[]{:S(2)}, u32[]{:S(2)}) collective-permute-start(bf16[384,384]{1,0:T(8,128)(2,1)S(1)} %collective-permute-done.9), channel_id=1, source_target_pairs={{0,4},{4,0},{8,12},{12,8},{16,20},{20,16},{24,28},{28,24},{1,5},{5... | collective-permute-start | bytes 884744 | tf_op jit(solution)/shard_map/ppermute | solution.py:482
  63.1 14.2 %collective-permute-start.19 = (bf16[192,768]{1,0:T(8,128)(2,1)S(1)}, bf16[192,768]{1,0:T(8,128)(2,1)S(1)}, u32[]{:S(2)}, u32[]{:S(2)}) collective-permute-start(bf16[192,768]{1,0:T(8,128)(2,1)S(1)} %collective-permute-done.15), channel_id=1, source_target_pairs={{0,4},{4,0},{8,12},{12,8},{16,20},{20,16},{24,28},{28,24},{1,5},{5... | collective-permute-start | bytes 884744 | tf_op jit(solution)/shard_map/ppermute | solution.py:482
  95.0 9.3 %collective-permute-start.25 = (bf16[2304,384]{1,0:T(8,128)(2,1)S(1)}, bf16[2304,384]{1,0:T(8,128)(2,1)S(1)}, u32[]{:S(2)}, u32[]{:S(2)}) collective-permute-start(bf16[2304,384]{1,0:T(8,128)(2,1)S(1)} %get-tuple-element.499), channel_id=1, source_target_pairs={{0,1},{1,0},{2,3},{3,2},{4,5},{5,4},{6,7},{7,6},{8,9},{9,8},{10,11... | collective-permute-start | bytes 5308424 | tf_op jit(solution)/shard_map/ppermute | solution.py:482
  95.2 15.6 %collective-permute-start.29 = (bf16[768,384]{1,0:T(8,128)(2,1)S(1)}, bf16[768,384]{1,0:T(8,128)(2,1)S(1)}, u32[]{:S(2)}, u32[]{:S(2)}) collective-permute-start(bf16[768,384]{1,0:T(8,128)(2,1)S(1)} %pad_maximum_fusion.1), channel_id=1, source_target_pairs={{0,4},{4,0},{8,12},{12,8},{16,20},{20,16},{24,28},{28,24},{1,5},{5... | collective-permute-start | bytes 1769480 | tf_op jit(solution)/shard_map/ppermute | solution.py:482
  96.7 28.8 %collective-permute-start.27 = (bf16[1536,384]{1,0:T(8,128)(2,1)S(1)}, bf16[1536,384]{1,0:T(8,128)(2,1)S(1)}, u32[]{:S(2)}, u32[]{:S(2)}) collective-permute-start(bf16[1536,384]{1,0:T(8,128)(2,1)S(1)} %add_convert_fusion), channel_id=1, source_target_pairs={{0,2},{1,3},{2,0},{3,1},{4,6},{5,7},{6,4},{7,5},{8,10},{9,11},{10,... | collective-permute-start | bytes 3538952 | tf_op jit(solution)/shard_map/ppermute | solution.py:482
  104.2 34.9 %collective-permute-start.32 = (f32[64,768]{1,0:T(8,128)S(1)}, f32[64,768]{1,0:T(8,128)S(1)}, u32[]{:S(2)}, u32[]{:S(2)}) collective-permute-start(f32[64,768]{1,0:T(8,128)S(1)} %pad_maximum_fusion.6), channel_id=1, source_target_pairs={{2,0},{3,1},{6,4},{7,5},{10,8},{11,9},{14,12},{15,13},{18,16},{19,... | collective-permute-start | bytes 589832 | tf_op jit(solution)/shard_map/ppermute | solution.py:487
  105.5 33.6 %collective-permute-start.26 = (f32[64,768]{1,0:T(8,128)S(1)}, f32[64,768]{1,0:T(8,128)S(1)}, u32[]{:S(2)}, u32[]{:S(2)}) collective-permute-start(f32[64,768]{1,0:T(8,128)S(1)} %pad_maximum_fusion.6), channel_id=1, source_target_pairs={{1,0},{2,1},{3,2},{5,4},{6,5},{7,6},{9,8},{10,9},{11,10},{13,12},{... | collective-permute-start | bytes 589832 | tf_op jit(solution)/shard_map/ppermute | solution.py:487
  111.3 15.8 %collective-permute-start.31 = (bf16[768,384]{1,0:T(8,128)(2,1)S(1)}, bf16[768,384]{1,0:T(8,128)(2,1)S(1)}, u32[]{:S(2)}, u32[]{:S(2)}) collective-permute-start(bf16[768,384]{1,0:T(8,128)(2,1)S(1)} %pad_maximum_fusion.3), channel_id=1, source_target_pairs={{0,4},{4,0},{8,12},{12,8},{16,20},{20,16},{24,28},{28,24},{1,5},{5... | collective-permute-start | bytes 1769480 | tf_op jit(solution)/shard_map/ppermute | solution.py:482
  125.5 13.6 %collective-permute-start.30 = (bf16[768,384]{1,0:T(8,128)(2,1)S(1)}, bf16[768,384]{1,0:T(8,128)(2,1)S(1)}, u32[]{:S(2)}, u32[]{:S(2)}) collective-permute-start(bf16[768,384]{1,0:T(8,128)(2,1)S(1)} %pad_maximum_fusion.2), channel_id=1, source_target_pairs={{0,8},{4,12},{8,0},{12,4},{16,24},{20,28},{24,16},{28,20},{1,9},{5... | collective-permute-start | bytes 1769480 | tf_op jit(solution)/shard_map/ppermute | solution.py:482
  126.5 21.5 %collective-permute-start.35 = (bf16[768,384]{1,0:T(8,128)(2,1)S(1)}, bf16[768,384]{1,0:T(8,128)(2,1)S(1)}, u32[]{:S(2)}, u32[]{:S(2)}) collective-permute-start(bf16[768,384]{1,0:T(8,128)(2,1)S(1)} %pad_maximum_fusion.4), channel_id=1, source_target_pairs={{0,4},{4,0},{8,12},{12,8},{16,20},{20,16},{24,28},{28,24},{1,5},{5... | collective-permute-start | bytes 1769480 | tf_op jit(solution)/shard_map/ppermute | solution.py:482
  127.1 20.8 %collective-permute-start.33 = (bf16[384,384]{1,0:T(8,128)(2,1)S(1)}, bf16[384,384]{1,0:T(8,128)(2,1)S(1)}, u32[]{:S(2)}, u32[]{:S(2)}) collective-permute-start(bf16[384,384]{1,0:T(8,128)(2,1)S(1)} %fusion.8), channel_id=1, source_target_pairs={{0,2},{1,3},{2,0},{3,1},{4,6},{5,7},{6,4},{7,5},{8,10},{9,11},{10,... | collective-permute-start | bytes 884744 | tf_op jit(solution)/shard_map/ppermute | solution.py:482
  147.4 14.3 %collective-permute-start.36 = (bf16[768,384]{1,0:T(8,128)(2,1)S(1)}, bf16[768,384]{1,0:T(8,128)(2,1)S(1)}, u32[]{:S(2)}, u32[]{:S(2)}) collective-permute-start(bf16[768,384]{1,0:T(8,128)(2,1)S(1)} %select_convert_fusion), channel_id=1, source_target_pairs={{0,8},{4,12},{8,0},{12,4},{16,24},{20,28},{24,16},{28,20},{1,9},{5... | collective-permute-start | bytes 1769480 | tf_op jit(solution)/shard_map/ppermute | solution.py:482
  148.2 15.1 %collective-permute-start.39 = (bf16[192,384]{1,0:T(8,128)(2,1)S(1)}, bf16[192,384]{1,0:T(8,128)(2,1)S(1)}, u32[]{:S(2)}, u32[]{:S(2)}) collective-permute-start(bf16[192,384]{1,0:T(8,128)(2,1)S(1)} %select_convert_fusion.13), channel_id=1, source_target_pairs={{0,8},{4,12},{8,0},{12,4},{16,24},{20,28},{24,16},{28,20},{1,9},{5... | collective-permute-start | bytes 442376 | tf_op jit(solution)/shard_map/ppermute | solution.py:482
  149.8 13.5 %collective-permute-start.38 = (bf16[384,384]{1,0:T(8,128)(2,1)S(1)}, bf16[384,384]{1,0:T(8,128)(2,1)S(1)}, u32[]{:S(2)}, u32[]{:S(2)}) collective-permute-start(bf16[384,384]{1,0:T(8,128)(2,1)S(1)} %fusion.7), channel_id=1, source_target_pairs={{0,2},{1,3},{2,0},{3,1},{4,6},{5,7},{6,4},{7,5},{8,10},{9,11},{10,... | collective-permute-start | bytes 884744 | tf_op jit(solution)/shard_map/ppermute | solution.py:482
  151.7 25.8 %collective-permute-start.44 = (bf16[384,384]{1,0:T(8,128)(2,1)S(1)}, bf16[384,384]{1,0:T(8,128)(2,1)S(1)}, u32[]{:S(2)}, u32[]{:S(2)}) collective-permute-start(bf16[384,384]{1,0:T(8,128)(2,1)S(1)} %fusion.5), channel_id=1, source_target_pairs={{0,2},{1,3},{2,0},{3,1},{4,6},{5,7},{6,4},{7,5},{8,10},{9,11},{10,... | collective-permute-start | bytes 884744 | tf_op jit(solution)/shard_map/ppermute | solution.py:482
  163.3 14.4 %collective-permute-start.42 = (bf16[192,384]{1,0:T(8,128)(2,1)S(1)}, bf16[192,384]{1,0:T(8,128)(2,1)S(1)}, u32[]{:S(2)}, u32[]{:S(2)}) collective-permute-start(bf16[192,384]{1,0:T(8,128)(2,1)S(1)} %fusion.20), channel_id=1, source_target_pairs={{0,16},{4,20},{8,24},{12,28},{16,0},{20,4},{24,8},{28,12},{1,17},{... | collective-permute-start | bytes 442376 | tf_op jit(solution)/shard_map/ppermute | solution.py:482
  167.6 10.3 %collective-permute-start.41 = (bf16[768,128]{1,0:T(8,128)(2,1)S(1)}, bf16[768,128]{1,0:T(8,128)(2,1)S(1)}, u32[]{:S(2)}, u32[]{:S(2)}) collective-permute-start(bf16[768,128]{1,0:T(8,128)(2,1)S(1)} %fusion.17), channel_id=1, source_target_pairs={{0,2},{1,3},{2,0},{3,1},{4,6},{5,7},{6,4},{7,5},{8,10},{9,11},{10,... | collective-permute-start | bytes 589832 | tf_op jit(solution)/shard_map/ppermute | solution.py:482
  169.5 7.9 %collective-permute-start.37 = (bf16[384,384]{1,0:T(8,128)(2,1)S(1)}, bf16[384,384]{1,0:T(8,128)(2,1)S(1)}, u32[]{:S(2)}, u32[]{:S(2)}) collective-permute-start(bf16[384,384]{1,0:T(8,128)(2,1)S(1)} %select_convert_fusion.1), channel_id=1, source_target_pairs={{0,4},{4,0},{8,12},{12,8},{16,20},{20,16},{24,28},{28,24},{1,5},{5... | collective-permute-start | bytes 884744 | tf_op jit(solution)/shard_map/ppermute | solution.py:482
  180.2 17.1 %collective-permute-start.50 = (bf16[384,384]{1,0:T(8,128)(2,1)S(1)}, bf16[384,384]{1,0:T(8,128)(2,1)S(1)}, u32[]{:S(2)}, u32[]{:S(2)}) collective-permute-start(bf16[384,384]{1,0:T(8,128)(2,1)S(1)} %fusion.24), channel_id=1, source_target_pairs={{0,16},{4,20},{8,24},{12,28},{16,0},{20,4},{24,8},{28,12},{1,17},{... | collective-permute-start | bytes 884744 | tf_op jit(solution)/shard_map/ppermute | solution.py:482
  189.7 8.3 %collective-permute-start.48 = (f32[40,768]{1,0:T(8,128)S(1)}, f32[40,768]{1,0:T(8,128)S(1)}, u32[]{:S(2)}, u32[]{:S(2)}) collective-permute-start(f32[40,768]{1,0:T(8,128)S(1)} %add.167), channel_id=1, source_target_pairs={{0,4},{4,0},{8,12},{12,8},{16,20},{20,16},{24,28},{28,24},{1,5},{5... | collective-permute-start | bytes 368648 | tf_op jit(solution)/shard_map/ppermute | solution.py:482
  192.3 14.1 %collective-permute-start.58 = (bf16[192,384]{1,0:T(8,128)(2,1)S(1)}, bf16[192,384]{1,0:T(8,128)(2,1)S(1)}, u32[]{:S(2)}, u32[]{:S(2)}) collective-permute-start(bf16[192,384]{1,0:T(8,128)(2,1)S(1)} %fusion.22), channel_id=1, source_target_pairs={{0,16},{4,20},{8,24},{12,28},{16,0},{20,4},{24,8},{28,12},{1,17},{... | collective-permute-start | bytes 442376 | tf_op jit(solution)/shard_map/ppermute | solution.py:482
  197.2 11.1 %collective-permute-start.53 = (bf16[192,384]{1,0:T(8,128)(2,1)S(1)}, bf16[192,384]{1,0:T(8,128)(2,1)S(1)}, u32[]{:S(2)}, u32[]{:S(2)}) collective-permute-start(bf16[192,384]{1,0:T(8,128)(2,1)S(1)} %fusion.21), channel_id=1, source_target_pairs={{0,16},{4,20},{8,24},{12,28},{16,0},{20,4},{24,8},{28,12},{1,17},{... | collective-permute-start | bytes 442376 | tf_op jit(solution)/shard_map/ppermute | solution.py:482
  197.3 12.1 %collective-permute-start.54 = (bf16[768,128]{1,0:T(8,128)(2,1)S(1)}, bf16[768,128]{1,0:T(8,128)(2,1)S(1)}, u32[]{:S(2)}, u32[]{:S(2)}) collective-permute-start(bf16[768,128]{1,0:T(8,128)(2,1)S(1)} %get-tuple-element.622), channel_id=1, source_target_pairs={{0,8},{4,12},{8,0},{12,4},{16,24},{20,28},{24,16},{28,20},{1,9},{5... | collective-permute-start | bytes 589832 | tf_op jit(solution)/shard_map/ppermute | solution.py:482
  197.9 26.7 %collective-permute-start.55 = (bf16[384,384]{1,0:T(8,128)(2,1)S(1)}, bf16[384,384]{1,0:T(8,128)(2,1)S(1)}, u32[]{:S(2)}, u32[]{:S(2)}) collective-permute-start(bf16[384,384]{1,0:T(8,128)(2,1)S(1)} %maximum_select_fusion.13), channel_id=1, source_target_pairs={{0,4},{4,0},{8,12},{12,8},{16,20},{20,16},{24,28},{28,24},{1,5},{5... | collective-permute-start | bytes 884744 | tf_op jit(solution)/shard_map/ppermute | solution.py:482
  200.0 25.1 %collective-permute-start.62 = (bf16[384,384]{1,0:T(8,128)(2,1)S(1)}, bf16[384,384]{1,0:T(8,128)(2,1)S(1)}, u32[]{:S(2)}, u32[]{:S(2)}) collective-permute-start(bf16[384,384]{1,0:T(8,128)(2,1)S(1)} %add_convert_fusion.1), channel_id=1, source_target_pairs={{0,4},{4,0},{8,12},{12,8},{16,20},{20,16},{24,28},{28,24},{1,5},{5... | collective-permute-start | bytes 884744 | tf_op jit(solution)/shard_map/ppermute | solution.py:482
  208.3 11.0 %collective-permute-start.66 = (bf16[192,384]{1,0:T(8,128)(2,1)S(1)}, bf16[192,384]{1,0:T(8,128)(2,1)S(1)}, u32[]{:S(2)}, u32[]{:S(2)}) collective-permute-start(bf16[192,384]{1,0:T(8,128)(2,1)S(1)} %fusion.23), channel_id=1, source_target_pairs={{0,16},{4,20},{8,24},{12,28},{16,0},{20,4},{24,8},{28,12},{1,17},{... | collective-permute-start | bytes 442376 | tf_op jit(solution)/shard_map/ppermute | solution.py:482
  209.5 9.9 %collective-permute-start.59 = (bf16[192,384]{1,0:T(8,128)(2,1)S(1)}, bf16[192,384]{1,0:T(8,128)(2,1)S(1)}, u32[]{:S(2)}, u32[]{:S(2)}) collective-permute-start(bf16[192,384]{1,0:T(8,128)(2,1)S(1)} %add_convert_fusion.3), channel_id=1, source_target_pairs={{0,8},{4,12},{8,0},{12,4},{16,24},{20,28},{24,16},{28,20},{1,9},{5... | collective-permute-start | bytes 442376 | tf_op jit(solution)/shard_map/ppermute | solution.py:482
  211.8 10.7 %collective-permute-start.61 = (bf16[192,384]{1,0:T(8,128)(2,1)S(1)}, bf16[192,384]{1,0:T(8,128)(2,1)S(1)}, u32[]{:S(2)}, u32[]{:S(2)}) collective-permute-start(bf16[192,384]{1,0:T(8,128)(2,1)S(1)} %add_convert_fusion.4), channel_id=1, source_target_pairs={{0,8},{4,12},{8,0},{12,4},{16,24},{20,28},{24,16},{28,20},{1,9},{5... | collective-permute-start | bytes 442376 | tf_op jit(solution)/shard_map/ppermute | solution.py:482
  219.3 12.4 %collective-permute-start.57 = (bf16[768,128]{1,0:T(8,128)(2,1)S(1)}, bf16[768,128]{1,0:T(8,128)(2,1)S(1)}, u32[]{:S(2)}, u32[]{:S(2)}) collective-permute-start(bf16[768,128]{1,0:T(8,128)(2,1)S(1)} %fusion.14), channel_id=1, source_target_pairs={{0,16},{4,20},{8,24},{12,28},{16,0},{20,4},{24,8},{28,12},{1,17},{... | collective-permute-start | bytes 589832 | tf_op jit(solution)/shard_map/ppermute | solution.py:482
  219.4 10.4 %collective-permute-start.56 = (f32[40,768]{1,0:T(8,128)S(1)}, f32[40,768]{1,0:T(8,128)S(1)}, u32[]{:S(2)}, u32[]{:S(2)}) collective-permute-start(f32[40,768]{1,0:T(8,128)S(1)} %add.178), channel_id=1, source_target_pairs={{0,16},{4,20},{8,24},{12,28},{16,0},{20,4},{24,8},{28,12},{1,17},{... | collective-permute-start | bytes 368648 | tf_op jit(solution)/shard_map/ppermute | solution.py:482
  222.5 10.1 %collective-permute-start.67 = (bf16[192,384]{1,0:T(8,128)(2,1)S(1)}, bf16[192,384]{1,0:T(8,128)(2,1)S(1)}, u32[]{:S(2)}, u32[]{:S(2)}) collective-permute-start(bf16[192,384]{1,0:T(8,128)(2,1)S(1)} %add_convert_fusion.2), channel_id=1, source_target_pairs={{0,4},{4,0},{8,12},{12,8},{16,20},{20,16},{24,28},{28,24},{1,5},{5... | collective-permute-start | bytes 442376 | tf_op jit(solution)/shard_map/ppermute | solution.py:482
  224.6 10.4 %collective-permute-start.63 = (bf16[384,384]{1,0:T(8,128)(2,1)S(1)}, bf16[384,384]{1,0:T(8,128)(2,1)S(1)}, u32[]{:S(2)}, u32[]{:S(2)}) collective-permute-start(bf16[384,384]{1,0:T(8,128)(2,1)S(1)} %maximum_select_fusion.15), channel_id=1, source_target_pairs={{0,4},{4,0},{8,12},{12,8},{16,20},{20,16},{24,28},{28,24},{1,5},{5... | collective-permute-start | bytes 884744 | tf_op jit(solution)/shard_map/ppermute | solution.py:482
  225.0 10.0 %collective-permute-start.60 = (bf16[384,384]{1,0:T(8,128)(2,1)S(1)}, bf16[384,384]{1,0:T(8,128)(2,1)S(1)}, u32[]{:S(2)}, u32[]{:S(2)}) collective-permute-start(bf16[384,384]{1,0:T(8,128)(2,1)S(1)} %maximum_select_fusion.14), channel_id=1, source_target_pairs={{0,4},{4,0},{8,12},{12,8},{16,20},{20,16},{24,28},{28,24},{1,5},{5... | collective-permute-start | bytes 884744 | tf_op jit(solution)/shard_map/ppermute | solution.py:482
  231.7 23.4 %collective-permute-start.69 = (bf16[768,384]{1,0:T(8,128)(2,1)S(1)}, bf16[768,384]{1,0:T(8,128)(2,1)S(1)}, u32[]{:S(2)}, u32[]{:S(2)}) collective-permute-start(bf16[768,384]{1,0:T(8,128)(2,1)S(1)} %maximum_select_fusion.12), channel_id=1, source_target_pairs={{0,8},{4,12},{8,0},{12,4},{16,24},{20,28},{24,16},{28,20},{1,9},{5... | collective-permute-start | bytes 1769480 | tf_op jit(solution)/shard_map/ppermute | solution.py:482
  232.7 21.2 %collective-permute-start.68 = (bf16[384,384]{1,0:T(8,128)(2,1)S(1)}, bf16[384,384]{1,0:T(8,128)(2,1)S(1)}, u32[]{:S(2)}, u32[]{:S(2)}) collective-permute-start(bf16[384,384]{1,0:T(8,128)(2,1)S(1)} %maximum_select_fusion.16), channel_id=1, source_target_pairs={{0,8},{4,12},{8,0},{12,4},{16,24},{20,28},{24,16},{28,20},{1,9},{5... | collective-permute-start | bytes 884744 | tf_op jit(solution)/shard_map/ppermute | solution.py:482
  234.9 22.9 %collective-permute-start.65 = (bf16[384,768]{1,0:T(8,128)(2,1)S(1)}, bf16[384,768]{1,0:T(8,128)(2,1)S(1)}, u32[]{:S(2)}, u32[]{:S(2)}) collective-permute-start(bf16[384,768]{1,0:T(8,128)(2,1)S(1)} %maximum_select_fusion.10), channel_id=1, source_target_pairs={{0,2},{1,3},{2,0},{3,1},{4,6},{5,7},{6,4},{7,5},{8,10},{9,11},{10,... | collective-permute-start | bytes 1769480 | tf_op jit(solution)/shard_map/ppermute | solution.py:482
  (45 other events, 196.5 us)

commit v3 on v2

--- a/solution.py
+++ b/solution.py
@@ -12,18 +12,18 @@
 CHUNKS = 8
 F32 = jnp.float32
 LOW = jnp.bfloat16
-KINDS = {"F": "w", "P": "x", "R": "x", "O": "z", "N": "x"}
+KINDS = {"I": "x", "U": "y", "P": "y", "R": "x", "O": "x", "N": "z"}
 ORDER = (
-    "+F0", "+F1", "Kbb", "-F0", "-F1", "+P0", "Kv1", "-P0", "+V1", "+F",
-    "+P", "Kv0", "-V1", "+V0", "Kt3", "-V0", "+dz", "+E", "-P", "+R",
-    "-dz", "+O", "-F", "+N", "-R", "+P", "-O", "+F", "-E", "Kt4",
-    "-P", "+R", "+sm", "-N", "+P", "-sm", "+N", "-F", "+F", "-P",
-    "+P", "-R", "+dz", "+R", "-F", "+sm", "-N", "+F", "-R", "+O",
-    "-P", "-dz", "+N", "+dz", "-sm", "+P", "-dz", "-O", "-N", "+R",
-    "+sm", "+dz", "-P", "+O", "-F", "+P", "-sm", "+N", "-O", "+sm",
-    "-dz", "+O", "-R", "+F", "-P", "+R", "-sm", "+dz", "-N", "+N",
-    "-F", "-R", "+R", "+F", "-O", "+O", "-N", "+N", "-dz", "-R",
-    "-O", "+sm", "+O", "-F", "-N", "-sm", "-O",
+    "+F0", "+F1", "-F0", "-F1", "+I", "+U", "Kback", "-I", "-U", "+R",
+    "+O", "+E", "+P", "-R", "+U", "-O", "+N", "-P", "+I", "-N",
+    "+R", "-E", "+N", "+P", "-U", "Kt4", "-I", "+O", "+I", "-R",
+    "+sm", "-N", "+R", "-sm", "+U", "-P", "-I", "+I", "+N", "-U",
+    "+P", "-R", "+U", "-O", "+R", "-I", "+O", "-N", "+I", "-P",
+    "+N", "-R", "+P", "-U", "+R", "-I", "+sm", "-O", "-N", "+O",
+    "-P", "+I", "+P", "-O", "+U", "-R", "-sm", "+R", "+sm", "-I",
+    "+O", "-U", "-P", "+P", "-R", "+U", "+N", "-sm", "+sm", "-P",
+    "+R", "-O", "-U", "+O", "+P", "-N", "-sm", "-R", "+sm", "+N",
+    "-O", "+O", "-P", "-N", "+N", "-O", "-sm", "-N",
 )
 
 
@@ -306,16 +306,17 @@
                 ].astype(pack_ref.dtype)
 
 
-def value_back(part, hidden_ref, normed_ref, mixed_ref, probs_ref, vpre_ref, rpre_ref, att_ref, united_ref, ga_ref, gb_ref, va_ref, ra_ref, vb_ref, rb_ref, ng_ref, mg_ref, pg_ref, keep_ref, send_ref):
+def value_back(part, hidden_ref, normed_ref, mixed_ref, probs_ref, vpre_ref, rpre_ref, att_ref, united_ref, ga_ref, gb_ref, va_ref, ra_ref, vb_ref, rb_ref, ng_ref, mg_ref, pg_ref, *packs):
     hidden, normed, mixed = hidden_ref[...], normed_ref[...], mixed_ref[...]
     tokens, depth = hidden.shape
     units = va_ref.shape[1]
     cols = ga_ref.shape[1] - units
     half = depth // 2
-    for i, (g_ref, v_ref, r_ref, pack_ref) in enumerate(
-        ((ga_ref, va_ref, ra_ref, keep_ref), (gb_ref, vb_ref, rb_ref, send_ref))
+    for i, (g_ref, v_ref, r_ref, pack) in enumerate(
+        ((ga_ref, va_ref, ra_ref, packs[:3]), (gb_ref, vb_ref, rb_ref, packs[3:]))
     ):
-        kind = pack_ref.dtype
+        reset_pack, out_pack, value_pack = pack
+        kind = reset_pack.dtype
         united_grad = dot_cols(hidden, g_ref[part, cols:, :])
         reset_pre, value_pre = rpre_ref[i], vpre_ref[i]
         reset_low = (united_grad * att_ref[i] * silu_slope(reset_pre)).astype(LOW)
@@ -326,21 +327,23 @@
             block = slice(start, start + STRETCH)
             parts.append(dot_rows(probs_ref[block, :].astype(LOW), attended_low[block]))
             back = dot_cols(attended_low[block], values[block])
-            pg_ref[block, :] = back if i == 0 else pg_ref[block, :] + back
+            first = i == 0 and part == 1
+            pg_ref[block, :] = back if first else pg_ref[block, :] + back
         value_low = (jnp.concatenate(parts, 0) * silu_slope(value_pre)).astype(LOW)
         into_normed = dot_cols(value_low, v_ref[...])
         into_mixed = dot_cols(reset_low, r_ref[...])
-        ng_ref[...] = into_normed if i == 0 else ng_ref[...] + into_normed
-        mg_ref[...] = into_mixed if i == 0 else mg_ref[...] + into_mixed
-        pack_ref[:depth, :] = dot_rows(mixed, reset_low).astype(kind)
+        first = i == 0 and part == 1
+        ng_ref[...] = into_normed if first else ng_ref[...] + into_normed
+        mg_ref[...] = into_mixed if first else mg_ref[...] + into_mixed
+        reset_pack[part] = dot_rows(mixed, reset_low).astype(kind)
         for h in range(2):
-            pack_ref[depth + h * units : depth + (h + 1) * units, :] = dot_rows(
+            out_pack[part, h * units : (h + 1) * units, :] = dot_rows(
                 united_ref[i], hidden[:, h * half : (h + 1) * half]
             ).astype(kind)
-        pack_ref[2 * depth :, :] = dot_rows(normed, value_low).astype(kind)
-
-
-def third_pass(rows, zpre_ref, probs_ref, p0_ref, p1_ref, qg_ref, qb_ref, kg_ref, wz_ref, mixed_ref, m0_ref, m1_ref, m2_ref, pre_ref, keep_ref, al_ref, de_ref, pg_ref, dz_ref, small_ref, im_ref, iv_ref, lm_ref, lv_ref, qk_ref):
+        value_pack[part] = dot_rows(normed, value_low).astype(kind)
+
+
+def third_pass(rows, zpre_ref, probs_ref, p_ref, qg_ref, qb_ref, kg_ref, wz_ref, mixed_ref, m0_ref, m1_ref, pre_ref, keep_ref, al_ref, de_ref, pg_ref, dz_ref, small_ref, im_ref, iv_ref, lm_ref, lv_ref, qk_ref):
     z_pre = zpre_ref[...]
     z_low = silu(z_pre).astype(LOW).astype(F32)
     queries = (z_low * qg_ref[...] + qb_ref[...]).astype(LOW)
@@ -348,7 +351,7 @@
     for start in range(0, z_low.shape[0], STRETCH):
         block = slice(start, start + STRETCH)
         probs = probs_ref[block, :]
-        grad = p0_ref[block, :] + p1_ref[block, :]
+        grad = p_ref[block, :]
         grad = probs * (grad - jnp.sum(probs * grad, -1, keepdims=True)) * z_low.shape[1] ** (-0.5)
         high = grad.astype(LOW)
         rest = (grad - high.astype(F32)).astype(LOW)
@@ -361,7 +364,7 @@
     small_ref[2:3, :] = jnp.sum(key_grad * z_low, 0, keepdims=True)
     z_grad = ((query_grad * qg_ref[...] + key_grad * kg_ref[...]) * silu_slope(z_pre)).astype(LOW)
     dz_ref[...] = dot_rows(mixed_ref[...], z_grad)
-    mixed_grad = m0_ref[...] + m1_ref[...] + m2_ref[...] + dot_cols(z_grad, wz_ref[...])
+    mixed_grad = m0_ref[...] + m1_ref[...] + dot_cols(z_grad, wz_ref[...])
     into_slabs(pg_ref, mixed_grad)
     pg_ref[...] = pg_ref[...] * silu_slope(pre_ref[...])
     dims, width = al_ref.shape
@@ -405,7 +408,31 @@
     lax.fori_loop(0, width // LANES, lane, 0)
 
 
-def fourth_pass(rows, pg_ref, normed_ref, im_ref, iv_ref, near_ref, far_ref, keep_ref, flag_ref, al_ref, de_ref, be_ref, eta_ref, om_ref, n0_ref, n1_ref, x_ref, g_ref, direct_ref, gg_ref, qk_ref, xg_ref, sums_ref, dec_ref, drv_ref, ng_ref):
+def back_pass(rows, *refs):
+    offs_ref, x_ref, cot_ref, blended_ref, s0_ref, s1_ref, o0_ref, o1_ref, hpre_ref, gate_ref = refs[:10]
+    mixed_ref, gain_ref, wu_ref, whid_ref, normed_ref, probs_ref = refs[10:16]
+    own_part, far_part, (ga_ref, gb_ref), weights = refs[16:20], refs[20:24], refs[24:26], refs[26:34]
+    zpre_ref, qg_ref, qb_ref, kg_ref, wz_ref, pre_ref, keep_ref, al_ref, de_ref = refs[34:43]
+    y_ref, direct_ref, gg_ref, pair_keep_ref, pair_send_ref, ng_ref = refs[43:49]
+    packs, outs = refs[49:55], refs[55:62]
+    mg_ref, p_ref, qk_ref, m0_ref, full_ref, hidden_ref = refs[62:]
+    blend_back(
+        offs_ref, x_ref, cot_ref, blended_ref, s0_ref, s1_ref, o0_ref, o1_ref, hpre_ref, gate_ref,
+        mixed_ref, gain_ref, wu_ref, whid_ref, y_ref, direct_ref, hidden_ref, m0_ref, gg_ref,
+        pair_keep_ref, pair_send_ref, full_ref,
+    )
+    for part, parts in ((1, far_part), (0, own_part)):
+        value_back(
+            part, hidden_ref, normed_ref, mixed_ref, probs_ref, *parts, ga_ref, gb_ref,
+            *weights[4 * part : 4 * part + 4], ng_ref, mg_ref, p_ref, *packs,
+        )
+    third_pass(
+        rows, zpre_ref, probs_ref, p_ref, qg_ref, qb_ref, kg_ref, wz_ref, mixed_ref, m0_ref,
+        mg_ref, pre_ref, keep_ref, al_ref, de_ref, *outs, qk_ref,
+    )
+
+
+def fourth_pass(rows, pg_ref, normed_ref, im_ref, iv_ref, near_ref, far_ref, keep_ref, flag_ref, al_ref, de_ref, be_ref, eta_ref, om_ref, n0_ref, x_ref, g_ref, direct_ref, gg_ref, qk_ref, xg_ref, sums_ref, dec_ref, drv_ref, ng_ref):
     rate_tables(al_ref, de_ref, be_ref, dec_ref, drv_ref)
     dims, width = al_ref.shape
     tokens = keep_ref.shape[0]
@@ -461,7 +488,7 @@
         return carry
 
     lax.fori_loop(0, width // LANES, lane, 0)
-    normed_grad = from_slabs(ng_ref[...], tokens) + n0_ref[...] + n1_ref[...]
+    normed_grad = from_slabs(ng_ref[...], tokens) + n0_ref[...]
     hat, scale = norm_parts(x_ref[...].astype(F32))
     at = 2 * dims
     for j in range(width // LANES):
@@ -516,11 +543,19 @@
     return pick(first, (low, high)), pick(first, (high, low)).astype(LOW)
 
 
-def reduction(kind, near, far, firsts):
+def reduction(kind, packs, firsts):
     bits = [1 << b for b in range(lax.axis_size("dp").bit_length() - 1)]
-    lead = {"x": [1], "z": [2]}.get(kind, [])
-    spread = {"x": [2], "z": [1], "y": [1, 2], "w": [2, 1]}[kind]
-    near, far = near(), far()
+    lead, spread, rest = {
+        "x": ([1], [2], []),
+        "z": ([2], [1], []),
+        "y": ([], [1, 2], []),
+        "w": ([], [2, 1], []),
+        "X": ([1], [], [2]),
+        "Z": ([2], [], [1]),
+        "Y": ([], [1], [2]),
+        "W": ([], [2], [1]),
+    }[kind]
+    near, far = yield from packs
     for bit in lead:
         near, away = halves(near, firsts[bit])
         far, far_away = halves(far, firsts[bit])
@@ -533,7 +568,7 @@
         total, away = halves(total, firsts[bit])
         got = yield "dp", bit, away
         total = total + got.astype(F32)
-    for bit in bits[2:]:
+    for bit in rest + bits[2:]:
         total = rounded(total)
         got = yield "dp", bit, total.astype(LOW)
         total = total + got.astype(F32)
@@ -549,13 +584,18 @@
     return got
 
 
-def everywhere(v, kind):
+def everywhere(coarse, fine):
+    at, end = coarse.shape[0], coarse.shape[0] + fine.shape[0]
     for axis in ("tensor", "dp"):
         for b in range(lax.axis_size(axis).bit_length() - 1):
-            v = lax.reduce_precision(v, 8, 7) if kind == LOW else v
-            got = yield axis, 1 << b, v.astype(kind)
-            v = v + got.astype(F32)
-    return v
+            coarse, high = rounded(coarse), rounded(fine)
+            low = rounded(fine - high)
+            packed = jnp.concatenate([coarse, high, low], 0).astype(LOW)
+            got = yield axis, 1 << b, packed
+            got = got.astype(F32)
+            coarse = coarse + got[:at]
+            fine = (high + low) + (got[at:end] + got[end:])
+    return coarse, fine
 
 
 class Pump:
@@ -678,12 +718,15 @@
     shares = (w_value, w_reset, w_join, w_ffn_in, w_ffn_out)
     bits = (1, 1, 2, 1, 1)
     pump = Pump(offs)
-    beside = [swap(w_value, "tensor", 1), swap(w_reset, "tensor", 1)]
+    beside = [swap(w, "tensor", 1) for w in (w_value, w_reset, w_ffn_in, w_ffn_out)]
     half_v, half_r, half_g, half_i, half_o = (
         pick(firsts[bit], split_rows(w)) for w, bit in zip(shares, bits, strict=True)
     )
 
     over_v = swap(half_v, "tensor", 2)
+    beside = [pump.gate(w) for w in beside]
+    over_r = swap(pump.gate(half_r), "tensor", 2)
+    x = pump.gate(x)
 
     normed, normed_low, init, last = call(
         functools.partial(first_pass, rows),
@@ -692,11 +735,15 @@
         ema,
         [vm(tab), vm(tab)],
     )
+    last = pump.gate(last)
+    over_v = pump.gate(over_v)
+    other_v = swap(over_v, "dp", 1)
     f1, f2 = shift(last, 1), shift(last, 2)
+    over_r = pump.gate(over_r)
+    other_r = swap(over_r, "dp", 1)
     f1, f2 = pump.gate(f1), pump.gate(f2)
-    beside = [pump.gate(w) for w in beside]
-    over_r = swap(pump.gate(half_r), "tensor", 2)
-    beside += [swap(pump.gate(w), "tensor", 1) for w in (w_ffn_in, w_ffn_out)]
+    over_g = swap(pump.gate(half_g), "tensor", 2)
+    half_i = pump.gate(half_i)
     pre, mixed_low, z_pre, gate, probs = call(
         functools.partial(second_pass, rows),
         [(slabs, F32), (wide, LOW), ((tokens, zd), F32), (wide, F32), ((tokens, STRETCH), F32)],
@@ -707,10 +754,8 @@
     )
     split = (2, tokens, units)
     mixed_low = pump.gate(mixed_low)
-    over_v = pump.gate(over_v)
-    other_v = swap(over_v, "dp", 1)
-    over_g = swap(pump.gate(half_g), "tensor", 2)
-    beside = [pump.gate(w) for w in beside]
+    over_i = swap(half_i, "tensor", 2)
+    other_v = pump.gate(other_v)
     mixed_low = pump.gate(mixed_low)
 
     def values(weights):
@@ -723,29 +768,25 @@
 
     own_part = values((w_value, w_reset, beside[0], beside[1]))
     united0 = pump.gate(own_part[3])
-    over_r = pump.gate(over_r)
-    other_r = swap(over_r, "dp", 1)
-    over_i = swap(pump.gate(half_i), "tensor", 2)
-    other_v = pump.gate(other_v)
-    full_v = pump.gate(joined(over_v, other_v, firsts[1]))
-    both_v = swap(full_v, "tensor", 1)
+    other_r = pump.gate(other_r)
     over_g = pump.gate(over_g)
     other_g = swap(over_g, "dp", 2)
     over_o = swap(pump.gate(half_o), "tensor", 2)
-    other_r = pump.gate(other_r)
+    over_i = pump.gate(over_i)
+    other_i = swap(over_i, "dp", 1)
+    over_o = pump.gate(over_o)
+    other_o = swap(over_o, "dp", 1)
+    full_v = pump.gate(joined(over_v, other_v, firsts[1]))
+    both_v = swap(full_v, "tensor", 1)
     full_r = pump.gate(joined(over_r, other_r, firsts[1]))
     both_r = swap(full_r, "tensor", 1)
+    other_g = pump.gate(other_g)
+    near_g = pump.gate(jnp.stack([w_join, joined(over_g, other_g, firsts[2])]))
+    beside_g = swap(near_g, "tensor", 1)
     both_v, both_r = pump.gate(both_v), pump.gate(both_r)
-    over_i = pump.gate(over_i)
     full_v = pump.gate(full_v)
     far_part = values((full_v, full_r, both_v, both_r))
     united1 = pump.gate(far_part[3])
-    other_i = swap(over_i, "dp", 1)
-    over_o = pump.gate(over_o)
-    other_o = swap(over_o, "dp", 1)
-    other_g = pump.gate(other_g)
-    near_g = pump.gate(jnp.stack([w_join, joined(over_g, other_g, firsts[2])]))
-    beside_g = swap(near_g, "tensor", 1)
     other_i = pump.gate(other_i)
     full_i = pump.gate(joined(over_i, other_i, firsts[1]))
     both_i = swap(full_i, "tensor", 1)
@@ -781,43 +822,27 @@
     pump.add("F0", one_swap("tensor", 1, ffn0[3]))
     pump.add("F1", one_swap("tensor", 1, ffn1[3]))
     own = (2, 4 * cols, width // 2)
-    pack_rows = 2 * width + 2 * units
     held = {}
 
-    def run_blend():
-        held["bb"] = call(
-            blend_back,
-            [(wide, LOW), (wide, F32), (wide, LOW), (wide, F32), ((1, width), F32), (own, F32), (own, LOW)],
+    def run_back():
+        pack = (2, width, units)
+        outs = call(
+            functools.partial(back_pass, rows),
+            [(wide, LOW), (wide, F32), ((1, width), F32), (own, F32), (own, LOW), (wide, F32),
+             *[(pack, F32)] * 3, *[(pack, LOW)] * 3,
+             (slabs, F32), ((width, zd), F32), ((8, zd), F32), (chunked, F32), (chunked, F32), (finals, F32), (finals, F32)],
             (offs, x, cot, pump.gate(blended), ffn1[1], back0, ffn0[0], ffn1[0], hidden_pre, gate,
-             mixed_low, g2, w_update, whid),
-            4 * mat * width,
-            [vm((width, width))],
+             mixed_low, g2, w_update, whid, normed_low, probs, *kept_parts[0], *kept_parts[1], *wg,
+             wv[0], wr[0], wv[1], wr[1], wv[2], wr[2], wv[3], wr[3],
+             z_pre, qg, qb, kg, w_z, pre, keep, alpha_raw, delta_raw),
+            (4 * width + 28 * units) * mat,
+            [vm(wide), vm((tokens, STRETCH)), vm((2, tokens, zd)), vm(wide), vm((width, width)),
+             pltpu.VMEM(wide, LOW)],
             smem=(0,),
         )
-        held["hidden"] = pump.gate(held["bb"][2])
-        pump.add("P0", one_swap("tensor", 1, held["bb"][6]))
-
-    def run_values(p):
-        held[p] = [*call(
-            functools.partial(value_back, p),
-            [(wide, F32), (wide, F32), ((tokens, STRETCH), F32), ((pack_rows, units), F32), ((pack_rows, units), LOW)],
-            (pump.gate(held["hidden"]), normed_low, mixed_low, probs, *kept_parts[p], *wg,
-             wv[2 * p], wr[2 * p], wv[2 * p + 1], wr[2 * p + 1]),
-            14 * mat * units,
-        )]
-        pump.token, held[p][2] = tied((pump.token, held[p][2]))
-        pump.add(f"V{p}", one_swap("tensor", 1, held[p][4]))
-
-    def run_third():
-        held["t3"] = call(
-            functools.partial(third_pass, rows),
-            [(slabs, F32), ((width, zd), F32), ((8, zd), F32), (chunked, F32), (chunked, F32), (finals, F32), (finals, F32)],
-            (pump.gate(z_pre), probs, held[0][2], held[1][2], qg, qb, kg, w_z, mixed_low, held["bb"][3],
-             held[0][1], held[1][1], pre, keep, alpha_raw, delta_raw),
-            2 * ema,
-            [vm((2, tokens, zd))],
-        )
-        pump.add("dz", everywhere(held["t3"][1], LOW))
+        held["bb"], held["v"] = outs[:5], outs[5:12]
+        held["t3"] = list(outs[12:])
+        pump.token, held["t3"][5] = tied((pump.token, held["t3"][5]))
 
     def send_back():
         back = pump.gate(jnp.concatenate([held["t3"][5], held["t3"][6]], 0))
@@ -832,32 +857,32 @@
             functools.partial(fourth_pass, rows),
             [(wide, LOW), ((2 * dims + 8, width), F32)],
             (t3[0], normed, t3[3], t3[4], *held["back"], keep, unbroken(1), alpha_raw,
-             delta_raw, ema_beta, ema_eta, om, held[0][0], held[1][0], x, g1, held["bb"][1],
-             held["bb"][4], t3[2]),
+             delta_raw, ema_beta, ema_eta, om, held["v"][0], x, g1, held["bb"][1],
+             held["bb"][2], t3[2]),
             2 * ema,
             [vm(tab), vm(tab), vm(slabs)],
         )
-        pump.add("sm", everywhere(pump.gate(held["t4"][1]), F32))
-
-    def pack(p, source, at, end):
-        kept = (ffn0, ffn1)[p][2] if source == "F" else held[p][3]
-        return kept[at:end] + pump.done[f"{source}{p}"][at:end].astype(F32)
+        sums = pump.gate(held["t4"][1])
+        sums = jnp.concatenate([sums[:, at : at + LANES] for at in range(0, width, LANES)], 0)
+        pump.add("sm", everywhere(held["t3"][1], sums))
+
+    def packs_of(name):
+        if name in "IU":
+            rows_of = slice(0, width) if name == "I" else slice(width, 2 * width)
+            return tuple(
+                keep[rows_of] + pump.done[swapped][rows_of].astype(F32)
+                for keep, swapped in ((ffn0[2], "F0"), (ffn1[2], "F1"))
+            )
+        kept, sent = held["bb"][3:] if name == "P" else held["v"]["RON".index(name) + 1 : 7 : 3]
+        got = yield "tensor", 1, sent
+        got = got.astype(F32)
+        return kept[0] + got[0], kept[1] + got[1]
 
     def add_flow(name):
-        if name == "P":
-            kept, got = held["bb"][5], pump.done["P0"].astype(F32)
-            near, far = (lambda: kept[0] + got[0]), (lambda: kept[1] + got[1])
-        else:
-            source = "F" if name == "F" else "V"
-            at, end = {"F": (0, 2 * width), "R": (0, width), "O": (width, 2 * width), "N": (2 * width, 3 * width)}[name]
-            near, far = (lambda: pack(0, source, at, end)), (lambda: pack(1, source, at, end))
-        pump.add(name, reduction(KINDS[name], near, far, firsts))
+        pump.add(name, reduction(KINDS[name], packs_of(name), firsts))
 
     kernels = {
-        "bb": run_blend,
-        "v1": lambda: run_values(1),
-        "v0": lambda: run_values(0),
-        "t3": run_third,
+        "back": run_back,
         "t4": run_fourth,
     }
     for word in ORDER:
@@ -874,8 +899,9 @@
             pump.finish(name)
     pump.drain()
     output, input_grad = held["bb"][0], held["t4"][0]
-    sums, dz_sum, pair_sum, ffn_sum = (pump.done[n] for n in ("sm", "dz", "P", "F"))
-    reset_sum, out_sum, value_sum = (pump.done[n] for n in "RON")
+    dz_sum, sums = pump.done["sm"]
+    sums = from_slabs(sums, 2 * dims + 8)
+    pair_sum, reset_sum, out_sum, value_sum, in_sum, fout_sum = (pump.done[n] for n in "PRONIU")
 
     alpha, sigma = jax.nn.sigmoid(alpha_raw), jax.nn.sigmoid(delta_raw)
     with_mu, with_nu = sums[:dims], sums[dims : 2 * dims]
@@ -904,8 +930,8 @@
         side_by_side(pair_sum[2 * cols :]).astype(F32),
         side_by_side(out_sum).astype(F32),
         sums[at + 2],
-        ffn_sum[:width].astype(F32),
-        side_by_side(ffn_sum[width:]).astype(F32),
+        in_sum.astype(F32),
+        side_by_side(fout_sum).astype(F32),
     )
 
 

time: 263 us -> 260 us (0.989)
  waiting for transfers between devices: 122 us -> 103 us
  starting transfers between devices: 68.2 us -> 79.8 us
  local copies, waits for them, and re-layouts: 5.82 us -> 9.19 us
    ppermute x66 -> x68, waiting for transfers between devices: 122 us -> 99.4 us  [swap(): return lax.ppermute(x, axis, [(i, i ^ bit) for i in range(size)])]
    ppermute x66 -> x68, starting transfers between devices: 58.9 us -> 72.8 us  [swap(): return lax.ppermute(x, axis, [(i, i ^ bit) for i in range(size)])]
    unnamed x47 -> x93, local copies, waits for them, and re-layouts: 3.52 us -> 7.57 us
    ppermute x4, waiting for transfers between devices: 0.01 us -> 3.72 us  [shift(): lax.ppermute(x, 'tensor', [(i, i + by) for i in range(size) if 0 <= i + b...]
    pallas_call x12 -> x9, Pallas kernels: 41.1 us -> 40.4 us  [call(): pl.pallas_call(kernel, out_shape=outs, in_specs=specs, out_specs=[pl.Bloc...]
  transfers between devices with their start and end apart: 70 -> 72, of which waited for: 27 -> 36; matrix products, arithmetic and copies ran while one was open for 7% -> 8% of each run, Pallas kernels for 15% -> 16%
where the time goes in v3:
time: 260 us; the launch traced here: 257 us
  waiting for transfers between devices  103 us (40%)
  starting transfers between devices  79.8 us (31%)
  Pallas kernels  40.4 us (16%)
  other arithmetic  22 us (8%)
  local copies, waits for them, and re-layouts  9.19 us (4%)
    ppermute x68, waiting for transfers between devices, swap(): return lax.ppermute(x, axis, [(i, i ^ bit) for i in range(size)])  99.4 us
    ppermute x68, starting transfers between devices, swap(): return lax.ppermute(x, axis, [(i, i ^ bit) for i in range(size)])  72.8 us
    pallas_call x9, Pallas kernels, call(): pl.pallas_call(kernel, out_shape=outs, in_specs=specs, out_specs=[pl.Bloc...  40.4 us
    unnamed x93, local copies, waits for them, and re-layouts  7.57 us
    ppermute x4, starting transfers between devices, shift(): lax.ppermute(x, 'tensor', [(i, i + by) for i in range(size) if 0 <= i + b...  7 us
  transfers between devices with their start and end apart: 72, of which 36 were waited for; matrix products, arithmetic and copies ran while one was open for 8% of the time, Pallas kernels for 16%

profile of v3, /device:TPU:0, one launch (start us, length us, event | category | flops | bytes accessed | tf_op | source)
XLA Modules:
  0.0 256.7 jit_solution(5732023537143352623)
XLA Ops:
  3.0 3.0 %collective-permute-start.6 = (bf16[384,384]{1,0:T(8,128)(2,1)S(1)}, bf16[384,384]{1,0:T(8,128)(2,1)S(1)}, u32[]{:S(2)}, u32[]{:S(2)}) collective-permute-start(bf16[384,384]{1,0:T(8,128)(2,1)S(1)} %slice_select_fusion.3), channel_id=1, source_target_pairs={{0,2},{1,3},{2,0},{3,1},{4,6},{5,7},{6,4},{7,5},{8,10},{9,11},{10,... | collective-permute-start | bytes 884744 | tf_op jit(solution)/shard_map/ppermute | solution.py:509
  6.8 1.6 collective-permute-start.5
  8.6 3.0 %shard_map.356 = (f32[1536,128]{1,0:T(8,128)S(1)}, bf16[256,768]{1,0:T(8,128)(2,1)S(1)}, f32[256,768]{1,0:T(8,128)S(1)}, f32[32,768]{1,0:T(8,128)S(1)}) custom-call(bf16[256,768]{1,0:T(8,128)(2,1)S(1)} %bitcast.57, f32[1,768]{1,0:T(1,128)S(1)} %broadcast_in_dim.34.g_ref, f32[16,768]{1,0:T(8,128)S(1)} %copy-done.6, f32[16,768]{1,0:T(8,128)S(1)} %copy-done.7, ...), custom_call_target="tpu_custom_call" | custom-call | flops 25165824 | bytes 2739200 | tf_op jit(solution)/shard_map/pallas_call | solution.py:72
  11.6 1.8 collective-permute-start.4
  13.4 2.5 collective-permute-start.7
  16.0 3.8 %collective-permute-done.5 = bf16[384,384]{1,0:T(8,128)(2,1)S(1)} collective-permute-done((bf16[384,384]{1,0:T(8,128)(2,1)S(1)}, bf16[384,384]{1,0:T(8,128)(2,1)S(1)}, u32[]{:S(2)}, u32[]{:S(2)}) %collective-permute-start.5) | collective-permute-done | bytes 294944 | tf_op jit(solution)/shard_map/ppermute | solution.py:509
  19.7 2.1 collective-permute-done.7.f2_ref
  21.8 2.5 collective-permute-start.9
  26.8 4.6 %shard_map.357 = (f32[1536,128]{1,0:T(8,128)S(1)}, bf16[256,768]{1,0:T(8,128)(2,1)S(1)}, f32[256,128]{1,0:T(8,128)S(1)}, f32[256,768]{1,0:T(8,128)S(1)}, f32[256,128]{1,0:T(8,128)S(1)}) custom-call(f32[1536,128]{1,0:T(8,128)S(1)} %get-tuple-element.336.normed_ref, f32[256,768]{1,0:T(8,128)S(1)} %get-tuple-element.337.init_ref, ...), custom_call_target="tpu_custom_call" | custom-call | flops 327155712 | bytes 5838336 | tf_op jit(solution)/shard_map/pallas_call | solution.py:72
  32.3 2.0 collective-permute-done.8
  35.5 4.1 %collective-permute-done.10 = bf16[384,384]{1,0:T(8,128)(2,1)S(1)} collective-permute-done((bf16[384,384]{1,0:T(8,128)(2,1)S(1)}, bf16[384,384]{1,0:T(8,128)(2,1)S(1)}, u32[]{:S(2)}, u32[]{:S(2)}) %collective-permute-start.10) | collective-permute-done | bytes 294944 | tf_op jit(solution)/shard_map/ppermute | solution.py:509
  41.5 1.7 collective-permute-start.11
  43.7 7.4 %collective-permute-done.12 = bf16[384,384]{1,0:T(8,128)(2,1)S(1)} collective-permute-done((bf16[384,384]{1,0:T(8,128)(2,1)S(1)}, bf16[384,384]{1,0:T(8,128)(2,1)S(1)}, u32[]{:S(2)}, u32[]{:S(2)}) %collective-permute-start.12) | collective-permute-done | bytes 294944 | tf_op jit(solution)/shard_map/ppermute | solution.py:509
  51.1 4.1 %collective-permute-done.11 = bf16[192,768]{1,0:T(8,128)(2,1)S(1)} collective-permute-done((bf16[192,768]{1,0:T(8,128)(2,1)S(1)}, bf16[192,768]{1,0:T(8,128)(2,1)S(1)}, u32[]{:S(2)}, u32[]{:S(2)}) %collective-permute-start.11) | collective-permute-done | bytes 294944 | tf_op jit(solution)/shard_map/ppermute | solution.py:509
  58.4 1.9 collective-permute-done.14.vb_ref.refs_32_
  62.2 4.0 %collective-permute-done.17 = bf16[384,384]{1,0:T(8,128)(2,1)S(1)} collective-permute-done((bf16[384,384]{1,0:T(8,128)(2,1)S(1)}, bf16[384,384]{1,0:T(8,128)(2,1)S(1)}, u32[]{:S(2)}, u32[]{:S(2)}) %collective-permute-start.17) | collective-permute-done | bytes 294944 | tf_op jit(solution)/shard_map/ppermute | solution.py:509
  66.6 2.2 shard_map.360
  68.8 2.7 %shard_map.361 = (f32[256,768]{1,0:T(8,128)S(1)}, f32[256,768]{1,0:T(8,128)S(1)}, f32[1536,384]{1,0:T(8,128)S(1)}, bf16[1536,384]{1,0:T(8,128)(2,1)S(1)}) custom-call(bf16[256,768]{1,0:T(8,128)(2,1)S(1)} %get-tuple-element.404.second_ref, bf16[256,768]{1,0:T(8,128)(2,1)S(1)} %bitcast.61, bf16[768,384]{1,0:T(8,128)(2,1)S(1)} %copy-done.18, ...), custom_call_target="tpu_custom_call" | custom-call | flops 1811939328 | bytes 8257536 | tf_op jit(solution)/shard_map/pallas_call | solution.py:72
  72.3 2.0 collective-permute-done.20.ob_ref
  74.4 2.7 %shard_map.362 = (f32[256,768]{1,0:T(8,128)S(1)}, f32[256,768]{1,0:T(8,128)S(1)}, f32[1536,384]{1,0:T(8,128)S(1)}, bf16[1536,384]{1,0:T(8,128)(2,1)S(1)}) custom-call(bf16[256,768]{1,0:T(8,128)(2,1)S(1)} %get-tuple-element.404.second_ref, bf16[256,768]{1,0:T(8,128)(2,1)S(1)} %bitcast.62, bf16[768,384]{1,0:T(8,128)(2,1)S(1)} %maximum_select_fusion.4.ia_ref, ...), custom_call_target="tpu_custom_call" | custom-call | flops 1811939328 | bytes 8257536 | tf_op jit(solution)/shard_map/pallas_call | solution.py:72
  87.2 14.7 %shard_map.363 = (bf16[256,768]{1,0:T(8,128)(2,1)}, f32[256,768]{1,0:T(8,128)S(1)}, f32[1,768]{1,0:T(1,128)S(1)}, f32[2,768,384]{2,1,0:T(8,128)S(1)}, bf16[2,768...) custom-call(s32[4]{0:T(128)S(1)} %xor_multiply_fusion.offs_ref.refs_, ...), custom_call_target="tpu_custom_call" | custom-call | flops 5435817984 | bytes 43757072 | tf_op jit(solution)/shard_map/pallas_call | solution.py:72
  110.1 2.2 collective-permute-start.33
  115.2 3.2 %collective-permute-done.31 = bf16[384,384]{1,0:T(8,128)(2,1)S(1)} collective-permute-done((bf16[384,384]{1,0:T(8,128)(2,1)S(1)}, bf16[384,384]{1,0:T(8,128)(2,1)S(1)}, u32[]{:S(2)}, u32[]{:S(2)}) %collective-permute-start.31) | collective-permute-done | bytes 294944 | tf_op jit(solution)/shard_map/ppermute | solution.py:509
  118.5 8.4 %shard_map.364 = (bf16[256,768]{1,0:T(8,128)(2,1)}, f32[40,768]{1,0:T(8,128)S(1)}) custom-call(f32[1536,128]{1,0:T(8,128)S(1)} %get-tuple-element.450.pg_ref, f32[1536,128]{1,0:T(8,128)S(1)} %get-tuple-element.336.normed_ref, f32[256,768]{1,0:T(8,128)S(1)} %get-tuple-element.451.im_ref, f32[256,768]{1,0:T(8,128)S(1)} %get-tuple-element.452.iv_ref, ...), custom_call_target="tpu_custom_call" | custom-call | flops 50331648 | bytes 6363136 | tf_op jit(solution)/shard_map/pallas_call | solution.py:72
  129.5 2.0 collective-permute-start.37
  131.5 11.6 %collective-permute-done.32 = bf16[768,384]{1,0:T(8,128)(2,1)S(1)} collective-permute-done((bf16[768,384]{1,0:T(8,128)(2,1)S(1)}, bf16[768,384]{1,0:T(8,128)(2,1)S(1)}, u32[]{:S(2)}, u32[]{:S(2)}) %collective-permute-start.32) | collective-permute-done | bytes 589856 | tf_op jit(solution)/shard_map/ppermute | solution.py:509
  144.4 1.9 collective-permute-start.39
  146.5 3.0 %collective-permute-done.36 = bf16[192,384]{1,0:T(8,128)(2,1)S(1)} collective-permute-done((bf16[192,384]{1,0:T(8,128)(2,1)S(1)}, bf16[192,384]{1,0:T(8,128)(2,1)S(1)}, u32[]{:S(2)}, u32[]{:S(2)}) %collective-permute-start.36) | collective-permute-done | bytes 147488 | tf_op jit(solution)/shard_map/ppermute | solution.py:509
  150.3 2.6 %collective-permute-start.38 = (bf16[192,384]{1,0:T(8,128)(2,1)S(1)}, bf16[192,384]{1,0:T(8,128)(2,1)S(1)}, u32[]{:S(2)}, u32[]{:S(2)}) collective-permute-start(bf16[192,384]{1,0:T(8,128)(2,1)S(1)} %fusion.47), channel_id=1, source_target_pairs={{0,16},{4,20},{8,24},{12,28},{16,0},{20,4},{24,8},{28,12},{1,17},{... | collective-permute-start | bytes 442376 | tf_op jit(solution)/shard_map/ppermute | solution.py:509
  154.3 3.8 %collective-permute-done.40 = bf16[192,384]{1,0:T(8,128)(2,1)S(1)} collective-permute-done((bf16[192,384]{1,0:T(8,128)(2,1)S(1)}, bf16[192,384]{1,0:T(8,128)(2,1)S(1)}, u32[]{:S(2)}, u32[]{:S(2)}) %collective-permute-start.40) | collective-permute-done | bytes 147488 | tf_op jit(solution)/shard_map/ppermute | solution.py:509
  161.5 2.6 %collective-permute-start.46 = (bf16[192,384]{1,0:T(8,128)(2,1)S(1)}, bf16[192,384]{1,0:T(8,128)(2,1)S(1)}, u32[]{:S(2)}, u32[]{:S(2)}) collective-permute-start(bf16[192,384]{1,0:T(8,128)(2,1)S(1)} %fusion.48), channel_id=1, source_target_pairs={{0,16},{4,20},{8,24},{12,28},{16,0},{20,4},{24,8},{28,12},{1,17},{... | collective-permute-start | bytes 442376 | tf_op jit(solution)/shard_map/ppermute | solution.py:509
  164.1 1.9 collective-permute-start.49
  168.7 2.7 %collective-permute-done.43 = bf16[192,384]{1,0:T(8,128)(2,1)S(1)} collective-permute-done((bf16[192,384]{1,0:T(8,128)(2,1)S(1)}, bf16[192,384]{1,0:T(8,128)(2,1)S(1)}, u32[]{:S(2)}, u32[]{:S(2)}) %collective-permute-start.43) | collective-permute-done | bytes 147488 | tf_op jit(solution)/shard_map/ppermute | solution.py:509
  171.8 1.6 collective-permute-start.50
  175.0 2.4 collective-permute-start.48
  178.8 2.6 %collective-permute-done.52 = bf16[192,384]{1,0:T(8,128)(2,1)S(1)} collective-permute-done((bf16[192,384]{1,0:T(8,128)(2,1)S(1)}, bf16[192,384]{1,0:T(8,128)(2,1)S(1)}, u32[]{:S(2)}, u32[]{:S(2)}) %collective-permute-start.52) | collective-permute-done | bytes 147488 | tf_op jit(solution)/shard_map/ppermute | solution.py:509
  182.1 2.7 %collective-permute-start.57 = (bf16[192,384]{1,0:T(8,128)(2,1)S(1)}, bf16[192,384]{1,0:T(8,128)(2,1)S(1)}, u32[]{:S(2)}, u32[]{:S(2)}) collective-permute-start(bf16[192,384]{1,0:T(8,128)(2,1)S(1)} %fusion.50), channel_id=1, source_target_pairs={{0,16},{4,20},{8,24},{12,28},{16,0},{20,4},{24,8},{28,12},{1,17},{... | collective-permute-start | bytes 442376 | tf_op jit(solution)/shard_map/ppermute | solution.py:509
  184.8 3.6 %collective-permute-done.51 = bf16[192,384]{1,0:T(8,128)(2,1)S(1)} collective-permute-done((bf16[192,384]{1,0:T(8,128)(2,1)S(1)}, bf16[192,384]{1,0:T(8,128)(2,1)S(1)}, u32[]{:S(2)}, u32[]{:S(2)}) %collective-permute-start.51) | collective-permute-done | bytes 147488 | tf_op jit(solution)/shard_map/ppermute | solution.py:509
  188.6 7.5 %collective-permute-done.57 = bf16[192,384]{1,0:T(8,128)(2,1)S(1)} collective-permute-done((bf16[192,384]{1,0:T(8,128)(2,1)S(1)}, bf16[192,384]{1,0:T(8,128)(2,1)S(1)}, u32[]{:S(2)}, u32[]{:S(2)}) %collective-permute-start.57) | collective-permute-done | bytes 147488 | tf_op jit(solution)/shard_map/ppermute | solution.py:509
  196.2 2.7 %collective-permute-start.68 = (bf16[192,384]{1,0:T(8,128)(2,1)S(1)}, bf16[192,384]{1,0:T(8,128)(2,1)S(1)}, u32[]{:S(2)}, u32[]{:S(2)}) collective-permute-start(bf16[192,384]{1,0:T(8,128)(2,1)S(1)} %fusion.52), channel_id=1, source_target_pairs={{0,16},{4,20},{8,24},{12,28},{16,0},{20,4},{24,8},{28,12},{1,17},{... | collective-permute-start | bytes 442376 | tf_op jit(solution)/shard_map/ppermute | solution.py:509
  199.3 2.1 collective-permute-start.56
  207.5 2.6 collective-permute-start.70
  214.3 2.5 collective-permute-start.62
  218.0 4.8 %collective-permute-done.69 = bf16[384,384]{1,0:T(8,128)(2,1)S(1)} collective-permute-done((bf16[384,384]{1,0:T(8,128)(2,1)S(1)}, bf16[384,384]{1,0:T(8,128)(2,1)S(1)}, u32[]{:S(2)}, u32[]{:S(2)}) %collective-permute-start.69) | collective-permute-done | bytes 294944 | tf_op jit(solution)/shard_map/ppermute | solution.py:509
  222.7 3.3 %collective-permute-start.58 = (bf16[1248,128]{1,0:T(8,128)(2,1)S(1)}, bf16[1248,128]{1,0:T(8,128)(2,1)S(1)}, u32[]{:S(2)}, u32[]{:S(2)}) collective-permute-start(bf16[1248,128]{1,0:T(8,128)(2,1)S(1)} %pad_maximum_fusion.8), channel_id=1, source_target_pairs={{0,8},{4,12},{8,0},{12,4},{16,24},{20,28},{24,16},{28,20},{1,9},{5... | collective-permute-start | bytes 958472 | tf_op jit(solution)/shard_map/ppermute | solution.py:509
  226.0 3.0 %collective-permute-done.65 = bf16[384,384]{1,0:T(8,128)(2,1)S(1)} collective-permute-done((bf16[384,384]{1,0:T(8,128)(2,1)S(1)}, bf16[384,384]{1,0:T(8,128)(2,1)S(1)}, u32[]{:S(2)}, u32[]{:S(2)}) %collective-permute-start.65) | collective-permute-done | bytes 294944 | tf_op jit(solution)/shard_map/ppermute | solution.py:509
  229.4 4.5 %collective-permute-done.64 = bf16[384,384]{1,0:T(8,128)(2,1)S(1)} collective-permute-done((bf16[384,384]{1,0:T(8,128)(2,1)S(1)}, bf16[384,384]{1,0:T(8,128)(2,1)S(1)}, u32[]{:S(2)}, u32[]{:S(2)}) %collective-permute-start.64) | collective-permute-done | bytes 294944 | tf_op jit(solution)/shard_map/ppermute | solution.py:509
  242.7 9.4 %collective-permute-done.59 = bf16[1248,128]{1,0:T(8,128)(2,1)S(1)} collective-permute-done((bf16[1248,128]{1,0:T(8,128)(2,1)S(1)}, bf16[1248,128]{1,0:T(8,128)(2,1)S(1)}, u32[]{:S(2)}, u32[]{:S(2)}) %collective-permute-start.59) | collective-permute-done | bytes 319520 | tf_op jit(solution)/shard_map/ppermute | solution.py:509
  (338 shorter events, 79.2 us)
Async XLA Ops:
  3.0 12.9 %collective-permute-start.6 = (bf16[384,384]{1,0:T(8,128)(2,1)S(1)}, bf16[384,384]{1,0:T(8,128)(2,1)S(1)}, u32[]{:S(2)}, u32[]{:S(2)}) collective-permute-start(bf16[384,384]{1,0:T(8,128)(2,1)S(1)} %slice_select_fusion.3), channel_id=1, source_target_pairs={{0,2},{1,3},{2,0},{3,1},{4,6},{5,7},{6,4},{7,5},{8,10},{9,11},{10,... | collective-permute-start | bytes 884744 | tf_op jit(solution)/shard_map/ppermute | solution.py:509
  6.8 12.9 %collective-permute-start.5 = (bf16[384,384]{1,0:T(8,128)(2,1)S(1)}, bf16[384,384]{1,0:T(8,128)(2,1)S(1)}, u32[]{:S(2)}, u32[]{:S(2)}) collective-permute-start(bf16[384,384]{1,0:T(8,128)(2,1)S(1)} %slice_select_fusion.4), channel_id=1, source_target_pairs={{0,2},{1,3},{2,0},{3,1},{4,6},{5,7},{6,4},{7,5},{8,10},{9,11},{10,... | collective-permute-start | bytes 884744 | tf_op jit(solution)/shard_map/ppermute | solution.py:509
  11.6 8.1 %collective-permute-start.4 = (f32[32,768]{1,0:T(8,128)S(1)}, f32[32,768]{1,0:T(8,128)S(1)}, u32[]{:S(2)}, u32[]{:S(2)}) collective-permute-start(f32[32,768]{1,0:T(8,128)S(1)} %get-tuple-element.340), channel_id=1, source_target_pairs={{0,1},{1,2},{2,3},{4,5},{5,6},{6,7},{8,9},{9,10},{10,11},{12,13},{... | collective-permute-start | bytes 294920 | tf_op jit(solution)/shard_map/ppermute | solution.py:514
  13.4 8.4 %collective-permute-start.7 = (f32[32,768]{1,0:T(8,128)S(1)}, f32[32,768]{1,0:T(8,128)S(1)}, u32[]{:S(2)}, u32[]{:S(2)}) collective-permute-start(f32[32,768]{1,0:T(8,128)S(1)} %get-tuple-element.340), channel_id=1, source_target_pairs={{0,2},{1,3},{4,6},{5,7},{8,10},{9,11},{12,14},{13,15},{16,18},{17,... | collective-permute-start | bytes 294920 | tf_op jit(solution)/shard_map/ppermute | solution.py:514
  21.8 17.7 %collective-permute-start.9 = (bf16[288,768]{1,0:T(8,128)(2,1)S(1)}, bf16[288,768]{1,0:T(8,128)(2,1)S(1)}, u32[]{:S(2)}, u32[]{:S(2)}) collective-permute-start(bf16[288,768]{1,0:T(8,128)(2,1)S(1)} %slice_select_fusion), channel_id=1, source_target_pairs={{0,2},{1,3},{2,0},{3,1},{4,6},{5,7},{6,4},{7,5},{8,10},{9,11},{10,... | collective-permute-start | bytes 1327112 | tf_op jit(solution)/shard_map/ppermute | solution.py:509
  24.4 9.9 %collective-permute-start.8 = (bf16[384,384]{1,0:T(8,128)(2,1)S(1)}, bf16[384,384]{1,0:T(8,128)(2,1)S(1)}, u32[]{:S(2)}, u32[]{:S(2)}) collective-permute-start(bf16[384,384]{1,0:T(8,128)(2,1)S(1)} %collective-permute-done.6), channel_id=1, source_target_pairs={{0,4},{4,0},{8,12},{12,8},{16,20},{20,16},{24,28},{28,24},{1,5},{5... | collective-permute-start | bytes 884744 | tf_op jit(solution)/shard_map/ppermute | solution.py:509
  26.1 13.4 %collective-permute-start.10 = (bf16[384,384]{1,0:T(8,128)(2,1)S(1)}, bf16[384,384]{1,0:T(8,128)(2,1)S(1)}, u32[]{:S(2)}, u32[]{:S(2)}) collective-permute-start(bf16[384,384]{1,0:T(8,128)(2,1)S(1)} %collective-permute-done.5), channel_id=1, source_target_pairs={{0,4},{4,0},{8,12},{12,8},{16,20},{20,16},{24,28},{28,24},{1,5},{5... | collective-permute-start | bytes 884744 | tf_op jit(solution)/shard_map/ppermute | solution.py:509
  39.5 15.6 %collective-permute-start.15 = (bf16[288,768]{1,0:T(8,128)(2,1)S(1)}, bf16[288,768]{1,0:T(8,128)(2,1)S(1)}, u32[]{:S(2)}, u32[]{:S(2)}) collective-permute-start(bf16[288,768]{1,0:T(8,128)(2,1)S(1)} %collective-permute-done.9), channel_id=1, source_target_pairs={{0,8},{4,12},{8,0},{12,4},{16,24},{20,28},{24,16},{28,20},{1,9},{5... | collective-permute-start | bytes 1327112 | tf_op jit(solution)/shard_map/ppermute | solution.py:509
  41.1 9.9 %collective-permute-start.12 = (bf16[384,384]{1,0:T(8,128)(2,1)S(1)}, bf16[384,384]{1,0:T(8,128)(2,1)S(1)}, u32[]{:S(2)}, u32[]{:S(2)}) collective-permute-start(bf16[384,384]{1,0:T(8,128)(2,1)S(1)} %slice_select_fusion.2), channel_id=1, source_target_pairs={{0,2},{1,3},{2,0},{3,1},{4,6},{5,7},{6,4},{7,5},{8,10},{9,11},{10,... | collective-permute-start | bytes 884744 | tf_op jit(solution)/shard_map/ppermute | solution.py:509
  41.5 13.6 %collective-permute-start.11 = (bf16[192,768]{1,0:T(8,128)(2,1)S(1)}, bf16[192,768]{1,0:T(8,128)(2,1)S(1)}, u32[]{:S(2)}, u32[]{:S(2)}) collective-permute-start(bf16[192,768]{1,0:T(8,128)(2,1)S(1)} %slice_select_fusion.1), channel_id=1, source_target_pairs={{0,2},{1,3},{2,0},{3,1},{4,6},{5,7},{6,4},{7,5},{8,10},{9,11},{10,... | collective-permute-start | bytes 884744 | tf_op jit(solution)/shard_map/ppermute | solution.py:509
  55.7 10.8 %collective-permute-start.16 = (bf16[2,576,768]{2,1,0:T(8,128)(2,1)S(1)}, bf16[2,576,768]{2,1,0:T(8,128)(2,1)S(1)}, u32[]{:S(2)}, u32[]{:S(2)}) collective-permute-start(bf16[2,576,768]{2,1,0:T(8,128)(2,1)S(1)} %pad_maximum_fusion.ga_ref.refs_24_), channel_id=1, source_target_pairs={{0,1},{1,0},{2,3},{3,2},{4,5},{5,4},{6,7},{7,6},{8,9},{9,8},{10,11... | collective-permute-start | bytes 5308424 | tf_op jit(solution)/shard_map/ppermute | solution.py:509
  56.3 9.9 %collective-permute-start.17 = (bf16[384,384]{1,0:T(8,128)(2,1)S(1)}, bf16[384,384]{1,0:T(8,128)(2,1)S(1)}, u32[]{:S(2)}, u32[]{:S(2)}) collective-permute-start(bf16[384,384]{1,0:T(8,128)(2,1)S(1)} %collective-permute-done.12), channel_id=1, source_target_pairs={{0,4},{4,0},{8,12},{12,8},{16,20},{20,16},{24,28},{28,24},{1,5},{5... | collective-permute-start | bytes 884744 | tf_op jit(solution)/shard_map/ppermute | solution.py:509
  57.8 14.2 %collective-permute-start.19 = (bf16[192,768]{1,0:T(8,128)(2,1)S(1)}, bf16[192,768]{1,0:T(8,128)(2,1)S(1)}, u32[]{:S(2)}, u32[]{:S(2)}) collective-permute-start(bf16[192,768]{1,0:T(8,128)(2,1)S(1)} %collective-permute-done.11), channel_id=1, source_target_pairs={{0,4},{4,0},{8,12},{12,8},{16,20},{20,16},{24,28},{28,24},{1,5},{5... | collective-permute-start | bytes 884744 | tf_op jit(solution)/shard_map/ppermute | solution.py:509
  81.6 20.3 %collective-permute-start.24 = (bf16[768,384]{1,0:T(8,128)(2,1)S(1)}, bf16[768,384]{1,0:T(8,128)(2,1)S(1)}, u32[]{:S(2)}, u32[]{:S(2)}) collective-permute-start(bf16[768,384]{1,0:T(8,128)(2,1)S(1)} %pad_maximum_fusion.1), channel_id=1, source_target_pairs={{0,4},{4,0},{8,12},{12,8},{16,20},{20,16},{24,28},{28,24},{1,5},{5... | collective-permute-start | bytes 1769480 | tf_op jit(solution)/shard_map/ppermute | solution.py:509
  83.2 18.7 %collective-permute-start.23 = (bf16[768,384]{1,0:T(8,128)(2,1)}, bf16[768,384]{1,0:T(8,128)(2,1)S(1)}, u32[]{:S(2)}, u32[]{:S(2)}) collective-permute-start(bf16[768,384]{1,0:T(8,128)(2,1)} %get-tuple-element.459), channel_id=1, source_target_pairs={{0,2},{1,3},{2,0},{3,1},{4,6},{5,7},{6,4},{7,5},{8,10},{9,11},{10,... | collective-permute-start | bytes 1769480 | tf_op jit(solution)/shard_map/ppermute | solution.py:509
  102.6 11.0 %collective-permute-start.25 = (f32[64,768]{1,0:T(8,128)S(1)}, f32[64,768]{1,0:T(8,128)S(1)}, u32[]{:S(2)}, u32[]{:S(2)}) collective-permute-start(f32[64,768]{1,0:T(8,128)S(1)} %pad_maximum_fusion.11), channel_id=1, source_target_pairs={{1,0},{2,1},{3,2},{5,4},{6,5},{7,6},{9,8},{10,9},{11,10},{13,12},{... | collective-permute-start | bytes 589832 | tf_op jit(solution)/shard_map/ppermute | solution.py:514
  104.0 11.2 %collective-permute-start.30 = (f32[64,768]{1,0:T(8,128)S(1)}, f32[64,768]{1,0:T(8,128)S(1)}, u32[]{:S(2)}, u32[]{:S(2)}) collective-permute-start(f32[64,768]{1,0:T(8,128)S(1)} %pad_maximum_fusion.11), channel_id=1, source_target_pairs={{2,0},{3,1},{6,4},{7,5},{10,8},{11,9},{14,12},{15,13},{18,16},{19,... | collective-permute-start | bytes 589832 | tf_op jit(solution)/shard_map/ppermute | solution.py:514
  109.1 9.4 %collective-permute-start.31 = (bf16[384,384]{1,0:T(8,128)(2,1)S(1)}, bf16[384,384]{1,0:T(8,128)(2,1)S(1)}, u32[]{:S(2)}, u32[]{:S(2)}) collective-permute-start(bf16[384,384]{1,0:T(8,128)(2,1)S(1)} %select_convert_fusion.5), channel_id=1, source_target_pairs={{0,4},{4,0},{8,12},{12,8},{16,20},{20,16},{24,28},{28,24},{1,5},{5... | collective-permute-start | bytes 884744 | tf_op jit(solution)/shard_map/ppermute | solution.py:509
  110.1 16.9 %collective-permute-start.33 = (bf16[384,384]{1,0:T(8,128)(2,1)S(1)}, bf16[384,384]{1,0:T(8,128)(2,1)S(1)}, u32[]{:S(2)}, u32[]{:S(2)}) collective-permute-start(bf16[384,384]{1,0:T(8,128)(2,1)S(1)} %fusion.12), channel_id=1, source_target_pairs={{0,2},{1,3},{2,0},{3,1},{4,6},{5,7},{6,4},{7,5},{8,10},{9,11},{10,... | collective-permute-start | bytes 884744 | tf_op jit(solution)/shard_map/ppermute | solution.py:509
  128.3 14.8 %collective-permute-start.32 = (bf16[768,384]{1,0:T(8,128)(2,1)S(1)}, bf16[768,384]{1,0:T(8,128)(2,1)S(1)}, u32[]{:S(2)}, u32[]{:S(2)}) collective-permute-start(bf16[768,384]{1,0:T(8,128)(2,1)S(1)} %pad_maximum_fusion.2), channel_id=1, source_target_pairs={{0,4},{4,0},{8,12},{12,8},{16,20},{20,16},{24,28},{28,24},{1,5},{5... | collective-permute-start | bytes 1769480 | tf_op jit(solution)/shard_map/ppermute | solution.py:509
  128.9 15.0 %collective-permute-start.35 = (bf16[768,384]{1,0:T(8,128)(2,1)S(1)}, bf16[768,384]{1,0:T(8,128)(2,1)S(1)}, u32[]{:S(2)}, u32[]{:S(2)}) collective-permute-start(bf16[768,384]{1,0:T(8,128)(2,1)S(1)} %pad_maximum_fusion.3), channel_id=1, source_target_pairs={{0,8},{4,12},{8,0},{12,4},{16,24},{20,28},{24,16},{28,20},{1,9},{5... | collective-permute-start | bytes 1769480 | tf_op jit(solution)/shard_map/ppermute | solution.py:509
  129.5 16.9 %collective-permute-start.37 = (bf16[768,384]{1,0:T(8,128)(2,1)S(1)}, bf16[768,384]{1,0:T(8,128)(2,1)S(1)}, u32[]{:S(2)}, u32[]{:S(2)}) collective-permute-start(bf16[768,384]{1,0:T(8,128)(2,1)S(1)} %fusion.4), channel_id=1, source_target_pairs={{0,2},{1,3},{2,0},{3,1},{4,6},{5,7},{6,4},{7,5},{8,10},{9,11},{10,... | collective-permute-start | bytes 1769480 | tf_op jit(solution)/shard_map/ppermute | solution.py:509
  143.7 15.5 %collective-permute-start.41 = (bf16[768,384]{1,0:T(8,128)(2,1)S(1)}, bf16[768,384]{1,0:T(8,128)(2,1)S(1)}, u32[]{:S(2)}, u32[]{:S(2)}) collective-permute-start(bf16[768,384]{1,0:T(8,128)(2,1)S(1)} %pad_maximum_fusion.4), channel_id=1, source_target_pairs={{0,4},{4,0},{8,12},{12,8},{16,20},{20,16},{24,28},{28,24},{1,5},{5... | collective-permute-start | bytes 1769480 | tf_op jit(solution)/shard_map/ppermute | solution.py:509
  144.4 13.8 %collective-permute-start.39 = (bf16[384,384]{1,0:T(8,128)(2,1)S(1)}, bf16[384,384]{1,0:T(8,128)(2,1)S(1)}, u32[]{:S(2)}, u32[]{:S(2)}) collective-permute-start(bf16[384,384]{1,0:T(8,128)(2,1)S(1)} %get-tuple-element.533), channel_id=1, source_target_pairs={{0,2},{1,3},{2,0},{3,1},{4,6},{5,7},{6,4},{7,5},{8,10},{9,11},{10,... | collective-permute-start | bytes 884744 | tf_op jit(solution)/shard_map/ppermute | solution.py:509
  149.5 8.6 %collective-permute-start.40 = (bf16[192,384]{1,0:T(8,128)(2,1)S(1)}, bf16[192,384]{1,0:T(8,128)(2,1)S(1)}, u32[]{:S(2)}, u32[]{:S(2)}) collective-permute-start(bf16[192,384]{1,0:T(8,128)(2,1)S(1)} %select_convert_fusion.14), channel_id=1, source_target_pairs={{0,8},{4,12},{8,0},{12,4},{16,24},{20,28},{24,16},{28,20},{1,9},{5... | collective-permute-start | bytes 442376 | tf_op jit(solution)/shard_map/ppermute | solution.py:509
  150.3 9.3 %collective-permute-start.38 = (bf16[192,384]{1,0:T(8,128)(2,1)S(1)}, bf16[192,384]{1,0:T(8,128)(2,1)S(1)}, u32[]{:S(2)}, u32[]{:S(2)}) collective-permute-start(bf16[192,384]{1,0:T(8,128)(2,1)S(1)} %fusion.47), channel_id=1, source_target_pairs={{0,16},{4,20},{8,24},{12,28},{16,0},{20,4},{24,8},{28,12},{1,17},{... | collective-permute-start | bytes 442376 | tf_op jit(solution)/shard_map/ppermute | solution.py:509
  152.9 13.1 %collective-permute-start.42 = (bf16[384,384]{1,0:T(8,128)(2,1)S(1)}, bf16[384,384]{1,0:T(8,128)(2,1)S(1)}, u32[]{:S(2)}, u32[]{:S(2)}) collective-permute-start(bf16[384,384]{1,0:T(8,128)(2,1)S(1)} %get-tuple-element.549), channel_id=1, source_target_pairs={{0,2},{1,3},{2,0},{3,1},{4,6},{5,7},{6,4},{7,5},{8,10},{9,11},{10,... | collective-permute-start | bytes 884744 | tf_op jit(solution)/shard_map/ppermute | solution.py:509
  159.5 8.3 %collective-permute-start.45 = (bf16[384,384]{1,0:T(8,128)(2,1)S(1)}, bf16[384,384]{1,0:T(8,128)(2,1)S(1)}, u32[]{:S(2)}, u32[]{:S(2)}) collective-permute-start(bf16[384,384]{1,0:T(8,128)(2,1)S(1)} %select_convert_fusion), channel_id=1, source_target_pairs={{0,4},{4,0},{8,12},{12,8},{16,20},{20,16},{24,28},{28,24},{1,5},{5... | collective-permute-start | bytes 884744 | tf_op jit(solution)/shard_map/ppermute | solution.py:509
  159.9 8.1 %collective-permute-start.44 = (bf16[192,384]{1,0:T(8,128)(2,1)S(1)}, bf16[192,384]{1,0:T(8,128)(2,1)S(1)}, u32[]{:S(2)}, u32[]{:S(2)}) collective-permute-start(bf16[192,384]{1,0:T(8,128)(2,1)S(1)} %select_convert_fusion.13), channel_id=1, source_target_pairs={{0,8},{4,12},{8,0},{12,4},{16,24},{20,28},{24,16},{28,20},{1,9},{5... | collective-permute-start | bytes 442376 | tf_op jit(solution)/shard_map/ppermute | solution.py:509
  175.0 21.1 %collective-permute-start.48 = (bf16[192,384]{1,0:T(8,128)(2,1)S(1)}, bf16[192,384]{1,0:T(8,128)(2,1)S(1)}, u32[]{:S(2)}, u32[]{:S(2)}) collective-permute-start(bf16[192,384]{1,0:T(8,128)(2,1)S(1)} %fusion.49), channel_id=1, source_target_pairs={{0,16},{4,20},{8,24},{12,28},{16,0},{20,4},{24,8},{28,12},{1,17},{... | collective-permute-start | bytes 442376 | tf_op jit(solution)/shard_map/ppermute | solution.py:509
  177.4 21.9 %collective-permute-start.47 = (bf16[1248,128]{1,0:T(8,128)(2,1)S(1)}, bf16[1248,128]{1,0:T(8,128)(2,1)S(1)}, u32[]{:S(2)}, u32[]{:S(2)}) collective-permute-start(bf16[1248,128]{1,0:T(8,128)(2,1)S(1)} %pad_maximum_fusion.6), channel_id=1, source_target_pairs={{0,2},{1,3},{2,0},{3,1},{4,6},{5,7},{6,4},{7,5},{8,10},{9,11},{10,... | collective-permute-start | bytes 958472 | tf_op jit(solution)/shard_map/ppermute | solution.py:509
  181.7 24.3 %collective-permute-start.55 = (bf16[384,384]{1,0:T(8,128)(2,1)S(1)}, bf16[384,384]{1,0:T(8,128)(2,1)S(1)}, u32[]{:S(2)}, u32[]{:S(2)}) collective-permute-start(bf16[384,384]{1,0:T(8,128)(2,1)S(1)} %maximum_select_fusion.13), channel_id=1, source_target_pairs={{0,4},{4,0},{8,12},{12,8},{16,20},{20,16},{24,28},{28,24},{1,5},{5... | collective-permute-start | bytes 884744 | tf_op jit(solution)/shard_map/ppermute | solution.py:509
  182.1 14.0 %collective-permute-start.57 = (bf16[192,384]{1,0:T(8,128)(2,1)S(1)}, bf16[192,384]{1,0:T(8,128)(2,1)S(1)}, u32[]{:S(2)}, u32[]{:S(2)}) collective-permute-start(bf16[192,384]{1,0:T(8,128)(2,1)S(1)} %fusion.50), channel_id=1, source_target_pairs={{0,16},{4,20},{8,24},{12,28},{16,0},{20,4},{24,8},{28,12},{1,17},{... | collective-permute-start | bytes 442376 | tf_op jit(solution)/shard_map/ppermute | solution.py:509
  188.4 10.8 %collective-permute-start.60 = (bf16[192,384]{1,0:T(8,128)(2,1)S(1)}, bf16[192,384]{1,0:T(8,128)(2,1)S(1)}, u32[]{:S(2)}, u32[]{:S(2)}) collective-permute-start(bf16[192,384]{1,0:T(8,128)(2,1)S(1)} %fusion.51), channel_id=1, source_target_pairs={{0,16},{4,20},{8,24},{12,28},{16,0},{20,4},{24,8},{28,12},{1,17},{... | collective-permute-start | bytes 442376 | tf_op jit(solution)/shard_map/ppermute | solution.py:509
  196.1 8.3 %collective-permute-start.54 = (bf16[192,384]{1,0:T(8,128)(2,1)S(1)}, bf16[192,384]{1,0:T(8,128)(2,1)S(1)}, u32[]{:S(2)}, u32[]{:S(2)}) collective-permute-start(bf16[192,384]{1,0:T(8,128)(2,1)S(1)} %add_convert_fusion.5), channel_id=1, source_target_pairs={{0,8},{4,12},{8,0},{12,4},{16,24},{20,28},{24,16},{28,20},{1,9},{5... | collective-permute-start | bytes 442376 | tf_op jit(solution)/shard_map/ppermute | solution.py:509
  199.2 8.3 %collective-permute-start.63 = (bf16[192,384]{1,0:T(8,128)(2,1)S(1)}, bf16[192,384]{1,0:T(8,128)(2,1)S(1)}, u32[]{:S(2)}, u32[]{:S(2)}) collective-permute-start(bf16[192,384]{1,0:T(8,128)(2,1)S(1)} %add_convert_fusion.3), channel_id=1, source_target_pairs={{0,8},{4,12},{8,0},{12,4},{16,24},{20,28},{24,16},{28,20},{1,9},{5... | collective-permute-start | bytes 442376 | tf_op jit(solution)/shard_map/ppermute | solution.py:509
  199.3 10.9 %collective-permute-start.56 = (bf16[192,384]{1,0:T(8,128)(2,1)S(1)}, bf16[192,384]{1,0:T(8,128)(2,1)S(1)}, u32[]{:S(2)}, u32[]{:S(2)}) collective-permute-start(bf16[192,384]{1,0:T(8,128)(2,1)S(1)} %add_convert_fusion.4), channel_id=1, source_target_pairs={{0,8},{4,12},{8,0},{12,4},{16,24},{20,28},{24,16},{28,20},{1,9},{5... | collective-permute-start | bytes 442376 | tf_op jit(solution)/shard_map/ppermute | solution.py:509
  202.8 8.7 %collective-permute-start.61 = (bf16[192,384]{1,0:T(8,128)(2,1)S(1)}, bf16[192,384]{1,0:T(8,128)(2,1)S(1)}, u32[]{:S(2)}, u32[]{:S(2)}) collective-permute-start(bf16[192,384]{1,0:T(8,128)(2,1)S(1)} %add_convert_fusion.2), channel_id=1, source_target_pairs={{0,4},{4,0},{8,12},{12,8},{16,20},{20,16},{24,28},{28,24},{1,5},{5... | collective-permute-start | bytes 442376 | tf_op jit(solution)/shard_map/ppermute | solution.py:509
  204.4 12.5 %collective-permute-start.53 = (bf16[1248,128]{1,0:T(8,128)(2,1)S(1)}, bf16[1248,128]{1,0:T(8,128)(2,1)S(1)}, u32[]{:S(2)}, u32[]{:S(2)}) collective-permute-start(bf16[1248,128]{1,0:T(8,128)(2,1)S(1)} %pad_maximum_fusion.7), channel_id=1, source_target_pairs={{0,4},{4,0},{8,12},{12,8},{16,20},{20,16},{24,28},{28,24},{1,5},{5... | collective-permute-start | bytes 958472 | tf_op jit(solution)/shard_map/ppermute | solution.py:509
  206.0 16.7 %collective-permute-start.69 = (bf16[384,384]{1,0:T(8,128)(2,1)S(1)}, bf16[384,384]{1,0:T(8,128)(2,1)S(1)}, u32[]{:S(2)}, u32[]{:S(2)}) collective-permute-start(bf16[384,384]{1,0:T(8,128)(2,1)S(1)} %maximum_select_fusion.18), channel_id=1, source_target_pairs={{0,4},{4,0},{8,12},{12,8},{16,20},{20,16},{24,28},{28,24},{1,5},{5... | collective-permute-start | bytes 884744 | tf_op jit(solution)/shard_map/ppermute | solution.py:509
  210.2 18.8 %collective-permute-start.65 = (bf16[384,384]{1,0:T(8,128)(2,1)S(1)}, bf16[384,384]{1,0:T(8,128)(2,1)S(1)}, u32[]{:S(2)}, u32[]{:S(2)}) collective-permute-start(bf16[384,384]{1,0:T(8,128)(2,1)S(1)} %maximum_select_fusion.16), channel_id=1, source_target_pairs={{0,4},{4,0},{8,12},{12,8},{16,20},{20,16},{24,28},{28,24},{1,5},{5... | collective-permute-start | bytes 884744 | tf_op jit(solution)/shard_map/ppermute | solution.py:509
  211.5 22.4 %collective-permute-start.64 = (bf16[384,384]{1,0:T(8,128)(2,1)S(1)}, bf16[384,384]{1,0:T(8,128)(2,1)S(1)}, u32[]{:S(2)}, u32[]{:S(2)}) collective-permute-start(bf16[384,384]{1,0:T(8,128)(2,1)S(1)} %maximum_select_fusion.15), channel_id=1, source_target_pairs={{0,4},{4,0},{8,12},{12,8},{16,20},{20,16},{24,28},{28,24},{1,5},{5... | collective-permute-start | bytes 884744 | tf_op jit(solution)/shard_map/ppermute | solution.py:509
  214.3 21.0 %collective-permute-start.62 = (bf16[384,384]{1,0:T(8,128)(2,1)S(1)}, bf16[384,384]{1,0:T(8,128)(2,1)S(1)}, u32[]{:S(2)}, u32[]{:S(2)}) collective-permute-start(bf16[384,384]{1,0:T(8,128)(2,1)S(1)} %maximum_select_fusion.14), channel_id=1, source_target_pairs={{0,8},{4,12},{8,0},{12,4},{16,24},{20,28},{24,16},{28,20},{1,9},{5... | collective-permute-start | bytes 884744 | tf_op jit(solution)/shard_map/ppermute | solution.py:509
  216.9 21.5 %collective-permute-start.71 = (bf16[384,384]{1,0:T(8,128)(2,1)S(1)}, bf16[384,384]{1,0:T(8,128)(2,1)S(1)}, u32[]{:S(2)}, u32[]{:S(2)}) collective-permute-start(bf16[384,384]{1,0:T(8,128)(2,1)S(1)} %maximum_select_fusion.17), channel_id=1, source_target_pairs={{0,4},{4,0},{8,12},{12,8},{16,20},{20,16},{24,28},{28,24},{1,5},{5... | collective-permute-start | bytes 884744 | tf_op jit(solution)/shard_map/ppermute | solution.py:509
  222.7 15.9 %collective-permute-start.58 = (bf16[1248,128]{1,0:T(8,128)(2,1)S(1)}, bf16[1248,128]{1,0:T(8,128)(2,1)S(1)}, u32[]{:S(2)}, u32[]{:S(2)}) collective-permute-start(bf16[1248,128]{1,0:T(8,128)(2,1)S(1)} %pad_maximum_fusion.8), channel_id=1, source_target_pairs={{0,8},{4,12},{8,0},{12,4},{16,24},{20,28},{24,16},{28,20},{1,9},{5... | collective-permute-start | bytes 958472 | tf_op jit(solution)/shard_map/ppermute | solution.py:509
  229.4 11.5 %collective-permute-start.66 = (bf16[192,768]{1,0:T(8,128)(2,1)S(1)}, bf16[192,768]{1,0:T(8,128)(2,1)S(1)}, u32[]{:S(2)}, u32[]{:S(2)}) collective-permute-start(bf16[192,768]{1,0:T(8,128)(2,1)S(1)} %pad_maximum_fusion.10), channel_id=1, source_target_pairs={{0,1},{1,0},{2,3},{3,2},{4,5},{5,4},{6,7},{7,6},{8,9},{9,8},{10,11... | collective-permute-start | bytes 884744 | tf_op jit(solution)/shard_map/ppermute | solution.py:509
  238.9 13.2 %collective-permute-start.59 = (bf16[1248,128]{1,0:T(8,128)(2,1)S(1)}, bf16[1248,128]{1,0:T(8,128)(2,1)S(1)}, u32[]{:S(2)}, u32[]{:S(2)}) collective-permute-start(bf16[1248,128]{1,0:T(8,128)(2,1)S(1)} %pad_maximum_fusion.9), channel_id=1, source_target_pairs={{0,16},{4,20},{8,24},{12,28},{16,0},{20,4},{24,8},{28,12},{1,17},{... | collective-permute-start | bytes 958472 | tf_op jit(solution)/shard_map/ppermute | solution.py:509
  241.0 13.9 %collective-permute-start.67 = (bf16[384,768]{1,0:T(8,128)(2,1)S(1)}, bf16[384,768]{1,0:T(8,128)(2,1)S(1)}, u32[]{:S(2)}, u32[]{:S(2)}) collective-permute-start(bf16[384,768]{1,0:T(8,128)(2,1)S(1)} %maximum_select_fusion.9), channel_id=1, source_target_pairs={{0,2},{1,3},{2,0},{3,1},{4,6},{5,7},{6,4},{7,5},{8,10},{9,11},{10,... | collective-permute-start | bytes 1769480 | tf_op jit(solution)/shard_map/ppermute | solution.py:509
  (65 other events, 447.6 us)

commit v4 on v3

--- a/solution.py
+++ b/solution.py
@@ -12,18 +12,17 @@
 CHUNKS = 8
 F32 = jnp.float32
 LOW = jnp.bfloat16
-KINDS = {"I": "x", "U": "y", "P": "y", "R": "x", "O": "x", "N": "z"}
+KINDS = {"I": "y", "U": "x", "Q": "z", "P": "x", "N": "y"}
 ORDER = (
-    "+F0", "+F1", "-F0", "-F1", "+I", "+U", "Kback", "-I", "-U", "+R",
-    "+O", "+E", "+P", "-R", "+U", "-O", "+N", "-P", "+I", "-N",
-    "+R", "-E", "+N", "+P", "-U", "Kt4", "-I", "+O", "+I", "-R",
-    "+sm", "-N", "+R", "-sm", "+U", "-P", "-I", "+I", "+N", "-U",
-    "+P", "-R", "+U", "-O", "+R", "-I", "+O", "-N", "+I", "-P",
-    "+N", "-R", "+P", "-U", "+R", "-I", "+sm", "-O", "-N", "+O",
-    "-P", "+I", "+P", "-O", "+U", "-R", "-sm", "+R", "+sm", "-I",
-    "+O", "-U", "-P", "+P", "-R", "+U", "+N", "-sm", "+sm", "-P",
-    "+R", "-O", "-U", "+O", "+P", "-N", "-sm", "-R", "+sm", "+N",
-    "-O", "+O", "-P", "-N", "+N", "-O", "-sm", "-N",
+    "+F0", "+F1", "-F0", "-F1", "+U", "+I", "Kback", "-U", "-I", "+Q",
+    "+U", "+P", "+I", "+N", "-Q", "+Q", "-P", "+P", "-N", "-U",
+    "+E", "-I", "+N", "-E", "Kt4", "-P", "-N", "-Q", "+P", "+sm",
+    "+U", "-sm", "+Q", "+N", "+I", "-U", "-P", "+U", "+P", "-I",
+    "+sm", "-N", "+I", "-Q", "-P", "-U", "+Q", "+U", "+P", "-sm",
+    "-I", "+sm", "+I", "-U", "-Q", "+N", "+Q", "-P", "-I", "+U",
+    "-sm", "-N", "+sm", "+I", "+P", "-U", "+N", "-Q", "-sm", "+Q",
+    "-I", "-P", "+sm", "+P", "-N", "+N", "-Q", "+Q", "-P", "-N",
+    "+N", "-sm", "-N", "-Q",
 )
 
 
@@ -313,10 +312,10 @@
     cols = ga_ref.shape[1] - units
     half = depth // 2
     for i, (g_ref, v_ref, r_ref, pack) in enumerate(
-        ((ga_ref, va_ref, ra_ref, packs[:3]), (gb_ref, vb_ref, rb_ref, packs[3:]))
+        ((ga_ref, va_ref, ra_ref, packs[:2]), (gb_ref, vb_ref, rb_ref, packs[2:]))
     ):
-        reset_pack, out_pack, value_pack = pack
-        kind = reset_pack.dtype
+        gate_pack, value_pack = pack
+        kind = gate_pack.dtype
         united_grad = dot_cols(hidden, g_ref[part, cols:, :])
         reset_pre, value_pre = rpre_ref[i], vpre_ref[i]
         reset_low = (united_grad * att_ref[i] * silu_slope(reset_pre)).astype(LOW)
@@ -335,9 +334,9 @@
         first = i == 0 and part == 1
         ng_ref[...] = into_normed if first else ng_ref[...] + into_normed
         mg_ref[...] = into_mixed if first else mg_ref[...] + into_mixed
-        reset_pack[part] = dot_rows(mixed, reset_low).astype(kind)
+        gate_pack[part, :depth, :] = dot_rows(mixed, reset_low).astype(kind)
         for h in range(2):
-            out_pack[part, h * units : (h + 1) * units, :] = dot_rows(
+            gate_pack[part, depth + h * units : depth + (h + 1) * units, :] = dot_rows(
                 united_ref[i], hidden[:, h * half : (h + 1) * half]
             ).astype(kind)
         value_pack[part] = dot_rows(normed, value_low).astype(kind)
@@ -414,8 +413,8 @@
     own_part, far_part, (ga_ref, gb_ref), weights = refs[16:20], refs[20:24], refs[24:26], refs[26:34]
     zpre_ref, qg_ref, qb_ref, kg_ref, wz_ref, pre_ref, keep_ref, al_ref, de_ref = refs[34:43]
     y_ref, direct_ref, gg_ref, pair_keep_ref, pair_send_ref, ng_ref = refs[43:49]
-    packs, outs = refs[49:55], refs[55:62]
-    mg_ref, p_ref, qk_ref, m0_ref, full_ref, hidden_ref = refs[62:]
+    packs, outs = refs[49:53], refs[53:60]
+    mg_ref, p_ref, qk_ref, m0_ref, full_ref, hidden_ref = refs[60:]
     blend_back(
         offs_ref, x_ref, cot_ref, blended_ref, s0_ref, s1_ref, o0_ref, o1_ref, hpre_ref, gate_ref,
         mixed_ref, gain_ref, wu_ref, whid_ref, y_ref, direct_ref, hidden_ref, m0_ref, gg_ref,
@@ -776,6 +775,7 @@
     other_i = swap(over_i, "dp", 1)
     over_o = pump.gate(over_o)
     other_o = swap(over_o, "dp", 1)
+    other_v, other_r = pump.gate(other_v), pump.gate(other_r)
     full_v = pump.gate(joined(over_v, other_v, firsts[1]))
     both_v = swap(full_v, "tensor", 1)
     full_r = pump.gate(joined(over_r, other_r, firsts[1]))
@@ -807,7 +807,7 @@
     def ffn_of(weights):
         return call(
             ffn_part,
-            [(wide, F32), (wide, F32), ((ffn_rows, units), F32), ((ffn_rows, units), LOW)],
+            [(wide, F32), (wide, F32), ((ffn_rows, units), LOW), ((ffn_rows, units), LOW)],
             (second, cot, *weights),
             12 * mat * units,
         )
@@ -825,11 +825,10 @@
     held = {}
 
     def run_back():
-        pack = (2, width, units)
         outs = call(
             functools.partial(back_pass, rows),
-            [(wide, LOW), (wide, F32), ((1, width), F32), (own, F32), (own, LOW), (wide, F32),
-             *[(pack, F32)] * 3, *[(pack, LOW)] * 3,
+            [(wide, LOW), (wide, F32), ((1, width), F32), (own, LOW), (own, LOW), (wide, F32),
+             *[((2, 2 * width, units), LOW), ((2, width, units), LOW)] * 2,
              (slabs, F32), ((width, zd), F32), ((8, zd), F32), (chunked, F32), (chunked, F32), (finals, F32), (finals, F32)],
             (offs, x, cot, pump.gate(blended), ffn1[1], back0, ffn0[0], ffn1[0], hidden_pre, gate,
              mixed_low, g2, w_update, whid, normed_low, probs, *kept_parts[0], *kept_parts[1], *wg,
@@ -840,8 +839,8 @@
              pltpu.VMEM(wide, LOW)],
             smem=(0,),
         )
-        held["bb"], held["v"] = outs[:5], outs[5:12]
-        held["t3"] = list(outs[12:])
+        held["bb"], held["v"] = outs[:5], outs[5:10]
+        held["t3"] = list(outs[10:])
         pump.token, held["t3"][5] = tied((pump.token, held["t3"][5]))
 
     def send_back():
@@ -870,13 +869,13 @@
         if name in "IU":
             rows_of = slice(0, width) if name == "I" else slice(width, 2 * width)
             return tuple(
-                keep[rows_of] + pump.done[swapped][rows_of].astype(F32)
+                keep[rows_of].astype(F32) + pump.done[swapped][rows_of].astype(F32)
                 for keep, swapped in ((ffn0[2], "F0"), (ffn1[2], "F1"))
             )
-        kept, sent = held["bb"][3:] if name == "P" else held["v"]["RON".index(name) + 1 : 7 : 3]
+        kept, sent = held["bb"][3:] if name == "P" else held["v"]["QN".index(name) + 1 : 5 : 2]
         got = yield "tensor", 1, sent
-        got = got.astype(F32)
-        return kept[0] + got[0], kept[1] + got[1]
+        both = kept.astype(F32) + got.astype(F32)
+        return both[0], both[1]
 
     def add_flow(name):
         pump.add(name, reduction(KINDS[name], packs_of(name), firsts))
@@ -901,7 +900,7 @@
     output, input_grad = held["bb"][0], held["t4"][0]
     dz_sum, sums = pump.done["sm"]
     sums = from_slabs(sums, 2 * dims + 8)
-    pair_sum, reset_sum, out_sum, value_sum, in_sum, fout_sum = (pump.done[n] for n in "PRONIU")
+    pair_sum, gate_sum, value_sum, in_sum, fout_sum = (pump.done[n] for n in "PQNIU")
 
     alpha, sigma = jax.nn.sigmoid(alpha_raw), jax.nn.sigmoid(delta_raw)
     with_mu, with_nu = sums[:dims], sums[dims : 2 * dims]
@@ -925,10 +924,10 @@
         sums[at + 3, zd : 2 * zd],
         sums[at + 3, 2 * zd : 3 * zd],
         value_sum.astype(F32),
-        reset_sum.astype(F32),
+        gate_sum[:width].astype(F32),
         update_grad.astype(F32),
         side_by_side(pair_sum[2 * cols :]).astype(F32),
-        side_by_side(out_sum).astype(F32),
+        side_by_side(gate_sum[width:]).astype(F32),
         sums[at + 2],
         in_sum.astype(F32),
         side_by_side(fout_sum).astype(F32),

time: 260 us -> 262 us (level)
  waiting for transfers between devices: 103 us -> 126 us
  starting transfers between devices: 79.8 us -> 68.4 us
  local copies, waits for them, and re-layouts: 9.19 us -> 1.86 us
    ppermute x68 -> x61, waiting for transfers between devices: 99.4 us -> 120 us  [swap(): return lax.ppermute(x, axis, [(i, i ^ bit) for i in range(size)])]
    ppermute x68 -> x61, starting transfers between devices: 72.8 us -> 61.6 us  [swap(): return lax.ppermute(x, axis, [(i, i ^ bit) for i in range(size)])]
    unnamed x93 -> x53, local copies, waits for them, and re-layouts: 7.57 us -> 0.17 us
  transfers between devices with their start and end apart: 72 -> 65, of which waited for: 36 -> 37; matrix products, arithmetic and copies ran while one was open for 8% -> 7% of each run, Pallas kernels for 16% -> 16%
where the time goes in v4:
time: 262 us; the launch traced here: 259 us
  waiting for transfers between devices  126 us (48%)
  starting transfers between devices  68.4 us (26%)
  Pallas kernels  40.4 us (15%)
  other arithmetic  20.5 us (8%)
    ppermute x61, waiting for transfers between devices, swap(): return lax.ppermute(x, axis, [(i, i ^ bit) for i in range(size)])  120 us
    ppermute x61, starting transfers between devices, swap(): return lax.ppermute(x, axis, [(i, i ^ bit) for i in range(size)])  61.6 us
    pallas_call x9, Pallas kernels, call(): pl.pallas_call(kernel, out_shape=outs, in_specs=specs, out_specs=[pl.Bloc...  40.4 us
    ppermute x4, starting transfers between devices, shift(): lax.ppermute(x, 'tensor', [(i, i + by) for i in range(size) if 0 <= i + b...  6.79 us
    ppermute x4, waiting for transfers between devices, shift(): lax.ppermute(x, 'tensor', [(i, i + by) for i in range(size) if 0 <= i + b...  6.32 us
  transfers between devices with their start and end apart: 65, of which 37 were waited for; matrix products, arithmetic and copies ran while one was open for 7% of the time, Pallas kernels for 16%

profile of v4, /device:TPU:0, one launch (start us, length us, event | category | flops | bytes accessed | tf_op | source)
XLA Modules:
  0.0 259.3 jit_solution(3767118885671911877)
XLA Ops:
  3.0 3.0 %collective-permute-start.6 = (bf16[384,384]{1,0:T(8,128)(2,1)S(1)}, bf16[384,384]{1,0:T(8,128)(2,1)S(1)}, u32[]{:S(2)}, u32[]{:S(2)}) collective-permute-start(bf16[384,384]{1,0:T(8,128)(2,1)S(1)} %slice_select_fusion.3), channel_id=1, source_target_pairs={{0,2},{1,3},{2,0},{3,1},{4,6},{5,7},{6,4},{7,5},{8,10},{9,11},{10,... | collective-permute-start | bytes 884744 | tf_op jit(solution)/shard_map/ppermute | solution.py:508
  8.6 3.0 %shard_map.356 = (f32[1536,128]{1,0:T(8,128)S(1)}, bf16[256,768]{1,0:T(8,128)(2,1)S(1)}, f32[256,768]{1,0:T(8,128)S(1)}, f32[32,768]{1,0:T(8,128)S(1)}) custom-call(bf16[256,768]{1,0:T(8,128)(2,1)S(1)} %bitcast.49, f32[1,768]{1,0:T(1,128)S(1)} %broadcast_in_dim.34.g_ref, f32[16,768]{1,0:T(8,128)S(1)} %copy-done.4, f32[16,768]{1,0:T(8,128)S(1)} %copy-done.5, ...), custom_call_target="tpu_custom_call" | custom-call | flops 25165824 | bytes 2739200 | tf_op jit(solution)/shard_map/pallas_call | solution.py:71
  11.6 1.8 collective-permute-start.4
  13.4 2.5 collective-permute-start.7
  15.9 3.8 %collective-permute-done.5 = bf16[384,384]{1,0:T(8,128)(2,1)S(1)} collective-permute-done((bf16[384,384]{1,0:T(8,128)(2,1)S(1)}, bf16[384,384]{1,0:T(8,128)(2,1)S(1)}, u32[]{:S(2)}, u32[]{:S(2)}) %collective-permute-start.5) | collective-permute-done | bytes 294944 | tf_op jit(solution)/shard_map/ppermute | solution.py:508
  19.7 2.1 collective-permute-done.7.f2_ref
  21.8 2.5 collective-permute-start.9
  26.8 4.6 %shard_map.357 = (f32[1536,128]{1,0:T(8,128)S(1)}, bf16[256,768]{1,0:T(8,128)(2,1)S(1)}, f32[256,128]{1,0:T(8,128)S(1)}, f32[256,768]{1,0:T(8,128)S(1)}, f32[256,128]{1,0:T(8,128)S(1)}) custom-call(f32[1536,128]{1,0:T(8,128)S(1)} %get-tuple-element.310.normed_ref, f32[256,768]{1,0:T(8,128)S(1)} %get-tuple-element.311.init_ref, ...), custom_call_target="tpu_custom_call" | custom-call | flops 327155712 | bytes 5838336 | tf_op jit(solution)/shard_map/pallas_call | solution.py:71
  31.4 3.0 %collective-permute-done.8 = bf16[384,384]{1,0:T(8,128)(2,1)S(1)} collective-permute-done((bf16[384,384]{1,0:T(8,128)(2,1)S(1)}, bf16[384,384]{1,0:T(8,128)(2,1)S(1)}, u32[]{:S(2)}, u32[]{:S(2)}) %collective-permute-start.8) | collective-permute-done | bytes 294944 | tf_op jit(solution)/shard_map/ppermute | solution.py:508
  35.4 4.1 %collective-permute-done.10 = bf16[384,384]{1,0:T(8,128)(2,1)S(1)} collective-permute-done((bf16[384,384]{1,0:T(8,128)(2,1)S(1)}, bf16[384,384]{1,0:T(8,128)(2,1)S(1)}, u32[]{:S(2)}, u32[]{:S(2)}) %collective-permute-start.10) | collective-permute-done | bytes 294944 | tf_op jit(solution)/shard_map/ppermute | solution.py:508
  43.2 7.9 %collective-permute-done.12 = bf16[384,384]{1,0:T(8,128)(2,1)S(1)} collective-permute-done((bf16[384,384]{1,0:T(8,128)(2,1)S(1)}, bf16[384,384]{1,0:T(8,128)(2,1)S(1)}, u32[]{:S(2)}, u32[]{:S(2)}) %collective-permute-start.12) | collective-permute-done | bytes 294944 | tf_op jit(solution)/shard_map/ppermute | solution.py:508
  51.1 4.1 %collective-permute-done.11 = bf16[192,768]{1,0:T(8,128)(2,1)S(1)} collective-permute-done((bf16[192,768]{1,0:T(8,128)(2,1)S(1)}, bf16[192,768]{1,0:T(8,128)(2,1)S(1)}, u32[]{:S(2)}, u32[]{:S(2)}) %collective-permute-start.11) | collective-permute-done | bytes 294944 | tf_op jit(solution)/shard_map/ppermute | solution.py:508
  58.8 1.9 collective-permute-done.14.vb_ref.refs_32_
  62.6 4.0 %collective-permute-done.17 = bf16[384,384]{1,0:T(8,128)(2,1)S(1)} collective-permute-done((bf16[384,384]{1,0:T(8,128)(2,1)S(1)}, bf16[384,384]{1,0:T(8,128)(2,1)S(1)}, u32[]{:S(2)}, u32[]{:S(2)}) %collective-permute-start.17) | collective-permute-done | bytes 294944 | tf_op jit(solution)/shard_map/ppermute | solution.py:508
  66.9 2.2 shard_map.360
  69.1 2.7 %shard_map.361 = (f32[256,768]{1,0:T(8,128)S(1)}, f32[256,768]{1,0:T(8,128)S(1)}, bf16[1536,384]{1,0:T(8,128)(2,1)S(1)}, bf16[1536,384]{1,0:T(8,128)(2,1)S(1)}) custom-call(bf16[256,768]{1,0:T(8,128)(2,1)S(1)} %get-tuple-element.382.second_ref, bf16[256,768]{1,0:T(8,128)(2,1)S(1)} %bitcast.53, bf16[768,384]{1,0:T(8,128)(2,1)S(1)} %copy-done.8, ...), custom_call_target="tpu_custom_call" | custom-call | flops 1811939328 | bytes 7077888 | tf_op jit(solution)/shard_map/pallas_call | solution.py:71
  72.7 2.0 collective-permute-done.20.ob_ref
  74.8 2.7 %shard_map.362 = (f32[256,768]{1,0:T(8,128)S(1)}, f32[256,768]{1,0:T(8,128)S(1)}, bf16[1536,384]{1,0:T(8,128)(2,1)S(1)}, bf16[1536,384]{1,0:T(8,128)(2,1)S(1)}) custom-call(bf16[256,768]{1,0:T(8,128)(2,1)S(1)} %get-tuple-element.382.second_ref, bf16[256,768]{1,0:T(8,128)(2,1)S(1)} %bitcast.54, bf16[768,384]{1,0:T(8,128)(2,1)S(1)} %maximum_select_fusion.5.ia_ref, ...), custom_call_target="tpu_custom_call" | custom-call | flops 1811939328 | bytes 7077888 | tf_op jit(solution)/shard_map/pallas_call | solution.py:71
  78.1 2.3 collective-permute-done.21
  80.8 1.8 collective-permute-start.23
  83.1 14.7 %shard_map.363 = (bf16[256,768]{1,0:T(8,128)(2,1)}, f32[256,768]{1,0:T(8,128)S(1)}, f32[1,768]{1,0:T(1,128)S(1)}, bf16[2,768,384]{2,1,0:T(8,128)(2,1)S(1)}, bf16...) custom-call(s32[4]{0:T(128)S(1)} %xor_multiply_fusion.offs_ref.refs_, ...), custom_call_target="tpu_custom_call" | custom-call | flops 5435817984 | bytes 39038480 | tf_op jit(solution)/shard_map/pallas_call | solution.py:71
  105.8 2.6 %collective-permute-done.25 = bf16[384,384]{1,0:T(8,128)(2,1)S(1)} collective-permute-done((bf16[384,384]{1,0:T(8,128)(2,1)S(1)}, bf16[384,384]{1,0:T(8,128)(2,1)S(1)}, u32[]{:S(2)}, u32[]{:S(2)}) %collective-permute-start.25) | collective-permute-done | bytes 294944 | tf_op jit(solution)/shard_map/ppermute | solution.py:508
  112.0 2.6 %collective-permute-start.34 = (bf16[768,384]{1,0:T(8,128)(2,1)S(1)}, bf16[768,384]{1,0:T(8,128)(2,1)S(1)}, u32[]{:S(2)}, u32[]{:S(2)}) collective-permute-start(bf16[768,384]{1,0:T(8,128)(2,1)S(1)} %fusion.6), channel_id=1, source_target_pairs={{0,2},{1,3},{2,0},{3,1},{4,6},{5,7},{6,4},{7,5},{8,10},{9,11},{10,... | collective-permute-start | bytes 1769480 | tf_op jit(solution)/shard_map/ppermute | solution.py:508
  115.5 4.2 %collective-permute-done.31.far_ref = f32[64,768]{1,0:T(8,128)S(1)} collective-permute-done((f32[64,768]{1,0:T(8,128)S(1)}, f32[64,768]{1,0:T(8,128)S(1)}, u32[]{:S(2)}, u32[]{:S(2)}) %collective-permute-start.31) | collective-permute-done | bytes 196640 | tf_op jit(solution)/shard_map/ppermute | solution.py:513
  119.7 8.5 %shard_map.364 = (bf16[256,768]{1,0:T(8,128)(2,1)}, f32[40,768]{1,0:T(8,128)S(1)}) custom-call(f32[1536,128]{1,0:T(8,128)S(1)} %get-tuple-element.428.pg_ref, f32[1536,128]{1,0:T(8,128)S(1)} %get-tuple-element.310.normed_ref, f32[256,768]{1,0:T(8,128)S(1)} %get-tuple-element.429.im_ref, f32[256,768]{1,0:T(8,128)S(1)} %get-tuple-element.430.iv_ref, ...), custom_call_target="tpu_custom_call" | custom-call | flops 50331648 | bytes 6363136 | tf_op jit(solution)/shard_map/pallas_call | solution.py:71
  128.3 3.9 %collective-permute-done.34 = bf16[768,384]{1,0:T(8,128)(2,1)S(1)} collective-permute-done((bf16[768,384]{1,0:T(8,128)(2,1)S(1)}, bf16[768,384]{1,0:T(8,128)(2,1)S(1)}, u32[]{:S(2)}, u32[]{:S(2)}) %collective-permute-start.34) | collective-permute-done | bytes 589856 | tf_op jit(solution)/shard_map/ppermute | solution.py:508
  132.5 10.3 %collective-permute-done.33 = bf16[1536,384]{1,0:T(8,128)(2,1)S(1)} collective-permute-done((bf16[1536,384]{1,0:T(8,128)(2,1)S(1)}, bf16[1536,384]{1,0:T(8,128)(2,1)S(1)}, u32[]{:S(2)}, u32[]{:S(2)}) %collective-permute-start.33) | collective-permute-done | bytes 1179680 | tf_op jit(solution)/shard_map/ppermute | solution.py:508
  144.4 4.9 %collective-permute-done.38 = bf16[192,384]{1,0:T(8,128)(2,1)S(1)} collective-permute-done((bf16[192,384]{1,0:T(8,128)(2,1)S(1)}, bf16[192,384]{1,0:T(8,128)(2,1)S(1)}, u32[]{:S(2)}, u32[]{:S(2)}) %collective-permute-start.38) | collective-permute-done | bytes 147488 | tf_op jit(solution)/shard_map/ppermute | solution.py:508
  149.6 3.4 %collective-permute-done.37 = bf16[384,384]{1,0:T(8,128)(2,1)S(1)} collective-permute-done((bf16[384,384]{1,0:T(8,128)(2,1)S(1)}, bf16[384,384]{1,0:T(8,128)(2,1)S(1)}, u32[]{:S(2)}, u32[]{:S(2)}) %collective-permute-start.37) | collective-permute-done | bytes 294944 | tf_op jit(solution)/shard_map/ppermute | solution.py:508
  156.3 2.0 collective-permute-done.36
  158.4 4.4 %collective-permute-done.42 = bf16[384,384]{1,0:T(8,128)(2,1)S(1)} collective-permute-done((bf16[384,384]{1,0:T(8,128)(2,1)S(1)}, bf16[384,384]{1,0:T(8,128)(2,1)S(1)}, u32[]{:S(2)}, u32[]{:S(2)}) %collective-permute-start.42) | collective-permute-done | bytes 294944 | tf_op jit(solution)/shard_map/ppermute | solution.py:508
  165.3 2.6 collective-permute-start.43
  170.6 1.9 collective-permute-start.55
  172.5 9.9 %collective-permute-done.55 = bf16[192,384]{1,0:T(8,128)(2,1)S(1)} collective-permute-done((bf16[192,384]{1,0:T(8,128)(2,1)S(1)}, bf16[192,384]{1,0:T(8,128)(2,1)S(1)}, u32[]{:S(2)}, u32[]{:S(2)}) %collective-permute-start.55) | collective-permute-done | bytes 147488 | tf_op jit(solution)/shard_map/ppermute | solution.py:508
  183.0 2.1 collective-permute-start.46
  185.4 3.1 %collective-permute-done.44 = bf16[192,384]{1,0:T(8,128)(2,1)S(1)} collective-permute-done((bf16[192,384]{1,0:T(8,128)(2,1)S(1)}, bf16[192,384]{1,0:T(8,128)(2,1)S(1)}, u32[]{:S(2)}, u32[]{:S(2)}) %collective-permute-start.44) | collective-permute-done | bytes 147488 | tf_op jit(solution)/shard_map/ppermute | solution.py:508
  191.3 2.6 %collective-permute-start.45 = (bf16[1248,128]{1,0:T(8,128)(2,1)S(1)}, bf16[1248,128]{1,0:T(8,128)(2,1)S(1)}, u32[]{:S(2)}, u32[]{:S(2)}) collective-permute-start(bf16[1248,128]{1,0:T(8,128)(2,1)S(1)} %pad_maximum_fusion.6), channel_id=1, source_target_pairs={{0,4},{4,0},{8,12},{12,8},{16,20},{20,16},{24,28},{28,24},{1,5},{5... | collective-permute-start | bytes 958472 | tf_op jit(solution)/shard_map/ppermute | solution.py:508
  195.0 2.9 %collective-permute-start.57 = (bf16[384,384]{1,0:T(8,128)(2,1)S(1)}, bf16[384,384]{1,0:T(8,128)(2,1)S(1)}, u32[]{:S(2)}, u32[]{:S(2)}) collective-permute-start(bf16[384,384]{1,0:T(8,128)(2,1)S(1)} %maximum_select_fusion.13), channel_id=1, source_target_pairs={{0,4},{4,0},{8,12},{12,8},{16,20},{20,16},{24,28},{28,24},{1,5},{5... | collective-permute-start | bytes 884744 | tf_op jit(solution)/shard_map/ppermute | solution.py:508
  200.6 5.3 %collective-permute-done.60 = bf16[192,384]{1,0:T(8,128)(2,1)S(1)} collective-permute-done((bf16[192,384]{1,0:T(8,128)(2,1)S(1)}, bf16[192,384]{1,0:T(8,128)(2,1)S(1)}, u32[]{:S(2)}, u32[]{:S(2)}) %collective-permute-start.60) | collective-permute-done | bytes 147488 | tf_op jit(solution)/shard_map/ppermute | solution.py:508
  206.2 2.5 collective-permute-start.61
  209.0 2.8 %collective-permute-done.57 = bf16[384,384]{1,0:T(8,128)(2,1)S(1)} collective-permute-done((bf16[384,384]{1,0:T(8,128)(2,1)S(1)}, bf16[384,384]{1,0:T(8,128)(2,1)S(1)}, u32[]{:S(2)}, u32[]{:S(2)}) %collective-permute-start.57) | collective-permute-done | bytes 294944 | tf_op jit(solution)/shard_map/ppermute | solution.py:508
  211.8 1.9 collective-permute-start.51
  214.9 3.2 %collective-permute-done.53 = bf16[384,384]{1,0:T(8,128)(2,1)S(1)} collective-permute-done((bf16[384,384]{1,0:T(8,128)(2,1)S(1)}, bf16[384,384]{1,0:T(8,128)(2,1)S(1)}, u32[]{:S(2)}, u32[]{:S(2)}) %collective-permute-start.53) | collective-permute-done | bytes 294944 | tf_op jit(solution)/shard_map/ppermute | solution.py:508
  218.4 6.0 %collective-permute-done.64 = bf16[384,384]{1,0:T(8,128)(2,1)S(1)} collective-permute-done((bf16[384,384]{1,0:T(8,128)(2,1)S(1)}, bf16[384,384]{1,0:T(8,128)(2,1)S(1)}, u32[]{:S(2)}, u32[]{:S(2)}) %collective-permute-start.64) | collective-permute-done | bytes 294944 | tf_op jit(solution)/shard_map/ppermute | solution.py:508
  228.3 2.0 collective-permute-done.61
  233.8 2.0 collective-permute-start.59
  236.9 11.9 %collective-permute-done.54 = bf16[1248,128]{1,0:T(8,128)(2,1)S(1)} collective-permute-done((bf16[1248,128]{1,0:T(8,128)(2,1)S(1)}, bf16[1248,128]{1,0:T(8,128)(2,1)S(1)}, u32[]{:S(2)}, u32[]{:S(2)}) %collective-permute-start.54) | collective-permute-done | bytes 319520 | tf_op jit(solution)/shard_map/ppermute | solution.py:508
  251.6 2.9 %collective-permute-done.59 = bf16[768,384]{1,0:T(8,128)(2,1)S(1)} collective-permute-done((bf16[768,384]{1,0:T(8,128)(2,1)S(1)}, bf16[768,384]{1,0:T(8,128)(2,1)S(1)}, u32[]{:S(2)}, u32[]{:S(2)}) %collective-permute-start.59) | collective-permute-done | bytes 589856 | tf_op jit(solution)/shard_map/ppermute | solution.py:508
  (268 shorter events, 68.2 us)
Async XLA Ops:
  3.0 12.9 %collective-permute-start.6 = (bf16[384,384]{1,0:T(8,128)(2,1)S(1)}, bf16[384,384]{1,0:T(8,128)(2,1)S(1)}, u32[]{:S(2)}, u32[]{:S(2)}) collective-permute-start(bf16[384,384]{1,0:T(8,128)(2,1)S(1)} %slice_select_fusion.3), channel_id=1, source_target_pairs={{0,2},{1,3},{2,0},{3,1},{4,6},{5,7},{6,4},{7,5},{8,10},{9,11},{10,... | collective-permute-start | bytes 884744 | tf_op jit(solution)/shard_map/ppermute | solution.py:508
  6.8 12.9 %collective-permute-start.5 = (bf16[384,384]{1,0:T(8,128)(2,1)S(1)}, bf16[384,384]{1,0:T(8,128)(2,1)S(1)}, u32[]{:S(2)}, u32[]{:S(2)}) collective-permute-start(bf16[384,384]{1,0:T(8,128)(2,1)S(1)} %slice_select_fusion.4), channel_id=1, source_target_pairs={{0,2},{1,3},{2,0},{3,1},{4,6},{5,7},{6,4},{7,5},{8,10},{9,11},{10,... | collective-permute-start | bytes 884744 | tf_op jit(solution)/shard_map/ppermute | solution.py:508
  11.6 8.1 %collective-permute-start.4 = (f32[32,768]{1,0:T(8,128)S(1)}, f32[32,768]{1,0:T(8,128)S(1)}, u32[]{:S(2)}, u32[]{:S(2)}) collective-permute-start(f32[32,768]{1,0:T(8,128)S(1)} %get-tuple-element.314), channel_id=1, source_target_pairs={{0,1},{1,2},{2,3},{4,5},{5,6},{6,7},{8,9},{9,10},{10,11},{12,13},{... | collective-permute-start | bytes 294920 | tf_op jit(solution)/shard_map/ppermute | solution.py:513
  13.4 8.4 %collective-permute-start.7 = (f32[32,768]{1,0:T(8,128)S(1)}, f32[32,768]{1,0:T(8,128)S(1)}, u32[]{:S(2)}, u32[]{:S(2)}) collective-permute-start(f32[32,768]{1,0:T(8,128)S(1)} %get-tuple-element.314), channel_id=1, source_target_pairs={{0,2},{1,3},{4,6},{5,7},{8,10},{9,11},{12,14},{13,15},{16,18},{17,... | collective-permute-start | bytes 294920 | tf_op jit(solution)/shard_map/ppermute | solution.py:513
  21.8 17.7 %collective-permute-start.9 = (bf16[288,768]{1,0:T(8,128)(2,1)S(1)}, bf16[288,768]{1,0:T(8,128)(2,1)S(1)}, u32[]{:S(2)}, u32[]{:S(2)}) collective-permute-start(bf16[288,768]{1,0:T(8,128)(2,1)S(1)} %slice_select_fusion), channel_id=1, source_target_pairs={{0,2},{1,3},{2,0},{3,1},{4,6},{5,7},{6,4},{7,5},{8,10},{9,11},{10,... | collective-permute-start | bytes 1327112 | tf_op jit(solution)/shard_map/ppermute | solution.py:508
  24.4 9.9 %collective-permute-start.8 = (bf16[384,384]{1,0:T(8,128)(2,1)S(1)}, bf16[384,384]{1,0:T(8,128)(2,1)S(1)}, u32[]{:S(2)}, u32[]{:S(2)}) collective-permute-start(bf16[384,384]{1,0:T(8,128)(2,1)S(1)} %collective-permute-done.6), channel_id=1, source_target_pairs={{0,4},{4,0},{8,12},{12,8},{16,20},{20,16},{24,28},{28,24},{1,5},{5... | collective-permute-start | bytes 884744 | tf_op jit(solution)/shard_map/ppermute | solution.py:508
  26.1 13.4 %collective-permute-start.10 = (bf16[384,384]{1,0:T(8,128)(2,1)S(1)}, bf16[384,384]{1,0:T(8,128)(2,1)S(1)}, u32[]{:S(2)}, u32[]{:S(2)}) collective-permute-start(bf16[384,384]{1,0:T(8,128)(2,1)S(1)} %collective-permute-done.5), channel_id=1, source_target_pairs={{0,4},{4,0},{8,12},{12,8},{16,20},{20,16},{24,28},{28,24},{1,5},{5... | collective-permute-start | bytes 884744 | tf_op jit(solution)/shard_map/ppermute | solution.py:508
  39.5 16.0 %collective-permute-start.15 = (bf16[288,768]{1,0:T(8,128)(2,1)S(1)}, bf16[288,768]{1,0:T(8,128)(2,1)S(1)}, u32[]{:S(2)}, u32[]{:S(2)}) collective-permute-start(bf16[288,768]{1,0:T(8,128)(2,1)S(1)} %collective-permute-done.9), channel_id=1, source_target_pairs={{0,8},{4,12},{8,0},{12,4},{16,24},{20,28},{24,16},{28,20},{1,9},{5... | collective-permute-start | bytes 1327112 | tf_op jit(solution)/shard_map/ppermute | solution.py:508
  41.1 9.9 %collective-permute-start.12 = (bf16[384,384]{1,0:T(8,128)(2,1)S(1)}, bf16[384,384]{1,0:T(8,128)(2,1)S(1)}, u32[]{:S(2)}, u32[]{:S(2)}) collective-permute-start(bf16[384,384]{1,0:T(8,128)(2,1)S(1)} %slice_select_fusion.2), channel_id=1, source_target_pairs={{0,2},{1,3},{2,0},{3,1},{4,6},{5,7},{6,4},{7,5},{8,10},{9,11},{10,... | collective-permute-start | bytes 884744 | tf_op jit(solution)/shard_map/ppermute | solution.py:508
  41.5 13.6 %collective-permute-start.11 = (bf16[192,768]{1,0:T(8,128)(2,1)S(1)}, bf16[192,768]{1,0:T(8,128)(2,1)S(1)}, u32[]{:S(2)}, u32[]{:S(2)}) collective-permute-start(bf16[192,768]{1,0:T(8,128)(2,1)S(1)} %slice_select_fusion.1), channel_id=1, source_target_pairs={{0,2},{1,3},{2,0},{3,1},{4,6},{5,7},{6,4},{7,5},{8,10},{9,11},{10,... | collective-permute-start | bytes 884744 | tf_op jit(solution)/shard_map/ppermute | solution.py:508
  56.1 10.8 %collective-permute-start.16 = (bf16[2,576,768]{2,1,0:T(8,128)(2,1)S(1)}, bf16[2,576,768]{2,1,0:T(8,128)(2,1)S(1)}, u32[]{:S(2)}, u32[]{:S(2)}) collective-permute-start(bf16[2,576,768]{2,1,0:T(8,128)(2,1)S(1)} %pad_maximum_fusion.ga_ref.refs_24_), channel_id=1, source_target_pairs={{0,1},{1,0},{2,3},{3,2},{4,5},{5,4},{6,7},{7,6},{8,9},{9,8},{10,11... | collective-permute-start | bytes 5308424 | tf_op jit(solution)/shard_map/ppermute | solution.py:508
  56.7 9.9 %collective-permute-start.17 = (bf16[384,384]{1,0:T(8,128)(2,1)S(1)}, bf16[384,384]{1,0:T(8,128)(2,1)S(1)}, u32[]{:S(2)}, u32[]{:S(2)}) collective-permute-start(bf16[384,384]{1,0:T(8,128)(2,1)S(1)} %collective-permute-done.12), channel_id=1, source_target_pairs={{0,4},{4,0},{8,12},{12,8},{16,20},{20,16},{24,28},{28,24},{1,5},{5... | collective-permute-start | bytes 884744 | tf_op jit(solution)/shard_map/ppermute | solution.py:508
  58.2 14.2 %collective-permute-start.19 = (bf16[192,768]{1,0:T(8,128)(2,1)S(1)}, bf16[192,768]{1,0:T(8,128)(2,1)S(1)}, u32[]{:S(2)}, u32[]{:S(2)}) collective-permute-start(bf16[192,768]{1,0:T(8,128)(2,1)S(1)} %collective-permute-done.11), channel_id=1, source_target_pairs={{0,4},{4,0},{8,12},{12,8},{16,20},{20,16},{24,28},{28,24},{1,5},{5... | collective-permute-start | bytes 884744 | tf_op jit(solution)/shard_map/ppermute | solution.py:508
  80.8 17.0 %collective-permute-start.23 = (bf16[768,384]{1,0:T(8,128)(2,1)S(1)}, bf16[768,384]{1,0:T(8,128)(2,1)S(1)}, u32[]{:S(2)}, u32[]{:S(2)}) collective-permute-start(bf16[768,384]{1,0:T(8,128)(2,1)S(1)} %pad_maximum_fusion.2), channel_id=1, source_target_pairs={{0,4},{4,0},{8,12},{12,8},{16,20},{20,16},{24,28},{28,24},{1,5},{5... | collective-permute-start | bytes 1769480 | tf_op jit(solution)/shard_map/ppermute | solution.py:508
  82.6 15.3 %collective-permute-start.24 = (bf16[768,384]{1,0:T(8,128)(2,1)S(1)}, bf16[768,384]{1,0:T(8,128)(2,1)S(1)}, u32[]{:S(2)}, u32[]{:S(2)}) collective-permute-start(bf16[768,384]{1,0:T(8,128)(2,1)S(1)} %get-tuple-element.439), channel_id=1, source_target_pairs={{0,2},{1,3},{2,0},{3,1},{4,6},{5,7},{6,4},{7,5},{8,10},{9,11},{10,... | collective-permute-start | bytes 1769480 | tf_op jit(solution)/shard_map/ppermute | solution.py:508
  99.0 6.8 %collective-permute-start.26 = (bf16[2,768,384]{2,1,0:T(8,128)(2,1)S(1)}, bf16[2,768,384]{2,1,0:T(8,128)(2,1)S(1)}, u32[]{:S(2)}, u32[]{:S(2)}) collective-permute-start(bf16[2,768,384]{2,1,0:T(8,128)(2,1)S(1)} %get-tuple-element.450), channel_id=1, source_target_pairs={{0,1},{1,0},{2,3},{3,2},{4,5},{5,4},{6,7},{7,6},{8,9},{9,8},{10,11... | collective-permute-start | bytes 3538952 | tf_op jit(solution)/shard_map/ppermute | solution.py:508
  99.1 9.3 %collective-permute-start.25 = (bf16[384,384]{1,0:T(8,128)(2,1)S(1)}, bf16[384,384]{1,0:T(8,128)(2,1)S(1)}, u32[]{:S(2)}, u32[]{:S(2)}) collective-permute-start(bf16[384,384]{1,0:T(8,128)(2,1)S(1)} %fusion.10), channel_id=1, source_target_pairs={{0,2},{1,3},{2,0},{3,1},{4,6},{5,7},{6,4},{7,5},{8,10},{9,11},{10,... | collective-permute-start | bytes 884744 | tf_op jit(solution)/shard_map/ppermute | solution.py:508
  100.5 10.5 %collective-permute-start.30 = (bf16[384,384]{1,0:T(8,128)(2,1)S(1)}, bf16[384,384]{1,0:T(8,128)(2,1)S(1)}, u32[]{:S(2)}, u32[]{:S(2)}) collective-permute-start(bf16[384,384]{1,0:T(8,128)(2,1)S(1)} %select_convert_fusion.6), channel_id=1, source_target_pairs={{0,4},{4,0},{8,12},{12,8},{16,20},{20,16},{24,28},{28,24},{1,5},{5... | collective-permute-start | bytes 884744 | tf_op jit(solution)/shard_map/ppermute | solution.py:508
  108.4 7.0 %collective-permute-start.29 = (f32[64,768]{1,0:T(8,128)S(1)}, f32[64,768]{1,0:T(8,128)S(1)}, u32[]{:S(2)}, u32[]{:S(2)}) collective-permute-start(f32[64,768]{1,0:T(8,128)S(1)} %pad_maximum_fusion.10), channel_id=1, source_target_pairs={{1,0},{2,1},{3,2},{5,4},{6,5},{7,6},{9,8},{10,9},{11,10},{13,12},{... | collective-permute-start | bytes 589832 | tf_op jit(solution)/shard_map/ppermute | solution.py:513
  109.7 10.0 %collective-permute-start.31 = (f32[64,768]{1,0:T(8,128)S(1)}, f32[64,768]{1,0:T(8,128)S(1)}, u32[]{:S(2)}, u32[]{:S(2)}) collective-permute-start(f32[64,768]{1,0:T(8,128)S(1)} %pad_maximum_fusion.10), channel_id=1, source_target_pairs={{2,0},{3,1},{6,4},{7,5},{10,8},{11,9},{14,12},{15,13},{18,16},{19,... | collective-permute-start | bytes 589832 | tf_op jit(solution)/shard_map/ppermute | solution.py:513
  111.4 16.9 %collective-permute-start.32 = (bf16[768,384]{1,0:T(8,128)(2,1)S(1)}, bf16[768,384]{1,0:T(8,128)(2,1)S(1)}, u32[]{:S(2)}, u32[]{:S(2)}) collective-permute-start(bf16[768,384]{1,0:T(8,128)(2,1)S(1)} %pad_maximum_fusion.3), channel_id=1, source_target_pairs={{0,4},{4,0},{8,12},{12,8},{16,20},{20,16},{24,28},{28,24},{1,5},{5... | collective-permute-start | bytes 1769480 | tf_op jit(solution)/shard_map/ppermute | solution.py:508
  112.0 20.2 %collective-permute-start.34 = (bf16[768,384]{1,0:T(8,128)(2,1)S(1)}, bf16[768,384]{1,0:T(8,128)(2,1)S(1)}, u32[]{:S(2)}, u32[]{:S(2)}) collective-permute-start(bf16[768,384]{1,0:T(8,128)(2,1)S(1)} %fusion.6), channel_id=1, source_target_pairs={{0,2},{1,3},{2,0},{3,1},{4,6},{5,7},{6,4},{7,5},{8,10},{9,11},{10,... | collective-permute-start | bytes 1769480 | tf_op jit(solution)/shard_map/ppermute | solution.py:508
  114.7 28.2 %collective-permute-start.33 = (bf16[1536,384]{1,0:T(8,128)(2,1)S(1)}, bf16[1536,384]{1,0:T(8,128)(2,1)S(1)}, u32[]{:S(2)}, u32[]{:S(2)}) collective-permute-start(bf16[1536,384]{1,0:T(8,128)(2,1)S(1)} %pad_maximum_fusion.1), channel_id=1, source_target_pairs={{0,8},{4,12},{8,0},{12,4},{16,24},{20,28},{24,16},{28,20},{1,9},{5... | collective-permute-start | bytes 3538952 | tf_op jit(solution)/shard_map/ppermute | solution.py:508
  143.0 6.3 %collective-permute-start.38 = (bf16[192,384]{1,0:T(8,128)(2,1)S(1)}, bf16[192,384]{1,0:T(8,128)(2,1)S(1)}, u32[]{:S(2)}, u32[]{:S(2)}) collective-permute-start(bf16[192,384]{1,0:T(8,128)(2,1)S(1)} %select_convert_fusion.12), channel_id=1, source_target_pairs={{0,8},{4,12},{8,0},{12,4},{16,24},{20,28},{24,16},{28,20},{1,9},{5... | collective-permute-start | bytes 442376 | tf_op jit(solution)/shard_map/ppermute | solution.py:508
  143.8 9.2 %collective-permute-start.37 = (bf16[384,384]{1,0:T(8,128)(2,1)S(1)}, bf16[384,384]{1,0:T(8,128)(2,1)S(1)}, u32[]{:S(2)}, u32[]{:S(2)}) collective-permute-start(bf16[384,384]{1,0:T(8,128)(2,1)S(1)} %fusion.9), channel_id=1, source_target_pairs={{0,2},{1,3},{2,0},{3,1},{4,6},{5,7},{6,4},{7,5},{8,10},{9,11},{10,... | collective-permute-start | bytes 884744 | tf_op jit(solution)/shard_map/ppermute | solution.py:508
  154.8 8.0 %collective-permute-start.42 = (bf16[384,384]{1,0:T(8,128)(2,1)S(1)}, bf16[384,384]{1,0:T(8,128)(2,1)S(1)}, u32[]{:S(2)}, u32[]{:S(2)}) collective-permute-start(bf16[384,384]{1,0:T(8,128)(2,1)S(1)} %select_convert_fusion.3), channel_id=1, source_target_pairs={{0,4},{4,0},{8,12},{12,8},{16,20},{20,16},{24,28},{28,24},{1,5},{5... | collective-permute-start | bytes 884744 | tf_op jit(solution)/shard_map/ppermute | solution.py:508
  162.9 7.6 %collective-permute-start.50 = (bf16[192,384]{1,0:T(8,128)(2,1)S(1)}, bf16[192,384]{1,0:T(8,128)(2,1)S(1)}, u32[]{:S(2)}, u32[]{:S(2)}) collective-permute-start(bf16[192,384]{1,0:T(8,128)(2,1)S(1)} %select_convert_fusion.9), channel_id=1, source_target_pairs={{0,8},{4,12},{8,0},{12,4},{16,24},{20,28},{24,16},{28,20},{1,9},{5... | collective-permute-start | bytes 442376 | tf_op jit(solution)/shard_map/ppermute | solution.py:508
  163.5 19.0 %collective-permute-start.41 = (bf16[768,384]{1,0:T(8,128)(2,1)S(1)}, bf16[768,384]{1,0:T(8,128)(2,1)S(1)}, u32[]{:S(2)}, u32[]{:S(2)}) collective-permute-start(bf16[768,384]{1,0:T(8,128)(2,1)S(1)} %fusion.1), channel_id=1, source_target_pairs={{0,2},{1,3},{2,0},{3,1},{4,6},{5,7},{6,4},{7,5},{8,10},{9,11},{10,... | collective-permute-start | bytes 1769480 | tf_op jit(solution)/shard_map/ppermute | solution.py:508
  163.7 19.1 %collective-permute-start.40 = (bf16[192,384]{1,0:T(8,128)(2,1)S(1)}, bf16[192,384]{1,0:T(8,128)(2,1)S(1)}, u32[]{:S(2)}, u32[]{:S(2)}) collective-permute-start(bf16[192,384]{1,0:T(8,128)(2,1)S(1)} %select_convert_fusion.10), channel_id=1, source_target_pairs={{0,8},{4,12},{8,0},{12,4},{16,24},{20,28},{24,16},{28,20},{1,9},{5... | collective-permute-start | bytes 442376 | tf_op jit(solution)/shard_map/ppermute | solution.py:508
  165.3 17.6 %collective-permute-start.43 = (bf16[192,384]{1,0:T(8,128)(2,1)S(1)}, bf16[192,384]{1,0:T(8,128)(2,1)S(1)}, u32[]{:S(2)}, u32[]{:S(2)}) collective-permute-start(bf16[192,384]{1,0:T(8,128)(2,1)S(1)} %fusion.40), channel_id=1, source_target_pairs={{0,16},{4,20},{8,24},{12,28},{16,0},{20,4},{24,8},{28,12},{1,17},{... | collective-permute-start | bytes 442376 | tf_op jit(solution)/shard_map/ppermute | solution.py:508
  167.9 17.3 %collective-permute-start.39 = (bf16[1248,128]{1,0:T(8,128)(2,1)S(1)}, bf16[1248,128]{1,0:T(8,128)(2,1)S(1)}, u32[]{:S(2)}, u32[]{:S(2)}) collective-permute-start(bf16[1248,128]{1,0:T(8,128)(2,1)S(1)} %pad_maximum_fusion.5), channel_id=1, source_target_pairs={{0,2},{1,3},{2,0},{3,1},{4,6},{5,7},{6,4},{7,5},{8,10},{9,11},{10,... | collective-permute-start | bytes 958472 | tf_op jit(solution)/shard_map/ppermute | solution.py:508
  170.6 11.8 %collective-permute-start.55 = (bf16[192,384]{1,0:T(8,128)(2,1)S(1)}, bf16[192,384]{1,0:T(8,128)(2,1)S(1)}, u32[]{:S(2)}, u32[]{:S(2)}) collective-permute-start(bf16[192,384]{1,0:T(8,128)(2,1)S(1)} %fusion.43), channel_id=1, source_target_pairs={{0,16},{4,20},{8,24},{12,28},{16,0},{20,4},{24,8},{28,12},{1,17},{... | collective-permute-start | bytes 442376 | tf_op jit(solution)/shard_map/ppermute | solution.py:508
  182.5 8.8 %collective-permute-start.56 = (bf16[192,384]{1,0:T(8,128)(2,1)S(1)}, bf16[192,384]{1,0:T(8,128)(2,1)S(1)}, u32[]{:S(2)}, u32[]{:S(2)}) collective-permute-start(bf16[192,384]{1,0:T(8,128)(2,1)S(1)} %add_convert_fusion.2), channel_id=1, source_target_pairs={{0,8},{4,12},{8,0},{12,4},{16,24},{20,28},{24,16},{28,20},{1,9},{5... | collective-permute-start | bytes 442376 | tf_op jit(solution)/shard_map/ppermute | solution.py:508
  183.0 12.0 %collective-permute-start.46 = (bf16[192,384]{1,0:T(8,128)(2,1)S(1)}, bf16[192,384]{1,0:T(8,128)(2,1)S(1)}, u32[]{:S(2)}, u32[]{:S(2)}) collective-permute-start(bf16[192,384]{1,0:T(8,128)(2,1)S(1)} %add_convert_fusion.5), channel_id=1, source_target_pairs={{0,8},{4,12},{8,0},{12,4},{16,24},{20,28},{24,16},{28,20},{1,9},{5... | collective-permute-start | bytes 442376 | tf_op jit(solution)/shard_map/ppermute | solution.py:508
  188.6 9.4 %collective-permute-start.47 = (bf16[192,384]{1,0:T(8,128)(2,1)S(1)}, bf16[192,384]{1,0:T(8,128)(2,1)S(1)}, u32[]{:S(2)}, u32[]{:S(2)}) collective-permute-start(bf16[192,384]{1,0:T(8,128)(2,1)S(1)} %add_convert_fusion.4), channel_id=1, source_target_pairs={{0,8},{4,12},{8,0},{12,4},{16,24},{20,28},{24,16},{28,20},{1,9},{5... | collective-permute-start | bytes 442376 | tf_op jit(solution)/shard_map/ppermute | solution.py:508
  188.7 11.7 %collective-permute-start.49 = (bf16[384,384]{1,0:T(8,128)(2,1)S(1)}, bf16[384,384]{1,0:T(8,128)(2,1)S(1)}, u32[]{:S(2)}, u32[]{:S(2)}) collective-permute-start(bf16[384,384]{1,0:T(8,128)(2,1)S(1)} %select_convert_fusion.2), channel_id=1, source_target_pairs={{0,4},{4,0},{8,12},{12,8},{16,20},{20,16},{24,28},{28,24},{1,5},{5... | collective-permute-start | bytes 884744 | tf_op jit(solution)/shard_map/ppermute | solution.py:508
  190.2 9.4 %collective-permute-start.48 = (bf16[192,384]{1,0:T(8,128)(2,1)S(1)}, bf16[192,384]{1,0:T(8,128)(2,1)S(1)}, u32[]{:S(2)}, u32[]{:S(2)}) collective-permute-start(bf16[192,384]{1,0:T(8,128)(2,1)S(1)} %fusion.42), channel_id=1, source_target_pairs={{0,16},{4,20},{8,24},{12,28},{16,0},{20,4},{24,8},{28,12},{1,17},{... | collective-permute-start | bytes 442376 | tf_op jit(solution)/shard_map/ppermute | solution.py:508
  191.3 14.9 %collective-permute-start.45 = (bf16[1248,128]{1,0:T(8,128)(2,1)S(1)}, bf16[1248,128]{1,0:T(8,128)(2,1)S(1)}, u32[]{:S(2)}, u32[]{:S(2)}) collective-permute-start(bf16[1248,128]{1,0:T(8,128)(2,1)S(1)} %pad_maximum_fusion.6), channel_id=1, source_target_pairs={{0,4},{4,0},{8,12},{12,8},{16,20},{20,16},{24,28},{28,24},{1,5},{5... | collective-permute-start | bytes 958472 | tf_op jit(solution)/shard_map/ppermute | solution.py:508
  195.0 16.8 %collective-permute-start.57 = (bf16[384,384]{1,0:T(8,128)(2,1)S(1)}, bf16[384,384]{1,0:T(8,128)(2,1)S(1)}, u32[]{:S(2)}, u32[]{:S(2)}) collective-permute-start(bf16[384,384]{1,0:T(8,128)(2,1)S(1)} %maximum_select_fusion.13), channel_id=1, source_target_pairs={{0,4},{4,0},{8,12},{12,8},{16,20},{20,16},{24,28},{28,24},{1,5},{5... | collective-permute-start | bytes 884744 | tf_op jit(solution)/shard_map/ppermute | solution.py:508
  198.0 20.1 %collective-permute-start.53 = (bf16[384,384]{1,0:T(8,128)(2,1)S(1)}, bf16[384,384]{1,0:T(8,128)(2,1)S(1)}, u32[]{:S(2)}, u32[]{:S(2)}) collective-permute-start(bf16[384,384]{1,0:T(8,128)(2,1)S(1)} %maximum_select_fusion.16), channel_id=1, source_target_pairs={{0,4},{4,0},{8,12},{12,8},{16,20},{20,16},{24,28},{28,24},{1,5},{5... | collective-permute-start | bytes 884744 | tf_op jit(solution)/shard_map/ppermute | solution.py:508
  199.6 24.8 %collective-permute-start.64 = (bf16[384,384]{1,0:T(8,128)(2,1)S(1)}, bf16[384,384]{1,0:T(8,128)(2,1)S(1)}, u32[]{:S(2)}, u32[]{:S(2)}) collective-permute-start(bf16[384,384]{1,0:T(8,128)(2,1)S(1)} %maximum_select_fusion.15), channel_id=1, source_target_pairs={{0,4},{4,0},{8,12},{12,8},{16,20},{20,16},{24,28},{28,24},{1,5},{5... | collective-permute-start | bytes 884744 | tf_op jit(solution)/shard_map/ppermute | solution.py:508
  205.9 20.7 %collective-permute-start.52 = (bf16[384,384]{1,0:T(8,128)(2,1)S(1)}, bf16[384,384]{1,0:T(8,128)(2,1)S(1)}, u32[]{:S(2)}, u32[]{:S(2)}) collective-permute-start(bf16[384,384]{1,0:T(8,128)(2,1)S(1)} %fusion.44), channel_id=1, source_target_pairs={{0,16},{4,20},{8,24},{12,28},{16,0},{20,4},{24,8},{28,12},{1,17},{... | collective-permute-start | bytes 884744 | tf_op jit(solution)/shard_map/ppermute | solution.py:508
  206.2 24.1 %collective-permute-start.61 = (bf16[384,384]{1,0:T(8,128)(2,1)S(1)}, bf16[384,384]{1,0:T(8,128)(2,1)S(1)}, u32[]{:S(2)}, u32[]{:S(2)}) collective-permute-start(bf16[384,384]{1,0:T(8,128)(2,1)S(1)} %maximum_select_fusion.14), channel_id=1, source_target_pairs={{0,4},{4,0},{8,12},{12,8},{16,20},{20,16},{24,28},{28,24},{1,5},{5... | collective-permute-start | bytes 884744 | tf_op jit(solution)/shard_map/ppermute | solution.py:508
  211.8 19.0 %collective-permute-start.51 = (bf16[1248,128]{1,0:T(8,128)(2,1)S(1)}, bf16[1248,128]{1,0:T(8,128)(2,1)S(1)}, u32[]{:S(2)}, u32[]{:S(2)}) collective-permute-start(bf16[1248,128]{1,0:T(8,128)(2,1)S(1)} %pad_maximum_fusion.7), channel_id=1, source_target_pairs={{0,8},{4,12},{8,0},{12,4},{16,24},{20,28},{24,16},{28,20},{1,9},{5... | collective-permute-start | bytes 958472 | tf_op jit(solution)/shard_map/ppermute | solution.py:508
  226.8 6.8 %collective-permute-start.58 = (bf16[384,384]{1,0:T(8,128)(2,1)S(1)}, bf16[384,384]{1,0:T(8,128)(2,1)S(1)}, u32[]{:S(2)}, u32[]{:S(2)}) collective-permute-start(bf16[384,384]{1,0:T(8,128)(2,1)S(1)} %add_convert_fusion.1), channel_id=1, source_target_pairs={{0,4},{4,0},{8,12},{12,8},{16,20},{20,16},{24,28},{28,24},{1,5},{5... | collective-permute-start | bytes 884744 | tf_op jit(solution)/shard_map/ppermute | solution.py:508
  231.0 17.8 %collective-permute-start.54 = (bf16[1248,128]{1,0:T(8,128)(2,1)S(1)}, bf16[1248,128]{1,0:T(8,128)(2,1)S(1)}, u32[]{:S(2)}, u32[]{:S(2)}) collective-permute-start(bf16[1248,128]{1,0:T(8,128)(2,1)S(1)} %pad_maximum_fusion.8), channel_id=1, source_target_pairs={{0,16},{4,20},{8,24},{12,28},{16,0},{20,4},{24,8},{28,12},{1,17},{... | collective-permute-start | bytes 958472 | tf_op jit(solution)/shard_map/ppermute | solution.py:508
  233.8 20.7 %collective-permute-start.59 = (bf16[768,384]{1,0:T(8,128)(2,1)S(1)}, bf16[768,384]{1,0:T(8,128)(2,1)S(1)}, u32[]{:S(2)}, u32[]{:S(2)}) collective-permute-start(bf16[768,384]{1,0:T(8,128)(2,1)S(1)} %maximum_select_fusion.8), channel_id=1, source_target_pairs={{0,8},{4,12},{8,0},{12,4},{16,24},{20,28},{24,16},{28,20},{1,9},{5... | collective-permute-start | bytes 1769480 | tf_op jit(solution)/shard_map/ppermute | solution.py:508
  236.0 21.2 %collective-permute-start.63 = (bf16[384,768]{1,0:T(8,128)(2,1)S(1)}, bf16[384,768]{1,0:T(8,128)(2,1)S(1)}, u32[]{:S(2)}, u32[]{:S(2)}) collective-permute-start(bf16[384,768]{1,0:T(8,128)(2,1)S(1)} %maximum_select_fusion.10), channel_id=1, source_target_pairs={{0,2},{1,3},{2,0},{3,1},{4,6},{5,7},{6,4},{7,5},{8,10},{9,11},{10,... | collective-permute-start | bytes 1769480 | tf_op jit(solution)/shard_map/ppermute | solution.py:508
  (38 other events, 272.2 us)

commit v5 on v4

--- a/solution.py
+++ b/solution.py
@@ -12,17 +12,17 @@
 CHUNKS = 8
 F32 = jnp.float32
 LOW = jnp.bfloat16
-KINDS = {"I": "y", "U": "x", "Q": "z", "P": "x", "N": "y"}
+KINDS = {"I": "z", "U": "W", "Q": "z", "P": "x", "N": "x"}
 ORDER = (
-    "+F0", "+F1", "-F0", "-F1", "+U", "+I", "Kback", "-U", "-I", "+Q",
-    "+U", "+P", "+I", "+N", "-Q", "+Q", "-P", "+P", "-N", "-U",
-    "+E", "-I", "+N", "-E", "Kt4", "-P", "-N", "-Q", "+P", "+sm",
-    "+U", "-sm", "+Q", "+N", "+I", "-U", "-P", "+U", "+P", "-I",
-    "+sm", "-N", "+I", "-Q", "-P", "-U", "+Q", "+U", "+P", "-sm",
-    "-I", "+sm", "+I", "-U", "-Q", "+N", "+Q", "-P", "-I", "+U",
-    "-sm", "-N", "+sm", "+I", "+P", "-U", "+N", "-Q", "-sm", "+Q",
-    "-I", "-P", "+sm", "+P", "-N", "+N", "-Q", "+Q", "-P", "-N",
-    "+N", "-sm", "-N", "-Q",
+    "+F0", "+F1", "-F0", "-F1", "+I", "+U", "Kback", "-I", "-U", "+P",
+    "+Q", "+U", "+I", "-P", "+N", "+P", "-Q", "+Q", "-N", "-U",
+    "+E", "-I", "+N", "-E", "-P", "+P", "+I", "Kt4", "-P", "-N",
+    "-Q", "-I", "+Q", "+P", "+U", "+I", "+sm", "-P", "-sm", "+P",
+    "+N", "-U", "+sm", "-Q", "-I", "+Q", "+U", "-N", "+I", "-P",
+    "-sm", "+P", "-Q", "+sm", "+N", "-I", "+Q", "-P", "-sm", "+P",
+    "-U", "-N", "+sm", "+I", "+N", "-sm", "-P", "+U", "+P", "-Q",
+    "+Q", "-I", "-P", "+sm", "+P", "-N", "+N", "-U", "-Q", "+Q",
+    "-sm", "-N", "+N", "-P", "-N", "-Q",
 )
 
 
@@ -413,8 +413,8 @@
     own_part, far_part, (ga_ref, gb_ref), weights = refs[16:20], refs[20:24], refs[24:26], refs[26:34]
     zpre_ref, qg_ref, qb_ref, kg_ref, wz_ref, pre_ref, keep_ref, al_ref, de_ref = refs[34:43]
     y_ref, direct_ref, gg_ref, pair_keep_ref, pair_send_ref, ng_ref = refs[43:49]
-    packs, outs = refs[49:53], refs[53:60]
-    mg_ref, p_ref, qk_ref, m0_ref, full_ref, hidden_ref = refs[60:]
+    packs, outs = refs[49:53], refs[53:59]
+    mg_ref, p_ref, qk_ref, m0_ref, full_ref, hidden_ref, dz_ref = refs[59:]
     blend_back(
         offs_ref, x_ref, cot_ref, blended_ref, s0_ref, s1_ref, o0_ref, o1_ref, hpre_ref, gate_ref,
         mixed_ref, gain_ref, wu_ref, whid_ref, y_ref, direct_ref, hidden_ref, m0_ref, gg_ref,
@@ -427,8 +427,19 @@
         )
     third_pass(
         rows, zpre_ref, probs_ref, p_ref, qg_ref, qb_ref, kg_ref, wz_ref, mixed_ref, m0_ref,
-        mg_ref, pre_ref, keep_ref, al_ref, de_ref, *outs, qk_ref,
-    )
+        mg_ref, pre_ref, keep_ref, al_ref, de_ref, outs[0], dz_ref, *outs[1:], qk_ref,
+    )
+    width, zd = dz_ref.shape
+    blocks, cols = width // (2 * zd), width // 4
+    share = cols // blocks
+    for r in range(4):
+        pack_ref = (pair_keep_ref, pair_send_ref)[r % 2]
+        for c in range(blocks):
+            rows_at = pl.ds(pl.multiple_of(offs_ref[r] + c * share, 64), share)
+            pack_ref[r // 2, 4 * cols : 4 * cols + share, c * zd : (c + 1) * zd] = dz_ref[
+                rows_at, :
+            ].astype(pack_ref.dtype)
+        pack_ref[r // 2, 4 * cols + share :, :] = jnp.zeros((share, width // 2), pack_ref.dtype)
 
 
 def fourth_pass(rows, pg_ref, normed_ref, im_ref, iv_ref, near_ref, far_ref, keep_ref, flag_ref, al_ref, de_ref, be_ref, eta_ref, om_ref, n0_ref, x_ref, g_ref, direct_ref, gg_ref, qk_ref, xg_ref, sums_ref, dec_ref, drv_ref, ng_ref):
@@ -583,18 +594,16 @@
     return got
 
 
-def everywhere(coarse, fine):
-    at, end = coarse.shape[0], coarse.shape[0] + fine.shape[0]
+def everywhere(v):
+    size = v.shape[0]
     for axis in ("tensor", "dp"):
         for b in range(lax.axis_size(axis).bit_length() - 1):
-            coarse, high = rounded(coarse), rounded(fine)
-            low = rounded(fine - high)
-            packed = jnp.concatenate([coarse, high, low], 0).astype(LOW)
-            got = yield axis, 1 << b, packed
+            high = rounded(v)
+            low = rounded(v - high)
+            got = yield axis, 1 << b, jnp.concatenate([high, low], 0).astype(LOW)
             got = got.astype(F32)
-            coarse = coarse + got[:at]
-            fine = (high + low) + (got[at:end] + got[end:])
-    return coarse, fine
+            v = (high + low) + (got[:size] + got[size:])
+    return v
 
 
 class Pump:
@@ -768,26 +777,26 @@
     own_part = values((w_value, w_reset, beside[0], beside[1]))
     united0 = pump.gate(own_part[3])
     other_r = pump.gate(other_r)
-    over_g = pump.gate(over_g)
+    over_g, over_i = pump.gate(over_g), pump.gate(over_i)
+    over_g, over_i, half_o = pump.gate(over_g), pump.gate(over_i), pump.gate(half_o)
+    over_o = swap(half_o, "tensor", 2)
     other_g = swap(over_g, "dp", 2)
-    over_o = swap(pump.gate(half_o), "tensor", 2)
-    over_i = pump.gate(over_i)
     other_i = swap(over_i, "dp", 1)
-    over_o = pump.gate(over_o)
-    other_o = swap(over_o, "dp", 1)
     other_v, other_r = pump.gate(other_v), pump.gate(other_r)
     full_v = pump.gate(joined(over_v, other_v, firsts[1]))
     both_v = swap(full_v, "tensor", 1)
     full_r = pump.gate(joined(over_r, other_r, firsts[1]))
     both_r = swap(full_r, "tensor", 1)
-    other_g = pump.gate(other_g)
-    near_g = pump.gate(jnp.stack([w_join, joined(over_g, other_g, firsts[2])]))
-    beside_g = swap(near_g, "tensor", 1)
     both_v, both_r = pump.gate(both_v), pump.gate(both_r)
     full_v = pump.gate(full_v)
     far_part = values((full_v, full_r, both_v, both_r))
     united1 = pump.gate(far_part[3])
+    over_o = pump.gate(over_o)
     other_i = pump.gate(other_i)
+    other_o = swap(over_o, "dp", 1)
+    other_g = pump.gate(other_g)
+    near_g = pump.gate(jnp.stack([w_join, joined(over_g, other_g, firsts[2])]))
+    beside_g = swap(near_g, "tensor", 1)
     full_i = pump.gate(joined(over_i, other_i, firsts[1]))
     both_i = swap(full_i, "tensor", 1)
     beside_g = pump.gate(beside_g)
@@ -821,7 +830,8 @@
     ffn1 = ffn_of((full_i, both_i, full_o, both_o))
     pump.add("F0", one_swap("tensor", 1, ffn0[3]))
     pump.add("F1", one_swap("tensor", 1, ffn1[3]))
-    own = (2, 4 * cols, width // 2)
+    share = cols * zd // (width // 2)
+    own = (2, 4 * cols + 2 * share, width // 2)
     held = {}
 
     def run_back():
@@ -829,22 +839,22 @@
             functools.partial(back_pass, rows),
             [(wide, LOW), (wide, F32), ((1, width), F32), (own, LOW), (own, LOW), (wide, F32),
              *[((2, 2 * width, units), LOW), ((2, width, units), LOW)] * 2,
-             (slabs, F32), ((width, zd), F32), ((8, zd), F32), (chunked, F32), (chunked, F32), (finals, F32), (finals, F32)],
+             (slabs, F32), ((8, zd), F32), (chunked, F32), (chunked, F32), (finals, F32), (finals, F32)],
             (offs, x, cot, pump.gate(blended), ffn1[1], back0, ffn0[0], ffn1[0], hidden_pre, gate,
              mixed_low, g2, w_update, whid, normed_low, probs, *kept_parts[0], *kept_parts[1], *wg,
              wv[0], wr[0], wv[1], wr[1], wv[2], wr[2], wv[3], wr[3],
              z_pre, qg, qb, kg, w_z, pre, keep, alpha_raw, delta_raw),
             (4 * width + 28 * units) * mat,
             [vm(wide), vm((tokens, STRETCH)), vm((2, tokens, zd)), vm(wide), vm((width, width)),
-             pltpu.VMEM(wide, LOW)],
+             pltpu.VMEM(wide, LOW), vm((width, zd))],
             smem=(0,),
         )
         held["bb"], held["v"] = outs[:5], outs[5:10]
         held["t3"] = list(outs[10:])
-        pump.token, held["t3"][5] = tied((pump.token, held["t3"][5]))
+        pump.token, held["t3"][4] = tied((pump.token, held["t3"][4]))
 
     def send_back():
-        back = pump.gate(jnp.concatenate([held["t3"][5], held["t3"][6]], 0))
+        back = pump.gate(jnp.concatenate([held["t3"][4], held["t3"][5]], 0))
         held["back"] = shift(back, -1), shift(back, -2)
 
     def take_back():
@@ -855,15 +865,15 @@
         held["t4"] = call(
             functools.partial(fourth_pass, rows),
             [(wide, LOW), ((2 * dims + 8, width), F32)],
-            (t3[0], normed, t3[3], t3[4], *held["back"], keep, unbroken(1), alpha_raw,
+            (t3[0], normed, t3[2], t3[3], *held["back"], keep, unbroken(1), alpha_raw,
              delta_raw, ema_beta, ema_eta, om, held["v"][0], x, g1, held["bb"][1],
-             held["bb"][2], t3[2]),
+             held["bb"][2], t3[1]),
             2 * ema,
             [vm(tab), vm(tab), vm(slabs)],
         )
         sums = pump.gate(held["t4"][1])
         sums = jnp.concatenate([sums[:, at : at + LANES] for at in range(0, width, LANES)], 0)
-        pump.add("sm", everywhere(held["t3"][1], sums))
+        pump.add("sm", everywhere(sums))
 
     def packs_of(name):
         if name in "IU":
@@ -877,8 +887,18 @@
         both = kept.astype(F32) + got.astype(F32)
         return both[0], both[1]
 
+    def with_shared():
+        low = yield from reduction(KINDS["P"], packs_of("P"), firsts)
+        v = jnp.concatenate([low[: 2 * cols], low[4 * cols : 4 * cols + share]], 0)
+        for bit, first in ((1, first_core), (2, first_chip)):
+            got = yield "tensor", bit, v
+            v = joined(v, got, first)
+        return low[2 * cols : 4 * cols], v.reshape(4, 2 * cols + share, width // 2)
+
     def add_flow(name):
-        pump.add(name, reduction(KINDS[name], packs_of(name), firsts))
+        pump.add(
+            name, with_shared() if name == "P" else reduction(KINDS[name], packs_of(name), firsts)
+        )
 
     kernels = {
         "back": run_back,
@@ -898,8 +918,7 @@
             pump.finish(name)
     pump.drain()
     output, input_grad = held["bb"][0], held["t4"][0]
-    dz_sum, sums = pump.done["sm"]
-    sums = from_slabs(sums, 2 * dims + 8)
+    sums = from_slabs(pump.done["sm"], 2 * dims + 8)
     pair_sum, gate_sum, value_sum, in_sum, fout_sum = (pump.done[n] for n in "PQNIU")
 
     alpha, sigma = jax.nn.sigmoid(alpha_raw), jax.nn.sigmoid(delta_raw)
@@ -907,9 +926,11 @@
     drive_grad = ema_eta * with_mu
     decay_grad = ema_eta * (alpha * ema_beta) * with_nu
     at = 2 * dims
-    quarter = side_by_side(pair_sum[: 2 * cols])
-    update_grad = joined(quarter, swap(quarter, "tensor", 1), first_core)
-    update_grad = joined(update_grad, swap(update_grad, "tensor", 2), first_chip)
+    hidden_sum, shared = pair_sum
+    update_grad = jnp.concatenate([side_by_side(v[: 2 * cols]) for v in shared], 0)
+    dz_sum = jnp.concatenate(
+        [v[2 * cols :, at : at + zd] for v in shared for at in range(0, width // 2, zd)], 0
+    )
     return (
         output.reshape(layer_input.shape),
         input_grad.reshape(layer_input.shape),
@@ -919,14 +940,14 @@
         alpha * drive_grad,
         (alpha * ema_beta) * with_mu,
         sums[at],
-        dz_sum,
+        dz_sum.astype(F32),
         sums[at + 3, :zd],
         sums[at + 3, zd : 2 * zd],
         sums[at + 3, 2 * zd : 3 * zd],
         value_sum.astype(F32),
         gate_sum[:width].astype(F32),
         update_grad.astype(F32),
-        side_by_side(pair_sum[2 * cols :]).astype(F32),
+        side_by_side(hidden_sum).astype(F32),
         side_by_side(gate_sum[width:]).astype(F32),
         sums[at + 2],
         in_sum.astype(F32),

time: 262 us -> 240 us (0.916)
  waiting for transfers between devices: 126 us -> 104 us
    ppermute x61 -> x60, waiting for transfers between devices: 120 us -> 95.4 us  [swap(): return lax.ppermute(x, axis, [(i, i ^ bit) for i in range(size)])]
    ppermute x61 -> x60, starting transfers between devices: 61.6 us -> 59.1 us  [swap(): return lax.ppermute(x, axis, [(i, i ^ bit) for i in range(size)])]
  transfers between devices with their start and end apart: 65 -> 64, of which waited for: 37 -> 31; matrix products, arithmetic and copies ran while one was open for 7% -> 8% of each run, Pallas kernels for 16% -> 17%
where the time goes in v5:
time: 240 us; the launch traced here: 237 us
  waiting for transfers between devices  104 us (43%)
  starting transfers between devices  66.5 us (28%)
  Pallas kernels  40.5 us (17%)
  other arithmetic  20.7 us (9%)
  local copies, waits for them, and re-layouts  2.98 us (1%)
  between operations  2.49 us (1%)
    ppermute x60, waiting for transfers between devices, swap(): return lax.ppermute(x, axis, [(i, i ^ bit) for i in range(size)])  95.4 us
    ppermute x60, starting transfers between devices, swap(): return lax.ppermute(x, axis, [(i, i ^ bit) for i in range(size)])  59.1 us
    pallas_call x9, Pallas kernels, call(): pl.pallas_call(kernel, out_shape=outs, in_specs=specs, out_specs=[pl.Bloc...  40.5 us
    ppermute x4, waiting for transfers between devices, shift(): lax.ppermute(x, 'tensor', [(i, i + by) for i in range(size) if 0 <= i + b...  8.77 us
    ppermute x4, starting transfers between devices, shift(): lax.ppermute(x, 'tensor', [(i, i + by) for i in range(size) if 0 <= i + b...  7.36 us
  transfers between devices with their start and end apart: 64, of which 31 were waited for; matrix products, arithmetic and copies ran while one was open for 8% of the time, Pallas kernels for 17%

profile of v5, /device:TPU:0, one launch (start us, length us, event | category | flops | bytes accessed | tf_op | source)
XLA Modules:
  0.0 237.3 jit_solution(6747644400715363088)
XLA Ops:
  3.0 3.0 %collective-permute-start.6 = (bf16[384,384]{1,0:T(8,128)(2,1)S(1)}, bf16[384,384]{1,0:T(8,128)(2,1)S(1)}, u32[]{:S(2)}, u32[]{:S(2)}) collective-permute-start(bf16[384,384]{1,0:T(8,128)(2,1)S(1)} %slice_select_fusion.3), channel_id=1, source_target_pairs={{0,2},{1,3},{2,0},{3,1},{4,6},{5,7},{6,4},{7,5},{8,10},{9,11},{10,... | collective-permute-start | bytes 884744 | tf_op jit(solution)/shard_map/ppermute | solution.py:519
  8.6 3.0 %shard_map.356 = (f32[1536,128]{1,0:T(8,128)S(1)}, bf16[256,768]{1,0:T(8,128)(2,1)S(1)}, f32[256,768]{1,0:T(8,128)S(1)}, f32[32,768]{1,0:T(8,128)S(1)}) custom-call(bf16[256,768]{1,0:T(8,128)(2,1)S(1)} %bitcast.51, f32[1,768]{1,0:T(1,128)S(1)} %broadcast_in_dim.34.g_ref, f32[16,768]{1,0:T(8,128)S(1)} %copy-done.4, f32[16,768]{1,0:T(8,128)S(1)} %copy-done.5, ...), custom_call_target="tpu_custom_call" | custom-call | flops 25165824 | bytes 2739200 | tf_op jit(solution)/shard_map/pallas_call | solution.py:71
  11.6 1.8 collective-permute-start.4
  13.4 3.0 %collective-permute-start.7 = (f32[32,768]{1,0:T(8,128)S(1)}, f32[32,768]{1,0:T(8,128)S(1)}, u32[]{:S(2)}, u32[]{:S(2)}) collective-permute-start(f32[32,768]{1,0:T(8,128)S(1)} %get-tuple-element.321), channel_id=1, source_target_pairs={{0,2},{1,3},{4,6},{5,7},{8,10},{9,11},{12,14},{13,15},{16,18},{17,... | collective-permute-start | bytes 294920 | tf_op jit(solution)/shard_map/ppermute | solution.py:524
  16.5 3.3 %collective-permute-done.5 = bf16[384,384]{1,0:T(8,128)(2,1)S(1)} collective-permute-done((bf16[384,384]{1,0:T(8,128)(2,1)S(1)}, bf16[384,384]{1,0:T(8,128)(2,1)S(1)}, u32[]{:S(2)}, u32[]{:S(2)}) %collective-permute-start.5) | collective-permute-done | bytes 294944 | tf_op jit(solution)/shard_map/ppermute | solution.py:519
  19.7 2.1 collective-permute-done.7.f2_ref
  21.8 2.5 %collective-permute-start.10 = (bf16[288,768]{1,0:T(8,128)(2,1)S(1)}, bf16[288,768]{1,0:T(8,128)(2,1)S(1)}, u32[]{:S(2)}, u32[]{:S(2)}) collective-permute-start(bf16[288,768]{1,0:T(8,128)(2,1)S(1)} %slice_select_fusion), channel_id=1, source_target_pairs={{0,2},{1,3},{2,0},{3,1},{4,6},{5,7},{6,4},{7,5},{8,10},{9,11},{10,... | collective-permute-start | bytes 1327112 | tf_op jit(solution)/shard_map/ppermute | solution.py:519
  26.8 4.6 %shard_map.357 = (f32[1536,128]{1,0:T(8,128)S(1)}, bf16[256,768]{1,0:T(8,128)(2,1)S(1)}, f32[256,128]{1,0:T(8,128)S(1)}, f32[256,768]{1,0:T(8,128)S(1)}, f32[256,128]{1,0:T(8,128)S(1)}) custom-call(f32[1536,128]{1,0:T(8,128)S(1)} %get-tuple-element.317.normed_ref, f32[256,768]{1,0:T(8,128)S(1)} %get-tuple-element.318.init_ref, ...), custom_call_target="tpu_custom_call" | custom-call | flops 327155712 | bytes 5838336 | tf_op jit(solution)/shard_map/pallas_call | solution.py:71
  31.4 2.9 %collective-permute-done.8 = bf16[384,384]{1,0:T(8,128)(2,1)S(1)} collective-permute-done((bf16[384,384]{1,0:T(8,128)(2,1)S(1)}, bf16[384,384]{1,0:T(8,128)(2,1)S(1)}, u32[]{:S(2)}, u32[]{:S(2)}) %collective-permute-start.8) | collective-permute-done | bytes 294944 | tf_op jit(solution)/shard_map/ppermute | solution.py:519
  35.4 4.1 %collective-permute-done.11 = bf16[384,384]{1,0:T(8,128)(2,1)S(1)} collective-permute-done((bf16[384,384]{1,0:T(8,128)(2,1)S(1)}, bf16[384,384]{1,0:T(8,128)(2,1)S(1)}, u32[]{:S(2)}, u32[]{:S(2)}) %collective-permute-start.11) | collective-permute-done | bytes 294944 | tf_op jit(solution)/shard_map/ppermute | solution.py:519
  39.5 1.6 collective-permute-done.9
  42.1 1.6 collective-permute-start.14
  43.7 1.7 collective-permute-start.16
  48.1 4.4 %collective-permute-done.16 = bf16[192,768]{1,0:T(8,128)(2,1)S(1)} collective-permute-done((bf16[192,768]{1,0:T(8,128)(2,1)S(1)}, bf16[192,768]{1,0:T(8,128)(2,1)S(1)}, u32[]{:S(2)}, u32[]{:S(2)}) %collective-permute-start.16) | collective-permute-done | bytes 294944 | tf_op jit(solution)/shard_map/ppermute | solution.py:519
  58.6 2.2 shard_map.360
  60.8 2.7 %shard_map.361 = (f32[256,768]{1,0:T(8,128)S(1)}, f32[256,768]{1,0:T(8,128)S(1)}, bf16[1536,384]{1,0:T(8,128)(2,1)S(1)}, bf16[1536,384]{1,0:T(8,128)(2,1)S(1)}) custom-call(bf16[256,768]{1,0:T(8,128)(2,1)S(1)} %get-tuple-element.393.second_ref, bf16[256,768]{1,0:T(8,128)(2,1)S(1)} %bitcast.55, bf16[768,384]{1,0:T(8,128)(2,1)S(1)} %copy-done.8, ...), custom_call_target="tpu_custom_call" | custom-call | flops 1811939328 | bytes 7077888 | tf_op jit(solution)/shard_map/pallas_call | solution.py:71
  64.6 2.0 collective-permute-done.20.ob_ref
  66.7 2.7 %shard_map.362 = (f32[256,768]{1,0:T(8,128)S(1)}, f32[256,768]{1,0:T(8,128)S(1)}, bf16[1536,384]{1,0:T(8,128)(2,1)S(1)}, bf16[1536,384]{1,0:T(8,128)(2,1)S(1)}) custom-call(bf16[256,768]{1,0:T(8,128)(2,1)S(1)} %get-tuple-element.393.second_ref, bf16[256,768]{1,0:T(8,128)(2,1)S(1)} %bitcast.56, bf16[768,384]{1,0:T(8,128)(2,1)S(1)} %maximum_select_fusion.7.ia_ref, ...), custom_call_target="tpu_custom_call" | custom-call | flops 1811939328 | bytes 7077888 | tf_op jit(solution)/shard_map/pallas_call | solution.py:71
  70.0 2.3 collective-permute-done.21
  72.7 1.6 collective-permute-start.24
  74.3 1.7 collective-permute-start.23
  76.3 14.8 %shard_map.363 = (bf16[256,768]{1,0:T(8,128)(2,1)}, f32[256,768]{1,0:T(8,128)S(1)}, f32[1,768]{1,0:T(1,128)S(1)}, bf16[2,896,384]{2,1,0:T(8,128)(2,1)S(1)}, bf16...) custom-call(s32[4]{0:T(128)S(1)} %xor_multiply_fusion.offs_ref.refs_, ...), custom_call_target="tpu_custom_call" | custom-call | flops 5435817984 | bytes 39038480 | tf_op jit(solution)/shard_map/pallas_call | solution.py:71
  92.9 4.7 %collective-permute-done.26 = bf16[2,896,384]{2,1,0:T(8,128)(2,1)S(1)} collective-permute-done((bf16[2,896,384]{2,1,0:T(8,128)(2,1)S(1)}, bf16[2,896,384]{2,1,0:T(8,128)(2,1)S(1)}, u32[]{:S(2)}, u32[]{:S(2)}) %collective-permute-start.26) | collective-permute-done | bytes 1376288 | tf_op jit(solution)/shard_map/ppermute | solution.py:519
  106.0 6.7 %collective-permute-done.31.far_ref = f32[64,768]{1,0:T(8,128)S(1)} collective-permute-done((f32[64,768]{1,0:T(8,128)S(1)}, f32[64,768]{1,0:T(8,128)S(1)}, u32[]{:S(2)}, u32[]{:S(2)}) %collective-permute-start.31) | collective-permute-done | bytes 196640 | tf_op jit(solution)/shard_map/ppermute | solution.py:524
  112.6 4.1 %collective-permute-done.32 = bf16[896,384]{1,0:T(8,128)(2,1)S(1)} collective-permute-done((bf16[896,384]{1,0:T(8,128)(2,1)S(1)}, bf16[896,384]{1,0:T(8,128)(2,1)S(1)}, u32[]{:S(2)}, u32[]{:S(2)}) %collective-permute-start.32) | collective-permute-done | bytes 688160 | tf_op jit(solution)/shard_map/ppermute | solution.py:519
  117.3 8.5 %shard_map.364 = (bf16[256,768]{1,0:T(8,128)(2,1)}, f32[40,768]{1,0:T(8,128)S(1)}) custom-call(f32[1536,128]{1,0:T(8,128)S(1)} %get-tuple-element.439.pg_ref, f32[1536,128]{1,0:T(8,128)S(1)} %get-tuple-element.317.normed_ref, f32[256,768]{1,0:T(8,128)S(1)} %get-tuple-element.440.im_ref, f32[256,768]{1,0:T(8,128)S(1)} %get-tuple-element.441.iv_ref, ...), custom_call_target="tpu_custom_call" | custom-call | flops 50331648 | bytes 6363136 | tf_op jit(solution)/shard_map/pallas_call | solution.py:71
  127.6 1.7 collective-permute-done.35
  130.1 1.8 collective-permute-done.33
  134.8 2.6 %collective-permute-start.42 = (bf16[192,384]{1,0:T(8,128)(2,1)S(1)}, bf16[192,384]{1,0:T(8,128)(2,1)S(1)}, u32[]{:S(2)}, u32[]{:S(2)}) collective-permute-start(bf16[192,384]{1,0:T(8,128)(2,1)S(1)} %fusion.36), channel_id=1, source_target_pairs={{0,16},{4,20},{8,24},{12,28},{16,0},{20,4},{24,8},{28,12},{1,17},{... | collective-permute-start | bytes 442376 | tf_op jit(solution)/shard_map/ppermute | solution.py:519
  138.9 2.1 collective-permute-start.41
  143.2 7.1 %collective-permute-done.43 = bf16[768,384]{1,0:T(8,128)(2,1)S(1)} collective-permute-done((bf16[768,384]{1,0:T(8,128)(2,1)S(1)}, bf16[768,384]{1,0:T(8,128)(2,1)S(1)}, u32[]{:S(2)}, u32[]{:S(2)}) %collective-permute-start.43) | collective-permute-done | bytes 589856 | tf_op jit(solution)/shard_map/ppermute | solution.py:519
  150.6 2.7 %collective-permute-start.50 = (bf16[384,384]{1,0:T(8,128)(2,1)S(1)}, bf16[384,384]{1,0:T(8,128)(2,1)S(1)}, u32[]{:S(2)}, u32[]{:S(2)}) collective-permute-start(bf16[384,384]{1,0:T(8,128)(2,1)S(1)} %fusion.12), channel_id=1, source_target_pairs={{0,16},{4,20},{8,24},{12,28},{16,0},{20,4},{24,8},{28,12},{1,17},{... | collective-permute-start | bytes 884744 | tf_op jit(solution)/shard_map/ppermute | solution.py:519
  153.3 3.3 %collective-permute-done.44 = bf16[384,384]{1,0:T(8,128)(2,1)S(1)} collective-permute-done((bf16[384,384]{1,0:T(8,128)(2,1)S(1)}, bf16[384,384]{1,0:T(8,128)(2,1)S(1)}, u32[]{:S(2)}, u32[]{:S(2)}) %collective-permute-start.44) | collective-permute-done | bytes 294944 | tf_op jit(solution)/shard_map/ppermute | solution.py:519
  158.9 1.6 collective-permute-start.47
  161.3 2.1 collective-permute-done.48
  163.5 1.6 collective-permute-start.62
  165.2 7.1 %collective-permute-done.49 = bf16[192,384]{1,0:T(8,128)(2,1)S(1)} collective-permute-done((bf16[192,384]{1,0:T(8,128)(2,1)S(1)}, bf16[192,384]{1,0:T(8,128)(2,1)S(1)}, u32[]{:S(2)}, u32[]{:S(2)}) %collective-permute-start.49) | collective-permute-done | bytes 147488 | tf_op jit(solution)/shard_map/ppermute | solution.py:519
  172.3 1.6 collective-permute-start.56
  174.8 2.5 %collective-permute-start.63 = (bf16[384,384]{1,0:T(8,128)(2,1)S(1)}, bf16[384,384]{1,0:T(8,128)(2,1)S(1)}, u32[]{:S(2)}, u32[]{:S(2)}) collective-permute-start(bf16[384,384]{1,0:T(8,128)(2,1)S(1)} %add_convert_fusion.2), channel_id=1, source_target_pairs={{0,8},{4,12},{8,0},{12,4},{16,24},{20,28},{24,16},{28,20},{1,9},{5... | collective-permute-start | bytes 884744 | tf_op jit(solution)/shard_map/ppermute | solution.py:519
  177.5 5.6 %collective-permute-done.56 = bf16[192,384]{1,0:T(8,128)(2,1)S(1)} collective-permute-done((bf16[192,384]{1,0:T(8,128)(2,1)S(1)}, bf16[192,384]{1,0:T(8,128)(2,1)S(1)}, u32[]{:S(2)}, u32[]{:S(2)}) %collective-permute-start.56) | collective-permute-done | bytes 147488 | tf_op jit(solution)/shard_map/ppermute | solution.py:519
  183.8 4.2 %collective-permute-done.46 = bf16[480,128]{1,0:T(8,128)(2,1)S(1)} collective-permute-done((bf16[480,128]{1,0:T(8,128)(2,1)S(1)}, bf16[480,128]{1,0:T(8,128)(2,1)S(1)}, u32[]{:S(2)}, u32[]{:S(2)}) %collective-permute-start.46) | collective-permute-done | bytes 122912 | tf_op jit(solution)/shard_map/ppermute | solution.py:519
  190.2 7.3 %collective-permute-done.57 = bf16[192,384]{1,0:T(8,128)(2,1)S(1)} collective-permute-done((bf16[192,384]{1,0:T(8,128)(2,1)S(1)}, bf16[192,384]{1,0:T(8,128)(2,1)S(1)}, u32[]{:S(2)}, u32[]{:S(2)}) %collective-permute-start.57) | collective-permute-done | bytes 147488 | tf_op jit(solution)/shard_map/ppermute | solution.py:519
  200.8 1.6 collective-permute-start.52
  205.5 4.6 %collective-permute-done.52 = bf16[480,128]{1,0:T(8,128)(2,1)S(1)} collective-permute-done((bf16[480,128]{1,0:T(8,128)(2,1)S(1)}, bf16[480,128]{1,0:T(8,128)(2,1)S(1)}, u32[]{:S(2)}, u32[]{:S(2)}) %collective-permute-start.52) | collective-permute-done | bytes 122912 | tf_op jit(solution)/shard_map/ppermute | solution.py:519
  211.0 1.9 collective-permute-done.60
  213.0 1.8 collective-permute-start.61
  218.2 9.5 %collective-permute-done.61 = bf16[768,384]{1,0:T(8,128)(2,1)S(1)} collective-permute-done((bf16[768,384]{1,0:T(8,128)(2,1)S(1)}, bf16[768,384]{1,0:T(8,128)(2,1)S(1)}, u32[]{:S(2)}, u32[]{:S(2)}) %collective-permute-start.61) | collective-permute-done | bytes 589856 | tf_op jit(solution)/shard_map/ppermute | solution.py:519
  230.3 3.5 %collective-permute-done.55 = bf16[896,384]{1,0:T(8,128)(2,1)S(1)} collective-permute-done((bf16[896,384]{1,0:T(8,128)(2,1)S(1)}, bf16[896,384]{1,0:T(8,128)(2,1)S(1)}, u32[]{:S(2)}, u32[]{:S(2)}) %collective-permute-start.55) | collective-permute-done | bytes 688160 | tf_op jit(solution)/shard_map/ppermute | solution.py:519
  (276 shorter events, 63.6 us)
Async XLA Ops:
  0.7 6.6 %collective-permute-start.3 = (bf16[768,384]{1,0:T(8,128)(2,1)}, bf16[768,384]{1,0:T(8,128)(2,1)S(1)}, u32[]{:S(2)}, u32[]{:S(2)}) collective-permute-start(bf16[768,384]{1,0:T(8,128)(2,1)} %refs_26_.1), channel_id=1, source_target_pairs={{0,1},{1,0},{2,3},{3,2},{4,5},{5,4},{6,7},{7,6},{8,9},{9,8},{10,11... | collective-permute-start | bytes 1769480 | tf_op jit(solution)/shard_map/ppermute | solution.py:519
  3.0 13.5 %collective-permute-start.6 = (bf16[384,384]{1,0:T(8,128)(2,1)S(1)}, bf16[384,384]{1,0:T(8,128)(2,1)S(1)}, u32[]{:S(2)}, u32[]{:S(2)}) collective-permute-start(bf16[384,384]{1,0:T(8,128)(2,1)S(1)} %slice_select_fusion.3), channel_id=1, source_target_pairs={{0,2},{1,3},{2,0},{3,1},{4,6},{5,7},{6,4},{7,5},{8,10},{9,11},{10,... | collective-permute-start | bytes 884744 | tf_op jit(solution)/shard_map/ppermute | solution.py:519
  7.3 12.4 %collective-permute-start.5 = (bf16[384,384]{1,0:T(8,128)(2,1)S(1)}, bf16[384,384]{1,0:T(8,128)(2,1)S(1)}, u32[]{:S(2)}, u32[]{:S(2)}) collective-permute-start(bf16[384,384]{1,0:T(8,128)(2,1)S(1)} %slice_select_fusion.4), channel_id=1, source_target_pairs={{0,2},{1,3},{2,0},{3,1},{4,6},{5,7},{6,4},{7,5},{8,10},{9,11},{10,... | collective-permute-start | bytes 884744 | tf_op jit(solution)/shard_map/ppermute | solution.py:519
  11.6 8.1 %collective-permute-start.4 = (f32[32,768]{1,0:T(8,128)S(1)}, f32[32,768]{1,0:T(8,128)S(1)}, u32[]{:S(2)}, u32[]{:S(2)}) collective-permute-start(f32[32,768]{1,0:T(8,128)S(1)} %get-tuple-element.321), channel_id=1, source_target_pairs={{0,1},{1,2},{2,3},{4,5},{5,6},{6,7},{8,9},{9,10},{10,11},{12,13},{... | collective-permute-start | bytes 294920 | tf_op jit(solution)/shard_map/ppermute | solution.py:524
  13.4 8.4 %collective-permute-start.7 = (f32[32,768]{1,0:T(8,128)S(1)}, f32[32,768]{1,0:T(8,128)S(1)}, u32[]{:S(2)}, u32[]{:S(2)}) collective-permute-start(f32[32,768]{1,0:T(8,128)S(1)} %get-tuple-element.321), channel_id=1, source_target_pairs={{0,2},{1,3},{4,6},{5,7},{8,10},{9,11},{12,14},{13,15},{16,18},{17,... | collective-permute-start | bytes 294920 | tf_op jit(solution)/shard_map/ppermute | solution.py:524
  21.8 17.7 %collective-permute-start.10 = (bf16[288,768]{1,0:T(8,128)(2,1)S(1)}, bf16[288,768]{1,0:T(8,128)(2,1)S(1)}, u32[]{:S(2)}, u32[]{:S(2)}) collective-permute-start(bf16[288,768]{1,0:T(8,128)(2,1)S(1)} %slice_select_fusion), channel_id=1, source_target_pairs={{0,2},{1,3},{2,0},{3,1},{4,6},{5,7},{6,4},{7,5},{8,10},{9,11},{10,... | collective-permute-start | bytes 1327112 | tf_op jit(solution)/shard_map/ppermute | solution.py:519
  24.4 9.9 %collective-permute-start.8 = (bf16[384,384]{1,0:T(8,128)(2,1)S(1)}, bf16[384,384]{1,0:T(8,128)(2,1)S(1)}, u32[]{:S(2)}, u32[]{:S(2)}) collective-permute-start(bf16[384,384]{1,0:T(8,128)(2,1)S(1)} %collective-permute-done.6), channel_id=1, source_target_pairs={{0,4},{4,0},{8,12},{12,8},{16,20},{20,16},{24,28},{28,24},{1,5},{5... | collective-permute-start | bytes 884744 | tf_op jit(solution)/shard_map/ppermute | solution.py:519
  26.1 13.4 %collective-permute-start.11 = (bf16[384,384]{1,0:T(8,128)(2,1)S(1)}, bf16[384,384]{1,0:T(8,128)(2,1)S(1)}, u32[]{:S(2)}, u32[]{:S(2)}) collective-permute-start(bf16[384,384]{1,0:T(8,128)(2,1)S(1)} %collective-permute-done.5), channel_id=1, source_target_pairs={{0,4},{4,0},{8,12},{12,8},{16,20},{20,16},{24,28},{28,24},{1,5},{5... | collective-permute-start | bytes 884744 | tf_op jit(solution)/shard_map/ppermute | solution.py:519
  26.7 14.4 %collective-permute-start.9 = (bf16[384,384]{1,0:T(8,128)(2,1)S(1)}, bf16[384,384]{1,0:T(8,128)(2,1)S(1)}, u32[]{:S(2)}, u32[]{:S(2)}) collective-permute-start(bf16[384,384]{1,0:T(8,128)(2,1)S(1)} %slice_select_fusion.2), channel_id=1, source_target_pairs={{0,2},{1,3},{2,0},{3,1},{4,6},{5,7},{6,4},{7,5},{8,10},{9,11},{10,... | collective-permute-start | bytes 884744 | tf_op jit(solution)/shard_map/ppermute | solution.py:519
  42.1 12.2 %collective-permute-start.14 = (bf16[288,768]{1,0:T(8,128)(2,1)S(1)}, bf16[288,768]{1,0:T(8,128)(2,1)S(1)}, u32[]{:S(2)}, u32[]{:S(2)}) collective-permute-start(bf16[288,768]{1,0:T(8,128)(2,1)S(1)} %collective-permute-done.10), channel_id=1, source_target_pairs={{0,8},{4,12},{8,0},{12,4},{16,24},{20,28},{24,16},{28,20},{1,9},{5... | collective-permute-start | bytes 1327112 | tf_op jit(solution)/shard_map/ppermute | solution.py:519
  43.7 8.7 %collective-permute-start.16 = (bf16[192,768]{1,0:T(8,128)(2,1)S(1)}, bf16[192,768]{1,0:T(8,128)(2,1)S(1)}, u32[]{:S(2)}, u32[]{:S(2)}) collective-permute-start(bf16[192,768]{1,0:T(8,128)(2,1)S(1)} %slice_select_fusion.1), channel_id=1, source_target_pairs={{0,2},{1,3},{2,0},{3,1},{4,6},{5,7},{6,4},{7,5},{8,10},{9,11},{10,... | collective-permute-start | bytes 884744 | tf_op jit(solution)/shard_map/ppermute | solution.py:519
  45.4 8.4 %collective-permute-start.15 = (bf16[384,384]{1,0:T(8,128)(2,1)S(1)}, bf16[384,384]{1,0:T(8,128)(2,1)S(1)}, u32[]{:S(2)}, u32[]{:S(2)}) collective-permute-start(bf16[384,384]{1,0:T(8,128)(2,1)S(1)} %collective-permute-done.9), channel_id=1, source_target_pairs={{0,4},{4,0},{8,12},{12,8},{16,20},{20,16},{24,28},{28,24},{1,5},{5... | collective-permute-start | bytes 884744 | tf_op jit(solution)/shard_map/ppermute | solution.py:519
  55.3 9.0 %collective-permute-start.19 = (bf16[192,768]{1,0:T(8,128)(2,1)S(1)}, bf16[192,768]{1,0:T(8,128)(2,1)S(1)}, u32[]{:S(2)}, u32[]{:S(2)}) collective-permute-start(bf16[192,768]{1,0:T(8,128)(2,1)S(1)} %collective-permute-done.16), channel_id=1, source_target_pairs={{0,4},{4,0},{8,12},{12,8},{16,20},{20,16},{24,28},{28,24},{1,5},{5... | collective-permute-start | bytes 884744 | tf_op jit(solution)/shard_map/ppermute | solution.py:519
  57.0 7.6 %collective-permute-start.18 = (bf16[768,384]{1,0:T(8,128)(2,1)S(1)}, bf16[768,384]{1,0:T(8,128)(2,1)S(1)}, u32[]{:S(2)}, u32[]{:S(2)}) collective-permute-start(bf16[768,384]{1,0:T(8,128)(2,1)S(1)} %maximum_select_fusion.7.ia_ref), channel_id=1, source_target_pairs={{0,1},{1,0},{2,3},{3,2},{4,5},{5,4},{6,7},{7,6},{8,9},{9,8},{10,11... | collective-permute-start | bytes 1769480 | tf_op jit(solution)/shard_map/ppermute | solution.py:519
  72.7 18.3 %collective-permute-start.24 = (bf16[768,384]{1,0:T(8,128)(2,1)S(1)}, bf16[768,384]{1,0:T(8,128)(2,1)S(1)}, u32[]{:S(2)}, u32[]{:S(2)}) collective-permute-start(bf16[768,384]{1,0:T(8,128)(2,1)S(1)} %pad_maximum_fusion.3), channel_id=1, source_target_pairs={{0,8},{4,12},{8,0},{12,4},{16,24},{20,28},{24,16},{28,20},{1,9},{5... | collective-permute-start | bytes 1769480 | tf_op jit(solution)/shard_map/ppermute | solution.py:519
  74.3 16.7 %collective-permute-start.23 = (bf16[768,384]{1,0:T(8,128)(2,1)S(1)}, bf16[768,384]{1,0:T(8,128)(2,1)S(1)}, u32[]{:S(2)}, u32[]{:S(2)}) collective-permute-start(bf16[768,384]{1,0:T(8,128)(2,1)S(1)} %get-tuple-element.446), channel_id=1, source_target_pairs={{0,2},{1,3},{2,0},{3,1},{4,6},{5,7},{6,4},{7,5},{8,10},{9,11},{10,... | collective-permute-start | bytes 1769480 | tf_op jit(solution)/shard_map/ppermute | solution.py:519
  91.0 8.8 %collective-permute-start.28 = (bf16[2,1536,384]{2,1,0:T(8,128)(2,1)S(1)}, bf16[2,1536,384]{2,1,0:T(8,128)(2,1)S(1)}, u32[]{:S(2)}, u32[]{:S(2)}) collective-permute-start(bf16[2,1536,384]{2,1,0:T(8,128)(2,1)S(1)} %get-tuple-element.465), channel_id=1, source_target_pairs={{0,1},{1,0},{2,3},{3,2},{4,5},{5,4},{6,7},{7,6},{8,9},{9,8},{10,11... | collective-permute-start | bytes 7077896 | tf_op jit(solution)/shard_map/ppermute | solution.py:519
  92.1 9.3 %collective-permute-start.25 = (bf16[384,384]{1,0:T(8,128)(2,1)S(1)}, bf16[384,384]{1,0:T(8,128)(2,1)S(1)}, u32[]{:S(2)}, u32[]{:S(2)}) collective-permute-start(bf16[384,384]{1,0:T(8,128)(2,1)S(1)} %select_convert_fusion.7), channel_id=1, source_target_pairs={{0,8},{4,12},{8,0},{12,4},{16,24},{20,28},{24,16},{28,20},{1,9},{5... | collective-permute-start | bytes 884744 | tf_op jit(solution)/shard_map/ppermute | solution.py:519
  92.6 11.7 %collective-permute-start.30 = (bf16[384,384]{1,0:T(8,128)(2,1)S(1)}, bf16[384,384]{1,0:T(8,128)(2,1)S(1)}, u32[]{:S(2)}, u32[]{:S(2)}) collective-permute-start(bf16[384,384]{1,0:T(8,128)(2,1)S(1)} %fusion.9), channel_id=1, source_target_pairs={{0,2},{1,3},{2,0},{3,1},{4,6},{5,7},{6,4},{7,5},{8,10},{9,11},{10,... | collective-permute-start | bytes 884744 | tf_op jit(solution)/shard_map/ppermute | solution.py:519
  98.4 18.3 %collective-permute-start.32 = (bf16[896,384]{1,0:T(8,128)(2,1)S(1)}, bf16[896,384]{1,0:T(8,128)(2,1)S(1)}, u32[]{:S(2)}, u32[]{:S(2)}) collective-permute-start(bf16[896,384]{1,0:T(8,128)(2,1)S(1)} %pad_maximum_fusion.2), channel_id=1, source_target_pairs={{0,4},{4,0},{8,12},{12,8},{16,20},{20,16},{24,28},{28,24},{1,5},{5... | collective-permute-start | bytes 2064392 | tf_op jit(solution)/shard_map/ppermute | solution.py:519
  100.9 28.8 %collective-permute-start.34 = (bf16[1536,384]{1,0:T(8,128)(2,1)S(1)}, bf16[1536,384]{1,0:T(8,128)(2,1)S(1)}, u32[]{:S(2)}, u32[]{:S(2)}) collective-permute-start(bf16[1536,384]{1,0:T(8,128)(2,1)S(1)} %pad_maximum_fusion.1), channel_id=1, source_target_pairs={{0,8},{4,12},{8,0},{12,4},{16,24},{20,28},{24,16},{28,20},{1,9},{5... | collective-permute-start | bytes 3538952 | tf_op jit(solution)/shard_map/ppermute | solution.py:519
  102.7 9.9 %collective-permute-start.31 = (f32[64,768]{1,0:T(8,128)S(1)}, f32[64,768]{1,0:T(8,128)S(1)}, u32[]{:S(2)}, u32[]{:S(2)}) collective-permute-start(f32[64,768]{1,0:T(8,128)S(1)} %pad_maximum_fusion.6), channel_id=1, source_target_pairs={{2,0},{3,1},{6,4},{7,5},{10,8},{11,9},{14,12},{15,13},{18,16},{19,... | collective-permute-start | bytes 589832 | tf_op jit(solution)/shard_map/ppermute | solution.py:524
  104.4 24.9 %collective-permute-start.35 = (bf16[768,384]{1,0:T(8,128)(2,1)S(1)}, bf16[768,384]{1,0:T(8,128)(2,1)S(1)}, u32[]{:S(2)}, u32[]{:S(2)}) collective-permute-start(bf16[768,384]{1,0:T(8,128)(2,1)S(1)} %pad_maximum_fusion.4), channel_id=1, source_target_pairs={{0,4},{4,0},{8,12},{12,8},{16,20},{20,16},{24,28},{28,24},{1,5},{5... | collective-permute-start | bytes 1769480 | tf_op jit(solution)/shard_map/ppermute | solution.py:519
  116.9 10.5 %collective-permute-start.36 = (bf16[448,384]{1,0:T(8,128)(2,1)S(1)}, bf16[448,384]{1,0:T(8,128)(2,1)S(1)}, u32[]{:S(2)}, u32[]{:S(2)}) collective-permute-start(bf16[448,384]{1,0:T(8,128)(2,1)S(1)} %fusion.3), channel_id=1, source_target_pairs={{0,2},{1,3},{2,0},{3,1},{4,6},{5,7},{6,4},{7,5},{8,10},{9,11},{10,... | collective-permute-start | bytes 1032200 | tf_op jit(solution)/shard_map/ppermute | solution.py:519
  132.5 9.4 %collective-permute-start.39 = (bf16[384,384]{1,0:T(8,128)(2,1)S(1)}, bf16[384,384]{1,0:T(8,128)(2,1)S(1)}, u32[]{:S(2)}, u32[]{:S(2)}) collective-permute-start(bf16[384,384]{1,0:T(8,128)(2,1)S(1)} %get-tuple-element.521), channel_id=1, source_target_pairs={{0,4},{4,0},{8,12},{12,8},{16,20},{20,16},{24,28},{28,24},{1,5},{5... | collective-permute-start | bytes 884744 | tf_op jit(solution)/shard_map/ppermute | solution.py:519
  134.1 16.2 %collective-permute-start.43 = (bf16[768,384]{1,0:T(8,128)(2,1)S(1)}, bf16[768,384]{1,0:T(8,128)(2,1)S(1)}, u32[]{:S(2)}, u32[]{:S(2)}) collective-permute-start(bf16[768,384]{1,0:T(8,128)(2,1)S(1)} %fusion.1), channel_id=1, source_target_pairs={{0,2},{1,3},{2,0},{3,1},{4,6},{5,7},{6,4},{7,5},{8,10},{9,11},{10,... | collective-permute-start | bytes 1769480 | tf_op jit(solution)/shard_map/ppermute | solution.py:519
  134.8 15.7 %collective-permute-start.42 = (bf16[192,384]{1,0:T(8,128)(2,1)S(1)}, bf16[192,384]{1,0:T(8,128)(2,1)S(1)}, u32[]{:S(2)}, u32[]{:S(2)}) collective-permute-start(bf16[192,384]{1,0:T(8,128)(2,1)S(1)} %fusion.36), channel_id=1, source_target_pairs={{0,16},{4,20},{8,24},{12,28},{16,0},{20,4},{24,8},{28,12},{1,17},{... | collective-permute-start | bytes 442376 | tf_op jit(solution)/shard_map/ppermute | solution.py:519
  137.8 18.8 %collective-permute-start.44 = (bf16[384,384]{1,0:T(8,128)(2,1)S(1)}, bf16[384,384]{1,0:T(8,128)(2,1)S(1)}, u32[]{:S(2)}, u32[]{:S(2)}) collective-permute-start(bf16[384,384]{1,0:T(8,128)(2,1)S(1)} %get-tuple-element.535), channel_id=1, source_target_pairs={{0,2},{1,3},{2,0},{3,1},{4,6},{5,7},{6,4},{7,5},{8,10},{9,11},{10,... | collective-permute-start | bytes 884744 | tf_op jit(solution)/shard_map/ppermute | solution.py:519
  138.9 18.4 %collective-permute-start.41 = (bf16[224,384]{1,0:T(8,128)(2,1)S(1)}, bf16[224,384]{1,0:T(8,128)(2,1)S(1)}, u32[]{:S(2)}, u32[]{:S(2)}) collective-permute-start(bf16[224,384]{1,0:T(8,128)(2,1)S(1)} %fusion.38), channel_id=1, source_target_pairs={{0,16},{4,20},{8,24},{12,28},{16,0},{20,4},{24,8},{28,12},{1,17},{... | collective-permute-start | bytes 516104 | tf_op jit(solution)/shard_map/ppermute | solution.py:519
  141.9 16.5 %collective-permute-start.40 = (bf16[480,128]{1,0:T(8,128)(2,1)S(1)}, bf16[480,128]{1,0:T(8,128)(2,1)S(1)}, u32[]{:S(2)}, u32[]{:S(2)}) collective-permute-start(bf16[480,128]{1,0:T(8,128)(2,1)S(1)} %pad_maximum_fusion.8), channel_id=1, source_target_pairs={{0,2},{1,3},{2,0},{3,1},{4,6},{5,7},{6,4},{7,5},{8,10},{9,11},{10,... | collective-permute-start | bytes 368648 | tf_op jit(solution)/shard_map/ppermute | solution.py:519
  150.6 24.0 %collective-permute-start.50 = (bf16[384,384]{1,0:T(8,128)(2,1)S(1)}, bf16[384,384]{1,0:T(8,128)(2,1)S(1)}, u32[]{:S(2)}, u32[]{:S(2)}) collective-permute-start(bf16[384,384]{1,0:T(8,128)(2,1)S(1)} %fusion.12), channel_id=1, source_target_pairs={{0,16},{4,20},{8,24},{12,28},{16,0},{20,4},{24,8},{28,12},{1,17},{... | collective-permute-start | bytes 884744 | tf_op jit(solution)/shard_map/ppermute | solution.py:519
  156.7 6.8 %collective-permute-start.48 = (bf16[192,384]{1,0:T(8,128)(2,1)S(1)}, bf16[192,384]{1,0:T(8,128)(2,1)S(1)}, u32[]{:S(2)}, u32[]{:S(2)}) collective-permute-start(bf16[192,384]{1,0:T(8,128)(2,1)S(1)} %add_convert_fusion.5), channel_id=1, source_target_pairs={{0,4},{4,0},{8,12},{12,8},{16,20},{20,16},{24,28},{28,24},{1,5},{5... | collective-permute-start | bytes 442376 | tf_op jit(solution)/shard_map/ppermute | solution.py:519
  158.4 18.9 %collective-permute-start.45 = (bf16[384,384]{1,0:T(8,128)(2,1)S(1)}, bf16[384,384]{1,0:T(8,128)(2,1)S(1)}, u32[]{:S(2)}, u32[]{:S(2)}) collective-permute-start(bf16[384,384]{1,0:T(8,128)(2,1)S(1)} %select_convert_fusion.4), channel_id=1, source_target_pairs={{0,4},{4,0},{8,12},{12,8},{16,20},{20,16},{24,28},{28,24},{1,5},{5... | collective-permute-start | bytes 884744 | tf_op jit(solution)/shard_map/ppermute | solution.py:519
  158.9 15.0 %collective-permute-start.47 = (bf16[224,384]{1,0:T(8,128)(2,1)S(1)}, bf16[224,384]{1,0:T(8,128)(2,1)S(1)}, u32[]{:S(2)}, u32[]{:S(2)}) collective-permute-start(bf16[224,384]{1,0:T(8,128)(2,1)S(1)} %add_convert_fusion.3), channel_id=1, source_target_pairs={{0,8},{4,12},{8,0},{12,4},{16,24},{20,28},{24,16},{28,20},{1,9},{5... | collective-permute-start | bytes 516104 | tf_op jit(solution)/shard_map/ppermute | solution.py:519
  160.7 11.6 %collective-permute-start.49 = (bf16[192,384]{1,0:T(8,128)(2,1)S(1)}, bf16[192,384]{1,0:T(8,128)(2,1)S(1)}, u32[]{:S(2)}, u32[]{:S(2)}) collective-permute-start(bf16[192,384]{1,0:T(8,128)(2,1)S(1)} %select_convert_fusion.11), channel_id=1, source_target_pairs={{0,8},{4,12},{8,0},{12,4},{16,24},{20,28},{24,16},{28,20},{1,9},{5... | collective-permute-start | bytes 442376 | tf_op jit(solution)/shard_map/ppermute | solution.py:519
  163.5 25.4 %collective-permute-start.62 = (bf16[384,384]{1,0:T(8,128)(2,1)S(1)}, bf16[384,384]{1,0:T(8,128)(2,1)S(1)}, u32[]{:S(2)}, u32[]{:S(2)}) collective-permute-start(bf16[384,384]{1,0:T(8,128)(2,1)S(1)} %maximum_select_fusion.15), channel_id=1, source_target_pairs={{0,8},{4,12},{8,0},{12,4},{16,24},{20,28},{24,16},{28,20},{1,9},{5... | collective-permute-start | bytes 884744 | tf_op jit(solution)/shard_map/ppermute | solution.py:519
  172.3 10.8 %collective-permute-start.56 = (bf16[192,384]{1,0:T(8,128)(2,1)S(1)}, bf16[192,384]{1,0:T(8,128)(2,1)S(1)}, u32[]{:S(2)}, u32[]{:S(2)}) collective-permute-start(bf16[192,384]{1,0:T(8,128)(2,1)S(1)} %fusion.37), channel_id=1, source_target_pairs={{0,16},{4,20},{8,24},{12,28},{16,0},{20,4},{24,8},{28,12},{1,17},{... | collective-permute-start | bytes 442376 | tf_op jit(solution)/shard_map/ppermute | solution.py:519
  174.0 25.3 %collective-permute-start.53 = (bf16[448,384]{1,0:T(8,128)(2,1)S(1)}, bf16[448,384]{1,0:T(8,128)(2,1)S(1)}, u32[]{:S(2)}, u32[]{:S(2)}) collective-permute-start(bf16[448,384]{1,0:T(8,128)(2,1)S(1)} %maximum_select_fusion.13), channel_id=1, source_target_pairs={{0,4},{4,0},{8,12},{12,8},{16,20},{20,16},{24,28},{28,24},{1,5},{5... | collective-permute-start | bytes 1032200 | tf_op jit(solution)/shard_map/ppermute | solution.py:519
  174.8 27.7 %collective-permute-start.63 = (bf16[384,384]{1,0:T(8,128)(2,1)S(1)}, bf16[384,384]{1,0:T(8,128)(2,1)S(1)}, u32[]{:S(2)}, u32[]{:S(2)}) collective-permute-start(bf16[384,384]{1,0:T(8,128)(2,1)S(1)} %add_convert_fusion.2), channel_id=1, source_target_pairs={{0,8},{4,12},{8,0},{12,4},{16,24},{20,28},{24,16},{28,20},{1,9},{5... | collective-permute-start | bytes 884744 | tf_op jit(solution)/shard_map/ppermute | solution.py:519
  177.4 25.3 %collective-permute-start.59 = (bf16[384,384]{1,0:T(8,128)(2,1)S(1)}, bf16[384,384]{1,0:T(8,128)(2,1)S(1)}, u32[]{:S(2)}, u32[]{:S(2)}) collective-permute-start(bf16[384,384]{1,0:T(8,128)(2,1)S(1)} %fusion.39), channel_id=1, source_target_pairs={{0,16},{4,20},{8,24},{12,28},{16,0},{20,4},{24,8},{28,12},{1,17},{... | collective-permute-start | bytes 884744 | tf_op jit(solution)/shard_map/ppermute | solution.py:519
  188.0 9.5 %collective-permute-start.57 = (bf16[192,384]{1,0:T(8,128)(2,1)S(1)}, bf16[192,384]{1,0:T(8,128)(2,1)S(1)}, u32[]{:S(2)}, u32[]{:S(2)}) collective-permute-start(bf16[192,384]{1,0:T(8,128)(2,1)S(1)} %add_convert_fusion.4), channel_id=1, source_target_pairs={{0,8},{4,12},{8,0},{12,4},{16,24},{20,28},{24,16},{28,20},{1,9},{5... | collective-permute-start | bytes 442376 | tf_op jit(solution)/shard_map/ppermute | solution.py:519
  189.0 11.7 %collective-permute-start.51 = (bf16[480,128]{1,0:T(8,128)(2,1)S(1)}, bf16[480,128]{1,0:T(8,128)(2,1)S(1)}, u32[]{:S(2)}, u32[]{:S(2)}) collective-permute-start(bf16[480,128]{1,0:T(8,128)(2,1)S(1)} %pad_maximum_fusion.10), channel_id=1, source_target_pairs={{0,8},{4,12},{8,0},{12,4},{16,24},{20,28},{24,16},{28,20},{1,9},{5... | collective-permute-start | bytes 368648 | tf_op jit(solution)/shard_map/ppermute | solution.py:519
  197.6 18.4 %collective-permute-start.58 = (bf16[384,384]{1,0:T(8,128)(2,1)S(1)}, bf16[384,384]{1,0:T(8,128)(2,1)S(1)}, u32[]{:S(2)}, u32[]{:S(2)}) collective-permute-start(bf16[384,384]{1,0:T(8,128)(2,1)S(1)} %maximum_select_fusion.14), channel_id=1, source_target_pairs={{0,4},{4,0},{8,12},{12,8},{16,20},{20,16},{24,28},{28,24},{1,5},{5... | collective-permute-start | bytes 884744 | tf_op jit(solution)/shard_map/ppermute | solution.py:519
  199.8 17.3 %collective-permute-start.54 = (bf16[448,384]{1,0:T(8,128)(2,1)S(1)}, bf16[448,384]{1,0:T(8,128)(2,1)S(1)}, u32[]{:S(2)}, u32[]{:S(2)}) collective-permute-start(bf16[448,384]{1,0:T(8,128)(2,1)S(1)} %pad_maximum_fusion.5), channel_id=1, source_target_pairs={{0,1},{1,0},{2,3},{3,2},{4,5},{5,4},{6,7},{7,6},{8,9},{9,8},{10,11... | collective-permute-start | bytes 1032200 | tf_op jit(solution)/shard_map/ppermute | solution.py:519
  200.8 9.3 %collective-permute-start.52 = (bf16[480,128]{1,0:T(8,128)(2,1)S(1)}, bf16[480,128]{1,0:T(8,128)(2,1)S(1)}, u32[]{:S(2)}, u32[]{:S(2)}) collective-permute-start(bf16[480,128]{1,0:T(8,128)(2,1)S(1)} %pad_maximum_fusion.11), channel_id=1, source_target_pairs={{0,16},{4,20},{8,24},{12,28},{16,0},{20,4},{24,8},{28,12},{1,17},{... | collective-permute-start | bytes 368648 | tf_op jit(solution)/shard_map/ppermute | solution.py:519
  202.9 10.0 %collective-permute-start.60 = (bf16[384,384]{1,0:T(8,128)(2,1)S(1)}, bf16[384,384]{1,0:T(8,128)(2,1)S(1)}, u32[]{:S(2)}, u32[]{:S(2)}) collective-permute-start(bf16[384,384]{1,0:T(8,128)(2,1)S(1)} %add_convert_fusion.1), channel_id=1, source_target_pairs={{0,4},{4,0},{8,12},{12,8},{16,20},{20,16},{24,28},{28,24},{1,5},{5... | collective-permute-start | bytes 884744 | tf_op jit(solution)/shard_map/ppermute | solution.py:519
  213.0 14.6 %collective-permute-start.61 = (bf16[768,384]{1,0:T(8,128)(2,1)S(1)}, bf16[768,384]{1,0:T(8,128)(2,1)S(1)}, u32[]{:S(2)}, u32[]{:S(2)}) collective-permute-start(bf16[768,384]{1,0:T(8,128)(2,1)S(1)} %maximum_select_fusion.10), channel_id=1, source_target_pairs={{0,8},{4,12},{8,0},{12,4},{16,24},{20,28},{24,16},{28,20},{1,9},{5... | collective-permute-start | bytes 1769480 | tf_op jit(solution)/shard_map/ppermute | solution.py:519
  217.4 16.5 %collective-permute-start.55 = (bf16[896,384]{1,0:T(8,128)(2,1)S(1)}, bf16[896,384]{1,0:T(8,128)(2,1)S(1)}, u32[]{:S(2)}, u32[]{:S(2)}) collective-permute-start(bf16[896,384]{1,0:T(8,128)(2,1)S(1)} %maximum_select_fusion.4), channel_id=1, source_target_pairs={{0,2},{1,3},{2,0},{3,1},{4,6},{5,7},{6,4},{7,5},{8,10},{9,11},{10,... | collective-permute-start | bytes 2064392 | tf_op jit(solution)/shard_map/ppermute | solution.py:519
  (37 other events, 256.7 us)

commit v6 on v5

--- a/solution.py
+++ b/solution.py
@@ -12,17 +12,17 @@
 CHUNKS = 8
 F32 = jnp.float32
 LOW = jnp.bfloat16
-KINDS = {"I": "z", "U": "W", "Q": "z", "P": "x", "N": "x"}
+KINDS = {"I": "y", "U": "z", "Q": "x", "P": "z", "N": "Z"}
 ORDER = (
     "+F0", "+F1", "-F0", "-F1", "+I", "+U", "Kback", "-I", "-U", "+P",
-    "+Q", "+U", "+I", "-P", "+N", "+P", "-Q", "+Q", "-N", "-U",
-    "+E", "-I", "+N", "-E", "-P", "+P", "+I", "Kt4", "-P", "-N",
-    "-Q", "-I", "+Q", "+P", "+U", "+I", "+sm", "-P", "-sm", "+P",
-    "+N", "-U", "+sm", "-Q", "-I", "+Q", "+U", "-N", "+I", "-P",
-    "-sm", "+P", "-Q", "+sm", "+N", "-I", "+Q", "-P", "-sm", "+P",
-    "-U", "-N", "+sm", "+I", "+N", "-sm", "-P", "+U", "+P", "-Q",
-    "+Q", "-I", "-P", "+sm", "+P", "-N", "+N", "-U", "-Q", "+Q",
-    "-sm", "-N", "+N", "-P", "-N", "-Q",
+    "+Q", "+I", "+U", "-P", "+N", "+P", "-Q", "+Q", "-N", "-I",
+    "+E", "-U", "+N", "-E", "-P", "+P", "Kt4", "-P", "-N", "-Q",
+    "+P", "+Q", "+I", "+U", "-P", "+sm", "+P", "-sm", "-I", "+N",
+    "-U", "+I", "-Q", "+Q", "+sm", "-P", "+P", "-N", "+U", "-I",
+    "-sm", "+I", "-Q", "-P", "+Q", "+N", "-I", "-U", "+P", "+U",
+    "+I", "-N", "+N", "-U", "+sm", "-Q", "-P", "+Q", "+P", "-I",
+    "-sm", "+sm", "+U", "-Q", "-N", "+Q", "-sm", "-P", "+sm", "+N",
+    "+P", "-U", "-P", "-sm", "-N", "-Q",
 )
 
 
@@ -890,10 +890,11 @@
     def with_shared():
         low = yield from reduction(KINDS["P"], packs_of("P"), firsts)
         v = jnp.concatenate([low[: 2 * cols], low[4 * cols : 4 * cols + share]], 0)
-        for bit, first in ((1, first_core), (2, first_chip)):
+        for bit, first in ((2, first_chip), (1, first_core)):
             got = yield "tensor", bit, v
             v = joined(v, got, first)
-        return low[2 * cols : 4 * cols], v.reshape(4, 2 * cols + share, width // 2)
+        v = v.reshape(2, 2, 2 * cols + share, width // 2)
+        return low[2 * cols : 4 * cols], [v[core, chip] for chip in range(2) for core in range(2)]
 
     def add_flow(name):
         pump.add(

time: 240 us -> 238 us (level)
  waiting for transfers between devices: 104 us -> 100 us
    ppermute x60, waiting for transfers between devices: 95.4 us -> 91.9 us  [swap(): return lax.ppermute(x, axis, [(i, i ^ bit) for i in range(size)])]
  transfers between devices with their start and end apart: 64 -> 64, of which waited for: 31 -> 28; matrix products, arithmetic and copies ran while one was open for 8% -> 8% of each run, Pallas kernels for 17% -> 17%
where the time goes in v6:
time: 238 us; the launch traced here: 235 us
  waiting for transfers between devices  100 us (42%)
  starting transfers between devices  67.7 us (28%)
  Pallas kernels  40.5 us (17%)
  other arithmetic  20.8 us (9%)
  local copies, waits for them, and re-layouts  3.12 us (1%)
  between operations  2.51 us (1%)
    ppermute x60, waiting for transfers between devices, swap(): return lax.ppermute(x, axis, [(i, i ^ bit) for i in range(size)])  91.9 us
    ppermute x60, starting transfers between devices, swap(): return lax.ppermute(x, axis, [(i, i ^ bit) for i in range(size)])  60.3 us
    pallas_call x9, Pallas kernels, call(): pl.pallas_call(kernel, out_shape=outs, in_specs=specs, out_specs=[pl.Bloc...  40.5 us
    ppermute x4, waiting for transfers between devices, shift(): lax.ppermute(x, 'tensor', [(i, i + by) for i in range(size) if 0 <= i + b...  8.45 us
    ppermute x4, starting transfers between devices, shift(): lax.ppermute(x, 'tensor', [(i, i + by) for i in range(size) if 0 <= i + b...  7.36 us
  transfers between devices with their start and end apart: 64, of which 28 were waited for; matrix products, arithmetic and copies ran while one was open for 8% of the time, Pallas kernels for 17%

profile of v6, /device:TPU:0, one launch (start us, length us, event | category | flops | bytes accessed | tf_op | source)
XLA Modules:
  0.0 235.0 jit_solution(12121940348898245351)
XLA Ops:
  3.0 3.0 %collective-permute-start.6 = (bf16[384,384]{1,0:T(8,128)(2,1)S(1)}, bf16[384,384]{1,0:T(8,128)(2,1)S(1)}, u32[]{:S(2)}, u32[]{:S(2)}) collective-permute-start(bf16[384,384]{1,0:T(8,128)(2,1)S(1)} %slice_select_fusion.3), channel_id=1, source_target_pairs={{0,2},{1,3},{2,0},{3,1},{4,6},{5,7},{6,4},{7,5},{8,10},{9,11},{10,... | collective-permute-start | bytes 884744 | tf_op jit(solution)/shard_map/ppermute | solution.py:519
  8.6 3.0 %shard_map.356 = (f32[1536,128]{1,0:T(8,128)S(1)}, bf16[256,768]{1,0:T(8,128)(2,1)S(1)}, f32[256,768]{1,0:T(8,128)S(1)}, f32[32,768]{1,0:T(8,128)S(1)}) custom-call(bf16[256,768]{1,0:T(8,128)(2,1)S(1)} %bitcast.77, f32[1,768]{1,0:T(1,128)S(1)} %broadcast_in_dim.34.g_ref, f32[16,768]{1,0:T(8,128)S(1)} %copy-done.4, f32[16,768]{1,0:T(8,128)S(1)} %copy-done.5, ...), custom_call_target="tpu_custom_call" | custom-call | flops 25165824 | bytes 2739200 | tf_op jit(solution)/shard_map/pallas_call | solution.py:71
  11.6 1.8 collective-permute-start.4
  13.4 3.0 %collective-permute-start.7 = (f32[32,768]{1,0:T(8,128)S(1)}, f32[32,768]{1,0:T(8,128)S(1)}, u32[]{:S(2)}, u32[]{:S(2)}) collective-permute-start(f32[32,768]{1,0:T(8,128)S(1)} %get-tuple-element.321), channel_id=1, source_target_pairs={{0,2},{1,3},{4,6},{5,7},{8,10},{9,11},{12,14},{13,15},{16,18},{17,... | collective-permute-start | bytes 294920 | tf_op jit(solution)/shard_map/ppermute | solution.py:524
  16.5 3.3 %collective-permute-done.5 = bf16[384,384]{1,0:T(8,128)(2,1)S(1)} collective-permute-done((bf16[384,384]{1,0:T(8,128)(2,1)S(1)}, bf16[384,384]{1,0:T(8,128)(2,1)S(1)}, u32[]{:S(2)}, u32[]{:S(2)}) %collective-permute-start.5) | collective-permute-done | bytes 294944 | tf_op jit(solution)/shard_map/ppermute | solution.py:519
  19.7 2.1 collective-permute-done.7.f2_ref
  21.8 2.5 %collective-permute-start.10 = (bf16[288,768]{1,0:T(8,128)(2,1)S(1)}, bf16[288,768]{1,0:T(8,128)(2,1)S(1)}, u32[]{:S(2)}, u32[]{:S(2)}) collective-permute-start(bf16[288,768]{1,0:T(8,128)(2,1)S(1)} %slice_select_fusion), channel_id=1, source_target_pairs={{0,2},{1,3},{2,0},{3,1},{4,6},{5,7},{6,4},{7,5},{8,10},{9,11},{10,... | collective-permute-start | bytes 1327112 | tf_op jit(solution)/shard_map/ppermute | solution.py:519
  26.8 4.6 %shard_map.357 = (f32[1536,128]{1,0:T(8,128)S(1)}, bf16[256,768]{1,0:T(8,128)(2,1)S(1)}, f32[256,128]{1,0:T(8,128)S(1)}, f32[256,768]{1,0:T(8,128)S(1)}, f32[256,128]{1,0:T(8,128)S(1)}) custom-call(f32[1536,128]{1,0:T(8,128)S(1)} %get-tuple-element.317.normed_ref, f32[256,768]{1,0:T(8,128)S(1)} %get-tuple-element.318.init_ref, ...), custom_call_target="tpu_custom_call" | custom-call | flops 327155712 | bytes 5838336 | tf_op jit(solution)/shard_map/pallas_call | solution.py:71
  31.4 2.9 %collective-permute-done.8 = bf16[384,384]{1,0:T(8,128)(2,1)S(1)} collective-permute-done((bf16[384,384]{1,0:T(8,128)(2,1)S(1)}, bf16[384,384]{1,0:T(8,128)(2,1)S(1)}, u32[]{:S(2)}, u32[]{:S(2)}) %collective-permute-start.8) | collective-permute-done | bytes 294944 | tf_op jit(solution)/shard_map/ppermute | solution.py:519
  35.4 4.1 %collective-permute-done.11 = bf16[384,384]{1,0:T(8,128)(2,1)S(1)} collective-permute-done((bf16[384,384]{1,0:T(8,128)(2,1)S(1)}, bf16[384,384]{1,0:T(8,128)(2,1)S(1)}, u32[]{:S(2)}, u32[]{:S(2)}) %collective-permute-start.11) | collective-permute-done | bytes 294944 | tf_op jit(solution)/shard_map/ppermute | solution.py:519
  39.5 1.6 collective-permute-done.9
  42.1 1.6 collective-permute-start.14
  43.7 1.7 collective-permute-start.16
  48.1 4.4 %collective-permute-done.16 = bf16[192,768]{1,0:T(8,128)(2,1)S(1)} collective-permute-done((bf16[192,768]{1,0:T(8,128)(2,1)S(1)}, bf16[192,768]{1,0:T(8,128)(2,1)S(1)}, u32[]{:S(2)}, u32[]{:S(2)}) %collective-permute-start.16) | collective-permute-done | bytes 294944 | tf_op jit(solution)/shard_map/ppermute | solution.py:519
  58.6 2.2 shard_map.360
  60.8 2.7 %shard_map.361 = (f32[256,768]{1,0:T(8,128)S(1)}, f32[256,768]{1,0:T(8,128)S(1)}, bf16[1536,384]{1,0:T(8,128)(2,1)S(1)}, bf16[1536,384]{1,0:T(8,128)(2,1)S(1)}) custom-call(bf16[256,768]{1,0:T(8,128)(2,1)S(1)} %get-tuple-element.393.second_ref, bf16[256,768]{1,0:T(8,128)(2,1)S(1)} %bitcast.81, bf16[768,384]{1,0:T(8,128)(2,1)S(1)} %copy-done.8, ...), custom_call_target="tpu_custom_call" | custom-call | flops 1811939328 | bytes 7077888 | tf_op jit(solution)/shard_map/pallas_call | solution.py:71
  64.6 2.0 collective-permute-done.19.ob_ref
  66.7 2.7 %shard_map.362 = (f32[256,768]{1,0:T(8,128)S(1)}, f32[256,768]{1,0:T(8,128)S(1)}, bf16[1536,384]{1,0:T(8,128)(2,1)S(1)}, bf16[1536,384]{1,0:T(8,128)(2,1)S(1)}) custom-call(bf16[256,768]{1,0:T(8,128)(2,1)S(1)} %get-tuple-element.393.second_ref, bf16[256,768]{1,0:T(8,128)(2,1)S(1)} %bitcast.82, bf16[768,384]{1,0:T(8,128)(2,1)S(1)} %maximum_select_fusion.7.ia_ref, ...), custom_call_target="tpu_custom_call" | custom-call | flops 1811939328 | bytes 7077888 | tf_op jit(solution)/shard_map/pallas_call | solution.py:71
  69.8 2.5 %collective-permute-done.22 = bf16[1536,384]{1,0:T(8,128)(2,1)S(1)} collective-permute-done((bf16[1536,384]{1,0:T(8,128)(2,1)S(1)}, bf16[1536,384]{1,0:T(8,128)(2,1)S(1)}, u32[]{:S(2)}, u32[]{:S(2)}) %collective-permute-start.22) | collective-permute-done | bytes 1179680 | tf_op jit(solution)/shard_map/ppermute | solution.py:519
  72.8 1.8 collective-permute-start.23
  74.7 1.6 collective-permute-start.24
  76.5 14.8 %shard_map.363 = (bf16[256,768]{1,0:T(8,128)(2,1)}, f32[256,768]{1,0:T(8,128)S(1)}, f32[1,768]{1,0:T(1,128)S(1)}, bf16[2,896,384]{2,1,0:T(8,128)(2,1)S(1)}, bf16...) custom-call(s32[4]{0:T(128)S(1)} %xor_multiply_fusion.offs_ref.refs_, ...), custom_call_target="tpu_custom_call" | custom-call | flops 5435817984 | bytes 39038480 | tf_op jit(solution)/shard_map/pallas_call | solution.py:71
  94.2 3.7 %collective-permute-done.26 = bf16[2,896,384]{2,1,0:T(8,128)(2,1)S(1)} collective-permute-done((bf16[2,896,384]{2,1,0:T(8,128)(2,1)S(1)}, bf16[2,896,384]{2,1,0:T(8,128)(2,1)S(1)}, u32[]{:S(2)}, u32[]{:S(2)}) %collective-permute-start.26) | collective-permute-done | bytes 1376288 | tf_op jit(solution)/shard_map/ppermute | solution.py:519
  104.7 1.6 collective-permute-start.35
  106.5 6.3 %collective-permute-done.31.far_ref = f32[64,768]{1,0:T(8,128)S(1)} collective-permute-done((f32[64,768]{1,0:T(8,128)S(1)}, f32[64,768]{1,0:T(8,128)S(1)}, u32[]{:S(2)}, u32[]{:S(2)}) %collective-permute-start.31) | collective-permute-done | bytes 196640 | tf_op jit(solution)/shard_map/ppermute | solution.py:524
  112.9 4.1 %collective-permute-done.32 = bf16[896,384]{1,0:T(8,128)(2,1)S(1)} collective-permute-done((bf16[896,384]{1,0:T(8,128)(2,1)S(1)}, bf16[896,384]{1,0:T(8,128)(2,1)S(1)}, u32[]{:S(2)}, u32[]{:S(2)}) %collective-permute-start.32) | collective-permute-done | bytes 688160 | tf_op jit(solution)/shard_map/ppermute | solution.py:519
  117.6 8.5 %shard_map.364 = (bf16[256,768]{1,0:T(8,128)(2,1)}, f32[40,768]{1,0:T(8,128)S(1)}) custom-call(f32[1536,128]{1,0:T(8,128)S(1)} %get-tuple-element.439.pg_ref, f32[1536,128]{1,0:T(8,128)S(1)} %get-tuple-element.317.normed_ref, f32[256,768]{1,0:T(8,128)S(1)} %get-tuple-element.440.im_ref, f32[256,768]{1,0:T(8,128)S(1)} %get-tuple-element.441.iv_ref, ...), custom_call_target="tpu_custom_call" | custom-call | flops 50331648 | bytes 6363136 | tf_op jit(solution)/shard_map/pallas_call | solution.py:71
  126.4 2.6 %collective-permute-done.35 = bf16[768,384]{1,0:T(8,128)(2,1)S(1)} collective-permute-done((bf16[768,384]{1,0:T(8,128)(2,1)S(1)}, bf16[768,384]{1,0:T(8,128)(2,1)S(1)}, u32[]{:S(2)}, u32[]{:S(2)}) %collective-permute-start.35) | collective-permute-done | bytes 589856 | tf_op jit(solution)/shard_map/ppermute | solution.py:519
  132.7 4.2 %collective-permute-done.36 = bf16[224,384]{1,0:T(8,128)(2,1)S(1)} collective-permute-done((bf16[224,384]{1,0:T(8,128)(2,1)S(1)}, bf16[224,384]{1,0:T(8,128)(2,1)S(1)}, u32[]{:S(2)}, u32[]{:S(2)}) %collective-permute-start.36) | collective-permute-done | bytes 172064 | tf_op jit(solution)/shard_map/ppermute | solution.py:519
  137.0 2.7 %collective-permute-start.44 = (bf16[224,384]{1,0:T(8,128)(2,1)S(1)}, bf16[224,384]{1,0:T(8,128)(2,1)S(1)}, u32[]{:S(2)}, u32[]{:S(2)}) collective-permute-start(bf16[224,384]{1,0:T(8,128)(2,1)S(1)} %fusion.39), channel_id=1, source_target_pairs={{0,16},{4,20},{8,24},{12,28},{16,0},{20,4},{24,8},{28,12},{1,17},{... | collective-permute-start | bytes 516104 | tf_op jit(solution)/shard_map/ppermute | solution.py:519
  141.6 7.1 %collective-permute-done.38 = bf16[768,384]{1,0:T(8,128)(2,1)S(1)} collective-permute-done((bf16[768,384]{1,0:T(8,128)(2,1)S(1)}, bf16[768,384]{1,0:T(8,128)(2,1)S(1)}, u32[]{:S(2)}, u32[]{:S(2)}) %collective-permute-start.38) | collective-permute-done | bytes 589856 | tf_op jit(solution)/shard_map/ppermute | solution.py:519
  149.0 1.9 collective-permute-done.44
  151.0 1.7 collective-permute-done.43
  152.7 2.6 %collective-permute-start.45 = (bf16[192,384]{1,0:T(8,128)(2,1)S(1)}, bf16[192,384]{1,0:T(8,128)(2,1)S(1)}, u32[]{:S(2)}, u32[]{:S(2)}) collective-permute-start(bf16[192,384]{1,0:T(8,128)(2,1)S(1)} %fusion.38), channel_id=1, source_target_pairs={{0,16},{4,20},{8,24},{12,28},{16,0},{20,4},{24,8},{28,12},{1,17},{... | collective-permute-start | bytes 442376 | tf_op jit(solution)/shard_map/ppermute | solution.py:519
  155.6 1.6 collective-permute-start.47
  160.2 1.6 collective-permute-start.46
  163.5 6.9 %collective-permute-done.51 = bf16[480,128]{1,0:T(8,128)(2,1)S(1)} collective-permute-done((bf16[480,128]{1,0:T(8,128)(2,1)S(1)}, bf16[480,128]{1,0:T(8,128)(2,1)S(1)}, u32[]{:S(2)}, u32[]{:S(2)}) %collective-permute-start.51) | collective-permute-done | bytes 122912 | tf_op jit(solution)/shard_map/ppermute | solution.py:519
  170.4 1.7 collective-permute-start.49
  173.4 3.7 %collective-permute-done.49 = bf16[192,384]{1,0:T(8,128)(2,1)S(1)} collective-permute-done((bf16[192,384]{1,0:T(8,128)(2,1)S(1)}, bf16[192,384]{1,0:T(8,128)(2,1)S(1)}, u32[]{:S(2)}, u32[]{:S(2)}) %collective-permute-start.49) | collective-permute-done | bytes 147488 | tf_op jit(solution)/shard_map/ppermute | solution.py:519
  177.1 1.7 collective-permute-start.52
  179.8 2.1 collective-permute-start.53
  182.0 2.5 %collective-permute-start.56 = (bf16[480,128]{1,0:T(8,128)(2,1)S(1)}, bf16[480,128]{1,0:T(8,128)(2,1)S(1)}, u32[]{:S(2)}, u32[]{:S(2)}) collective-permute-start(bf16[480,128]{1,0:T(8,128)(2,1)S(1)} %pad_maximum_fusion.11), channel_id=1, source_target_pairs={{0,16},{4,20},{8,24},{12,28},{16,0},{20,4},{24,8},{28,12},{1,17},{... | collective-permute-start | bytes 368648 | tf_op jit(solution)/shard_map/ppermute | solution.py:519
  184.6 14.9 %collective-permute-done.56 = bf16[480,128]{1,0:T(8,128)(2,1)S(1)} collective-permute-done((bf16[480,128]{1,0:T(8,128)(2,1)S(1)}, bf16[480,128]{1,0:T(8,128)(2,1)S(1)}, u32[]{:S(2)}, u32[]{:S(2)}) %collective-permute-start.56) | collective-permute-done | bytes 122912 | tf_op jit(solution)/shard_map/ppermute | solution.py:519
  199.5 3.4 %collective-permute-start.59 = (bf16[384,384]{1,0:T(8,128)(2,1)S(1)}, bf16[384,384]{1,0:T(8,128)(2,1)S(1)}, u32[]{:S(2)}, u32[]{:S(2)}) collective-permute-start(bf16[384,384]{1,0:T(8,128)(2,1)S(1)} %fusion.13), channel_id=1, source_target_pairs={{0,16},{4,20},{8,24},{12,28},{16,0},{20,4},{24,8},{28,12},{1,17},{... | collective-permute-start | bytes 884744 | tf_op jit(solution)/shard_map/ppermute | solution.py:519
  206.5 5.8 %collective-permute-done.59 = bf16[384,384]{1,0:T(8,128)(2,1)S(1)} collective-permute-done((bf16[384,384]{1,0:T(8,128)(2,1)S(1)}, bf16[384,384]{1,0:T(8,128)(2,1)S(1)}, u32[]{:S(2)}, u32[]{:S(2)}) %collective-permute-start.59) | collective-permute-done | bytes 294944 | tf_op jit(solution)/shard_map/ppermute | solution.py:519
  214.0 1.8 collective-permute-start.57
  218.3 2.5 %collective-permute-done.60 = bf16[384,384]{1,0:T(8,128)(2,1)S(1)} collective-permute-done((bf16[384,384]{1,0:T(8,128)(2,1)S(1)}, bf16[384,384]{1,0:T(8,128)(2,1)S(1)}, u32[]{:S(2)}, u32[]{:S(2)}) %collective-permute-start.60) | collective-permute-done | bytes 294944 | tf_op jit(solution)/shard_map/ppermute | solution.py:519
  222.3 6.4 %collective-permute-done.62 = bf16[768,384]{1,0:T(8,128)(2,1)S(1)} collective-permute-done((bf16[768,384]{1,0:T(8,128)(2,1)S(1)}, bf16[768,384]{1,0:T(8,128)(2,1)S(1)}, u32[]{:S(2)}, u32[]{:S(2)}) %collective-permute-start.62) | collective-permute-done | bytes 589856 | tf_op jit(solution)/shard_map/ppermute | solution.py:519
  (277 shorter events, 59.3 us)
Async XLA Ops:
  3.0 13.5 %collective-permute-start.6 = (bf16[384,384]{1,0:T(8,128)(2,1)S(1)}, bf16[384,384]{1,0:T(8,128)(2,1)S(1)}, u32[]{:S(2)}, u32[]{:S(2)}) collective-permute-start(bf16[384,384]{1,0:T(8,128)(2,1)S(1)} %slice_select_fusion.3), channel_id=1, source_target_pairs={{0,2},{1,3},{2,0},{3,1},{4,6},{5,7},{6,4},{7,5},{8,10},{9,11},{10,... | collective-permute-start | bytes 884744 | tf_op jit(solution)/shard_map/ppermute | solution.py:519
  7.3 12.4 %collective-permute-start.5 = (bf16[384,384]{1,0:T(8,128)(2,1)S(1)}, bf16[384,384]{1,0:T(8,128)(2,1)S(1)}, u32[]{:S(2)}, u32[]{:S(2)}) collective-permute-start(bf16[384,384]{1,0:T(8,128)(2,1)S(1)} %slice_select_fusion.4), channel_id=1, source_target_pairs={{0,2},{1,3},{2,0},{3,1},{4,6},{5,7},{6,4},{7,5},{8,10},{9,11},{10,... | collective-permute-start | bytes 884744 | tf_op jit(solution)/shard_map/ppermute | solution.py:519
  11.6 8.1 %collective-permute-start.4 = (f32[32,768]{1,0:T(8,128)S(1)}, f32[32,768]{1,0:T(8,128)S(1)}, u32[]{:S(2)}, u32[]{:S(2)}) collective-permute-start(f32[32,768]{1,0:T(8,128)S(1)} %get-tuple-element.321), channel_id=1, source_target_pairs={{0,1},{1,2},{2,3},{4,5},{5,6},{6,7},{8,9},{9,10},{10,11},{12,13},{... | collective-permute-start | bytes 294920 | tf_op jit(solution)/shard_map/ppermute | solution.py:524
  13.4 8.4 %collective-permute-start.7 = (f32[32,768]{1,0:T(8,128)S(1)}, f32[32,768]{1,0:T(8,128)S(1)}, u32[]{:S(2)}, u32[]{:S(2)}) collective-permute-start(f32[32,768]{1,0:T(8,128)S(1)} %get-tuple-element.321), channel_id=1, source_target_pairs={{0,2},{1,3},{4,6},{5,7},{8,10},{9,11},{12,14},{13,15},{16,18},{17,... | collective-permute-start | bytes 294920 | tf_op jit(solution)/shard_map/ppermute | solution.py:524
  21.8 17.7 %collective-permute-start.10 = (bf16[288,768]{1,0:T(8,128)(2,1)S(1)}, bf16[288,768]{1,0:T(8,128)(2,1)S(1)}, u32[]{:S(2)}, u32[]{:S(2)}) collective-permute-start(bf16[288,768]{1,0:T(8,128)(2,1)S(1)} %slice_select_fusion), channel_id=1, source_target_pairs={{0,2},{1,3},{2,0},{3,1},{4,6},{5,7},{6,4},{7,5},{8,10},{9,11},{10,... | collective-permute-start | bytes 1327112 | tf_op jit(solution)/shard_map/ppermute | solution.py:519
  24.4 9.9 %collective-permute-start.8 = (bf16[384,384]{1,0:T(8,128)(2,1)S(1)}, bf16[384,384]{1,0:T(8,128)(2,1)S(1)}, u32[]{:S(2)}, u32[]{:S(2)}) collective-permute-start(bf16[384,384]{1,0:T(8,128)(2,1)S(1)} %collective-permute-done.6), channel_id=1, source_target_pairs={{0,4},{4,0},{8,12},{12,8},{16,20},{20,16},{24,28},{28,24},{1,5},{5... | collective-permute-start | bytes 884744 | tf_op jit(solution)/shard_map/ppermute | solution.py:519
  26.1 13.4 %collective-permute-start.11 = (bf16[384,384]{1,0:T(8,128)(2,1)S(1)}, bf16[384,384]{1,0:T(8,128)(2,1)S(1)}, u32[]{:S(2)}, u32[]{:S(2)}) collective-permute-start(bf16[384,384]{1,0:T(8,128)(2,1)S(1)} %collective-permute-done.5), channel_id=1, source_target_pairs={{0,4},{4,0},{8,12},{12,8},{16,20},{20,16},{24,28},{28,24},{1,5},{5... | collective-permute-start | bytes 884744 | tf_op jit(solution)/shard_map/ppermute | solution.py:519
  26.7 14.4 %collective-permute-start.9 = (bf16[384,384]{1,0:T(8,128)(2,1)S(1)}, bf16[384,384]{1,0:T(8,128)(2,1)S(1)}, u32[]{:S(2)}, u32[]{:S(2)}) collective-permute-start(bf16[384,384]{1,0:T(8,128)(2,1)S(1)} %slice_select_fusion.2), channel_id=1, source_target_pairs={{0,2},{1,3},{2,0},{3,1},{4,6},{5,7},{6,4},{7,5},{8,10},{9,11},{10,... | collective-permute-start | bytes 884744 | tf_op jit(solution)/shard_map/ppermute | solution.py:519
  42.1 12.2 %collective-permute-start.14 = (bf16[288,768]{1,0:T(8,128)(2,1)S(1)}, bf16[288,768]{1,0:T(8,128)(2,1)S(1)}, u32[]{:S(2)}, u32[]{:S(2)}) collective-permute-start(bf16[288,768]{1,0:T(8,128)(2,1)S(1)} %collective-permute-done.10), channel_id=1, source_target_pairs={{0,8},{4,12},{8,0},{12,4},{16,24},{20,28},{24,16},{28,20},{1,9},{5... | collective-permute-start | bytes 1327112 | tf_op jit(solution)/shard_map/ppermute | solution.py:519
  43.7 8.7 %collective-permute-start.16 = (bf16[192,768]{1,0:T(8,128)(2,1)S(1)}, bf16[192,768]{1,0:T(8,128)(2,1)S(1)}, u32[]{:S(2)}, u32[]{:S(2)}) collective-permute-start(bf16[192,768]{1,0:T(8,128)(2,1)S(1)} %slice_select_fusion.1), channel_id=1, source_target_pairs={{0,2},{1,3},{2,0},{3,1},{4,6},{5,7},{6,4},{7,5},{8,10},{9,11},{10,... | collective-permute-start | bytes 884744 | tf_op jit(solution)/shard_map/ppermute | solution.py:519
  45.4 8.4 %collective-permute-start.15 = (bf16[384,384]{1,0:T(8,128)(2,1)S(1)}, bf16[384,384]{1,0:T(8,128)(2,1)S(1)}, u32[]{:S(2)}, u32[]{:S(2)}) collective-permute-start(bf16[384,384]{1,0:T(8,128)(2,1)S(1)} %collective-permute-done.9), channel_id=1, source_target_pairs={{0,4},{4,0},{8,12},{12,8},{16,20},{20,16},{24,28},{28,24},{1,5},{5... | collective-permute-start | bytes 884744 | tf_op jit(solution)/shard_map/ppermute | solution.py:519
  55.3 9.0 %collective-permute-start.18 = (bf16[192,768]{1,0:T(8,128)(2,1)S(1)}, bf16[192,768]{1,0:T(8,128)(2,1)S(1)}, u32[]{:S(2)}, u32[]{:S(2)}) collective-permute-start(bf16[192,768]{1,0:T(8,128)(2,1)S(1)} %collective-permute-done.16), channel_id=1, source_target_pairs={{0,4},{4,0},{8,12},{12,8},{16,20},{20,16},{24,28},{28,24},{1,5},{5... | collective-permute-start | bytes 884744 | tf_op jit(solution)/shard_map/ppermute | solution.py:519
  57.0 7.6 %collective-permute-start.20 = (bf16[768,384]{1,0:T(8,128)(2,1)S(1)}, bf16[768,384]{1,0:T(8,128)(2,1)S(1)}, u32[]{:S(2)}, u32[]{:S(2)}) collective-permute-start(bf16[768,384]{1,0:T(8,128)(2,1)S(1)} %maximum_select_fusion.7.ia_ref), channel_id=1, source_target_pairs={{0,1},{1,0},{2,3},{3,2},{4,5},{5,4},{6,7},{7,6},{8,9},{9,8},{10,11... | collective-permute-start | bytes 1769480 | tf_op jit(solution)/shard_map/ppermute | solution.py:519
  72.8 18.5 %collective-permute-start.23 = (bf16[768,384]{1,0:T(8,128)(2,1)S(1)}, bf16[768,384]{1,0:T(8,128)(2,1)S(1)}, u32[]{:S(2)}, u32[]{:S(2)}) collective-permute-start(bf16[768,384]{1,0:T(8,128)(2,1)S(1)} %get-tuple-element.446), channel_id=1, source_target_pairs={{0,2},{1,3},{2,0},{3,1},{4,6},{5,7},{6,4},{7,5},{8,10},{9,11},{10,... | collective-permute-start | bytes 1769480 | tf_op jit(solution)/shard_map/ppermute | solution.py:519
  74.7 16.6 %collective-permute-start.24 = (bf16[768,384]{1,0:T(8,128)(2,1)S(1)}, bf16[768,384]{1,0:T(8,128)(2,1)S(1)}, u32[]{:S(2)}, u32[]{:S(2)}) collective-permute-start(bf16[768,384]{1,0:T(8,128)(2,1)S(1)} %pad_maximum_fusion.3), channel_id=1, source_target_pairs={{0,8},{4,12},{8,0},{12,4},{16,24},{20,28},{24,16},{28,20},{1,9},{5... | collective-permute-start | bytes 1769480 | tf_op jit(solution)/shard_map/ppermute | solution.py:519
  91.3 7.8 %collective-permute-start.28 = (bf16[2,1536,384]{2,1,0:T(8,128)(2,1)S(1)}, bf16[2,1536,384]{2,1,0:T(8,128)(2,1)S(1)}, u32[]{:S(2)}, u32[]{:S(2)}) collective-permute-start(bf16[2,1536,384]{2,1,0:T(8,128)(2,1)S(1)} %get-tuple-element.465), channel_id=1, source_target_pairs={{0,1},{1,0},{2,3},{3,2},{4,5},{5,4},{6,7},{7,6},{8,9},{9,8},{10,11... | collective-permute-start | bytes 7077896 | tf_op jit(solution)/shard_map/ppermute | solution.py:519
  92.4 9.3 %collective-permute-start.25 = (bf16[384,384]{1,0:T(8,128)(2,1)S(1)}, bf16[384,384]{1,0:T(8,128)(2,1)S(1)}, u32[]{:S(2)}, u32[]{:S(2)}) collective-permute-start(bf16[384,384]{1,0:T(8,128)(2,1)S(1)} %select_convert_fusion.7), channel_id=1, source_target_pairs={{0,4},{4,0},{8,12},{12,8},{16,20},{20,16},{24,28},{28,24},{1,5},{5... | collective-permute-start | bytes 884744 | tf_op jit(solution)/shard_map/ppermute | solution.py:519
  93.9 10.7 %collective-permute-start.30 = (bf16[384,384]{1,0:T(8,128)(2,1)S(1)}, bf16[384,384]{1,0:T(8,128)(2,1)S(1)}, u32[]{:S(2)}, u32[]{:S(2)}) collective-permute-start(bf16[384,384]{1,0:T(8,128)(2,1)S(1)} %fusion.10), channel_id=1, source_target_pairs={{0,2},{1,3},{2,0},{3,1},{4,6},{5,7},{6,4},{7,5},{8,10},{9,11},{10,... | collective-permute-start | bytes 884744 | tf_op jit(solution)/shard_map/ppermute | solution.py:519
  98.6 18.3 %collective-permute-start.32 = (bf16[896,384]{1,0:T(8,128)(2,1)S(1)}, bf16[896,384]{1,0:T(8,128)(2,1)S(1)}, u32[]{:S(2)}, u32[]{:S(2)}) collective-permute-start(bf16[896,384]{1,0:T(8,128)(2,1)S(1)} %pad_maximum_fusion.2), channel_id=1, source_target_pairs={{0,8},{4,12},{8,0},{12,4},{16,24},{20,28},{24,16},{28,20},{1,9},{5... | collective-permute-start | bytes 2064392 | tf_op jit(solution)/shard_map/ppermute | solution.py:519
  100.1 29.4 %collective-permute-start.34 = (bf16[1536,384]{1,0:T(8,128)(2,1)S(1)}, bf16[1536,384]{1,0:T(8,128)(2,1)S(1)}, u32[]{:S(2)}, u32[]{:S(2)}) collective-permute-start(bf16[1536,384]{1,0:T(8,128)(2,1)S(1)} %pad_maximum_fusion.1), channel_id=1, source_target_pairs={{0,4},{4,0},{8,12},{12,8},{16,20},{20,16},{24,28},{28,24},{1,5},{5... | collective-permute-start | bytes 3538952 | tf_op jit(solution)/shard_map/ppermute | solution.py:519
  102.9 9.9 %collective-permute-start.31 = (f32[64,768]{1,0:T(8,128)S(1)}, f32[64,768]{1,0:T(8,128)S(1)}, u32[]{:S(2)}, u32[]{:S(2)}) collective-permute-start(f32[64,768]{1,0:T(8,128)S(1)} %pad_maximum_fusion.6), channel_id=1, source_target_pairs={{2,0},{3,1},{6,4},{7,5},{10,8},{11,9},{14,12},{15,13},{18,16},{19,... | collective-permute-start | bytes 589832 | tf_op jit(solution)/shard_map/ppermute | solution.py:524
  104.7 24.3 %collective-permute-start.35 = (bf16[768,384]{1,0:T(8,128)(2,1)S(1)}, bf16[768,384]{1,0:T(8,128)(2,1)S(1)}, u32[]{:S(2)}, u32[]{:S(2)}) collective-permute-start(bf16[768,384]{1,0:T(8,128)(2,1)S(1)} %pad_maximum_fusion.4), channel_id=1, source_target_pairs={{0,8},{4,12},{8,0},{12,4},{16,24},{20,28},{24,16},{28,20},{1,9},{5... | collective-permute-start | bytes 1769480 | tf_op jit(solution)/shard_map/ppermute | solution.py:519
  117.2 9.0 %collective-permute-start.33 = (bf16[448,384]{1,0:T(8,128)(2,1)S(1)}, bf16[448,384]{1,0:T(8,128)(2,1)S(1)}, u32[]{:S(2)}, u32[]{:S(2)}) collective-permute-start(bf16[448,384]{1,0:T(8,128)(2,1)S(1)} %fusion.3), channel_id=1, source_target_pairs={{0,2},{1,3},{2,0},{3,1},{4,6},{5,7},{6,4},{7,5},{8,10},{9,11},{10,... | collective-permute-start | bytes 1032200 | tf_op jit(solution)/shard_map/ppermute | solution.py:519
  129.6 7.3 %collective-permute-start.36 = (bf16[224,384]{1,0:T(8,128)(2,1)S(1)}, bf16[224,384]{1,0:T(8,128)(2,1)S(1)}, u32[]{:S(2)}, u32[]{:S(2)}) collective-permute-start(bf16[224,384]{1,0:T(8,128)(2,1)S(1)} %select_convert_fusion.10), channel_id=1, source_target_pairs={{0,4},{4,0},{8,12},{12,8},{16,20},{20,16},{24,28},{28,24},{1,5},{5... | collective-permute-start | bytes 516104 | tf_op jit(solution)/shard_map/ppermute | solution.py:519
  131.4 8.2 %collective-permute-start.39 = (bf16[192,384]{1,0:T(8,128)(2,1)S(1)}, bf16[192,384]{1,0:T(8,128)(2,1)S(1)}, u32[]{:S(2)}, u32[]{:S(2)}) collective-permute-start(bf16[192,384]{1,0:T(8,128)(2,1)S(1)} %select_convert_fusion.11), channel_id=1, source_target_pairs={{0,8},{4,12},{8,0},{12,4},{16,24},{20,28},{24,16},{28,20},{1,9},{5... | collective-permute-start | bytes 442376 | tf_op jit(solution)/shard_map/ppermute | solution.py:519
  131.9 7.8 %collective-permute-start.40 = (bf16[192,384]{1,0:T(8,128)(2,1)S(1)}, bf16[192,384]{1,0:T(8,128)(2,1)S(1)}, u32[]{:S(2)}, u32[]{:S(2)}) collective-permute-start(bf16[192,384]{1,0:T(8,128)(2,1)S(1)} %select_convert_fusion.12), channel_id=1, source_target_pairs={{0,4},{4,0},{8,12},{12,8},{16,20},{20,16},{24,28},{28,24},{1,5},{5... | collective-permute-start | bytes 442376 | tf_op jit(solution)/shard_map/ppermute | solution.py:519
  132.5 16.2 %collective-permute-start.38 = (bf16[768,384]{1,0:T(8,128)(2,1)S(1)}, bf16[768,384]{1,0:T(8,128)(2,1)S(1)}, u32[]{:S(2)}, u32[]{:S(2)}) collective-permute-start(bf16[768,384]{1,0:T(8,128)(2,1)S(1)} %fusion.1), channel_id=1, source_target_pairs={{0,2},{1,3},{2,0},{3,1},{4,6},{5,7},{6,4},{7,5},{8,10},{9,11},{10,... | collective-permute-start | bytes 1769480 | tf_op jit(solution)/shard_map/ppermute | solution.py:519
  137.0 13.9 %collective-permute-start.44 = (bf16[224,384]{1,0:T(8,128)(2,1)S(1)}, bf16[224,384]{1,0:T(8,128)(2,1)S(1)}, u32[]{:S(2)}, u32[]{:S(2)}) collective-permute-start(bf16[224,384]{1,0:T(8,128)(2,1)S(1)} %fusion.39), channel_id=1, source_target_pairs={{0,16},{4,20},{8,24},{12,28},{16,0},{20,4},{24,8},{28,12},{1,17},{... | collective-permute-start | bytes 516104 | tf_op jit(solution)/shard_map/ppermute | solution.py:519
  139.8 12.9 %collective-permute-start.43 = (bf16[384,384]{1,0:T(8,128)(2,1)S(1)}, bf16[384,384]{1,0:T(8,128)(2,1)S(1)}, u32[]{:S(2)}, u32[]{:S(2)}) collective-permute-start(bf16[384,384]{1,0:T(8,128)(2,1)S(1)} %get-tuple-element.535), channel_id=1, source_target_pairs={{0,2},{1,3},{2,0},{3,1},{4,6},{5,7},{6,4},{7,5},{8,10},{9,11},{10,... | collective-permute-start | bytes 884744 | tf_op jit(solution)/shard_map/ppermute | solution.py:519
  140.1 15.2 %collective-permute-start.42 = (bf16[192,384]{1,0:T(8,128)(2,1)S(1)}, bf16[192,384]{1,0:T(8,128)(2,1)S(1)}, u32[]{:S(2)}, u32[]{:S(2)}) collective-permute-start(bf16[192,384]{1,0:T(8,128)(2,1)S(1)} %fusion.37), channel_id=1, source_target_pairs={{0,16},{4,20},{8,24},{12,28},{16,0},{20,4},{24,8},{28,12},{1,17},{... | collective-permute-start | bytes 442376 | tf_op jit(solution)/shard_map/ppermute | solution.py:519
  152.7 9.2 %collective-permute-start.45 = (bf16[192,384]{1,0:T(8,128)(2,1)S(1)}, bf16[192,384]{1,0:T(8,128)(2,1)S(1)}, u32[]{:S(2)}, u32[]{:S(2)}) collective-permute-start(bf16[192,384]{1,0:T(8,128)(2,1)S(1)} %fusion.38), channel_id=1, source_target_pairs={{0,16},{4,20},{8,24},{12,28},{16,0},{20,4},{24,8},{28,12},{1,17},{... | collective-permute-start | bytes 442376 | tf_op jit(solution)/shard_map/ppermute | solution.py:519
  155.6 23.4 %collective-permute-start.47 = (bf16[384,384]{1,0:T(8,128)(2,1)S(1)}, bf16[384,384]{1,0:T(8,128)(2,1)S(1)}, u32[]{:S(2)}, u32[]{:S(2)}) collective-permute-start(bf16[384,384]{1,0:T(8,128)(2,1)S(1)} %select_convert_fusion.4), channel_id=1, source_target_pairs={{0,8},{4,12},{8,0},{12,4},{16,24},{20,28},{24,16},{28,20},{1,9},{5... | collective-permute-start | bytes 884744 | tf_op jit(solution)/shard_map/ppermute | solution.py:519
  157.1 22.0 %collective-permute-start.48 = (bf16[224,384]{1,0:T(8,128)(2,1)S(1)}, bf16[224,384]{1,0:T(8,128)(2,1)S(1)}, u32[]{:S(2)}, u32[]{:S(2)}) collective-permute-start(bf16[224,384]{1,0:T(8,128)(2,1)S(1)} %add_convert_fusion.3), channel_id=1, source_target_pairs={{0,4},{4,0},{8,12},{12,8},{16,20},{20,16},{24,28},{28,24},{1,5},{5... | collective-permute-start | bytes 516104 | tf_op jit(solution)/shard_map/ppermute | solution.py:519
  158.8 21.0 %collective-permute-start.50 = (bf16[384,384]{1,0:T(8,128)(2,1)S(1)}, bf16[384,384]{1,0:T(8,128)(2,1)S(1)}, u32[]{:S(2)}, u32[]{:S(2)}) collective-permute-start(bf16[384,384]{1,0:T(8,128)(2,1)S(1)} %get-tuple-element.564), channel_id=1, source_target_pairs={{0,4},{4,0},{8,12},{12,8},{16,20},{20,16},{24,28},{28,24},{1,5},{5... | collective-permute-start | bytes 884744 | tf_op jit(solution)/shard_map/ppermute | solution.py:519
  160.2 12.1 %collective-permute-start.46 = (bf16[192,384]{1,0:T(8,128)(2,1)S(1)}, bf16[192,384]{1,0:T(8,128)(2,1)S(1)}, u32[]{:S(2)}, u32[]{:S(2)}) collective-permute-start(bf16[192,384]{1,0:T(8,128)(2,1)S(1)} %add_convert_fusion.5), channel_id=1, source_target_pairs={{0,8},{4,12},{8,0},{12,4},{16,24},{20,28},{24,16},{28,20},{1,9},{5... | collective-permute-start | bytes 442376 | tf_op jit(solution)/shard_map/ppermute | solution.py:519
  161.9 8.5 %collective-permute-start.51 = (bf16[480,128]{1,0:T(8,128)(2,1)S(1)}, bf16[480,128]{1,0:T(8,128)(2,1)S(1)}, u32[]{:S(2)}, u32[]{:S(2)}) collective-permute-start(bf16[480,128]{1,0:T(8,128)(2,1)S(1)} %pad_maximum_fusion.9), channel_id=1, source_target_pairs={{0,4},{4,0},{8,12},{12,8},{16,20},{20,16},{24,28},{28,24},{1,5},{5... | collective-permute-start | bytes 368648 | tf_op jit(solution)/shard_map/ppermute | solution.py:519
  172.2 9.6 %collective-permute-start.55 = (bf16[480,128]{1,0:T(8,128)(2,1)S(1)}, bf16[480,128]{1,0:T(8,128)(2,1)S(1)}, u32[]{:S(2)}, u32[]{:S(2)}) collective-permute-start(bf16[480,128]{1,0:T(8,128)(2,1)S(1)} %pad_maximum_fusion.10), channel_id=1, source_target_pairs={{0,8},{4,12},{8,0},{12,4},{16,24},{20,28},{24,16},{28,20},{1,9},{5... | collective-permute-start | bytes 368648 | tf_op jit(solution)/shard_map/ppermute | solution.py:519
  177.1 27.8 %collective-permute-start.52 = (bf16[384,384]{1,0:T(8,128)(2,1)S(1)}, bf16[384,384]{1,0:T(8,128)(2,1)S(1)}, u32[]{:S(2)}, u32[]{:S(2)}) collective-permute-start(bf16[384,384]{1,0:T(8,128)(2,1)S(1)} %maximum_select_fusion.14), channel_id=1, source_target_pairs={{0,4},{4,0},{8,12},{12,8},{16,20},{20,16},{24,28},{28,24},{1,5},{5... | collective-permute-start | bytes 884744 | tf_op jit(solution)/shard_map/ppermute | solution.py:519
  179.0 27.3 %collective-permute-start.63 = (bf16[384,384]{1,0:T(8,128)(2,1)S(1)}, bf16[384,384]{1,0:T(8,128)(2,1)S(1)}, u32[]{:S(2)}, u32[]{:S(2)}) collective-permute-start(bf16[384,384]{1,0:T(8,128)(2,1)S(1)} %maximum_select_fusion.15), channel_id=1, source_target_pairs={{0,8},{4,12},{8,0},{12,4},{16,24},{20,28},{24,16},{28,20},{1,9},{5... | collective-permute-start | bytes 884744 | tf_op jit(solution)/shard_map/ppermute | solution.py:519
  179.1 26.9 %collective-permute-start.54 = (bf16[384,384]{1,0:T(8,128)(2,1)S(1)}, bf16[384,384]{1,0:T(8,128)(2,1)S(1)}, u32[]{:S(2)}, u32[]{:S(2)}) collective-permute-start(bf16[384,384]{1,0:T(8,128)(2,1)S(1)} %fusion.40), channel_id=1, source_target_pairs={{0,16},{4,20},{8,24},{12,28},{16,0},{20,4},{24,8},{28,12},{1,17},{... | collective-permute-start | bytes 884744 | tf_op jit(solution)/shard_map/ppermute | solution.py:519
  179.8 33.9 %collective-permute-start.53 = (bf16[448,384]{1,0:T(8,128)(2,1)S(1)}, bf16[448,384]{1,0:T(8,128)(2,1)S(1)}, u32[]{:S(2)}, u32[]{:S(2)}) collective-permute-start(bf16[448,384]{1,0:T(8,128)(2,1)S(1)} %maximum_select_fusion.13), channel_id=1, source_target_pairs={{0,8},{4,12},{8,0},{12,4},{16,24},{20,28},{24,16},{28,20},{1,9},{5... | collective-permute-start | bytes 1032200 | tf_op jit(solution)/shard_map/ppermute | solution.py:519
  182.0 17.5 %collective-permute-start.56 = (bf16[480,128]{1,0:T(8,128)(2,1)S(1)}, bf16[480,128]{1,0:T(8,128)(2,1)S(1)}, u32[]{:S(2)}, u32[]{:S(2)}) collective-permute-start(bf16[480,128]{1,0:T(8,128)(2,1)S(1)} %pad_maximum_fusion.11), channel_id=1, source_target_pairs={{0,16},{4,20},{8,24},{12,28},{16,0},{20,4},{24,8},{28,12},{1,17},{... | collective-permute-start | bytes 368648 | tf_op jit(solution)/shard_map/ppermute | solution.py:519
  199.5 12.8 %collective-permute-start.59 = (bf16[384,384]{1,0:T(8,128)(2,1)S(1)}, bf16[384,384]{1,0:T(8,128)(2,1)S(1)}, u32[]{:S(2)}, u32[]{:S(2)}) collective-permute-start(bf16[384,384]{1,0:T(8,128)(2,1)S(1)} %fusion.13), channel_id=1, source_target_pairs={{0,16},{4,20},{8,24},{12,28},{16,0},{20,4},{24,8},{28,12},{1,17},{... | collective-permute-start | bytes 884744 | tf_op jit(solution)/shard_map/ppermute | solution.py:519
  206.2 10.5 %collective-permute-start.61 = (bf16[384,384]{1,0:T(8,128)(2,1)S(1)}, bf16[384,384]{1,0:T(8,128)(2,1)S(1)}, u32[]{:S(2)}, u32[]{:S(2)}) collective-permute-start(bf16[384,384]{1,0:T(8,128)(2,1)S(1)} %add_convert_fusion.2), channel_id=1, source_target_pairs={{0,8},{4,12},{8,0},{12,4},{16,24},{20,28},{24,16},{28,20},{1,9},{5... | collective-permute-start | bytes 884744 | tf_op jit(solution)/shard_map/ppermute | solution.py:519
  212.4 8.4 %collective-permute-start.60 = (bf16[384,384]{1,0:T(8,128)(2,1)S(1)}, bf16[384,384]{1,0:T(8,128)(2,1)S(1)}, u32[]{:S(2)}, u32[]{:S(2)}) collective-permute-start(bf16[384,384]{1,0:T(8,128)(2,1)S(1)} %add_convert_fusion.1), channel_id=1, source_target_pairs={{0,8},{4,12},{8,0},{12,4},{16,24},{20,28},{24,16},{28,20},{1,9},{5... | collective-permute-start | bytes 884744 | tf_op jit(solution)/shard_map/ppermute | solution.py:519
  214.0 7.9 %collective-permute-start.57 = (bf16[448,384]{1,0:T(8,128)(2,1)S(1)}, bf16[448,384]{1,0:T(8,128)(2,1)S(1)}, u32[]{:S(2)}, u32[]{:S(2)}) collective-permute-start(bf16[448,384]{1,0:T(8,128)(2,1)S(1)} %pad_maximum_fusion.5), channel_id=1, source_target_pairs={{0,2},{1,3},{2,0},{3,1},{4,6},{5,7},{6,4},{7,5},{8,10},{9,11},{10,... | collective-permute-start | bytes 1032200 | tf_op jit(solution)/shard_map/ppermute | solution.py:519
  217.0 11.8 %collective-permute-start.62 = (bf16[768,384]{1,0:T(8,128)(2,1)S(1)}, bf16[768,384]{1,0:T(8,128)(2,1)S(1)}, u32[]{:S(2)}, u32[]{:S(2)}) collective-permute-start(bf16[768,384]{1,0:T(8,128)(2,1)S(1)} %maximum_select_fusion.10), channel_id=1, source_target_pairs={{0,4},{4,0},{8,12},{12,8},{16,20},{20,16},{24,28},{28,24},{1,5},{5... | collective-permute-start | bytes 1769480 | tf_op jit(solution)/shard_map/ppermute | solution.py:519
  222.2 9.2 %collective-permute-start.58 = (bf16[896,384]{1,0:T(8,128)(2,1)S(1)}, bf16[896,384]{1,0:T(8,128)(2,1)S(1)}, u32[]{:S(2)}, u32[]{:S(2)}) collective-permute-start(bf16[896,384]{1,0:T(8,128)(2,1)S(1)} %maximum_select_fusion.4), channel_id=1, source_target_pairs={{0,1},{1,0},{2,3},{3,2},{4,5},{5,4},{6,7},{7,6},{8,9},{9,8},{10,11... | collective-permute-start | bytes 2064392 | tf_op jit(solution)/shard_map/ppermute | solution.py:519
  (37 other events, 255.9 us)

commit v7 on v6

--- a/solution.py
+++ b/solution.py
@@ -905,7 +905,8 @@
         "back": run_back,
         "t4": run_fourth,
     }
-    for word in ORDER:
+    last_small = max(i for i, word in enumerate(ORDER) if word == "+sm")
+    for step, word in enumerate(ORDER):
         sign, name = word[0], word[1:]
         if sign == "K":
             kernels[name]()
@@ -914,6 +915,10 @@
         elif sign == "+":
             if name in KINDS and name not in pump.flows:
                 add_flow(name)
+            if step == last_small:
+                axis, bit, v = pump.ready["sm"]
+                hold = 0.0 * jnp.clip(pump.ready["N"][2][:1, :1].astype(F32), -1.0, 1.0)
+                pump.ready["sm"] = axis, bit, v + hold.astype(v.dtype)
             pump.issue(name)
         else:
             pump.finish(name)

time: 238 us -> 238 us (level)
  waiting for transfers between devices: 100 us -> 96.8 us
    ppermute x60, waiting for transfers between devices: 91.9 us -> 88.4 us  [swap(): return lax.ppermute(x, axis, [(i, i ^ bit) for i in range(size)])]
  transfers between devices with their start and end apart: 64 -> 64, of which waited for: 28 -> 26; matrix products, arithmetic and copies ran while one was open for 8% -> 8% of each run, Pallas kernels for 17% -> 17%
where the time goes in v7:
time: 238 us; the launch traced here: 235 us
  waiting for transfers between devices  96.8 us (41%)
  starting transfers between devices  69.8 us (29%)
  Pallas kernels  40.5 us (17%)
  other arithmetic  20.8 us (9%)
  local copies, waits for them, and re-layouts  3.63 us (2%)
  between operations  3.18 us (1%)
    ppermute x60, waiting for transfers between devices, swap(): return lax.ppermute(x, axis, [(i, i ^ bit) for i in range(size)])  88.4 us
    ppermute x60, starting transfers between devices, swap(): return lax.ppermute(x, axis, [(i, i ^ bit) for i in range(size)])  62.4 us
    pallas_call x9, Pallas kernels, call(): pl.pallas_call(kernel, out_shape=outs, in_specs=specs, out_specs=[pl.Bloc...  40.5 us
    ppermute x4, waiting for transfers between devices, shift(): lax.ppermute(x, 'tensor', [(i, i + by) for i in range(size) if 0 <= i + b...  8.45 us
    ppermute x4, starting transfers between devices, shift(): lax.ppermute(x, 'tensor', [(i, i + by) for i in range(size) if 0 <= i + b...  7.36 us
  transfers between devices with their start and end apart: 64, of which 26 were waited for; matrix products, arithmetic and copies ran while one was open for 8% of the time, Pallas kernels for 17%

profile of v7, /device:TPU:0, one launch (start us, length us, event | category | flops | bytes accessed | tf_op | source)
XLA Modules:
  0.0 234.7 jit_solution(1643510081624232036)
XLA Ops:
  3.0 3.0 %collective-permute-start.6 = (bf16[384,384]{1,0:T(8,128)(2,1)S(1)}, bf16[384,384]{1,0:T(8,128)(2,1)S(1)}, u32[]{:S(2)}, u32[]{:S(2)}) collective-permute-start(bf16[384,384]{1,0:T(8,128)(2,1)S(1)} %slice_select_fusion.3), channel_id=1, source_target_pairs={{0,2},{1,3},{2,0},{3,1},{4,6},{5,7},{6,4},{7,5},{8,10},{9,11},{10,... | collective-permute-start | bytes 884744 | tf_op jit(solution)/shard_map/ppermute | solution.py:519
  8.6 3.0 %shard_map.356 = (f32[1536,128]{1,0:T(8,128)S(1)}, bf16[256,768]{1,0:T(8,128)(2,1)S(1)}, f32[256,768]{1,0:T(8,128)S(1)}, f32[32,768]{1,0:T(8,128)S(1)}) custom-call(bf16[256,768]{1,0:T(8,128)(2,1)S(1)} %bitcast.78, f32[1,768]{1,0:T(1,128)S(1)} %broadcast_in_dim.34.g_ref, f32[16,768]{1,0:T(8,128)S(1)} %copy-done.4, f32[16,768]{1,0:T(8,128)S(1)} %copy-done.5, ...), custom_call_target="tpu_custom_call" | custom-call | flops 25165824 | bytes 2739200 | tf_op jit(solution)/shard_map/pallas_call | solution.py:71
  11.6 1.8 collective-permute-start.4
  13.4 3.0 %collective-permute-start.7 = (f32[32,768]{1,0:T(8,128)S(1)}, f32[32,768]{1,0:T(8,128)S(1)}, u32[]{:S(2)}, u32[]{:S(2)}) collective-permute-start(f32[32,768]{1,0:T(8,128)S(1)} %get-tuple-element.321), channel_id=1, source_target_pairs={{0,2},{1,3},{4,6},{5,7},{8,10},{9,11},{12,14},{13,15},{16,18},{17,... | collective-permute-start | bytes 294920 | tf_op jit(solution)/shard_map/ppermute | solution.py:524
  16.5 3.3 %collective-permute-done.5 = bf16[384,384]{1,0:T(8,128)(2,1)S(1)} collective-permute-done((bf16[384,384]{1,0:T(8,128)(2,1)S(1)}, bf16[384,384]{1,0:T(8,128)(2,1)S(1)}, u32[]{:S(2)}, u32[]{:S(2)}) %collective-permute-start.5) | collective-permute-done | bytes 294944 | tf_op jit(solution)/shard_map/ppermute | solution.py:519
  19.7 2.1 collective-permute-done.7.f2_ref
  21.8 2.5 %collective-permute-start.10 = (bf16[288,768]{1,0:T(8,128)(2,1)S(1)}, bf16[288,768]{1,0:T(8,128)(2,1)S(1)}, u32[]{:S(2)}, u32[]{:S(2)}) collective-permute-start(bf16[288,768]{1,0:T(8,128)(2,1)S(1)} %slice_select_fusion), channel_id=1, source_target_pairs={{0,2},{1,3},{2,0},{3,1},{4,6},{5,7},{6,4},{7,5},{8,10},{9,11},{10,... | collective-permute-start | bytes 1327112 | tf_op jit(solution)/shard_map/ppermute | solution.py:519
  26.8 4.6 %shard_map.357 = (f32[1536,128]{1,0:T(8,128)S(1)}, bf16[256,768]{1,0:T(8,128)(2,1)S(1)}, f32[256,128]{1,0:T(8,128)S(1)}, f32[256,768]{1,0:T(8,128)S(1)}, f32[256,128]{1,0:T(8,128)S(1)}) custom-call(f32[1536,128]{1,0:T(8,128)S(1)} %get-tuple-element.317.normed_ref, f32[256,768]{1,0:T(8,128)S(1)} %get-tuple-element.318.init_ref, ...), custom_call_target="tpu_custom_call" | custom-call | flops 327155712 | bytes 5838336 | tf_op jit(solution)/shard_map/pallas_call | solution.py:71
  31.4 2.9 %collective-permute-done.8 = bf16[384,384]{1,0:T(8,128)(2,1)S(1)} collective-permute-done((bf16[384,384]{1,0:T(8,128)(2,1)S(1)}, bf16[384,384]{1,0:T(8,128)(2,1)S(1)}, u32[]{:S(2)}, u32[]{:S(2)}) %collective-permute-start.8) | collective-permute-done | bytes 294944 | tf_op jit(solution)/shard_map/ppermute | solution.py:519
  35.4 4.1 %collective-permute-done.11 = bf16[384,384]{1,0:T(8,128)(2,1)S(1)} collective-permute-done((bf16[384,384]{1,0:T(8,128)(2,1)S(1)}, bf16[384,384]{1,0:T(8,128)(2,1)S(1)}, u32[]{:S(2)}, u32[]{:S(2)}) %collective-permute-start.11) | collective-permute-done | bytes 294944 | tf_op jit(solution)/shard_map/ppermute | solution.py:519
  39.5 1.6 collective-permute-done.9
  42.1 1.6 collective-permute-start.14
  43.7 1.7 collective-permute-start.16
  48.1 4.4 %collective-permute-done.16 = bf16[192,768]{1,0:T(8,128)(2,1)S(1)} collective-permute-done((bf16[192,768]{1,0:T(8,128)(2,1)S(1)}, bf16[192,768]{1,0:T(8,128)(2,1)S(1)}, u32[]{:S(2)}, u32[]{:S(2)}) %collective-permute-start.16) | collective-permute-done | bytes 294944 | tf_op jit(solution)/shard_map/ppermute | solution.py:519
  58.6 2.2 shard_map.360
  60.8 2.7 %shard_map.361 = (f32[256,768]{1,0:T(8,128)S(1)}, f32[256,768]{1,0:T(8,128)S(1)}, bf16[1536,384]{1,0:T(8,128)(2,1)S(1)}, bf16[1536,384]{1,0:T(8,128)(2,1)S(1)}) custom-call(bf16[256,768]{1,0:T(8,128)(2,1)S(1)} %get-tuple-element.393.second_ref, bf16[256,768]{1,0:T(8,128)(2,1)S(1)} %bitcast.82, bf16[768,384]{1,0:T(8,128)(2,1)S(1)} %copy-done.8, ...), custom_call_target="tpu_custom_call" | custom-call | flops 1811939328 | bytes 7077888 | tf_op jit(solution)/shard_map/pallas_call | solution.py:71
  64.6 2.0 collective-permute-done.19.ob_ref
  66.7 2.7 %shard_map.362 = (f32[256,768]{1,0:T(8,128)S(1)}, f32[256,768]{1,0:T(8,128)S(1)}, bf16[1536,384]{1,0:T(8,128)(2,1)S(1)}, bf16[1536,384]{1,0:T(8,128)(2,1)S(1)}) custom-call(bf16[256,768]{1,0:T(8,128)(2,1)S(1)} %get-tuple-element.393.second_ref, bf16[256,768]{1,0:T(8,128)(2,1)S(1)} %bitcast.83, bf16[768,384]{1,0:T(8,128)(2,1)S(1)} %maximum_select_fusion.7.ia_ref, ...), custom_call_target="tpu_custom_call" | custom-call | flops 1811939328 | bytes 7077888 | tf_op jit(solution)/shard_map/pallas_call | solution.py:71
  69.8 2.5 %collective-permute-done.22 = bf16[1536,384]{1,0:T(8,128)(2,1)S(1)} collective-permute-done((bf16[1536,384]{1,0:T(8,128)(2,1)S(1)}, bf16[1536,384]{1,0:T(8,128)(2,1)S(1)}, u32[]{:S(2)}, u32[]{:S(2)}) %collective-permute-start.22) | collective-permute-done | bytes 1179680 | tf_op jit(solution)/shard_map/ppermute | solution.py:519
  72.8 1.8 collective-permute-start.23
  74.7 1.6 collective-permute-start.24
  76.5 14.8 %shard_map.363 = (bf16[256,768]{1,0:T(8,128)(2,1)}, f32[256,768]{1,0:T(8,128)S(1)}, f32[1,768]{1,0:T(1,128)S(1)}, bf16[2,896,384]{2,1,0:T(8,128)(2,1)S(1)}, bf16...) custom-call(s32[4]{0:T(128)S(1)} %xor_multiply_fusion.offs_ref.refs_, ...), custom_call_target="tpu_custom_call" | custom-call | flops 5435817984 | bytes 39038480 | tf_op jit(solution)/shard_map/pallas_call | solution.py:71
  94.2 3.7 %collective-permute-done.26 = bf16[2,896,384]{2,1,0:T(8,128)(2,1)S(1)} collective-permute-done((bf16[2,896,384]{2,1,0:T(8,128)(2,1)S(1)}, bf16[2,896,384]{2,1,0:T(8,128)(2,1)S(1)}, u32[]{:S(2)}, u32[]{:S(2)}) %collective-permute-start.26) | collective-permute-done | bytes 1376288 | tf_op jit(solution)/shard_map/ppermute | solution.py:519
  104.7 1.6 collective-permute-start.35
  106.5 6.3 %collective-permute-done.31.far_ref = f32[64,768]{1,0:T(8,128)S(1)} collective-permute-done((f32[64,768]{1,0:T(8,128)S(1)}, f32[64,768]{1,0:T(8,128)S(1)}, u32[]{:S(2)}, u32[]{:S(2)}) %collective-permute-start.31) | collective-permute-done | bytes 196640 | tf_op jit(solution)/shard_map/ppermute | solution.py:524
  112.9 4.1 %collective-permute-done.32 = bf16[896,384]{1,0:T(8,128)(2,1)S(1)} collective-permute-done((bf16[896,384]{1,0:T(8,128)(2,1)S(1)}, bf16[896,384]{1,0:T(8,128)(2,1)S(1)}, u32[]{:S(2)}, u32[]{:S(2)}) %collective-permute-start.32) | collective-permute-done | bytes 688160 | tf_op jit(solution)/shard_map/ppermute | solution.py:519
  117.6 8.5 %shard_map.364 = (bf16[256,768]{1,0:T(8,128)(2,1)}, f32[40,768]{1,0:T(8,128)S(1)}) custom-call(f32[1536,128]{1,0:T(8,128)S(1)} %get-tuple-element.439.pg_ref, f32[1536,128]{1,0:T(8,128)S(1)} %get-tuple-element.317.normed_ref, f32[256,768]{1,0:T(8,128)S(1)} %get-tuple-element.440.im_ref, f32[256,768]{1,0:T(8,128)S(1)} %get-tuple-element.441.iv_ref, ...), custom_call_target="tpu_custom_call" | custom-call | flops 50331648 | bytes 6363136 | tf_op jit(solution)/shard_map/pallas_call | solution.py:71
  126.4 2.6 %collective-permute-done.35 = bf16[768,384]{1,0:T(8,128)(2,1)S(1)} collective-permute-done((bf16[768,384]{1,0:T(8,128)(2,1)S(1)}, bf16[768,384]{1,0:T(8,128)(2,1)S(1)}, u32[]{:S(2)}, u32[]{:S(2)}) %collective-permute-start.35) | collective-permute-done | bytes 589856 | tf_op jit(solution)/shard_map/ppermute | solution.py:519
  132.7 4.2 %collective-permute-done.36 = bf16[224,384]{1,0:T(8,128)(2,1)S(1)} collective-permute-done((bf16[224,384]{1,0:T(8,128)(2,1)S(1)}, bf16[224,384]{1,0:T(8,128)(2,1)S(1)}, u32[]{:S(2)}, u32[]{:S(2)}) %collective-permute-start.36) | collective-permute-done | bytes 172064 | tf_op jit(solution)/shard_map/ppermute | solution.py:519
  137.0 2.7 %collective-permute-start.44 = (bf16[224,384]{1,0:T(8,128)(2,1)S(1)}, bf16[224,384]{1,0:T(8,128)(2,1)S(1)}, u32[]{:S(2)}, u32[]{:S(2)}) collective-permute-start(bf16[224,384]{1,0:T(8,128)(2,1)S(1)} %fusion.39), channel_id=1, source_target_pairs={{0,16},{4,20},{8,24},{12,28},{16,0},{20,4},{24,8},{28,12},{1,17},{... | collective-permute-start | bytes 516104 | tf_op jit(solution)/shard_map/ppermute | solution.py:519
  141.6 7.1 %collective-permute-done.38 = bf16[768,384]{1,0:T(8,128)(2,1)S(1)} collective-permute-done((bf16[768,384]{1,0:T(8,128)(2,1)S(1)}, bf16[768,384]{1,0:T(8,128)(2,1)S(1)}, u32[]{:S(2)}, u32[]{:S(2)}) %collective-permute-start.38) | collective-permute-done | bytes 589856 | tf_op jit(solution)/shard_map/ppermute | solution.py:519
  149.0 1.9 collective-permute-done.44
  151.0 1.7 collective-permute-done.43
  152.7 2.6 %collective-permute-start.45 = (bf16[192,384]{1,0:T(8,128)(2,1)S(1)}, bf16[192,384]{1,0:T(8,128)(2,1)S(1)}, u32[]{:S(2)}, u32[]{:S(2)}) collective-permute-start(bf16[192,384]{1,0:T(8,128)(2,1)S(1)} %fusion.38), channel_id=1, source_target_pairs={{0,16},{4,20},{8,24},{12,28},{16,0},{20,4},{24,8},{28,12},{1,17},{... | collective-permute-start | bytes 442376 | tf_op jit(solution)/shard_map/ppermute | solution.py:519
  155.6 1.6 collective-permute-start.47
  160.2 1.6 collective-permute-start.46
  163.5 6.9 %collective-permute-done.51 = bf16[480,128]{1,0:T(8,128)(2,1)S(1)} collective-permute-done((bf16[480,128]{1,0:T(8,128)(2,1)S(1)}, bf16[480,128]{1,0:T(8,128)(2,1)S(1)}, u32[]{:S(2)}, u32[]{:S(2)}) %collective-permute-start.51) | collective-permute-done | bytes 122912 | tf_op jit(solution)/shard_map/ppermute | solution.py:519
  170.4 1.7 collective-permute-start.49
  173.4 3.7 %collective-permute-done.49 = bf16[192,384]{1,0:T(8,128)(2,1)S(1)} collective-permute-done((bf16[192,384]{1,0:T(8,128)(2,1)S(1)}, bf16[192,384]{1,0:T(8,128)(2,1)S(1)}, u32[]{:S(2)}, u32[]{:S(2)}) %collective-permute-start.49) | collective-permute-done | bytes 147488 | tf_op jit(solution)/shard_map/ppermute | solution.py:519
  177.1 1.7 collective-permute-start.52
  179.8 2.1 collective-permute-start.53
  181.9 2.5 %collective-permute-start.56 = (bf16[384,384]{1,0:T(8,128)(2,1)S(1)}, bf16[384,384]{1,0:T(8,128)(2,1)S(1)}, u32[]{:S(2)}, u32[]{:S(2)}) collective-permute-start(bf16[384,384]{1,0:T(8,128)(2,1)S(1)} %fusion.13), channel_id=1, source_target_pairs={{0,16},{4,20},{8,24},{12,28},{16,0},{20,4},{24,8},{28,12},{1,17},{... | collective-permute-start | bytes 884744 | tf_op jit(solution)/shard_map/ppermute | solution.py:519
  185.7 16.5 %collective-permute-done.56 = bf16[384,384]{1,0:T(8,128)(2,1)S(1)} collective-permute-done((bf16[384,384]{1,0:T(8,128)(2,1)S(1)}, bf16[384,384]{1,0:T(8,128)(2,1)S(1)}, u32[]{:S(2)}, u32[]{:S(2)}) %collective-permute-start.56) | collective-permute-done | bytes 294944 | tf_op jit(solution)/shard_map/ppermute | solution.py:519
  203.2 3.8 %collective-permute-start.61 = (bf16[384,384]{1,0:T(8,128)(2,1)S(1)}, bf16[384,384]{1,0:T(8,128)(2,1)S(1)}, u32[]{:S(2)}, u32[]{:S(2)}) collective-permute-start(bf16[384,384]{1,0:T(8,128)(2,1)S(1)} %add_convert_fusion.2), channel_id=1, source_target_pairs={{0,8},{4,12},{8,0},{12,4},{16,24},{20,28},{24,16},{28,20},{1,9},{5... | collective-permute-start | bytes 884744 | tf_op jit(solution)/shard_map/ppermute | solution.py:519
  207.8 1.7 collective-permute-start.57
  211.0 1.8 collective-permute-start.58
  213.6 3.8 %collective-permute-done.57 = bf16[480,128]{1,0:T(8,128)(2,1)S(1)} collective-permute-done((bf16[480,128]{1,0:T(8,128)(2,1)S(1)}, bf16[480,128]{1,0:T(8,128)(2,1)S(1)}, u32[]{:S(2)}, u32[]{:S(2)}) %collective-permute-start.57) | collective-permute-done | bytes 122912 | tf_op jit(solution)/shard_map/ppermute | solution.py:519
  221.7 6.7 %collective-permute-done.62 = bf16[768,384]{1,0:T(8,128)(2,1)S(1)} collective-permute-done((bf16[768,384]{1,0:T(8,128)(2,1)S(1)}, bf16[768,384]{1,0:T(8,128)(2,1)S(1)}, u32[]{:S(2)}, u32[]{:S(2)}) %collective-permute-start.62) | collective-permute-done | bytes 589856 | tf_op jit(solution)/shard_map/ppermute | solution.py:519
  (278 shorter events, 59.0 us)
Async XLA Ops:
  3.0 13.5 %collective-permute-start.6 = (bf16[384,384]{1,0:T(8,128)(2,1)S(1)}, bf16[384,384]{1,0:T(8,128)(2,1)S(1)}, u32[]{:S(2)}, u32[]{:S(2)}) collective-permute-start(bf16[384,384]{1,0:T(8,128)(2,1)S(1)} %slice_select_fusion.3), channel_id=1, source_target_pairs={{0,2},{1,3},{2,0},{3,1},{4,6},{5,7},{6,4},{7,5},{8,10},{9,11},{10,... | collective-permute-start | bytes 884744 | tf_op jit(solution)/shard_map/ppermute | solution.py:519
  7.3 12.4 %collective-permute-start.5 = (bf16[384,384]{1,0:T(8,128)(2,1)S(1)}, bf16[384,384]{1,0:T(8,128)(2,1)S(1)}, u32[]{:S(2)}, u32[]{:S(2)}) collective-permute-start(bf16[384,384]{1,0:T(8,128)(2,1)S(1)} %slice_select_fusion.4), channel_id=1, source_target_pairs={{0,2},{1,3},{2,0},{3,1},{4,6},{5,7},{6,4},{7,5},{8,10},{9,11},{10,... | collective-permute-start | bytes 884744 | tf_op jit(solution)/shard_map/ppermute | solution.py:519
  11.6 8.1 %collective-permute-start.4 = (f32[32,768]{1,0:T(8,128)S(1)}, f32[32,768]{1,0:T(8,128)S(1)}, u32[]{:S(2)}, u32[]{:S(2)}) collective-permute-start(f32[32,768]{1,0:T(8,128)S(1)} %get-tuple-element.321), channel_id=1, source_target_pairs={{0,1},{1,2},{2,3},{4,5},{5,6},{6,7},{8,9},{9,10},{10,11},{12,13},{... | collective-permute-start | bytes 294920 | tf_op jit(solution)/shard_map/ppermute | solution.py:524
  13.4 8.4 %collective-permute-start.7 = (f32[32,768]{1,0:T(8,128)S(1)}, f32[32,768]{1,0:T(8,128)S(1)}, u32[]{:S(2)}, u32[]{:S(2)}) collective-permute-start(f32[32,768]{1,0:T(8,128)S(1)} %get-tuple-element.321), channel_id=1, source_target_pairs={{0,2},{1,3},{4,6},{5,7},{8,10},{9,11},{12,14},{13,15},{16,18},{17,... | collective-permute-start | bytes 294920 | tf_op jit(solution)/shard_map/ppermute | solution.py:524
  21.8 17.7 %collective-permute-start.10 = (bf16[288,768]{1,0:T(8,128)(2,1)S(1)}, bf16[288,768]{1,0:T(8,128)(2,1)S(1)}, u32[]{:S(2)}, u32[]{:S(2)}) collective-permute-start(bf16[288,768]{1,0:T(8,128)(2,1)S(1)} %slice_select_fusion), channel_id=1, source_target_pairs={{0,2},{1,3},{2,0},{3,1},{4,6},{5,7},{6,4},{7,5},{8,10},{9,11},{10,... | collective-permute-start | bytes 1327112 | tf_op jit(solution)/shard_map/ppermute | solution.py:519
  24.4 9.9 %collective-permute-start.8 = (bf16[384,384]{1,0:T(8,128)(2,1)S(1)}, bf16[384,384]{1,0:T(8,128)(2,1)S(1)}, u32[]{:S(2)}, u32[]{:S(2)}) collective-permute-start(bf16[384,384]{1,0:T(8,128)(2,1)S(1)} %collective-permute-done.6), channel_id=1, source_target_pairs={{0,4},{4,0},{8,12},{12,8},{16,20},{20,16},{24,28},{28,24},{1,5},{5... | collective-permute-start | bytes 884744 | tf_op jit(solution)/shard_map/ppermute | solution.py:519
  26.1 13.4 %collective-permute-start.11 = (bf16[384,384]{1,0:T(8,128)(2,1)S(1)}, bf16[384,384]{1,0:T(8,128)(2,1)S(1)}, u32[]{:S(2)}, u32[]{:S(2)}) collective-permute-start(bf16[384,384]{1,0:T(8,128)(2,1)S(1)} %collective-permute-done.5), channel_id=1, source_target_pairs={{0,4},{4,0},{8,12},{12,8},{16,20},{20,16},{24,28},{28,24},{1,5},{5... | collective-permute-start | bytes 884744 | tf_op jit(solution)/shard_map/ppermute | solution.py:519
  26.7 14.4 %collective-permute-start.9 = (bf16[384,384]{1,0:T(8,128)(2,1)S(1)}, bf16[384,384]{1,0:T(8,128)(2,1)S(1)}, u32[]{:S(2)}, u32[]{:S(2)}) collective-permute-start(bf16[384,384]{1,0:T(8,128)(2,1)S(1)} %slice_select_fusion.2), channel_id=1, source_target_pairs={{0,2},{1,3},{2,0},{3,1},{4,6},{5,7},{6,4},{7,5},{8,10},{9,11},{10,... | collective-permute-start | bytes 884744 | tf_op jit(solution)/shard_map/ppermute | solution.py:519
  42.1 12.2 %collective-permute-start.14 = (bf16[288,768]{1,0:T(8,128)(2,1)S(1)}, bf16[288,768]{1,0:T(8,128)(2,1)S(1)}, u32[]{:S(2)}, u32[]{:S(2)}) collective-permute-start(bf16[288,768]{1,0:T(8,128)(2,1)S(1)} %collective-permute-done.10), channel_id=1, source_target_pairs={{0,8},{4,12},{8,0},{12,4},{16,24},{20,28},{24,16},{28,20},{1,9},{5... | collective-permute-start | bytes 1327112 | tf_op jit(solution)/shard_map/ppermute | solution.py:519
  43.7 8.7 %collective-permute-start.16 = (bf16[192,768]{1,0:T(8,128)(2,1)S(1)}, bf16[192,768]{1,0:T(8,128)(2,1)S(1)}, u32[]{:S(2)}, u32[]{:S(2)}) collective-permute-start(bf16[192,768]{1,0:T(8,128)(2,1)S(1)} %slice_select_fusion.1), channel_id=1, source_target_pairs={{0,2},{1,3},{2,0},{3,1},{4,6},{5,7},{6,4},{7,5},{8,10},{9,11},{10,... | collective-permute-start | bytes 884744 | tf_op jit(solution)/shard_map/ppermute | solution.py:519
  45.4 8.4 %collective-permute-start.15 = (bf16[384,384]{1,0:T(8,128)(2,1)S(1)}, bf16[384,384]{1,0:T(8,128)(2,1)S(1)}, u32[]{:S(2)}, u32[]{:S(2)}) collective-permute-start(bf16[384,384]{1,0:T(8,128)(2,1)S(1)} %collective-permute-done.9), channel_id=1, source_target_pairs={{0,4},{4,0},{8,12},{12,8},{16,20},{20,16},{24,28},{28,24},{1,5},{5... | collective-permute-start | bytes 884744 | tf_op jit(solution)/shard_map/ppermute | solution.py:519
  55.3 9.0 %collective-permute-start.18 = (bf16[192,768]{1,0:T(8,128)(2,1)S(1)}, bf16[192,768]{1,0:T(8,128)(2,1)S(1)}, u32[]{:S(2)}, u32[]{:S(2)}) collective-permute-start(bf16[192,768]{1,0:T(8,128)(2,1)S(1)} %collective-permute-done.16), channel_id=1, source_target_pairs={{0,4},{4,0},{8,12},{12,8},{16,20},{20,16},{24,28},{28,24},{1,5},{5... | collective-permute-start | bytes 884744 | tf_op jit(solution)/shard_map/ppermute | solution.py:519
  57.0 7.6 %collective-permute-start.20 = (bf16[768,384]{1,0:T(8,128)(2,1)S(1)}, bf16[768,384]{1,0:T(8,128)(2,1)S(1)}, u32[]{:S(2)}, u32[]{:S(2)}) collective-permute-start(bf16[768,384]{1,0:T(8,128)(2,1)S(1)} %maximum_select_fusion.7.ia_ref), channel_id=1, source_target_pairs={{0,1},{1,0},{2,3},{3,2},{4,5},{5,4},{6,7},{7,6},{8,9},{9,8},{10,11... | collective-permute-start | bytes 1769480 | tf_op jit(solution)/shard_map/ppermute | solution.py:519
  72.8 18.5 %collective-permute-start.23 = (bf16[768,384]{1,0:T(8,128)(2,1)S(1)}, bf16[768,384]{1,0:T(8,128)(2,1)S(1)}, u32[]{:S(2)}, u32[]{:S(2)}) collective-permute-start(bf16[768,384]{1,0:T(8,128)(2,1)S(1)} %get-tuple-element.446), channel_id=1, source_target_pairs={{0,2},{1,3},{2,0},{3,1},{4,6},{5,7},{6,4},{7,5},{8,10},{9,11},{10,... | collective-permute-start | bytes 1769480 | tf_op jit(solution)/shard_map/ppermute | solution.py:519
  74.7 16.6 %collective-permute-start.24 = (bf16[768,384]{1,0:T(8,128)(2,1)S(1)}, bf16[768,384]{1,0:T(8,128)(2,1)S(1)}, u32[]{:S(2)}, u32[]{:S(2)}) collective-permute-start(bf16[768,384]{1,0:T(8,128)(2,1)S(1)} %pad_maximum_fusion.3), channel_id=1, source_target_pairs={{0,8},{4,12},{8,0},{12,4},{16,24},{20,28},{24,16},{28,20},{1,9},{5... | collective-permute-start | bytes 1769480 | tf_op jit(solution)/shard_map/ppermute | solution.py:519
  91.3 7.8 %collective-permute-start.28 = (bf16[2,1536,384]{2,1,0:T(8,128)(2,1)S(1)}, bf16[2,1536,384]{2,1,0:T(8,128)(2,1)S(1)}, u32[]{:S(2)}, u32[]{:S(2)}) collective-permute-start(bf16[2,1536,384]{2,1,0:T(8,128)(2,1)S(1)} %get-tuple-element.465), channel_id=1, source_target_pairs={{0,1},{1,0},{2,3},{3,2},{4,5},{5,4},{6,7},{7,6},{8,9},{9,8},{10,11... | collective-permute-start | bytes 7077896 | tf_op jit(solution)/shard_map/ppermute | solution.py:519
  92.4 9.3 %collective-permute-start.25 = (bf16[384,384]{1,0:T(8,128)(2,1)S(1)}, bf16[384,384]{1,0:T(8,128)(2,1)S(1)}, u32[]{:S(2)}, u32[]{:S(2)}) collective-permute-start(bf16[384,384]{1,0:T(8,128)(2,1)S(1)} %select_convert_fusion.7), channel_id=1, source_target_pairs={{0,4},{4,0},{8,12},{12,8},{16,20},{20,16},{24,28},{28,24},{1,5},{5... | collective-permute-start | bytes 884744 | tf_op jit(solution)/shard_map/ppermute | solution.py:519
  93.9 10.7 %collective-permute-start.30 = (bf16[384,384]{1,0:T(8,128)(2,1)S(1)}, bf16[384,384]{1,0:T(8,128)(2,1)S(1)}, u32[]{:S(2)}, u32[]{:S(2)}) collective-permute-start(bf16[384,384]{1,0:T(8,128)(2,1)S(1)} %fusion.10), channel_id=1, source_target_pairs={{0,2},{1,3},{2,0},{3,1},{4,6},{5,7},{6,4},{7,5},{8,10},{9,11},{10,... | collective-permute-start | bytes 884744 | tf_op jit(solution)/shard_map/ppermute | solution.py:519
  98.6 18.3 %collective-permute-start.32 = (bf16[896,384]{1,0:T(8,128)(2,1)S(1)}, bf16[896,384]{1,0:T(8,128)(2,1)S(1)}, u32[]{:S(2)}, u32[]{:S(2)}) collective-permute-start(bf16[896,384]{1,0:T(8,128)(2,1)S(1)} %pad_maximum_fusion.2), channel_id=1, source_target_pairs={{0,8},{4,12},{8,0},{12,4},{16,24},{20,28},{24,16},{28,20},{1,9},{5... | collective-permute-start | bytes 2064392 | tf_op jit(solution)/shard_map/ppermute | solution.py:519
  100.1 29.4 %collective-permute-start.34 = (bf16[1536,384]{1,0:T(8,128)(2,1)S(1)}, bf16[1536,384]{1,0:T(8,128)(2,1)S(1)}, u32[]{:S(2)}, u32[]{:S(2)}) collective-permute-start(bf16[1536,384]{1,0:T(8,128)(2,1)S(1)} %pad_maximum_fusion.1), channel_id=1, source_target_pairs={{0,4},{4,0},{8,12},{12,8},{16,20},{20,16},{24,28},{28,24},{1,5},{5... | collective-permute-start | bytes 3538952 | tf_op jit(solution)/shard_map/ppermute | solution.py:519
  102.9 9.9 %collective-permute-start.31 = (f32[64,768]{1,0:T(8,128)S(1)}, f32[64,768]{1,0:T(8,128)S(1)}, u32[]{:S(2)}, u32[]{:S(2)}) collective-permute-start(f32[64,768]{1,0:T(8,128)S(1)} %pad_maximum_fusion.6), channel_id=1, source_target_pairs={{2,0},{3,1},{6,4},{7,5},{10,8},{11,9},{14,12},{15,13},{18,16},{19,... | collective-permute-start | bytes 589832 | tf_op jit(solution)/shard_map/ppermute | solution.py:524
  104.7 24.3 %collective-permute-start.35 = (bf16[768,384]{1,0:T(8,128)(2,1)S(1)}, bf16[768,384]{1,0:T(8,128)(2,1)S(1)}, u32[]{:S(2)}, u32[]{:S(2)}) collective-permute-start(bf16[768,384]{1,0:T(8,128)(2,1)S(1)} %pad_maximum_fusion.4), channel_id=1, source_target_pairs={{0,8},{4,12},{8,0},{12,4},{16,24},{20,28},{24,16},{28,20},{1,9},{5... | collective-permute-start | bytes 1769480 | tf_op jit(solution)/shard_map/ppermute | solution.py:519
  117.2 9.0 %collective-permute-start.33 = (bf16[448,384]{1,0:T(8,128)(2,1)S(1)}, bf16[448,384]{1,0:T(8,128)(2,1)S(1)}, u32[]{:S(2)}, u32[]{:S(2)}) collective-permute-start(bf16[448,384]{1,0:T(8,128)(2,1)S(1)} %fusion.3), channel_id=1, source_target_pairs={{0,2},{1,3},{2,0},{3,1},{4,6},{5,7},{6,4},{7,5},{8,10},{9,11},{10,... | collective-permute-start | bytes 1032200 | tf_op jit(solution)/shard_map/ppermute | solution.py:519
  129.6 7.3 %collective-permute-start.36 = (bf16[224,384]{1,0:T(8,128)(2,1)S(1)}, bf16[224,384]{1,0:T(8,128)(2,1)S(1)}, u32[]{:S(2)}, u32[]{:S(2)}) collective-permute-start(bf16[224,384]{1,0:T(8,128)(2,1)S(1)} %select_convert_fusion.10), channel_id=1, source_target_pairs={{0,4},{4,0},{8,12},{12,8},{16,20},{20,16},{24,28},{28,24},{1,5},{5... | collective-permute-start | bytes 516104 | tf_op jit(solution)/shard_map/ppermute | solution.py:519
  131.4 8.2 %collective-permute-start.39 = (bf16[192,384]{1,0:T(8,128)(2,1)S(1)}, bf16[192,384]{1,0:T(8,128)(2,1)S(1)}, u32[]{:S(2)}, u32[]{:S(2)}) collective-permute-start(bf16[192,384]{1,0:T(8,128)(2,1)S(1)} %select_convert_fusion.11), channel_id=1, source_target_pairs={{0,8},{4,12},{8,0},{12,4},{16,24},{20,28},{24,16},{28,20},{1,9},{5... | collective-permute-start | bytes 442376 | tf_op jit(solution)/shard_map/ppermute | solution.py:519
  131.9 7.8 %collective-permute-start.40 = (bf16[192,384]{1,0:T(8,128)(2,1)S(1)}, bf16[192,384]{1,0:T(8,128)(2,1)S(1)}, u32[]{:S(2)}, u32[]{:S(2)}) collective-permute-start(bf16[192,384]{1,0:T(8,128)(2,1)S(1)} %select_convert_fusion.12), channel_id=1, source_target_pairs={{0,4},{4,0},{8,12},{12,8},{16,20},{20,16},{24,28},{28,24},{1,5},{5... | collective-permute-start | bytes 442376 | tf_op jit(solution)/shard_map/ppermute | solution.py:519
  132.5 16.2 %collective-permute-start.38 = (bf16[768,384]{1,0:T(8,128)(2,1)S(1)}, bf16[768,384]{1,0:T(8,128)(2,1)S(1)}, u32[]{:S(2)}, u32[]{:S(2)}) collective-permute-start(bf16[768,384]{1,0:T(8,128)(2,1)S(1)} %fusion.1), channel_id=1, source_target_pairs={{0,2},{1,3},{2,0},{3,1},{4,6},{5,7},{6,4},{7,5},{8,10},{9,11},{10,... | collective-permute-start | bytes 1769480 | tf_op jit(solution)/shard_map/ppermute | solution.py:519
  137.0 13.9 %collective-permute-start.44 = (bf16[224,384]{1,0:T(8,128)(2,1)S(1)}, bf16[224,384]{1,0:T(8,128)(2,1)S(1)}, u32[]{:S(2)}, u32[]{:S(2)}) collective-permute-start(bf16[224,384]{1,0:T(8,128)(2,1)S(1)} %fusion.39), channel_id=1, source_target_pairs={{0,16},{4,20},{8,24},{12,28},{16,0},{20,4},{24,8},{28,12},{1,17},{... | collective-permute-start | bytes 516104 | tf_op jit(solution)/shard_map/ppermute | solution.py:519
  139.8 12.9 %collective-permute-start.43 = (bf16[384,384]{1,0:T(8,128)(2,1)S(1)}, bf16[384,384]{1,0:T(8,128)(2,1)S(1)}, u32[]{:S(2)}, u32[]{:S(2)}) collective-permute-start(bf16[384,384]{1,0:T(8,128)(2,1)S(1)} %get-tuple-element.535), channel_id=1, source_target_pairs={{0,2},{1,3},{2,0},{3,1},{4,6},{5,7},{6,4},{7,5},{8,10},{9,11},{10,... | collective-permute-start | bytes 884744 | tf_op jit(solution)/shard_map/ppermute | solution.py:519
  140.1 15.2 %collective-permute-start.42 = (bf16[192,384]{1,0:T(8,128)(2,1)S(1)}, bf16[192,384]{1,0:T(8,128)(2,1)S(1)}, u32[]{:S(2)}, u32[]{:S(2)}) collective-permute-start(bf16[192,384]{1,0:T(8,128)(2,1)S(1)} %fusion.37), channel_id=1, source_target_pairs={{0,16},{4,20},{8,24},{12,28},{16,0},{20,4},{24,8},{28,12},{1,17},{... | collective-permute-start | bytes 442376 | tf_op jit(solution)/shard_map/ppermute | solution.py:519
  152.7 9.2 %collective-permute-start.45 = (bf16[192,384]{1,0:T(8,128)(2,1)S(1)}, bf16[192,384]{1,0:T(8,128)(2,1)S(1)}, u32[]{:S(2)}, u32[]{:S(2)}) collective-permute-start(bf16[192,384]{1,0:T(8,128)(2,1)S(1)} %fusion.38), channel_id=1, source_target_pairs={{0,16},{4,20},{8,24},{12,28},{16,0},{20,4},{24,8},{28,12},{1,17},{... | collective-permute-start | bytes 442376 | tf_op jit(solution)/shard_map/ppermute | solution.py:519
  155.6 23.4 %collective-permute-start.47 = (bf16[384,384]{1,0:T(8,128)(2,1)S(1)}, bf16[384,384]{1,0:T(8,128)(2,1)S(1)}, u32[]{:S(2)}, u32[]{:S(2)}) collective-permute-start(bf16[384,384]{1,0:T(8,128)(2,1)S(1)} %select_convert_fusion.4), channel_id=1, source_target_pairs={{0,8},{4,12},{8,0},{12,4},{16,24},{20,28},{24,16},{28,20},{1,9},{5... | collective-permute-start | bytes 884744 | tf_op jit(solution)/shard_map/ppermute | solution.py:519
  157.1 22.0 %collective-permute-start.48 = (bf16[224,384]{1,0:T(8,128)(2,1)S(1)}, bf16[224,384]{1,0:T(8,128)(2,1)S(1)}, u32[]{:S(2)}, u32[]{:S(2)}) collective-permute-start(bf16[224,384]{1,0:T(8,128)(2,1)S(1)} %add_convert_fusion.3), channel_id=1, source_target_pairs={{0,4},{4,0},{8,12},{12,8},{16,20},{20,16},{24,28},{28,24},{1,5},{5... | collective-permute-start | bytes 516104 | tf_op jit(solution)/shard_map/ppermute | solution.py:519
  158.8 21.0 %collective-permute-start.50 = (bf16[384,384]{1,0:T(8,128)(2,1)S(1)}, bf16[384,384]{1,0:T(8,128)(2,1)S(1)}, u32[]{:S(2)}, u32[]{:S(2)}) collective-permute-start(bf16[384,384]{1,0:T(8,128)(2,1)S(1)} %get-tuple-element.564), channel_id=1, source_target_pairs={{0,4},{4,0},{8,12},{12,8},{16,20},{20,16},{24,28},{28,24},{1,5},{5... | collective-permute-start | bytes 884744 | tf_op jit(solution)/shard_map/ppermute | solution.py:519
  160.2 12.1 %collective-permute-start.46 = (bf16[192,384]{1,0:T(8,128)(2,1)S(1)}, bf16[192,384]{1,0:T(8,128)(2,1)S(1)}, u32[]{:S(2)}, u32[]{:S(2)}) collective-permute-start(bf16[192,384]{1,0:T(8,128)(2,1)S(1)} %add_convert_fusion.5), channel_id=1, source_target_pairs={{0,8},{4,12},{8,0},{12,4},{16,24},{20,28},{24,16},{28,20},{1,9},{5... | collective-permute-start | bytes 442376 | tf_op jit(solution)/shard_map/ppermute | solution.py:519
  161.9 8.5 %collective-permute-start.51 = (bf16[480,128]{1,0:T(8,128)(2,1)S(1)}, bf16[480,128]{1,0:T(8,128)(2,1)S(1)}, u32[]{:S(2)}, u32[]{:S(2)}) collective-permute-start(bf16[480,128]{1,0:T(8,128)(2,1)S(1)} %pad_maximum_fusion.9), channel_id=1, source_target_pairs={{0,4},{4,0},{8,12},{12,8},{16,20},{20,16},{24,28},{28,24},{1,5},{5... | collective-permute-start | bytes 368648 | tf_op jit(solution)/shard_map/ppermute | solution.py:519
  172.2 9.7 %collective-permute-start.55 = (bf16[480,128]{1,0:T(8,128)(2,1)S(1)}, bf16[480,128]{1,0:T(8,128)(2,1)S(1)}, u32[]{:S(2)}, u32[]{:S(2)}) collective-permute-start(bf16[480,128]{1,0:T(8,128)(2,1)S(1)} %pad_maximum_fusion.10), channel_id=1, source_target_pairs={{0,8},{4,12},{8,0},{12,4},{16,24},{20,28},{24,16},{28,20},{1,9},{5... | collective-permute-start | bytes 368648 | tf_op jit(solution)/shard_map/ppermute | solution.py:519
  177.1 7.4 %collective-permute-start.52 = (bf16[384,384]{1,0:T(8,128)(2,1)S(1)}, bf16[384,384]{1,0:T(8,128)(2,1)S(1)}, u32[]{:S(2)}, u32[]{:S(2)}) collective-permute-start(bf16[384,384]{1,0:T(8,128)(2,1)S(1)} %maximum_select_fusion.14), channel_id=1, source_target_pairs={{0,4},{4,0},{8,12},{12,8},{16,20},{20,16},{24,28},{28,24},{1,5},{5... | collective-permute-start | bytes 884744 | tf_op jit(solution)/shard_map/ppermute | solution.py:519
  178.9 23.9 %collective-permute-start.63 = (bf16[384,384]{1,0:T(8,128)(2,1)S(1)}, bf16[384,384]{1,0:T(8,128)(2,1)S(1)}, u32[]{:S(2)}, u32[]{:S(2)}) collective-permute-start(bf16[384,384]{1,0:T(8,128)(2,1)S(1)} %maximum_select_fusion.15), channel_id=1, source_target_pairs={{0,8},{4,12},{8,0},{12,4},{16,24},{20,28},{24,16},{28,20},{1,9},{5... | collective-permute-start | bytes 884744 | tf_op jit(solution)/shard_map/ppermute | solution.py:519
  179.1 23.9 %collective-permute-start.54 = (bf16[384,384]{1,0:T(8,128)(2,1)S(1)}, bf16[384,384]{1,0:T(8,128)(2,1)S(1)}, u32[]{:S(2)}, u32[]{:S(2)}) collective-permute-start(bf16[384,384]{1,0:T(8,128)(2,1)S(1)} %fusion.40), channel_id=1, source_target_pairs={{0,16},{4,20},{8,24},{12,28},{16,0},{20,4},{24,8},{28,12},{1,17},{... | collective-permute-start | bytes 884744 | tf_op jit(solution)/shard_map/ppermute | solution.py:519
  179.8 30.8 %collective-permute-start.53 = (bf16[448,384]{1,0:T(8,128)(2,1)S(1)}, bf16[448,384]{1,0:T(8,128)(2,1)S(1)}, u32[]{:S(2)}, u32[]{:S(2)}) collective-permute-start(bf16[448,384]{1,0:T(8,128)(2,1)S(1)} %maximum_select_fusion.13), channel_id=1, source_target_pairs={{0,8},{4,12},{8,0},{12,4},{16,24},{20,28},{24,16},{28,20},{1,9},{5... | collective-permute-start | bytes 1032200 | tf_op jit(solution)/shard_map/ppermute | solution.py:519
  181.9 20.2 %collective-permute-start.56 = (bf16[384,384]{1,0:T(8,128)(2,1)S(1)}, bf16[384,384]{1,0:T(8,128)(2,1)S(1)}, u32[]{:S(2)}, u32[]{:S(2)}) collective-permute-start(bf16[384,384]{1,0:T(8,128)(2,1)S(1)} %fusion.13), channel_id=1, source_target_pairs={{0,16},{4,20},{8,24},{12,28},{16,0},{20,4},{24,8},{28,12},{1,17},{... | collective-permute-start | bytes 884744 | tf_op jit(solution)/shard_map/ppermute | solution.py:519
  203.2 15.1 %collective-permute-start.61 = (bf16[384,384]{1,0:T(8,128)(2,1)S(1)}, bf16[384,384]{1,0:T(8,128)(2,1)S(1)}, u32[]{:S(2)}, u32[]{:S(2)}) collective-permute-start(bf16[384,384]{1,0:T(8,128)(2,1)S(1)} %add_convert_fusion.2), channel_id=1, source_target_pairs={{0,8},{4,12},{8,0},{12,4},{16,24},{20,28},{24,16},{28,20},{1,9},{5... | collective-permute-start | bytes 884744 | tf_op jit(solution)/shard_map/ppermute | solution.py:519
  207.0 13.3 %collective-permute-start.60 = (bf16[384,384]{1,0:T(8,128)(2,1)S(1)}, bf16[384,384]{1,0:T(8,128)(2,1)S(1)}, u32[]{:S(2)}, u32[]{:S(2)}) collective-permute-start(bf16[384,384]{1,0:T(8,128)(2,1)S(1)} %add_convert_fusion.1), channel_id=1, source_target_pairs={{0,8},{4,12},{8,0},{12,4},{16,24},{20,28},{24,16},{28,20},{1,9},{5... | collective-permute-start | bytes 884744 | tf_op jit(solution)/shard_map/ppermute | solution.py:519
  207.8 9.7 %collective-permute-start.57 = (bf16[480,128]{1,0:T(8,128)(2,1)S(1)}, bf16[480,128]{1,0:T(8,128)(2,1)S(1)}, u32[]{:S(2)}, u32[]{:S(2)}) collective-permute-start(bf16[480,128]{1,0:T(8,128)(2,1)S(1)} %maximum_add_fusion), channel_id=1, source_target_pairs={{0,16},{4,20},{8,24},{12,28},{16,0},{20,4},{24,8},{28,12},{1,17},{... | collective-permute-start | bytes 368648 | tf_op jit(solution)/shard_map/ppermute | solution.py:519
  211.0 10.4 %collective-permute-start.58 = (bf16[448,384]{1,0:T(8,128)(2,1)S(1)}, bf16[448,384]{1,0:T(8,128)(2,1)S(1)}, u32[]{:S(2)}, u32[]{:S(2)}) collective-permute-start(bf16[448,384]{1,0:T(8,128)(2,1)S(1)} %pad_maximum_fusion.5), channel_id=1, source_target_pairs={{0,2},{1,3},{2,0},{3,1},{4,6},{5,7},{6,4},{7,5},{8,10},{9,11},{10,... | collective-permute-start | bytes 1032200 | tf_op jit(solution)/shard_map/ppermute | solution.py:519
  218.5 9.9 %collective-permute-start.62 = (bf16[768,384]{1,0:T(8,128)(2,1)S(1)}, bf16[768,384]{1,0:T(8,128)(2,1)S(1)}, u32[]{:S(2)}, u32[]{:S(2)}) collective-permute-start(bf16[768,384]{1,0:T(8,128)(2,1)S(1)} %maximum_select_fusion.10), channel_id=1, source_target_pairs={{0,4},{4,0},{8,12},{12,8},{16,20},{20,16},{24,28},{28,24},{1,5},{5... | collective-permute-start | bytes 1769480 | tf_op jit(solution)/shard_map/ppermute | solution.py:519
  221.6 9.5 %collective-permute-start.59 = (bf16[896,384]{1,0:T(8,128)(2,1)S(1)}, bf16[896,384]{1,0:T(8,128)(2,1)S(1)}, u32[]{:S(2)}, u32[]{:S(2)}) collective-permute-start(bf16[896,384]{1,0:T(8,128)(2,1)S(1)} %maximum_select_fusion.4), channel_id=1, source_target_pairs={{0,1},{1,0},{2,3},{3,2},{4,5},{5,4},{6,7},{7,6},{8,9},{9,8},{10,11... | collective-permute-start | bytes 2064392 | tf_op jit(solution)/shard_map/ppermute | solution.py:519
  (37 other events, 255.9 us)
